TPU v7x, 32 devices: a whole 2x2x4 slice. The times are simulated.
32 devices in a mesh: seq: 2 (over x), ctx: 8 (over z, y), wt: 2 (over core).
Axes of the slice: x: 2, y: 2, z: 4, core: 2. Of those that a mesh axis runs over, the one named last changes fastest.
Arguments:
- tokens: bfloat16 [8, 1024, 1280], P('seq', 'ctx'), may hold values from -6 to 6
- segments: int32 [8, 1024], P('seq', 'ctx'), may hold values from 0 to 2, as said below
- adapter_index: int32 [8], P('seq'), may hold values from 0 to 7, each once
- w_attn_in: bfloat16 [3, 1280, 1280], P(None, None, 'wt'), may hold values from -0.15625 to 0.15625
- w_attn_out: bfloat16 [1280, 1280], P('wt'), may hold values from -0.15625 to 0.15625
- w_gate_up: bfloat16 [2, 1280, 5120], P(None, None, 'wt'), may hold values from -0.15625 to 0.15625
- w_down: bfloat16 [5120, 1280], P('wt'), may hold values from -0.078125 to 0.078125
- qk_scale: float32 [1280], P('wt'), may hold values from 1 to 2
- mix_rates: float32 [2, 1280], replicated, may hold values from 0.2 to 0.8
- mlp_scales: float32 [2, 5120], P(None, 'wt'), may hold values from 0.5 to 2
- a_model: bfloat16 [8, 5, 16, 1280], replicated, may hold values from -0.15625 to 0.15625
- b_model: bfloat16 [8, 2, 16, 1280], replicated, may hold values from -0.75 to 0.75
- a_heads: bfloat16 [8, 16, 20, 64], P(None, None, 'wt'), may hold values from -0.15625 to 0.15625
- b_heads: bfloat16 [8, 3, 16, 20, 64], P(None, None, None, 'wt'), may hold values from -0.75 to 0.75
- a_hidden: bfloat16 [8, 16, 40, 128], P(None, None, 'wt'), may hold values from -0.078125 to 0.078125
- b_hidden: bfloat16 [8, 2, 16, 40, 128], P(None, None, None, 'wt'), may hold values from -0.75 to 0.75
- cotangent: bfloat16 [8, 1024, 1280], P('seq', 'ctx'), may hold values from -6 to 6
Outputs:
- layer_out: bfloat16 [8, 1024, 1280], P('seq', 'ctx')
- input_grad: float32 [8, 1024, 1280], P('seq', 'ctx')
- grad_a_model: float32 [8, 5, 16, 1280], P(None, None, None, ('seq', 'ctx', 'wt'))
- grad_b_model: float32 [8, 2, 16, 1280], P(None, None, None, ('seq', 'ctx'))
- grad_a_heads: float32 [8, 16, 20, 64], P(None, None, 'wt', ('seq', 'ctx'))
- grad_b_heads: float32 [8, 3, 16, 20, 64], P(None, None, None, 'wt', ('seq', 'ctx'))
- grad_a_hidden: float32 [8, 16, 40, 128], P(None, None, 'wt', ('seq', 'ctx'))
- grad_b_hidden: float32 [8, 2, 16, 40, 128], P(None, None, None, 'wt', ('seq', 'ctx'))
Inputs may be any that keep to these rules, and one draw needn't show every extreme that they name: `segments`: segment numbers never fall along a sequence. Sequences come in groups of 8 / 2 consecutive ones; in each group exactly one sequence is a single document of all 1024 tokens (segment 0 throughout), and each other sequence packs exactly 3 documents of 51 to 512 tokens, the longest of exactly 512 tokens. `adapter_index`: each adapter serves exactly one sequence.
All inputs are finite; a program needn't handle non-finite values.
Results may differ from a plain program's by a relative error of at most 0.023.
Values may be sent and summed in bfloat16 or wider, within the bound.
No kernel may reach another device: no remote copies, remote signals or barrier semaphores. Data moves between devices by JAX's collectives and lax.ppermute only.
A program may use at most 512 MiB of HBM per device.

v0:
```python
import jax
import jax.numpy as jnp
from jax import lax
from jax.sharding import PartitionSpec as P

epsilon = 1e-06
masked_value = -1e30


def normalize(values):
    return values * lax.rsqrt(jnp.mean(values * values, axis=-1, keepdims=True) + epsilon)


def angles(positions, half_dim):
    frequency = 10000.0 ** (-jnp.arange(half_dim, dtype=jnp.float32) / half_dim)
    turn_angle = positions.astype(jnp.float32)[:, None] * frequency[None, :]
    return (jnp.cos(turn_angle), jnp.sin(turn_angle))


def rotate(values, cosine_table, sine_table):
    half_dim = values.shape[-1] // 2
    lower_half = values[..., :half_dim]
    upper_half = values[..., half_dim:]
    cosine_part = cosine_table[:, None, :]
    sine_part = sine_table[:, None, :]
    return jnp.concatenate(
        [
            lower_half * cosine_part - upper_half * sine_part,
            lower_half * sine_part + upper_half * cosine_part,
        ],
        axis=-1,
    )


def head_prep(raw, cosine_table, sine_table, scale, head_dim):
    reshaped = raw.reshape(raw.shape[:-1] + (raw.shape[-1] // head_dim, head_dim))
    return normalize(rotate(reshaped, cosine_table, sine_table)).reshape(raw.shape) * scale


def mix_state(state, branch, rate):
    return normalize(state + rate * (normalize(branch) - state))


def swiglu(gate, up_value, scales):
    return up_value * scales[0] * jax.nn.silu(gate * scales[1])


def select_rows(onehot, table):
    return jnp.einsum("ga,a...->g...", onehot, table.astype(jnp.float32)).astype(jnp.bfloat16)


def to_tables(onehot, per_seq):
    return jnp.einsum("ga,g...->a...", onehot, per_seq)


def body(
    tokens,
    segments,
    adapter_index,
    w_attn_in,
    w_attn_out,
    w_gate_up,
    w_down,
    qk_scale,
    mix_rates,
    mlp_scales,
    a_model,
    b_model,
    a_heads,
    b_heads,
    a_hidden,
    b_hidden,
    cotangent,
):
    seq_groups, seq_span, model_width = tokens.shape
    local_width = w_attn_out.shape[0]
    local_hidden = w_down.shape[0]
    head_dim = a_heads.shape[-1]
    local_heads = local_width // head_dim
    low_rank = a_model.shape[2]
    num_adapters = a_model.shape[0]
    row_width = a_hidden.shape[-1]
    ctx_place = lax.axis_index("ctx")
    first_pos = ctx_place * seq_span
    positions = first_pos + jnp.arange(seq_span, dtype=jnp.int32)
    cosine_table, sine_table = angles(positions, head_dim // 2)
    onehot = (adapter_index[:, None] == jnp.arange(num_adapters, dtype=jnp.int32)[None, :]).astype(
        jnp.float32
    )
    sel_am = select_rows(onehot, a_model)
    sel_bm = select_rows(onehot, b_model)
    sel_ah = select_rows(onehot, a_heads.reshape(num_adapters, low_rank, local_width))
    sel_bh = select_rows(onehot, b_heads.reshape(num_adapters, 3, low_rank, local_width))
    sel_ad = select_rows(onehot, a_hidden.reshape(num_adapters, low_rank, local_hidden))
    sel_bd = select_rows(onehot, b_hidden.reshape(num_adapters, 2, low_rank, local_hidden))
    tokens_f32 = tokens.astype(jnp.float32)
    head_shape = (seq_groups, seq_span, local_heads, head_dim)
    low_qkv = jnp.einsum(
        "gtd,gjrd->gtjr", tokens, sel_am[:, :3], preferred_element_type=jnp.float32
    ).astype(jnp.bfloat16)
    raw_qkv = jnp.einsum("gtd,jde->gtje", tokens, w_attn_in, preferred_element_type=jnp.float32)
    raw_qkv = raw_qkv + jnp.einsum(
        "gtjr,gjre->gtje", low_qkv, sel_bh, preferred_element_type=jnp.float32
    )

    def prepare(query_raw, key_raw):
        return (
            head_prep(query_raw, cosine_table, sine_table, qk_scale, head_dim),
            head_prep(key_raw, cosine_table, sine_table, qk_scale, head_dim),
        )

    (query_fin, key_fin), prep_pull = jax.vjp(prepare, raw_qkv[:, :, 0], raw_qkv[:, :, 1])
    query_low = query_fin.astype(jnp.bfloat16)
    key_low = key_fin.astype(jnp.bfloat16)
    value_low = raw_qkv[:, :, 2].astype(jnp.bfloat16)
    query_heads = query_low.reshape(head_shape)
    key_heads = key_low.reshape(head_shape)
    value_heads = value_low.reshape(head_shape)

    def scores_for(query_part, key_part, query_pos, key_pos, query_seg, key_seg):
        scores = (
            jnp.einsum("gqhd,gkhd->ghqk", query_part, key_part, preferred_element_type=jnp.float32)
            * 0.125
        )
        allowed = (key_pos[None, :] <= query_pos[:, None])[None, None] & (
            query_seg[:, None, :, None] == key_seg[:, None, None, :]
        )
        return (scores, allowed)

    start_state = (
        jnp.full((seq_groups, local_heads, seq_span), masked_value, jnp.float32),
        jnp.zeros((seq_groups, local_heads, seq_span), jnp.float32),
        jnp.zeros(head_shape, jnp.float32),
    )
    key_part = lax.all_gather(key_low, "ctx", axis=1, tiled=True)
    value_part = lax.all_gather(value_low, "ctx", axis=1, tiled=True)
    key_seg = lax.all_gather(segments, "ctx", axis=1, tiled=True)
    width_in = key_part.shape[1]
    key_part4 = key_part.reshape(seq_groups, width_in, local_heads, head_dim)
    value_part4 = value_part.reshape(seq_groups, width_in, local_heads, head_dim)

    def update(state):
        row_top, row_total, row_sum = state
        scores, allowed = scores_for(
            query_heads,
            key_part4,
            positions,
            jnp.arange(width_in, dtype=jnp.int32),
            segments,
            key_seg,
        )
        scores = jnp.where(allowed, scores, masked_value)
        new_top = jnp.maximum(row_top, jnp.max(scores, axis=-1))
        shrink = jnp.exp(row_top - new_top)
        weights = jnp.where(allowed, jnp.exp(scores - new_top[..., None]), 0.0)
        row_total = jnp.sum(weights, axis=-1)
        row_sum = row_sum * jnp.transpose(shrink, (0, 2, 1))[..., None]
        row_sum = jnp.einsum(
            "ghqk,gkhd->gqhd",
            weights.astype(jnp.bfloat16),
            value_part4,
            preferred_element_type=jnp.float32,
        )
        return (new_top, row_total, row_sum)

    row_top, row_total, row_sum = update(start_state)
    attended = row_sum / jnp.transpose(row_total, (0, 2, 1))[..., None]
    log_total = row_top + jnp.log(row_total)
    attn_low = attended.reshape(seq_groups, seq_span, local_width).astype(jnp.bfloat16)
    low_out_part = jnp.einsum("gte,gre->gtr", attn_low, sel_ah, preferred_element_type=jnp.float32)
    attn_part = jnp.einsum("gte,ed->gtd", attn_low, w_attn_out, preferred_element_type=jnp.float32)
    attn_raw, low_out = lax.psum((attn_part, low_out_part), "wt")
    low_out_b = low_out.astype(jnp.bfloat16)
    attn_raw = attn_raw + jnp.einsum(
        "gtr,grd->gtd", low_out_b, sel_bm[:, 0], preferred_element_type=jnp.float32
    )

    def first_mix(state, branch):
        return mix_state(state, branch, mix_rates[0])

    middle, first_pull = jax.vjp(first_mix, tokens_f32, attn_raw)
    middle_low = middle.astype(jnp.bfloat16)
    low_gate_up = jnp.einsum(
        "gtd,gjrd->gtjr", middle_low, sel_am[:, 3:], preferred_element_type=jnp.float32
    ).astype(jnp.bfloat16)
    gate_up = jnp.einsum("gtd,jdf->gtjf", middle_low, w_gate_up, preferred_element_type=jnp.float32)
    gate_up = gate_up + jnp.einsum(
        "gtjr,gjrf->gtjf", low_gate_up, sel_bd, preferred_element_type=jnp.float32
    )

    def feed(gate, up_value):
        return swiglu(gate, up_value, mlp_scales)

    hidden, feed_pull = jax.vjp(feed, gate_up[:, :, 0], gate_up[:, :, 1])
    hidden_low = hidden.astype(jnp.bfloat16)
    low_down_part = jnp.einsum(
        "gtf,grf->gtr", hidden_low, sel_ad, preferred_element_type=jnp.float32
    )
    down_part = jnp.einsum("gtf,fd->gtd", hidden_low, w_down, preferred_element_type=jnp.float32)
    down_raw, low_down = lax.psum((down_part, low_down_part), "wt")
    low_down_b = low_down.astype(jnp.bfloat16)
    down_raw = down_raw + jnp.einsum(
        "gtr,grd->gtd", low_down_b, sel_bm[:, 1], preferred_element_type=jnp.float32
    )

    def second_mix(state, branch):
        return mix_state(state, branch, mix_rates[1])

    layer_out, second_pull = jax.vjp(second_mix, middle, down_raw)
    grad_mid_res, grad_down = second_pull(cotangent.astype(jnp.float32))
    grad_down_b = grad_down.astype(jnp.bfloat16)
    grad_bm_down = jnp.einsum(
        "gtr,gtd->grd", low_down_b, grad_down_b, preferred_element_type=jnp.float32
    )
    grad_low_down = jnp.einsum(
        "gtd,grd->gtr", grad_down_b, sel_bm[:, 1], preferred_element_type=jnp.float32
    ).astype(jnp.bfloat16)
    grad_ad = jnp.einsum(
        "gtr,gtf->grf", grad_low_down, hidden_low, preferred_element_type=jnp.float32
    )
    grad_hidden = jnp.einsum("gtd,fd->gtf", grad_down_b, w_down, preferred_element_type=jnp.float32)
    grad_hidden = grad_hidden + jnp.einsum(
        "gtr,grf->gtf", grad_low_down, sel_ad, preferred_element_type=jnp.float32
    )
    grad_gate, grad_up = feed_pull(grad_hidden)
    grad_gate_up = jnp.stack([grad_gate, grad_up], axis=2).astype(jnp.bfloat16)
    grad_bd = jnp.einsum(
        "gtjr,gtjf->gjrf", low_gate_up, grad_gate_up, preferred_element_type=jnp.float32
    )
    grad_low_gu = jnp.einsum(
        "gtjf,gjrf->gtjr", grad_gate_up, sel_bd, preferred_element_type=jnp.float32
    ).astype(jnp.bfloat16)
    grad_am_gu = jnp.einsum(
        "gtjr,gtd->gjrd", grad_low_gu, middle_low, preferred_element_type=jnp.float32
    )
    middle_part = jnp.einsum(
        "gtjf,jdf->gtd", grad_gate_up, w_gate_up, preferred_element_type=jnp.float32
    )
    middle_part = middle_part + jnp.einsum(
        "gtjr,gjrd->gtd", grad_low_gu, sel_am[:, 3:], preferred_element_type=jnp.float32
    )
    grad_middle = grad_mid_res + lax.psum(middle_part, "wt")
    grad_input_res, grad_attn = first_pull(grad_middle)
    grad_attn_b = grad_attn.astype(jnp.bfloat16)
    grad_bm_attn = jnp.einsum(
        "gtr,gtd->grd", low_out_b, grad_attn_b, preferred_element_type=jnp.float32
    )
    grad_low_out = jnp.einsum(
        "gtd,grd->gtr", grad_attn_b, sel_bm[:, 0], preferred_element_type=jnp.float32
    ).astype(jnp.bfloat16)
    grad_ah = jnp.einsum("gtr,gte->gre", grad_low_out, attn_low, preferred_element_type=jnp.float32)
    grad_attended = jnp.einsum(
        "gtd,ed->gte", grad_attn_b, w_attn_out, preferred_element_type=jnp.float32
    )
    grad_attended = grad_attended + jnp.einsum(
        "gtr,gre->gte", grad_low_out, sel_ah, preferred_element_type=jnp.float32
    )
    grad_attended_b = grad_attended.astype(jnp.bfloat16)
    grad_out_heads = grad_attended_b.reshape(head_shape)
    delta_rows = jnp.sum(grad_out_heads.astype(jnp.float32) * attended, axis=-1)
    delta_heads = jnp.transpose(delta_rows, (0, 2, 1))
    log_rows = jnp.transpose(log_total, (0, 2, 1))
    zero_heads = jnp.zeros(head_shape, jnp.float32)
    key_part = lax.all_gather(key_low, "ctx", axis=1, tiled=True)
    value_part = lax.all_gather(value_low, "ctx", axis=1, tiled=True)
    pull_key_seg = lax.all_gather(segments, "ctx", axis=1, tiled=True)
    pull_width_in = key_part.shape[1]
    pull_key_part4 = key_part.reshape(seq_groups, pull_width_in, local_heads, head_dim)
    pull_value_part4 = value_part.reshape(seq_groups, pull_width_in, local_heads, head_dim)

    def update(grad_query):
        scores, allowed = scores_for(
            query_heads,
            pull_key_part4,
            positions,
            jnp.arange(pull_width_in, dtype=jnp.int32),
            segments,
            pull_key_seg,
        )
        weights = jnp.where(allowed, jnp.exp(scores - log_total[..., None]), 0.0)
        grad_weights = jnp.einsum(
            "gqhd,gkhd->ghqk", grad_out_heads, pull_value_part4, preferred_element_type=jnp.float32
        )
        grad_scores = (weights * (grad_weights - delta_heads[..., None])).astype(jnp.bfloat16)
        return (
            jnp.einsum(
                "ghqk,gkhd->gqhd", grad_scores, pull_key_part4, preferred_element_type=jnp.float32
            )
            * 0.125
        )

    grad_query = update(zero_heads)
    whole_logs, whole_deltas = (
        lax.all_gather(log_rows, "ctx", axis=1, tiled=True),
        lax.all_gather(delta_rows, "ctx", axis=1, tiled=True),
    )

    def pull_keys(running, incoming):
        query_part, grad_part, query_seg = incoming
        width_in = query_part.shape[1]
        query_part4 = query_part.reshape(seq_groups, width_in, local_heads, head_dim)
        grad_part4 = grad_part.reshape(seq_groups, width_in, local_heads, head_dim)

        def update(state):
            scores, allowed = scores_for(
                query_part4,
                key_heads,
                jnp.arange(width_in, dtype=jnp.int32),
                positions,
                query_seg,
                segments,
            )
            weights = jnp.where(
                allowed, jnp.exp(scores - jnp.transpose(whole_logs, (0, 2, 1))[..., None]), 0.0
            )
            grad_value = jnp.einsum(
                "ghqk,gqhd->gkhd",
                weights.astype(jnp.bfloat16),
                grad_part4,
                preferred_element_type=jnp.float32,
            )
            grad_weights = jnp.einsum(
                "gqhd,gkhd->ghqk", grad_part4, value_heads, preferred_element_type=jnp.float32
            )
            grad_scores = (
                weights * (grad_weights - jnp.transpose(whole_deltas, (0, 2, 1))[..., None])
            ).astype(jnp.bfloat16)
            grad_key = (
                jnp.einsum(
                    "ghqk,gqhd->gkhd", grad_scores, query_part4, preferred_element_type=jnp.float32
                )
                * 0.125
            )
            return (grad_key, grad_value)

        return update(running)

    grad_key, grad_value = pull_keys(
        (zero_heads, zero_heads),
        (
            lax.all_gather(query_low, "ctx", axis=1, tiled=True),
            lax.all_gather(grad_attended_b, "ctx", axis=1, tiled=True),
            lax.all_gather(segments, "ctx", axis=1, tiled=True),
        ),
    )
    grad_q_raw, grad_k_raw = prep_pull(
        (
            grad_query.reshape(seq_groups, seq_span, local_width),
            grad_key.reshape(seq_groups, seq_span, local_width),
        )
    )
    grad_qkv = jnp.stack(
        [grad_q_raw, grad_k_raw, grad_value.reshape(seq_groups, seq_span, local_width)], axis=2
    ).astype(jnp.bfloat16)
    grad_bh = jnp.einsum("gtjr,gtje->gjre", low_qkv, grad_qkv, preferred_element_type=jnp.float32)
    grad_low_qkv = jnp.einsum(
        "gtje,gjre->gtjr", grad_qkv, sel_bh, preferred_element_type=jnp.float32
    ).astype(jnp.bfloat16)
    grad_am_qkv = jnp.einsum(
        "gtjr,gtd->gjrd", grad_low_qkv, tokens, preferred_element_type=jnp.float32
    )
    input_part = jnp.einsum(
        "gtje,jde->gtd", grad_qkv, w_attn_in, preferred_element_type=jnp.float32
    )
    input_part = input_part + jnp.einsum(
        "gtjr,gjrd->gtd", grad_low_qkv, sel_am[:, :3], preferred_element_type=jnp.float32
    )
    input_grad = grad_input_res + lax.psum(input_part, "wt")
    table_am = to_tables(onehot, jnp.concatenate([grad_am_qkv, grad_am_gu], axis=1))
    table_bm = to_tables(onehot, jnp.stack([grad_bm_attn, grad_bm_down], axis=1))
    table_ah = to_tables(onehot, grad_ah).reshape(num_adapters, low_rank, local_heads, head_dim)
    table_bh = to_tables(onehot, grad_bh).reshape(num_adapters, 3, low_rank, local_heads, head_dim)
    table_ad = to_tables(onehot, grad_ad).reshape(
        num_adapters, low_rank, local_hidden // row_width, row_width
    )
    table_bd = to_tables(onehot, grad_bd).reshape(
        num_adapters, 2, low_rank, local_hidden // row_width, row_width
    )
    owned_am = lax.psum_scatter(table_am, ("seq", "ctx", "wt"), scatter_dimension=3, tiled=True)
    owned_bm, owned_ah, owned_bh, owned_ad, owned_bd = (
        lax.psum_scatter(table_bm, ("seq", "ctx"), scatter_dimension=3, tiled=True),
        lax.psum_scatter(table_ah, ("seq", "ctx"), scatter_dimension=3, tiled=True),
        lax.psum_scatter(table_bh, ("seq", "ctx"), scatter_dimension=4, tiled=True),
        lax.psum_scatter(table_ad, ("seq", "ctx"), scatter_dimension=3, tiled=True),
        lax.psum_scatter(table_bd, ("seq", "ctx"), scatter_dimension=4, tiled=True),
    )
    return (
        layer_out.astype(jnp.bfloat16),
        input_grad,
        owned_am,
        owned_bm,
        owned_ah,
        owned_bh,
        owned_ad,
        owned_bd,
    )


def solution(mesh):
    return jax.shard_map(
        body,
        mesh=mesh,
        in_specs=(
            P("seq", "ctx", None),
            P("seq", "ctx"),
            P("seq"),
            P(None, None, "wt"),
            P("wt", None),
            P(None, None, "wt"),
            P("wt", None),
            P("wt"),
            P(),
            P(None, "wt"),
            P(),
            P(),
            P(None, None, "wt", None),
            P(None, None, None, "wt", None),
            P(None, None, "wt", None),
            P(None, None, None, "wt", None),
            P("seq", "ctx", None),
        ),
        out_specs=(
            P("seq", "ctx", None),
            P("seq", "ctx", None),
            P(None, None, None, ("seq", "ctx", "wt")),
            P(None, None, None, ("seq", "ctx")),
            P(None, None, "wt", ("seq", "ctx")),
            P(None, None, None, "wt", ("seq", "ctx")),
            P(None, None, "wt", ("seq", "ctx")),
            P(None, None, None, "wt", ("seq", "ctx")),
        ),
        check_vma=False,
    )
```

profile of v0, /device:TPU:0, one launch (start us, length us, event | category | flops | bytes accessed | tf_op | source)
XLA Modules:
  0.0 1578.6 jit_solution(8123864830062802318)
XLA Ops:
  38.0 28.5 %all_gather.26 = s32[4,1024]{1,0:T(4,128)S(1)} all-gather(s32[4,128]{1,0:T(4,128)S(1)} %copy-done.103), channel_id=1, replica_groups=mesh['seq'=2,'ctx'=8,'wt'=2] {'ctx'}, dimensions={1}, use_global_device_ids=true | all-gather | bytes 18432 | tf_op jit(solution)/shard_map/all_gather | solution.py:137
  67.0 58.7 %all-gather.6.cloned.1.call-done = bf16[4,1024,640]{1,2,0:T(8,128)(2,1)} async-done(((bf16[4,128,640]{1,2,0:T(8,128)(2,1)}), bf16[4,1024,640]{1,2,0:T(8,128)(2,1)}) %all-gather.6.cloned.1.call-update) | async-done | bytes 5242896 | tf_op jit(solution)/shard_map/all_gather | solution.py:135
  125.8 14.1 select_reduce_fusion
  151.2 61.3 %all-gather.12.cloned.1.call-done = bf16[4,1024,1,640]{3,1,2,0:T(8,128)(2,1)} async-done(((bf16[4,128,1,640]{3,1,2,0:T(8,128)(2,1)}), bf16[4,1024,1,640]{3,1,2,0:T(8,128)(2,1)}) %all-gather.12.cloned.1.call-update) | async-done | bytes 5242896 | tf_op jit(solution)/shard_map/all_gather | solution.py:136
  220.4 12.2 fusion.166
  267.7 11.7 bitcast_add_fusion
  302.1 14.1 all-reduce.13.cloned.1.call-done
  335.2 10.9 fusion.47
  349.2 22.5 %all-reduce.15.cloned.1.call-done = f32[4,128,1280]{2,1,0:T(8,128)} async-done(((f32[4,128,1280]{2,1,0:T(8,128)}), f32[4,128,1280]{2,1,0:T(8,128)}) %all-reduce.15.cloned.1.call-update) | async-done | bytes 2621456 | tf_op jit(solution)/shard_map/psum | solution.py:242
  389.1 33.6 %all_gather.29 = f32[4,1024,10]{1,2,0:T(8,128)} all-gather(f32[4,128,10]{1,2,0:T(8,128)S(1)} %bitcast_add_fusion.2), channel_id=1, replica_groups=mesh['seq'=2,'ctx'=8,'wt'=2] {'ctx'}, dimensions={1}, use_global_device_ids=true | all-gather | bytes 184320 | tf_op jit(solution)/shard_map/all_gather | solution.py:294
  423.4 40.7 %all-gather.8.cloned.1.call-done = bf16[4,1024,640]{1,2,0:T(8,128)(2,1)} async-done(((bf16[4,128,640]{1,2,0:T(8,128)(2,1)}), bf16[4,1024,640]{1,2,0:T(8,128)(2,1)}) %all-gather.8.cloned.1.call-update) | async-done | bytes 5242896 | tf_op jit(solution)/shard_map/all_gather | solution.py:341
  464.1 11.1 fusion.100
  484.7 16.2 %multiply_reduce_fusion.8 = (f32[4,128,10]{1,2,0:T(8,128)S(1)}, f32[4,128,10,64]{1,3,2,0:T(8,128)}) fusion(f32[4,128,10,32]{1,3,2,0:T(8,128)S(1)} %copy-done.32, f32[4,128,10,32]{1,3,2,0:T(8,128)S(1)} %copy-done.30, f32[10,64]{1,0:T(8,128)S(1)} %broadcast_multiply_fusion.2, bf16[4,1024,10,64]{1,3,2,0:T(8,128)(2,1)} %bitcast.261, ...), kind=kOutput, calls=%fused_computation.132 | convolution fusion | flops 1374940160 | bytes 35322368 | tf_op jit(solution)/shard_map/ghqk,gkhd->gqhd/dot_general | solution.py:286
  511.8 16.5 %reshape.375 = f32[1280,256]{1,0:T(8,128)} reshape(f32[1280,2,16,8]{3,2,1,0:T(8,128)} %bitcast.245) | data formatting | bytes 2621440
  528.2 33.4 %all_gather.31 = f32[4,1024,10]{1,2,0:T(8,128)} all-gather(f32[4,128,10]{1,2,0:T(8,128)S(1)} %multiply_reduce_fusion.9), channel_id=1, replica_groups=mesh['seq'=2,'ctx'=8,'wt'=2] {'ctx'}, dimensions={1}, use_global_device_ids=true | all-gather | bytes 184320 | tf_op jit(solution)/shard_map/all_gather | solution.py:295
  570.1 17.4 %multiply_convert_fusion.11.clone.4 = bf16[4,10,1024,128]{3,2,1,0:T(8,128)(2,1)S(1)} fusion(f32[4,10,1024,128]{3,2,1,0:T(8,128)} %fusion.100, f32[4,10,1024]{2,1,0:T(8,128)} %bitcast.271, f32[4,10,1024]{2,1,0:T(8,128)} %bitcast.269, pred[4,1024,128]{2,1,0:T(8,128)(4,1)} %compare_and_fusion, ...), kind=kOutput, calls=%fused_computation.clone.clone.clone.clone.clone.clone.clone.clone.1 | convolution fusion | flops 702545920 | bytes 38207488 | tf_op jit(solution)/shard_map/gqhd,gkhd->ghqk/dot_general | solution.py:322
  592.5 11.5 fusion.70
  614.7 10.9 copy.167
  659.5 55.7 %reduce-scatter.17.cloned.1.call-done = f32[80,256]{1,0:T(8,128)} async-done(((f32[1280,256]{1,0:T(8,128)}), f32[80,256]{1,0:T(8,128)}) %reduce-scatter.17.cloned.1.call-update) | async-done | bytes 81936
  718.2 138.1 %all-reduce.19.cloned.1.call-done = f32[8,5,16,1280]{3,0,2,1:T(8,128)} async-done(((f32[8,5,16,1280]{3,0,2,1:T(8,128)}), f32[8,5,16,1280]{3,0,2,1:T(8,128)}) %all-reduce.19.cloned.1.call-update) | async-done | bytes 3276816
  858.3 158.4 %reduce-scatter.11.cloned.1.call-done = f32[8,3,16,10,4]{2,0,3,1,4:T(8,128)} async-done(((f32[8,3,16,10,64]{2,0,3,1,4:T(8,128)}), f32[8,3,16,10,4]{2,0,3,1,4:T(8,128)}) %reduce-scatter.11.cloned.1.call-update) | async-done | bytes 61456 | tf_op jit(solution)/shard_map/reduce_scatter | solution.py:383
  1018.8 22.2 %all-reduce.17.cloned.1.call-done = f32[4,128,1280]{2,1,0:T(8,128)} async-done(((f32[4,128,1280]{2,1,0:T(8,128)}), f32[4,128,1280]{2,1,0:T(8,128)}) %all-reduce.17.cloned.1.call-update) | async-done | bytes 2621456 | tf_op jit(solution)/shard_map/psum | solution.py:368
  1045.4 177.6 %reduce-scatter.13.cloned.1.call-done = f32[8,16,20,8]{2,3,1,0:T(8,128)} async-done(((f32[8,16,20,128]{2,3,1,0:T(8,128)}), f32[8,16,20,8]{2,3,1,0:T(8,128)}) %reduce-scatter.13.cloned.1.call-update) | async-done | bytes 81936 | tf_op jit(solution)/shard_map/reduce_scatter | solution.py:384
  1222.9 348.8 %reduce-scatter.15.cloned.1.call-done = f32[8,2,16,20,8]{3,4,2,1,0:T(8,128)} async-done(((f32[8,2,16,20,128]{3,4,2,1,0:T(8,128)}), f32[8,2,16,20,8]{3,4,2,1,0:T(8,128)}) %reduce-scatter.15.cloned.1.call-update) | async-done | bytes 163856 | tf_op jit(solution)/shard_map/reduce_scatter | solution.py:385
  (405 shorter events, 237.0 us)
Async XLA Ops:
  7.2 226.3 %copy-start = (bf16[640,1280]{1,0:T(8,128)(2,1)S(1)}, bf16[640,1280]{1,0:T(8,128)(2,1)}, u32[]{:S(2)}) copy-start(bf16[640,1280]{1,0:T(8,128)(2,1)} %param.21) | copy-start | bytes 4915204
  7.2 118.6 %all-gather.6.cloned.1.call-start = ((), (), s32[]{:S(2)}) async-start(), calls=%async_computation.5 | async-start | bytes 5898240 | tf_op jit(solution)/shard_map/all_gather | solution.py:135
  35.5 176.9 %all-gather.12.cloned.1.call-start = ((), (), s32[]{:S(2)}) async-start(), calls=%async_computation.16 | async-start | bytes 5898240 | tf_op jit(solution)/shard_map/all_gather | solution.py:136
  37.8 218.8 %all-reduce.11.cloned.1.call-start = ((), (), s32[]{:S(2)}) async-start(), calls=%async_computation.6 | async-start | bytes 5242880 | tf_op jit(solution)/shard_map/psum | solution.py:172
  66.5 73.4 %copy-start.82 = (s32[4,1024]{1,0:T(4,128)}, s32[4,1024]{1,0:T(4,128)S(1)}, u32[]{:S(2)}) copy-start(s32[4,1024]{1,0:T(4,128)S(1)} %all_gather.26) | copy-start | bytes 49156
  66.5 73.4 %copy-start.110 = (s32[128]{0:T(128)}, s32[128]{0:T(128)S(1)}, u32[]{:S(2)}) copy-start(s32[128]{0:T(128)S(1)} %iota_add_fusion) | copy-start | bytes 1540
  67.0 153.3 %copy-start.39 = (pred[4,128,1024]{2,1,0:T(8,128)(4,1)}, pred[4,128,1024]{2,1,0:T(8,128)(4,1)S(1)}, u32[]{:S(2)}) copy-start(pred[4,128,1024]{2,1,0:T(8,128)(4,1)S(1)} %compare_and_fusion.1) | copy-start | bytes 1572868
  151.2 69.2 %copy-start.63 = (f32[4,10,128]{2,1,0:T(8,128)}, f32[4,10,128]{2,1,0:T(8,128)S(1)}, u32[]{:S(2)}) copy-start(f32[4,10,128]{2,1,0:T(8,128)S(1)} %fusion.1) | copy-start | bytes 61444
  236.2 80.0 %all-reduce.13.cloned.1.call-start = ((), (), s32[]{:S(2)}) async-start(), calls=%async_computation.7 | async-start | bytes 5242880 | tf_op jit(solution)/shard_map/psum | solution.py:200
  243.7 35.7 %copy-start.94 = (f32[2560]{0:T(1024)}, f32[2560]{0:T(1024)S(1)}, u32[]{:S(2)}) copy-start(f32[2560]{0:T(1024)S(1)} %get-tuple-element.34) | copy-start | bytes 30724
  260.7 58.0 %copy-start.98 = (f32[4,128]{1,0:T(4,128)}, f32[4,128]{1,0:T(4,128)S(1)}, u32[]{:S(2)}) copy-start(f32[4,128]{1,0:T(4,128)S(1)} %fusion.139) | copy-start | bytes 6148
  292.7 79.0 %all-reduce.15.cloned.1.call-start = ((), (), s32[]{:S(2)}) async-start(), calls=%async_computation.8 | async-start | bytes 5242880 | tf_op jit(solution)/shard_map/psum | solution.py:242
  348.2 115.9 %all-gather.8.cloned.1.call-start = ((), (), s32[]{:S(2)}) async-start(), calls=%async_computation.9 | async-start | bytes 5898240 | tf_op jit(solution)/shard_map/all_gather | solution.py:341
  348.8 213.2 %all-gather.10.cloned.1.call-start = ((), (), s32[]{:S(2)}) async-start(), calls=%async_computation.10 | async-start | bytes 5898240 | tf_op jit(solution)/shard_map/all_gather | solution.py:342
  384.7 79.3 %copy-start.21 = (f32[4,128,10,64]{1,3,2,0:T(8,128)S(1)}, f32[4,128,10,64]{1,3,2,0:T(8,128)}, u32[]{:S(2)}) copy-start(f32[4,128,10,64]{1,3,2,0:T(8,128)} %copy-done.20) | copy-start | bytes 3932164
  386.0 271.9 %reduce-scatter.9.cloned.1.call-start = ((), (), s32[]{:S(2)}) async-start(), calls=%async_computation.12 | async-start | bytes 2785280 | tf_op jit(solution)/shard_map/reduce_scatter | solution.py:382
  484.4 230.8 %reduce-scatter.17.cloned.1.call-start = ((), (), s32[]{:S(2)}) async-start(), calls=%async_computation.17 | async-start | bytes 1392640
  511.8 49.9 %copy-start.72 = (f32[4,128,10]{1,2,0:T(8,128)S(1)}, f32[4,128,10]{1,2,0:T(8,128)}, u32[]{:S(2)}) copy-start(f32[4,128,10]{1,2,0:T(8,128)} %copy-done.71) | copy-start | bytes 61444
  561.7 294.6 %all-reduce.19.cloned.1.call-start = ((), (), s32[]{:S(2)}) async-start(), calls=%async_computation.18 | async-start | bytes 6553600
  610.3 406.4 %reduce-scatter.11.cloned.1.call-start = ((), (), s32[]{:S(2)}) async-start(), calls=%async_computation.13 | async-start | bytes 8355840 | tf_op jit(solution)/shard_map/reduce_scatter | solution.py:383
  625.6 415.3 %all-reduce.17.cloned.1.call-start = ((), (), s32[]{:S(2)}) async-start(), calls=%async_computation.11 | async-start | bytes 5242880 | tf_op jit(solution)/shard_map/psum | solution.py:368
  633.2 589.7 %reduce-scatter.13.cloned.1.call-start = ((), (), s32[]{:S(2)}) async-start(), calls=%async_computation.14 | async-start | bytes 8912896 | tf_op jit(solution)/shard_map/reduce_scatter | solution.py:384
  641.3 930.4 %reduce-scatter.15.cloned.1.call-start = ((), (), s32[]{:S(2)}) async-start(), calls=%async_computation.15 | async-start | bytes 17825792 | tf_op jit(solution)/shard_map/reduce_scatter | solution.py:385
  1016.7 555.1 %copy-start.1 = (bf16[640,1280]{1,0:T(8,128)(2,1)S(1)}, bf16[640,1280]{1,0:T(8,128)(2,1)}, u32[]{:S(2)}) copy-start(bf16[640,1280]{1,0:T(8,128)(2,1)} %param.21) | copy-start | bytes 4915204
  (111 other events, 557.0 us)
Sparse Core Ops, SparseCore 0:
  35.6 90.0 all-gather.5
  128.0 84.4 all-gather.11
  236.3 20.3 all-reduce.10
  292.8 23.3 all-reduce.12
  348.3 23.3 all-reduce.14
  373.8 90.2 all-gather.7
  467.0 87.0 all-gather.9
  556.5 80.3 reduce-scatter.8
  639.3 75.8 reduce-scatter.16
  721.5 134.7 all-reduce.18
  861.7 154.9 reduce-scatter.10
  1019.6 21.3 all-reduce.16
  1043.9 179.0 reduce-scatter.12
  1225.7 346.0 reduce-scatter.14
where the time goes:
time: 1590 us; the launch traced here: 1580 us
  waiting for transfers between devices  1100 us (69%)
  matrix products  185 us (12%)
  local copies, waits for them, and re-layouts  130 us (8%)
  blocking collectives  103 us (6%)
  other arithmetic  40.4 us (3%)
    reduce_scatter x1, waiting for transfers between devices, body(): lax.psum_scatter(table_bd, ('seq', 'ctx'), scatter_dimension=4, tiled=True)  349 us
    unnamed x16, waiting for transfers between devices  194 us
    reduce_scatter x1, waiting for transfers between devices, body(): lax.psum_scatter(table_ad, ('seq', 'ctx'), scatter_dimension=3, tiled=True)  178 us
    reduce_scatter x1, waiting for transfers between devices, body(): lax.psum_scatter(table_bh, ('seq', 'ctx'), scatter_dimension=4, tiled=True)  158 us
    all_gather x1, waiting for transfers between devices, body(): value_part = lax.all_gather(value_low, 'ctx', axis=1, tiled=True)  61.3 us
    all_gather x1, waiting for transfers between devices, body(): key_part = lax.all_gather(key_low, 'ctx', axis=1, tiled=True)  58.7 us
    unnamed x250, local copies, waits for them, and re-layouts  55.7 us
    all_gather x1, waiting for transfers between devices, body(): lax.all_gather(query_low, 'ctx', axis=1, tiled=True)  40.7 us
  transfers between devices with their start and end apart: 14, of which 12 were waited for; matrix products, arithmetic and copies ran while one was open for 14% of the time, Pallas kernels for 0%

commit v1 on v0

v1 whole, which is shorter than its diff:
```python
import functools

import jax
import jax.numpy as jnp
from jax import lax
from jax.experimental import pallas as pl
from jax.experimental.pallas import tpu as pltpu
from jax.sharding import PartitionSpec as P

epsilon = 1e-06
f32 = jnp.float32
bf16 = jnp.bfloat16
VMEM_LIMIT = 56 * 1024 * 1024
log2e = 1.4426950408889634


def dot(left, right, contract):
    return lax.dot_general(left, right, (contract, ((), ())), preferred_element_type=f32)


def nn(left, right):
    return dot(left, right, ((1,), (0,)))


def nt(left, right):
    return dot(left, right, ((1,), (1,)))


def tn(left, right):
    return dot(left, right, ((0,), (0,)))


def normalize(values):
    return values * lax.rsqrt(jnp.mean(values * values, axis=-1, keepdims=True) + epsilon)


def mix_state(state, branch, rate):
    return normalize(state + rate * (normalize(branch) - state))


def swiglu(gate, up_value, scales):
    return up_value * scales[0] * jax.nn.silu(gate * scales[1])


def lane_iota(shape):
    return lax.broadcasted_iota(jnp.int32, shape, len(shape) - 1)


def swap_halves(tile, half):
    lower = lane_iota(tile.shape) % (2 * half) < half
    return jnp.where(lower, pltpu.roll(tile, 128 - half, 1), pltpu.roll(tile, half, 1))


def head_sums(tile, head_dim):
    rows = lax.broadcasted_iota(jnp.int32, (128, 128), 0) // head_dim
    cols = lax.broadcasted_iota(jnp.int32, (128, 128), 1) // head_dim
    ones = jnp.where(rows == cols, 1.0, 0.0).astype(bf16)
    high = tile.astype(bf16)
    rest = (tile - high.astype(f32)).astype(bf16)
    return nn(high, ones) + nn(rest, ones)


def prep_tile(raw, cosine, sine, scale, head_dim):
    mean = head_sums(raw * raw, head_dim) * (1.0 / head_dim)
    inverse = lax.rsqrt(mean + epsilon)
    turned = raw * cosine + swap_halves(raw, head_dim // 2) * sine
    return (turned * inverse * scale).astype(bf16), inverse


def prep_tile_back(grad, low, inverse, cosine, sine, scale, head_dim):
    unit = low.astype(f32) / scale
    grad_unit = grad * scale
    mean = head_sums(grad_unit * unit, head_dim) * (1.0 / head_dim)
    grad_turned = inverse * (grad_unit - unit * mean)
    return grad_turned * cosine - swap_halves(grad_turned, head_dim // 2) * sine


def qkv_kernel(
    dims, place, h_ref, w_ref, a_ref, b_ref, cos_ref, sin_ref, scale_ref,
    q_ref, k_ref, v_ref, u_ref, qi_ref, ki_ref,
):
    chunk, head_dim, rank = dims
    width = w_ref.shape[2]
    own = pl.ds(pl.multiple_of(place[0] * chunk, chunk), chunk)
    h = h_ref[...]
    low = nt(h, a_ref[...]).astype(bf16)
    u_ref[...] = low
    keys = nn(h, w_ref[1]) + nn(low[:, rank : 2 * rank], b_ref[1])
    cosine = cos_ref[...]
    sine = sin_ref[...]
    for tile in range(width // 128):
        cols = slice(tile * 128, tile * 128 + 128)
        k_ref[:, cols], ki_ref[:, cols] = prep_tile(
            keys[:, cols], cosine, sine, scale_ref[:, cols], head_dim
        )
    v_ref[...] = (nn(h, w_ref[2]) + nn(low[:, 2 * rank :], b_ref[2])).astype(bf16)
    h_own = h_ref[own, :]
    low_own = nt(h_own, a_ref[:rank, :]).astype(bf16)
    queries = nn(h_own, w_ref[0]) + nn(low_own, b_ref[0])
    cosine = cos_ref[own, :]
    sine = sin_ref[own, :]
    for tile in range(width // 128):
        cols = slice(tile * 128, tile * 128 + 128)
        q_ref[:, cols], qi_ref[:, cols] = prep_tile(
            queries[:, cols], cosine, sine, scale_ref[:, cols], head_dim
        )


def run_qkv(place, h_full, w, a, b, cos, sin, scale, chunks, chunk, head_dim):
    rows, model = h_full.shape
    width = w.shape[2]
    rank = b.shape[1]
    block = rows // chunks
    whole = lambda *shape: pl.BlockSpec(shape, lambda i, s: (0,) * len(shape))
    row = lambda size, cols: pl.BlockSpec((size, cols), lambda i, s: (i, 0))
    return pl.pallas_call(
        functools.partial(qkv_kernel, (chunk, head_dim, rank)),
        grid_spec=pltpu.PrefetchScalarGridSpec(
            num_scalar_prefetch=1,
            grid=(chunks,),
            in_specs=[
                row(block, model),
                whole(3, model, width),
                whole(3 * rank, model),
                whole(3, rank, width),
                row(block, 128),
                row(block, 128),
                whole(1, width),
            ],
            out_specs=[
                row(chunk, width),
                row(block, width),
                row(block, width),
                row(block, 3 * rank),
                row(chunk, width),
                row(block, width),
            ],
        ),
        out_shape=[
            jax.ShapeDtypeStruct((chunks * chunk, width), bf16),
            jax.ShapeDtypeStruct((rows, width), bf16),
            jax.ShapeDtypeStruct((rows, width), bf16),
            jax.ShapeDtypeStruct((rows, 3 * rank), bf16),
            jax.ShapeDtypeStruct((chunks * chunk, width), f32),
            jax.ShapeDtypeStruct((rows, width), f32),
        ],
        compiler_params=pltpu.CompilerParams(vmem_limit_bytes=VMEM_LIMIT),
        name="qkv",
    )(place, h_full, w, a, b, cos, sin, scale)


def spread_pair(tile, head_dim):
    lower = lane_iota(tile.shape) < head_dim
    zero = jnp.zeros_like(tile)
    return jnp.concatenate([jnp.where(lower, tile, zero), jnp.where(lower, zero, tile)], axis=0)


def allowed_mask(first, last, key_start, rows, diagonal):
    keys = key_start + lax.broadcasted_iota(jnp.int32, (rows, first.shape[1]), 0)
    mask = keys >= first
    if diagonal:
        mask = mask & (keys <= last)
    return mask


def query_bounds(start_ref, m, place, group, chunk):
    first = start_ref[:, m * chunk : (m + 1) * chunk]
    last = (m * group + place) * chunk + lane_iota((1, chunk))
    return jnp.concatenate([first, first], axis=1), jnp.concatenate([last, last], axis=1)


def attend_kernel(dims, place, start_ref, q_ref, k_ref, v_ref, o_ref, of_ref, inv_ref, vt_ref):
    chunks, chunk, group, head_dim = dims
    block = group * chunk
    vt_ref[...] = v_ref[...].T
    for m in range(chunks):
        own = slice(m * chunk, (m + 1) * chunk)
        pair = spread_pair(q_ref[own, :], head_dim)
        first, last = query_bounds(start_ref, m, place[0], group, chunk)
        total = jnp.zeros((1, 2 * chunk), f32)
        gathered = jnp.zeros((128, 2 * chunk), f32)
        for b in range(m + 1):
            at = slice(b * block, (b + 1) * block)
            scores = nt(k_ref[at, :], pair)
            mask = allowed_mask(first, last, b * block, block, b == m)
            weights = jnp.where(mask, jnp.exp2(scores * (0.125 * log2e)), 0.0)
            total = total + jnp.sum(weights, axis=0, keepdims=True)
            gathered = gathered + nn(vt_ref[:, at], weights.astype(bf16))
        inverse = 1.0 / total
        gathered = gathered * inverse
        upper = lax.broadcasted_iota(jnp.int32, (128, chunk), 0) < head_dim
        final = jnp.where(upper, gathered[:, :chunk], gathered[:, chunk:])
        of_ref[0, :, own] = final
        o_ref[own, :] = final.T.astype(bf16)
        inv_ref[0, m : m + 1, :] = inverse


def run_attend(place, start, q, k, v, chunks, chunk, group, head_dim):
    rows, width = q.shape
    keys = k.shape[0]
    pairs = width // 128
    col = lambda size: pl.BlockSpec((size, 128), lambda p, s: (0, p))
    return pl.pallas_call(
        functools.partial(attend_kernel, (chunks, chunk, group, head_dim)),
        grid_spec=pltpu.PrefetchScalarGridSpec(
            num_scalar_prefetch=1,
            grid=(pairs,),
            in_specs=[
                pl.BlockSpec((1, rows), lambda p, s: (0, 0)),
                col(rows),
                col(keys),
                col(keys),
            ],
            out_specs=[
                col(rows),
                pl.BlockSpec((1, 128, rows), lambda p, s: (p, 0, 0)),
                pl.BlockSpec((1, chunks, 2 * chunk), lambda p, s: (p, 0, 0)),
            ],
            scratch_shapes=[pltpu.VMEM((128, keys), bf16)],
        ),
        out_shape=[
            jax.ShapeDtypeStruct((rows, width), bf16),
            jax.ShapeDtypeStruct((pairs, 128, rows), f32),
            jax.ShapeDtypeStruct((pairs, chunks, 2 * chunk), f32),
        ],
        compiler_params=pltpu.CompilerParams(vmem_limit_bytes=VMEM_LIMIT),
        name="attend",
    )(place, start, q, k, v)


def attend_back_kernel(
    dims, place, start_ref, q_ref, k_ref, v_ref, g_ref, of_ref, inv_ref, qi_ref, ki_ref,
    cos_ref, sin_ref, scale_ref, gq_ref, gk_ref, gv_ref, kt_ref, gqt_ref,
):
    chunks, chunk, group, head_dim = dims
    block = group * chunk
    kt_ref[...] = k_ref[...].T
    scale = scale_ref[...]
    pairs_q, pairs_g, deltas, bounds = [], [], [], []
    for m in range(chunks):
        own = slice(m * chunk, (m + 1) * chunk)
        pairs_q.append(spread_pair(q_ref[own, :], head_dim))
        grad = g_ref[own, :]
        pairs_g.append(spread_pair(grad, head_dim))
        products = grad.astype(f32).T * of_ref[0, :, own]
        deltas.append(
            jnp.concatenate(
                [
                    jnp.sum(products[:head_dim], axis=0, keepdims=True),
                    jnp.sum(products[head_dim:], axis=0, keepdims=True),
                ],
                axis=1,
            )
        )
        bounds.append(query_bounds(start_ref, m, place[0], group, chunk))
    for b in range(chunks):
        at = slice(b * block, (b + 1) * block)
        grad_key = jnp.zeros((block, 128), f32)
        grad_value = jnp.zeros((block, 128), f32)
        for m in range(b, chunks):
            first, last = bounds[m]
            scores = nt(k_ref[at, :], pairs_q[m])
            mask = allowed_mask(first, last, b * block, block, b == m)
            weights = jnp.exp2(scores * (0.125 * log2e)) * inv_ref[0, m : m + 1, :]
            weights = jnp.where(mask, weights, 0.0)
            grad_value = grad_value + nn(weights.astype(bf16), pairs_g[m])
            grad_weights = nt(v_ref[at, :], pairs_g[m])
            grad_scores = (weights * (grad_weights - deltas[m])).astype(bf16)
            grad_key = grad_key + nn(grad_scores, pairs_q[m])
            part = nn(kt_ref[:, at], grad_scores)
            if b == 0:
                gqt_ref[m] = part
            else:
                gqt_ref[m] += part
        gv_ref[at, :] = grad_value.astype(bf16)
        gk_ref[at, :] = prep_tile_back(
            grad_key * 0.125, k_ref[at, :], ki_ref[at, :], cos_ref[at, :], sin_ref[at, :],
            scale, head_dim,
        ).astype(bf16)
    upper = lax.broadcasted_iota(jnp.int32, (128, chunk), 0) < head_dim
    for m in range(chunks):
        own = slice(m * chunk, (m + 1) * chunk)
        both = gqt_ref[m]
        grad = jnp.where(upper, both[:, :chunk], both[:, chunk:]).T * 0.125
        rows = pl.ds(pl.multiple_of((m * group + place[0]) * chunk, chunk), chunk)
        gq_ref[own, :] = prep_tile_back(
            grad, q_ref[own, :], qi_ref[own, :], cos_ref[rows, :], sin_ref[rows, :],
            scale, head_dim,
        ).astype(bf16)


def run_attend_back(
    place, start, q, k, v, grad, o_full, inverse, q_inv, k_inv, cos, sin, scale,
    chunks, chunk, group, head_dim,
):
    rows, width = q.shape
    keys = k.shape[0]
    pairs = width // 128
    col = lambda size: pl.BlockSpec((size, 128), lambda p, s: (0, p))
    whole = pl.BlockSpec((keys, 128), lambda p, s: (0, 0))
    return pl.pallas_call(
        functools.partial(attend_back_kernel, (chunks, chunk, group, head_dim)),
        grid_spec=pltpu.PrefetchScalarGridSpec(
            num_scalar_prefetch=1,
            grid=(pairs,),
            in_specs=[
                pl.BlockSpec((1, rows), lambda p, s: (0, 0)),
                col(rows),
                col(keys),
                col(keys),
                col(rows),
                pl.BlockSpec((1, 128, rows), lambda p, s: (p, 0, 0)),
                pl.BlockSpec((1, chunks, 2 * chunk), lambda p, s: (p, 0, 0)),
                col(rows),
                col(keys),
                whole,
                whole,
                col(1),
            ],
            out_specs=[col(rows), col(keys), col(keys)],
            scratch_shapes=[
                pltpu.VMEM((128, keys), bf16),
                pltpu.VMEM((chunks, 128, 2 * chunk), f32),
            ],
        ),
        out_shape=[
            jax.ShapeDtypeStruct((rows, width), bf16),
            jax.ShapeDtypeStruct((keys, width), bf16),
            jax.ShapeDtypeStruct((keys, width), bf16),
        ],
        compiler_params=pltpu.CompilerParams(vmem_limit_bytes=VMEM_LIMIT),
        name="attend_back",
    )(place, start, q, k, v, grad, o_full, inverse, q_inv, k_inv, cos, sin, scale)


def pick(array, index):
    return lax.dynamic_index_in_dim(array, index, 0, keepdims=False)


def body(
    tokens, segments, adapter_index, w_attn_in, w_attn_out, w_gate_up, w_down, qk_scale,
    mix_rates, mlp_scales, a_model, b_model, a_heads, b_heads, a_hidden, b_hidden, cotangent,
):
    slabs, chunk, model = tokens.shape
    n_seq = lax.axis_size("seq")
    n_ctx = lax.axis_size("ctx")
    group = n_ctx // slabs
    local_width = w_attn_out.shape[0]
    local_hidden = w_down.shape[0]
    head_dim = a_heads.shape[-1]
    local_heads = local_width // head_dim
    rank = a_model.shape[2]
    adapters = a_model.shape[0]
    row_width = a_hidden.shape[-1]
    half = model // 2
    place = lax.axis_index("ctx")
    slab = place // group
    inner = place % group
    core = lax.axis_index("wt")
    owners = n_seq * n_ctx
    rows = slabs * chunk
    length = rows * group

    def to_slab(array, shift):
        pairs = [(c, (c + shift * group) % n_ctx) for c in range(n_ctx)]
        return lax.ppermute(array, "ctx", pairs)

    def within_slab(array, shift):
        pairs = [(c, c - c % group + (c % group + shift) % group) for c in range(n_ctx)]
        return lax.ppermute(array, "ctx", pairs)

    def other_core(array):
        return lax.ppermute(array, "wt", [(0, 1), (1, 0)])

    def both_halves(mine):
        other = other_core(mine)
        return jnp.where(
            core == 0,
            jnp.concatenate([mine, other], axis=-1),
            jnp.concatenate([other, mine], axis=-1),
        )

    def half_cols(array, which):
        return lax.dynamic_slice_in_dim(array, which * half, half, array.ndim - 1)

    def exchange_slabs(pieces):
        result = lax.dynamic_update_index_in_dim(
            jnp.zeros_like(pieces), pick(pieces, slab), slab, 0
        )
        for shift in range(1, slabs):
            got = to_slab(pick(pieces, (slab + shift) % slabs), shift)
            result = lax.dynamic_update_index_in_dim(result, got, (slab - shift) % slabs, 0)
        return result

    def gather_inner(own):
        result = lax.dynamic_update_index_in_dim(
            jnp.zeros((group,) + own.shape, own.dtype), own, inner, 0
        )
        for shift in range(1, group):
            got = within_slab(own, shift)
            result = lax.dynamic_update_index_in_dim(result, got, (inner - shift) % group, 0)
        return result

    own_half = exchange_slabs(half_cols(tokens, core))
    full_half = jnp.moveaxis(gather_inner(own_half), 0, 1)
    h_full = both_halves(full_half.reshape(length, half))
    h_own = pick(
        jnp.moveaxis(h_full.reshape(slabs, group, chunk, model), 1, 0), inner
    ).reshape(rows, model)
    own_seg = exchange_slabs(segments)
    full_seg = jnp.moveaxis(gather_inner(own_seg), 0, 1).reshape(1, length)
    start = jnp.sum(
        (full_seg < own_seg.reshape(rows, 1)).astype(jnp.int32), axis=1
    ).reshape(1, rows)
    g_out = both_halves(exchange_slabs(half_cols(cotangent, core))).reshape(rows, model)

    adapter = pick(adapter_index, slab)
    am = pick(a_model, adapter)
    bm = pick(b_model, adapter)
    ah = pick(a_heads, adapter).reshape(rank, local_width)
    bh = pick(b_heads, adapter).reshape(3, rank, local_width)
    ad = pick(a_hidden, adapter).reshape(rank, local_hidden)
    bd = pick(b_hidden, adapter).reshape(2, rank, local_hidden)

    frequency = 10000.0 ** (-jnp.arange(head_dim // 2, dtype=f32) / (head_dim // 2))
    turn = jnp.arange(length, dtype=jnp.int32).astype(f32)[:, None] * frequency[None, :]
    cos = jnp.tile(jnp.cos(turn), (1, 256 // head_dim))
    sine = jnp.sin(turn)
    sin = jnp.tile(jnp.concatenate([-sine, sine], axis=1), (1, 128 // head_dim))
    scale = qk_scale[None, :]
    inner_arg = inner[None].astype(jnp.int32)

    q, k, v, low_qkv, q_inv, k_inv = run_qkv(
        inner_arg, h_full, w_attn_in, am[:3].reshape(3 * rank, model), bh, cos, sin, scale,
        slabs, chunk, head_dim,
    )
    attn_low, o_full, inverse = run_attend(
        inner_arg, start, q, k, v, slabs, chunk, group, head_dim
    )
    h_own32 = h_own.astype(f32)
    attn_part = nn(attn_low, w_attn_out)
    low_out_part = nt(attn_low, ah)
    attn_sum = attn_part + other_core(attn_part)
    low_out = (low_out_part + other_core(low_out_part)).astype(bf16)
    attn_raw = attn_sum + nn(low_out, bm[0])

    def first_mix(state, branch):
        return mix_state(state, branch, mix_rates[0])

    middle, first_pull = jax.vjp(first_mix, h_own32, attn_raw)
    middle_low = middle.astype(bf16)
    low_gate = nt(middle_low, am[3]).astype(bf16)
    low_up = nt(middle_low, am[4]).astype(bf16)
    gate = nn(middle_low, w_gate_up[0]) + nn(low_gate, bd[0])
    up_value = nn(middle_low, w_gate_up[1]) + nn(low_up, bd[1])

    def feed(gate, up_value):
        return swiglu(gate, up_value, mlp_scales)

    hidden, feed_pull = jax.vjp(feed, gate, up_value)
    hidden_low = hidden.astype(bf16)
    down_part = nn(hidden_low, w_down)
    low_down_part = nt(hidden_low, ad)
    low_down = (low_down_part + other_core(low_down_part)).astype(bf16)
    down_raw = down_part + other_core(down_part) + nn(low_down, bm[1])

    def second_mix(state, branch):
        return mix_state(state, branch, mix_rates[1])

    layer_out, second_pull = jax.vjp(second_mix, middle, down_raw)
    out_half = half_cols(layer_out.astype(bf16), core).reshape(slabs, chunk, half)
    layer_out_own = both_halves(exchange_slabs(out_half))

    grad_mid_res, grad_down = second_pull(g_out.astype(f32))
    grad_down_b = grad_down.astype(bf16)
    grad_bm_down = tn(low_down, grad_down_b)
    grad_low_down = nt(grad_down_b, bm[1]).astype(bf16)
    grad_ad = tn(grad_low_down, hidden_low)
    grad_hidden = nt(grad_down_b, w_down) + nn(grad_low_down, ad)
    grad_gate, grad_up = feed_pull(grad_hidden)
    grad_gate = grad_gate.astype(bf16)
    grad_up = grad_up.astype(bf16)
    grad_bd = jnp.stack([tn(low_gate, grad_gate), tn(low_up, grad_up)])
    grad_low_gate = nt(grad_gate, bd[0]).astype(bf16)
    grad_low_up = nt(grad_up, bd[1]).astype(bf16)
    grad_am_gu = jnp.stack([tn(grad_low_gate, middle_low), tn(grad_low_up, middle_low)])
    middle_part = (
        nt(grad_gate, w_gate_up[0])
        + nt(grad_up, w_gate_up[1])
        + nn(grad_low_gate, am[3])
        + nn(grad_low_up, am[4])
    )
    grad_middle = grad_mid_res + middle_part + other_core(middle_part)
    grad_input_res, grad_attn = first_pull(grad_middle)
    grad_attn_b = grad_attn.astype(bf16)
    grad_bm_attn = tn(low_out, grad_attn_b)
    grad_low_out = nt(grad_attn_b, bm[0]).astype(bf16)
    grad_ah = tn(grad_low_out, attn_low)
    grad_attended = (nt(grad_attn_b, w_attn_out) + nn(grad_low_out, ah)).astype(bf16)

    grad_q, grad_k, grad_v = run_attend_back(
        inner_arg, start, q, k, v, grad_attended, o_full, inverse, q_inv, k_inv, cos, sin,
        scale, slabs, chunk, group, head_dim,
    )

    def own_rows(array):
        parts = jnp.moveaxis(array.reshape(slabs, group, chunk, array.shape[-1]), 1, 0)
        return pick(parts, inner).reshape(rows, array.shape[-1])

    low_q = own_rows(low_qkv[:, :rank])
    low_k = low_qkv[:, rank : 2 * rank]
    low_v = low_qkv[:, 2 * rank :]
    grad_bh = jnp.stack([tn(low_q, grad_q), tn(low_k, grad_k), tn(low_v, grad_v)])
    grad_low_q = nt(grad_q, bh[0]).astype(bf16)
    grad_low_k = nt(grad_k, bh[1]).astype(bf16)
    grad_low_v = nt(grad_v, bh[2]).astype(bf16)
    grad_am_qkv = jnp.stack(
        [tn(grad_low_q, h_own), tn(grad_low_k, h_full), tn(grad_low_v, h_full)]
    )
    input_kv = (
        nt(grad_k, w_attn_in[1])
        + nt(grad_v, w_attn_in[2])
        + nn(grad_low_k, am[1])
        + nn(grad_low_v, am[2])
    )
    input_q = nt(grad_q, w_attn_in[0]) + nn(grad_low_q, am[0])

    kv_parts = jnp.moveaxis(input_kv.reshape(slabs, group, chunk, model), 1, 0)
    mine = half_cols(kv_parts, core)
    theirs = half_cols(kv_parts, 1 - core).astype(bf16)
    kv_sum = mine + other_core(theirs).astype(f32)
    input_half = (
        half_cols(input_q, core)
        + other_core(half_cols(input_q, 1 - core).astype(bf16)).astype(f32)
        + half_cols(grad_input_res, core)
        + pick(kv_sum, inner).reshape(rows, half)
    )
    for shift in range(1, group):
        sent = pick(kv_sum, (inner + shift) % group).reshape(rows, half).astype(bf16)
        input_half = input_half + within_slab(sent, shift).astype(f32)
    input_half = input_half.astype(bf16).reshape(slabs, chunk, half)
    input_grad = both_halves(exchange_slabs(input_half)).astype(f32)

    def pieces(array, lead, split):
        return array

    def by_owner(array, unit):
        lead = array.shape[:-1]
        units = array.shape[-1] // unit
        shaped = array.reshape(lead + (units, owners, unit // owners))
        return jnp.moveaxis(shaped, -2, 0).reshape(owners, -1)

    grad_am = jnp.concatenate([grad_am_qkv, grad_am_gu], axis=0)
    am_split = grad_am.reshape(5, rank, owners, 2, model // (2 * owners))
    am_split = jnp.transpose(am_split, (3, 2, 0, 1, 4)).reshape(2, owners, -1)
    am_sum = pick(am_split, core) + other_core(pick(am_split, 1 - core).astype(bf16)).astype(f32)
    flat = jnp.concatenate(
        [
            am_sum,
            by_owner(jnp.stack([grad_bm_attn, grad_bm_down]), model),
            by_owner(grad_ah, head_dim),
            by_owner(grad_bh, head_dim),
            by_owner(grad_ad, row_width),
            by_owner(grad_bd, row_width),
        ],
        axis=1,
    )
    sizes = flat.shape[1]
    by_inner = jnp.moveaxis(flat.reshape(n_seq, slabs, group, sizes), 2, 0)
    table = pick(by_inner, inner)
    for shift in range(1, group):
        sent = pick(by_inner, (inner + shift) % group).astype(bf16)
        table = table + within_slab(sent, shift).astype(f32)
    table = jnp.moveaxis(table, 1, 0).astype(bf16)
    table = exchange_slabs(table)
    seq_place = lax.axis_index("seq")
    by_seq = jnp.moveaxis(table, 1, 0)
    collected = jnp.zeros_like(by_seq)
    indices = jnp.zeros((n_seq,) + adapter_index.shape, jnp.int32)
    collected = lax.dynamic_update_index_in_dim(collected, pick(by_seq, seq_place), seq_place, 0)
    indices = lax.dynamic_update_index_in_dim(indices, adapter_index, seq_place, 0)
    for shift in range(1, n_seq):
        pairs = [(c, (c + shift) % n_seq) for c in range(n_seq)]
        got = lax.ppermute(pick(by_seq, (seq_place + shift) % n_seq), "seq", pairs)
        got_index = lax.ppermute(adapter_index, "seq", pairs)
        collected = lax.dynamic_update_index_in_dim(
            collected, got, (seq_place - shift) % n_seq, 0
        )
        indices = lax.dynamic_update_index_in_dim(
            indices, got_index, (seq_place - shift) % n_seq, 0
        )
    onehot = (
        jnp.arange(adapters, dtype=jnp.int32)[:, None] == indices.reshape(1, -1)
    ).astype(bf16)
    owned = nn(onehot, collected.reshape(n_seq * slabs, sizes))
    shapes = [
        (5, rank, model // (2 * owners)),
        (2, rank, model // owners),
        (rank, local_heads, head_dim // owners),
        (3, rank, local_heads, head_dim // owners),
        (rank, local_hidden // row_width, row_width // owners),
        (2, rank, local_hidden // row_width, row_width // owners),
    ]
    outputs = []
    at = 0
    for shape in shapes:
        count = 1
        for extent in shape:
            count *= extent
        outputs.append(owned[:, at : at + count].reshape((adapters,) + shape))
        at += count
    return (layer_out_own, input_grad, *outputs)


def solution(mesh):
    return jax.shard_map(
        body,
        mesh=mesh,
        in_specs=(
            P("seq", "ctx", None),
            P("seq", "ctx"),
            P("seq"),
            P(None, None, "wt"),
            P("wt", None),
            P(None, None, "wt"),
            P("wt", None),
            P("wt"),
            P(),
            P(None, "wt"),
            P(),
            P(),
            P(None, None, "wt", None),
            P(None, None, None, "wt", None),
            P(None, None, "wt", None),
            P(None, None, None, "wt", None),
            P("seq", "ctx", None),
        ),
        out_specs=(
            P("seq", "ctx", None),
            P("seq", "ctx", None),
            P(None, None, None, ("seq", "ctx", "wt")),
            P(None, None, None, ("seq", "ctx")),
            P(None, None, "wt", ("seq", "ctx")),
            P(None, None, None, "wt", ("seq", "ctx")),
            P(None, None, "wt", ("seq", "ctx")),
            P(None, None, None, "wt", ("seq", "ctx")),
        ),
        check_vma=False,
    )
```

time: 1590 us -> 453 us (0.28)
  waiting for transfers between devices: 1100 us -> 82.9 us
  blocking collectives: 103 us -> 0 us
  matrix products: 185 us -> 117 us
  Pallas kernels: 0 us -> 46.9 us
  starting transfers between devices: 2 us -> 34.9 us
    reduce_scatter x4 -> x0, waiting for transfers between devices: 685 us -> none  [the longest x1 349 us: body(): lax.psum_scatter(table_bd, ('seq', 'ctx'), scatter_dimension=4, tiled=True)]
    unnamed x16 -> x0, waiting for transfers between devices: 194 us -> none
    all_gather x4 -> x0, waiting for transfers between devices: 161 us -> none  [the longest x1 61.3 us: body(): value_part = lax.all_gather(value_low, 'ctx', axis=1, tiled=True)]
    all_gather x3 -> x0, blocking collectives: 95.5 us -> none  [the longest x1 33.6 us: body(): lax.all_gather(log_rows, 'ctx', axis=1, tiled=True)]
    ppermute x0 -> x36, waiting for transfers between devices: none -> 82.9 us  [the longest x18 46.3 us: to_slab(): return lax.ppermute(array, 'ctx', pairs)]
    dot_general x51 -> x48, matrix products: 185 us -> 117 us  [dot(): lax.dot_general(left, right, (contract, ((), ())), preferred_element_type...]
    psum x4 -> x0, waiting for transfers between devices: 62.4 us -> none  [the longest x1 22.5 us: body(): grad_middle = grad_mid_res + lax.psum(middle_part, 'wt')]
    pallas_call x0 -> x3, Pallas kernels: none -> 46.9 us  [the longest x1 21.7 us: run_attend_back(): pl.pallas_call(functools.partial(attend_back_kernel, (chunks, chunk, grou...]
  transfers between devices with their start and end apart: 14 -> 36, of which waited for: 12 -> 10; matrix products, arithmetic and copies ran while one was open for 14% -> 31% of each run, Pallas kernels for 0% -> 0%
where the time goes in v1:
time: 453 us; the launch traced here: 448 us
  local copies, waits for them, and re-layouts  126 us (28%)
  matrix products  117 us (26%)
  waiting for transfers between devices  82.9 us (18%)
  Pallas kernels  46.9 us (10%)
  other arithmetic  35.9 us (8%)
  starting transfers between devices  34.9 us (8%)
    dot_general x48, matrix products, dot(): lax.dot_general(left, right, (contract, ((), ())), preferred_element_type...  117 us
    ppermute x18, waiting for transfers between devices, to_slab(): return lax.ppermute(array, 'ctx', pairs)  46.3 us
    ppermute x4, waiting for transfers between devices, within_slab(): return lax.ppermute(array, 'ctx', pairs)  35.4 us
    ppermute x18, starting transfers between devices, to_slab(): return lax.ppermute(array, 'ctx', pairs)  25.9 us
    pallas_call x1, Pallas kernels, run_attend_back(): pl.pallas_call(functools.partial(attend_back_kernel, (chunks, chunk, grou...  21.7 us
    transpose x4, local copies, waits for them, and re-layouts, by_owner(): return jnp.moveaxis(shaped, -2, 0).reshape(owners, -1)  17.8 us
    unnamed x166, local copies, waits for them, and re-layouts  17.5 us
    concatenate x7, local copies, waits for them, and re-layouts, body(): jnp.concatenate([am_sum, by_owner(jnp.stack([grad_bm_attn, grad_bm_down])...  16.8 us
  transfers between devices with their start and end apart: 36, of which 10 were waited for; matrix products, arithmetic and copies ran while one was open for 31% of the time, Pallas kernels for 0%

profile of v1, /device:TPU:0, one launch (start us, length us, event | category | flops | bytes accessed | tf_op | source)
XLA Modules:
  0.0 447.6 jit_solution(5346581111950477685)
XLA Ops:
  14.6 8.9 %collective-permute-done.1 = bf16[128,640]{1,0:T(8,128)(2,1)S(1)} collective-permute-done((bf16[128,640]{1,0:T(8,128)(2,1)S(1)}, bf16[128,640]{1,0:T(8,128)(2,1)S(1)}, u32[]{:S(2)}, u32[]{:S(2)}) %collective-permute-start.1) | collective-permute-done | bytes 163872 | tf_op jit(solution)/shard_map/ppermute | solution.py:366
  27.7 14.1 %collective-permute-done.3 = bf16[4,128,640]{2,1,0:T(8,128)(2,1)} collective-permute-done((bf16[4,128,640]{2,1,0:T(8,128)(2,1)}, bf16[4,128,640]{2,1,0:T(8,128)(2,1)}, u32[]{:S(2)}, u32[]{:S(2)}) %collective-permute-start.3) | collective-permute-done | bytes 655392 | tf_op jit(solution)/shard_map/ppermute | solution.py:370
  63.0 16.7 %qkv.1 = (bf16[512,640]{1,0:T(8,128)(2,1)}, bf16[1024,640]{1,0:T(8,128)(2,1)}, bf16[1024,640]{1,0:T(8,128)(2,1)}, bf16[1024,48]{1,0:T(8,128)(2,1)}, f32[512,640]{1,0:T(8,128)}, /*index=5*/f32[1024,640]{1,0:T(8,128)}) custom-call(s32[1]{0:T(128)} %bitcast.14.place, bf16[1024,1280]{1,0:T(8,128)(2,1)} %maximum_select_fusion.h_ref, bf16[3,1280,640]{2,1,0:T(8,128)(2,1)} %w_ref.1, ...), custom_call_target="tpu_custom_call" | custom-call | tf_op jit(solution)/shard_map/qkv/pallas_call | solution.py:116
  79.7 8.6 %attend.1 = (bf16[512,640]{1,0:T(8,128)(2,1)}, f32[5,128,512]{2,1,0:T(8,128)}, f32[5,4,256]{2,1,0:T(4,128)}) custom-call(s32[1]{0:T(128)} %bitcast.14.place, s32[1,512]{1,0:T(1,128)} %bitcast.370, bf16[512,640]{1,0:T(8,128)(2,1)} %get-tuple-element.20.q_ref, bf16[1024,640]{1,0:T(8,128)(2,1)} %get-tuple-element.21.k_ref, ...), custom_call_target="tpu_custom_call" | custom-call | tf_op jit(solution)/shard_map/attend/pallas_call | solution.py:203
  103.1 6.8 %fusion.2 = f32[512,2560]{1,0:T(8,128)S(1)} fusion(bf16[512,1280]{1,0:T(8,128)(2,1)S(1)} %multiply_convert_fusion.2, bf16[2,1280,2560]{2,1,0:T(8,128)(2,1)} %param.22), kind=kOutput, calls=%fused_computation.3 | convolution fusion | flops 3355443200 | bytes 13107200 | tf_op jit(solution)/shard_map/dot_general | solution.py:18
  110.4 5.3 %fusion.6 = f32[512,2560]{1,0:T(8,128)} fusion(bf16[512,1280]{1,0:T(8,128)(2,1)S(1)} %multiply_convert_fusion.2, bf16[2,1280,2560]{2,1,0:T(8,128)(2,1)S(1)} %bitcast.382), kind=kOutput, calls=%fused_computation.7 | convolution fusion | flops 3355443200 | bytes 13107200 | tf_op jit(solution)/shard_map/dot_general | solution.py:18
  117.5 5.6 %multiply_convert_fusion.1 = (bf16[512,2560]{1,0:T(8,128)(2,1)S(1)}, f32[512,2560]{1,0:T(8,128)}) fusion(f32[512,2560]{1,0:T(8,128)S(1)} %add_multiply_fusion, f32[2560]{0:T(1024)S(1)} %get-tuple-element.67, f32[512,2560]{1,0:T(8,128)} %fusion.6, bf16[512,16]{0,1:T(8,128)(2,1)S(1)} %convolution_convert_fusion.5, bf16[2,8,20,128]{3,2,1,0:T(8,128)(2,1)S(1)} %bitcast.365), kind=kOutput, calls=%fused_computation.19 | convolution fusion | flops 52428800 | bytes 18458624 | tf_op jit(solution)/shard_map/dot_general | solution.py:18
  123.1 7.4 %fusion.94 = f32[512,1280]{1,0:T(8,128)S(1)} fusion(bf16[512,2560]{1,0:T(8,128)(2,1)S(1)} %get-tuple-element.118, bf16[2560,1280]{1,0:T(8,128)(2,1)} %param.23), kind=kOutput, calls=%fused_computation.255 | convolution fusion | flops 3355443200 | bytes 11796480 | tf_op jit(solution)/shard_map/dot_general | solution.py:18
  140.0 10.1 %collective-permute-done.18 = bf16[128,640]{1,0:T(8,128)(2,1)S(1)} collective-permute-done((bf16[128,640]{1,0:T(8,128)(2,1)S(1)}, bf16[128,640]{1,0:T(8,128)(2,1)S(1)}, u32[]{:S(2)}, u32[]{:S(2)}) %collective-permute-start.18) | collective-permute-done | bytes 163872 | tf_op jit(solution)/shard_map/ppermute | solution.py:366
  159.3 8.2 %fusion.95 = f32[512,2560]{1,0:T(8,128)} fusion(bf16[512,1280]{1,0:T(8,128)(2,1)S(1)} %fusion.22, bf16[2560,1280]{1,0:T(8,128)(2,1)} %param.23), kind=kOutput, calls=%fused_computation.256 | convolution fusion | flops 3355443200 | bytes 13107200 | tf_op jit(solution)/shard_map/dot_general | solution.py:18
  167.5 6.0 %multiply_convert_fusion = (bf16[512,2560]{1,0:T(8,128)(2,1)S(1)}, bf16[512,2560]{1,0:T(8,128)(2,1)S(1)}) fusion(f32[2560]{0:T(1024)S(1)} %get-tuple-element.67, f32[512,2560]{1,0:T(8,128)S(1)} %add_multiply_fusion, f32[2560]{0:T(1024)S(1)} %get-tuple-element.66, f32[512,2560]{1,0:T(8,128)} %get-tuple-element.119, f32[512,2560]{1,0:T(8,128)} %fusion.95, ...), kind=kOutput, calls=%fused_computation.18 | convolution fusion | flops 64225280 | bytes 21090304 | tf_op jit(solution)/shard_map/dot_general | solution.py:18
  215.6 5.5 %copy.172 = f32[16,2,16,20,8]{4,3,2,1,0:T(8,128)} copy(f32[16,2,16,20,8]{2,4,0,3,1:T(8,128)} %maximum_bitcast_fusion) | data formatting | bytes 655360 | tf_op jit(solution)/shard_map/transpose | solution.py:551
  221.1 5.5 %concatenate.96 = f32[2,4,2,5120]{3,2,1,0:T(2,128)} reshape(f32[16,2,16,20,8]{4,3,2,1,0:T(8,128)} %copy.172) | data formatting | bytes 655360 | tf_op jit(solution)/shard_map/concatenate | solution.py:557
  226.6 5.0 %multiply_reduce_fusion.1 = (f32[512]{0:T(512)S(1)}, f32[512,1280]{1,0:T(8,128)S(1)}) fusion(f32[512,1280]{1,0:T(8,128)} %copy-done.1, f32[512,1280]{1,0:T(8,128)} %collective-permute-done.21, f32[512,1280]{1,0:T(8,128)} %convolution_add_fusion.2, f32[1280]{0:T(1024)S(1)} %get-tuple-element.68, f32[512,1280]{1,0:T(8,128)} %copy-done.3, ...), kind=kLoop, calls=%fused_computation.51 | loop fusion | flops 13762048 | bytes 14429185 | tf_op jit(solution)/shard_map/transpose(jvp())/reduce_sum | solution.py:34
  241.2 21.7 %attend_back.1 = (bf16[512,640]{1,0:T(8,128)(2,1)}, bf16[1024,640]{1,0:T(8,128)(2,1)}, bf16[1024,640]{1,0:T(8,128)(2,1)}) custom-call(s32[1]{0:T(128)} %bitcast.14.place, s32[1,512]{1,0:T(1,128)} %bitcast.371, bf16[512,640]{1,0:T(8,128)(2,1)} %get-tuple-element.20.q_ref, bf16[1024,640]{1,0:T(8,128)(2,1)} %get-tuple-element.21.k_ref, ...), custom_call_target="tpu_custom_call" | custom-call | tf_op jit(solution)/shard_map/attend_back/pallas_call | solution.py:301
  265.0 6.0 %fusion.25 = f32[1024,1280]{1,0:T(8,128)} fusion(bf16[1024,640]{1,0:T(8,128)(2,1)} %get-tuple-element.30, bf16[3,1280,640]{2,1,0:T(8,128)(2,1)S(1)} %bitcast.345), kind=kOutput, calls=%fused_computation.63 | convolution fusion | flops 1677721600 | bytes 8192000 | tf_op jit(solution)/shard_map/dot_general | solution.py:18
  272.5 4.6 %fusion.27 = f32[1024,1280]{1,0:T(8,128)} fusion(bf16[1024,640]{1,0:T(8,128)(2,1)S(1)} %copy-done.24, bf16[3,1280,640]{2,1,0:T(8,128)(2,1)S(1)} %bitcast.345), kind=kOutput, calls=%fused_computation.65 | convolution fusion | flops 1677721600 | bytes 8192000 | tf_op jit(solution)/shard_map/dot_general | solution.py:18
  283.1 4.3 fusion.29
  315.9 7.4 %add_add_fusion = f32[1024,1280]{1,0:T(8,128)} fusion(f32[1024,1280]{1,0:T(8,128)S(1)} %bitcast.325, f32[1024,1280]{1,0:T(8,128)} %fusion.27, f32[1024,1280]{1,0:T(8,128)} %fusion.25, bf16[1024,16]{0,1:T(8,128)(2,1)S(1)} %copy-done.43, bf16[8,5,16,1280]{3,2,1,0:T(8,128)(2,1)S(1)} %copy-done, s32[]{:T(128)S(6)} %select_n.327, s32[]{:T(128)S(6)} %add.474), kind=kOutput, calls=%fused_computation.17 | convolution fusion | flops 45875200 | bytes 21045256 | tf_op jit(solution)/shard_map/dot_general | solution.py:18
  323.4 6.6 %copy.167 = f32[16,3,16,10,4]{4,3,2,1,0:T(8,128)} copy(f32[16,3,16,10,4]{0,2,4,3,1:T(8,128)S(1)} %maximum_bitcast_fusion.1) | data formatting | bytes 245760 | tf_op jit(solution)/shard_map/transpose | solution.py:551
  330.0 4.4 concatenate.94
  337.3 7.2 %collective-permute-done.31 = bf16[2,4,16000]{2,1,0:T(4,128)(2,1)S(1)} collective-permute-done((bf16[2,4,16000]{2,1,0:T(4,128)(2,1)S(1)}, bf16[2,4,16000]{2,1,0:T(4,128)(2,1)S(1)}, u32[]{:S(2)}, u32[]{:S(2)}) %collective-permute-start.31) | collective-permute-done | bytes 256032 | tf_op jit(solution)/shard_map/ppermute | solution.py:370
  372.9 14.1 %collective-permute-done.24 = bf16[512,640]{1,0:T(8,128)(2,1)} collective-permute-done((bf16[512,640]{1,0:T(8,128)(2,1)S(1)}, bf16[512,640]{1,0:T(8,128)(2,1)}, u32[]{:S(2)}, u32[]{:S(2)}) %collective-permute-start.24) | collective-permute-done | bytes 655392 | tf_op jit(solution)/shard_map/ppermute | solution.py:370
  403.3 20.3 %collective-permute-done.26 = bf16[128,640]{1,0:T(8,128)(2,1)S(1)} collective-permute-done((bf16[128,640]{1,0:T(8,128)(2,1)S(1)}, bf16[128,640]{1,0:T(8,128)(2,1)S(1)}, u32[]{:S(2)}, u32[]{:S(2)}) %collective-permute-start.26) | collective-permute-done | bytes 163872 | tf_op jit(solution)/shard_map/ppermute | solution.py:366
  (425 shorter events, 233.2 us)
Async XLA Ops:
  3.8 10.1 %collective-permute-start = (bf16[128,640]{1,0:T(8,128)(2,1)S(1)}, bf16[128,640]{1,0:T(8,128)(2,1)S(1)}, u32[]{:S(2)}, u32[]{:S(2)}) collective-permute-start(bf16[128,640]{1,0:T(8,128)(2,1)S(1)} %get-tuple-element.83), channel_id=1, source_target_pairs={{0,4},{2,6},{4,8},{6,10},{8,12},{10,14},{12,0},{14,2},{1,5},{3,7},... | collective-permute-start | bytes 491528 | tf_op jit(solution)/shard_map/ppermute | solution.py:366
  6.8 17.4 %collective-permute-start.2 = (bf16[128,640]{1,0:T(8,128)(2,1)S(1)}, bf16[128,640]{1,0:T(8,128)(2,1)S(1)}, u32[]{:S(2)}, u32[]{:S(2)}) collective-permute-start(bf16[128,640]{1,0:T(8,128)(2,1)S(1)} %get-tuple-element.82), channel_id=1, source_target_pairs={{0,12},{2,14},{4,0},{6,2},{8,4},{10,6},{12,8},{14,10},{1,13},{3,15... | collective-permute-start | bytes 491528 | tf_op jit(solution)/shard_map/ppermute | solution.py:366
  8.9 14.6 %collective-permute-start.1 = (bf16[128,640]{1,0:T(8,128)(2,1)S(1)}, bf16[128,640]{1,0:T(8,128)(2,1)S(1)}, u32[]{:S(2)}, u32[]{:S(2)}) collective-permute-start(bf16[128,640]{1,0:T(8,128)(2,1)S(1)} %get-tuple-element.85), channel_id=1, source_target_pairs={{0,8},{2,10},{4,12},{6,14},{8,0},{10,2},{12,4},{14,6},{1,9},{3,11}... | collective-permute-start | bytes 491528 | tf_op jit(solution)/shard_map/ppermute | solution.py:366
  24.9 17.0 %collective-permute-start.3 = (bf16[4,128,640]{2,1,0:T(8,128)(2,1)}, bf16[4,128,640]{2,1,0:T(8,128)(2,1)}, u32[]{:S(2)}, u32[]{:S(2)}) collective-permute-start(bf16[4,128,640]{2,1,0:T(8,128)(2,1)} %bitcast_dynamic-update-slice_fusion.11), channel_id=1, source_target_pairs={{0,2},{2,0},{4,6},{6,4},{8,10},{10,8},{12,14},{14,12},{1,3},{3,1},... | collective-permute-start | bytes 1966088 | tf_op jit(solution)/shard_map/ppermute | solution.py:370
  43.1 16.4 %collective-permute-start.4 = (bf16[1024,640]{1,0:T(8,128)(2,1)S(1)}, bf16[1024,640]{1,0:T(8,128)(2,1)}, u32[]{:S(2)}, u32[]{:S(2)}) collective-permute-start(bf16[1024,640]{1,0:T(8,128)(2,1)S(1)} %bitcast.333), channel_id=1, source_target_pairs={{0,1},{1,0},{2,3},{3,2},{4,5},{5,4},{6,7},{7,6},{8,9},{9,8},{10,11... | collective-permute-start | bytes 3932168 | tf_op jit(solution)/shard_map/ppermute | solution.py:373
  130.5 21.5 %collective-permute-start.11 = (f32[512,1280]{1,0:T(8,128)S(1)}, f32[512,1280]{1,0:T(8,128)S(1)}, u32[]{:S(2)}, u32[]{:S(2)}) collective-permute-start(f32[512,1280]{1,0:T(8,128)S(1)} %fusion.94), channel_id=1, source_target_pairs={{0,1},{1,0},{2,3},{3,2},{4,5},{5,4},{6,7},{7,6},{8,9},{9,8},{10,11... | collective-permute-start | bytes 7864328 | tf_op jit(solution)/shard_map/ppermute | solution.py:373
  131.0 8.9 %collective-permute-start.17 = (bf16[128,640]{1,0:T(8,128)(2,1)S(1)}, bf16[128,640]{1,0:T(8,128)(2,1)S(1)}, u32[]{:S(2)}, u32[]{:S(2)}) collective-permute-start(bf16[128,640]{1,0:T(8,128)(2,1)S(1)} %get-tuple-element.87), channel_id=1, source_target_pairs={{0,4},{2,6},{4,8},{6,10},{8,12},{10,14},{12,0},{14,2},{1,5},{3,7},... | collective-permute-start | bytes 491528 | tf_op jit(solution)/shard_map/ppermute | solution.py:366
  134.0 16.9 %collective-permute-start.19 = (bf16[128,640]{1,0:T(8,128)(2,1)S(1)}, bf16[128,640]{1,0:T(8,128)(2,1)S(1)}, u32[]{:S(2)}, u32[]{:S(2)}) collective-permute-start(bf16[128,640]{1,0:T(8,128)(2,1)S(1)} %get-tuple-element.86), channel_id=1, source_target_pairs={{0,12},{2,14},{4,0},{6,2},{8,4},{10,6},{12,8},{14,10},{1,13},{3,15... | collective-permute-start | bytes 491528 | tf_op jit(solution)/shard_map/ppermute | solution.py:366
  134.9 15.1 %collective-permute-start.18 = (bf16[128,640]{1,0:T(8,128)(2,1)S(1)}, bf16[128,640]{1,0:T(8,128)(2,1)S(1)}, u32[]{:S(2)}, u32[]{:S(2)}) collective-permute-start(bf16[128,640]{1,0:T(8,128)(2,1)S(1)} %get-tuple-element.89), channel_id=1, source_target_pairs={{0,8},{2,10},{4,12},{6,14},{8,0},{10,2},{12,4},{14,6},{1,9},{3,11}... | collective-permute-start | bytes 491528 | tf_op jit(solution)/shard_map/ppermute | solution.py:366
  184.9 41.7 %collective-permute-start.21 = (f32[512,1280]{1,0:T(8,128)}, f32[512,1280]{1,0:T(8,128)}, u32[]{:S(2)}, u32[]{:S(2)}) collective-permute-start(f32[512,1280]{1,0:T(8,128)} %convolution_add_fusion.2), channel_id=1, source_target_pairs={{0,1},{1,0},{2,3},{3,2},{4,5},{5,4},{6,7},{7,6},{8,9},{9,8},{10,11... | collective-permute-start | bytes 7864328 | tf_op jit(solution)/shard_map/ppermute | solution.py:373
  300.4 33.9 %collective-permute-start.30 = (bf16[16,3200]{1,0:T(8,128)(2,1)}, bf16[16,3200]{1,0:T(8,128)(2,1)}, u32[]{:S(2)}, u32[]{:S(2)}) collective-permute-start(bf16[16,3200]{1,0:T(8,128)(2,1)} %fusion.52), channel_id=1, source_target_pairs={{0,1},{1,0},{2,3},{3,2},{4,5},{5,4},{6,7},{7,6},{8,9},{9,8},{10,11... | collective-permute-start | bytes 307208 | tf_op jit(solution)/shard_map/ppermute | solution.py:373
  314.5 58.4 %collective-permute-start.22 = (bf16[512,640]{1,0:T(8,128)(2,1)}, bf16[512,640]{1,0:T(8,128)(2,1)}, u32[]{:S(2)}, u32[]{:S(2)}) collective-permute-start(bf16[512,640]{1,0:T(8,128)(2,1)} %dynamic-slice_convert_fusion.1), channel_id=1, source_target_pairs={{0,1},{1,0},{2,3},{3,2},{4,5},{5,4},{6,7},{7,6},{8,9},{9,8},{10,11... | collective-permute-start | bytes 1966088 | tf_op jit(solution)/shard_map/ppermute | solution.py:373
  336.3 8.2 %collective-permute-start.31 = (bf16[2,4,16000]{2,1,0:T(4,128)(2,1)S(1)}, bf16[2,4,16000]{2,1,0:T(4,128)(2,1)S(1)}, u32[]{:S(2)}, u32[]{:S(2)}) collective-permute-start(bf16[2,4,16000]{2,1,0:T(4,128)(2,1)S(1)} %bitcast.367), channel_id=1, source_target_pairs={{0,2},{2,0},{4,6},{6,4},{8,10},{10,8},{12,14},{14,12},{1,3},{3,1},... | collective-permute-start | bytes 768008 | tf_op jit(solution)/shard_map/ppermute | solution.py:370
  346.1 8.7 %collective-permute-start.33 = (bf16[2,16000]{1,0:T(2,128)(2,1)S(1)}, bf16[2,16000]{1,0:T(2,128)(2,1)}, u32[]{:S(2)}, u32[]{:S(2)}) collective-permute-start(bf16[2,16000]{1,0:T(2,128)(2,1)S(1)} %bitcast.369), channel_id=1, source_target_pairs={{0,8},{2,10},{4,12},{6,14},{8,0},{10,2},{12,4},{14,6},{1,9},{3,11}... | collective-permute-start | bytes 192008 | tf_op jit(solution)/shard_map/ppermute | solution.py:366
  351.8 14.2 %collective-permute-start.23 = (bf16[2,4,128,640]{3,2,1,0:T(8,128)(2,1)S(1)}, bf16[2,4,128,640]{3,2,1,0:T(8,128)(2,1)}, u32[]{:S(2)}, u32[]{:S(2)}) collective-permute-start(bf16[2,4,128,640]{3,2,1,0:T(8,128)(2,1)S(1)} %fusion.35), channel_id=1, source_target_pairs={{0,1},{1,0},{2,3},{3,2},{4,5},{5,4},{6,7},{7,6},{8,9},{9,8},{10,11... | collective-permute-start | bytes 3932168 | tf_op jit(solution)/shard_map/ppermute | solution.py:373
  370.0 17.0 %collective-permute-start.24 = (bf16[512,640]{1,0:T(8,128)(2,1)S(1)}, bf16[512,640]{1,0:T(8,128)(2,1)}, u32[]{:S(2)}, u32[]{:S(2)}) collective-permute-start(bf16[512,640]{1,0:T(8,128)(2,1)S(1)} %bitcast.360), channel_id=1, source_target_pairs={{0,2},{2,0},{4,6},{6,4},{8,10},{10,8},{12,14},{14,12},{1,3},{3,1},... | collective-permute-start | bytes 1966088 | tf_op jit(solution)/shard_map/ppermute | solution.py:370
  391.7 10.0 %collective-permute-start.25 = (bf16[128,640]{1,0:T(8,128)(2,1)S(1)}, bf16[128,640]{1,0:T(8,128)(2,1)S(1)}, u32[]{:S(2)}, u32[]{:S(2)}) collective-permute-start(bf16[128,640]{1,0:T(8,128)(2,1)S(1)} %get-tuple-element.95), channel_id=1, source_target_pairs={{0,4},{2,6},{4,8},{6,10},{8,12},{10,14},{12,0},{14,2},{1,5},{3,7},... | collective-permute-start | bytes 491528 | tf_op jit(solution)/shard_map/ppermute | solution.py:366
  394.5 31.9 %collective-permute-start.15 = (bf16[128,640]{1,0:T(8,128)(2,1)S(1)}, bf16[128,640]{1,0:T(8,128)(2,1)S(1)}, u32[]{:S(2)}, u32[]{:S(2)}) collective-permute-start(bf16[128,640]{1,0:T(8,128)(2,1)S(1)} %get-tuple-element.97), channel_id=1, source_target_pairs={{0,12},{2,14},{4,0},{6,2},{8,4},{10,6},{12,8},{14,10},{1,13},{3,15... | collective-permute-start | bytes 491528 | tf_op jit(solution)/shard_map/ppermute | solution.py:366
  397.5 28.2 %collective-permute-start.14 = (bf16[128,640]{1,0:T(8,128)(2,1)S(1)}, bf16[128,640]{1,0:T(8,128)(2,1)S(1)}, u32[]{:S(2)}, u32[]{:S(2)}) collective-permute-start(bf16[128,640]{1,0:T(8,128)(2,1)S(1)} %get-tuple-element.98), channel_id=1, source_target_pairs={{0,8},{2,10},{4,12},{6,14},{8,0},{10,2},{12,4},{14,6},{1,9},{3,11}... | collective-permute-start | bytes 491528 | tf_op jit(solution)/shard_map/ppermute | solution.py:366
  397.7 27.2 %collective-permute-start.13 = (bf16[128,640]{1,0:T(8,128)(2,1)S(1)}, bf16[128,640]{1,0:T(8,128)(2,1)S(1)}, u32[]{:S(2)}, u32[]{:S(2)}) collective-permute-start(bf16[128,640]{1,0:T(8,128)(2,1)S(1)} %get-tuple-element.99), channel_id=1, source_target_pairs={{0,4},{2,6},{4,8},{6,10},{8,12},{10,14},{12,0},{14,2},{1,5},{3,7},... | collective-permute-start | bytes 491528 | tf_op jit(solution)/shard_map/ppermute | solution.py:366
  398.0 26.2 %collective-permute-start.27 = (bf16[128,640]{1,0:T(8,128)(2,1)S(1)}, bf16[128,640]{1,0:T(8,128)(2,1)S(1)}, u32[]{:S(2)}, u32[]{:S(2)}) collective-permute-start(bf16[128,640]{1,0:T(8,128)(2,1)S(1)} %get-tuple-element.93), channel_id=1, source_target_pairs={{0,12},{2,14},{4,0},{6,2},{8,4},{10,6},{12,8},{14,10},{1,13},{3,15... | collective-permute-start | bytes 491528 | tf_op jit(solution)/shard_map/ppermute | solution.py:366
  401.7 21.8 %collective-permute-start.26 = (bf16[128,640]{1,0:T(8,128)(2,1)S(1)}, bf16[128,640]{1,0:T(8,128)(2,1)S(1)}, u32[]{:S(2)}, u32[]{:S(2)}) collective-permute-start(bf16[128,640]{1,0:T(8,128)(2,1)S(1)} %get-tuple-element.94), channel_id=1, source_target_pairs={{0,8},{2,10},{4,12},{6,14},{8,0},{10,2},{12,4},{14,6},{1,9},{3,11}... | collective-permute-start | bytes 491528 | tf_op jit(solution)/shard_map/ppermute | solution.py:366
  424.9 19.0 %collective-permute-start.28 = (bf16[4,128,640]{2,1,0:T(8,128)(2,1)}, bf16[4,128,640]{2,1,0:T(8,128)(2,1)}, u32[]{:S(2)}, u32[]{:S(2)}) collective-permute-start(bf16[4,128,640]{2,1,0:T(8,128)(2,1)} %bitcast_dynamic-update-slice_fusion.2), channel_id=1, source_target_pairs={{0,1},{1,0},{2,3},{3,2},{4,5},{5,4},{6,7},{7,6},{8,9},{9,8},{10,11... | collective-permute-start | bytes 1966088 | tf_op jit(solution)/shard_map/ppermute | solution.py:373
  427.0 13.9 %collective-permute-start.16 = (bf16[4,128,640]{2,1,0:T(8,128)(2,1)}, bf16[4,128,640]{2,1,0:T(8,128)(2,1)}, u32[]{:S(2)}, u32[]{:S(2)}) collective-permute-start(bf16[4,128,640]{2,1,0:T(8,128)(2,1)} %bitcast_dynamic-update-slice_fusion.8), channel_id=1, source_target_pairs={{0,1},{1,0},{2,3},{3,2},{4,5},{5,4},{6,7},{7,6},{8,9},{9,8},{10,11... | collective-permute-start | bytes 1966088 | tf_op jit(solution)/shard_map/ppermute | solution.py:373
  (88 other events, 800.0 us)

commit v2 on v1

v2 whole, which is shorter than its diff:
```python
import functools

import jax
import jax.numpy as jnp
from jax import lax
from jax.experimental import pallas as pl
from jax.experimental.pallas import tpu as pltpu
from jax.sharding import PartitionSpec as P

epsilon = 1e-06
f32 = jnp.float32
bf16 = jnp.bfloat16
i32 = jnp.int32
VMEM_LIMIT = 58 * 1024 * 1024
log2e = 1.4426950408889634
LANES = 128


def dot(left, right, contract):
    return lax.dot_general(left, right, (contract, ((), ())), preferred_element_type=f32)


def nn(left, right):
    return dot(left, right, ((1,), (0,)))


def nt(left, right):
    return dot(left, right, ((1,), (1,)))


def tn(left, right):
    return dot(left, right, ((0,), (0,)))


def lane_iota(shape):
    return lax.broadcasted_iota(i32, shape, len(shape) - 1)


def row_iota(shape):
    return lax.broadcasted_iota(i32, shape, 0)


def row_mean(values):
    return jnp.mean(values, axis=-1, keepdims=True)


def inverse_rms(values):
    return lax.rsqrt(row_mean(values * values) + epsilon)


def at_rows(index, size):
    return pl.ds(pl.multiple_of(index * size, size), size)


def by_rows(total, size, step):
    lax.fori_loop(0, total // size, lambda i, c: (step(at_rows(i, size)), c)[1], 0)


def swap_halves(tile, half):
    lower = lane_iota(tile.shape) % (2 * half) < half
    return jnp.where(lower, pltpu.roll(tile, LANES - half, 1), pltpu.roll(tile, half, 1))


def head_sums(tile, head_dim):
    same = row_iota((LANES, LANES)) // head_dim == lane_iota((LANES, LANES)) // head_dim
    ones = jnp.where(same, 1.0, 0.0).astype(bf16)
    high = tile.astype(bf16)
    rest = (tile - high.astype(f32)).astype(bf16)
    return nn(high, ones) + nn(rest, ones)


def prep_tile(raw, cosine, sine, scale, head_dim):
    mean = head_sums(raw * raw, head_dim) * (1.0 / head_dim)
    inverse = lax.rsqrt(mean + epsilon)
    turned = raw * cosine + swap_halves(raw, head_dim // 2) * sine
    return (turned * inverse * scale).astype(bf16), inverse


def prep_tile_back(grad, low, inverse, cosine, sine, scale, head_dim):
    unit = low.astype(f32) / scale
    grad_unit = grad * scale
    mean = head_sums(grad_unit * unit, head_dim) * (1.0 / head_dim)
    grad_turned = inverse * (grad_unit - unit * mean)
    return (grad_turned * cosine - swap_halves(grad_turned, head_dim // 2) * sine).astype(bf16)


def spread_pair(tile, head_dim):
    lower = lane_iota(tile.shape) < head_dim
    zero = jnp.zeros_like(tile)
    return jnp.concatenate([jnp.where(lower, tile, zero), jnp.where(lower, zero, tile)], axis=0)


def allowed_mask(first, last, key_start, rows, diagonal):
    keys = key_start + row_iota((rows, first.shape[1]))
    mask = keys >= first
    if diagonal:
        mask = mask & (keys <= last)
    return mask


def query_bounds(start_ref, m, place, group, chunk):
    first = start_ref[:, m * chunk : (m + 1) * chunk]
    last = (m * group + place) * chunk + lane_iota((1, chunk))
    return jnp.concatenate([first, first], axis=1), jnp.concatenate([last, last], axis=1)


def whole_spec(shape):
    return pl.BlockSpec(shape, lambda *a: (0,) * len(shape))


def col_spec(size, width=LANES):
    return pl.BlockSpec((size, width), lambda p, s: (0, p))


def params():
    return pltpu.CompilerParams(vmem_limit_bytes=VMEM_LIMIT)


def attend_kernel(dims, place, *refs):
    slabs, chunk, group, head_dim, rank, half = dims
    count = 1 + (slabs - 1) * 2 + (group - 1) * slabs * 2
    pieces = refs[:count]
    (
        start_ref, w_ref, a_ref, b_ref, cos_ref, sin_ref, scale_ref, wout_ref, ah_ref,
        h_ref, own_ref, u_ref, q_ref, k_ref, v_ref, qi_ref, ki_ref, o_ref, of_ref, inv_ref,
        msg_ref, vt_ref, acc_ref,
    ) = refs[count:]
    inner, slab, core = place[0], place[1], place[2]
    block = group * chunk
    length = slabs * block
    rows = slabs * chunk
    model = 2 * half
    step = pl.program_id(0)

    @pl.when(step == 0)
    def _():
        mine = pl.ds(pl.multiple_of(core * half, half), half)
        other = pl.ds(pl.multiple_of((1 - core) * half, half), half)
        h_ref[at_rows(slab * group + inner, chunk), :] = pieces[0][0]
        own_ref[at_rows(slab, chunk), :] = pieces[0][0]
        at = 1
        for shift in range(1, slabs):
            source = lax.rem(slab - shift + slabs, slabs)
            rows_at = at_rows(source * group + inner, chunk)
            h_ref[rows_at, mine] = pieces[at][...]
            h_ref[rows_at, other] = pieces[at + 1][...]
            own_ref[at_rows(source, chunk), mine] = pieces[at][...]
            own_ref[at_rows(source, chunk), other] = pieces[at + 1][...]
            at += 2
        for turn in range(1, group):
            peer = lax.rem(inner - turn + group, group)
            for shift in range(slabs):
                source = lax.rem(slab - shift + slabs, slabs)
                rows_at = at_rows(source * group + peer, chunk)
                h_ref[rows_at, mine] = pieces[at][...]
                h_ref[rows_at, other] = pieces[at + 1][...]
                at += 2

        def low_rows(sl):
            u_ref[sl, :] = nt(h_ref[sl, :], a_ref[...]).astype(bf16)

        by_rows(length, 512, low_rows)
        acc_ref[...] = jnp.zeros_like(acc_ref)

    scale = scale_ref[...]
    w_kv = jnp.concatenate([w_ref[1], w_ref[2]], axis=1)

    def keys_rows(sl):
        both = nn(h_ref[sl, :], w_kv)
        low = u_ref[sl, :]
        raw = both[:, :LANES] + nn(low[:, rank : 2 * rank], b_ref[1])
        k_ref[sl, :], ki_ref[sl, :] = prep_tile(
            raw, cos_ref[sl, :], sin_ref[sl, :], scale, head_dim
        )
        v_ref[sl, :] = (both[:, LANES:] + nn(low[:, 2 * rank :], b_ref[2])).astype(bf16)

    by_rows(length, 512, keys_rows)
    queries = nn(own_ref[...], w_ref[0])
    for m in range(slabs):
        own = slice(m * chunk, (m + 1) * chunk)
        there = at_rows(m * group + inner, chunk)
        raw = queries[own] + nn(u_ref[there, :rank], b_ref[0])
        q_ref[own, :], qi_ref[own, :] = prep_tile(
            raw, cos_ref[there, :], sin_ref[there, :], scale, head_dim
        )
    vt_ref[...] = v_ref[...].T
    for m in range(slabs):
        own = slice(m * chunk, (m + 1) * chunk)
        pair = spread_pair(q_ref[own, :], head_dim)
        first, last = query_bounds(start_ref, m, inner, group, chunk)
        total = jnp.zeros((1, 2 * chunk), f32)
        gathered = jnp.zeros((LANES, 2 * chunk), f32)
        for b in range(m + 1):
            at = slice(b * block, (b + 1) * block)
            scores = nt(k_ref[at, :], pair)
            mask = allowed_mask(first, last, b * block, block, b == m)
            weights = jnp.where(mask, jnp.exp2(scores * (0.125 * log2e)), 0.0)
            total = total + jnp.sum(weights, axis=0, keepdims=True)
            gathered = gathered + nn(vt_ref[:, at], weights.astype(bf16))
        inverse = 1.0 / total
        gathered = gathered * inverse
        upper = row_iota((LANES, chunk)) < head_dim
        final = jnp.where(upper, gathered[:, :chunk], gathered[:, chunk:])
        of_ref[0, :, own] = final
        o_ref[own, :] = final.T.astype(bf16)
        inv_ref[0, m : m + 1, :] = inverse
    low_o = o_ref[...]
    acc_ref[:, :model] += nn(low_o, wout_ref[...])
    acc_ref[:, model:] += nt(low_o, ah_ref[...])

    @pl.when(step == pl.num_programs(0) - 1)
    def _():
        msg_ref[...] = acc_ref[...].astype(bf16)


def run_attend(place, tokens, pieces, start, w, a, b, cos, sin, scale, wout, ah, group, head_dim):
    slabs, chunk, model = tokens.shape
    width = w.shape[2]
    rank = b.shape[1]
    half = model // 2
    rows = slabs * chunk
    length = rows * group
    pairs = width // LANES
    in_specs = [pl.BlockSpec((1, chunk, model), lambda p, s: (s[1], 0, 0))]
    in_specs += [whole_spec((chunk, half))] * len(pieces)
    in_specs += [
        whole_spec((1, rows)),
        pl.BlockSpec((3, model, LANES), lambda p, s: (0, 0, p)),
        whole_spec((3 * rank, model)),
        pl.BlockSpec((3, rank, LANES), lambda p, s: (0, 0, p)),
        whole_spec((length, LANES)),
        whole_spec((length, LANES)),
        col_spec(1),
        pl.BlockSpec((LANES, model), lambda p, s: (p, 0)),
        col_spec(LANES),
    ]
    out = [
        ((length, model), bf16, whole_spec((length, model))),
        ((rows, model), bf16, whole_spec((rows, model))),
        ((length, 3 * rank), bf16, whole_spec((length, 3 * rank))),
        ((rows, width), bf16, col_spec(rows)),
        ((length, width), bf16, col_spec(length)),
        ((length, width), bf16, col_spec(length)),
        ((rows, width), f32, col_spec(rows)),
        ((length, width), f32, col_spec(length)),
        ((rows, width), bf16, col_spec(rows)),
        ((pairs, LANES, rows), f32, pl.BlockSpec((1, LANES, rows), lambda p, s: (p, 0, 0))),
        (
            (pairs, slabs, 2 * chunk),
            f32,
            pl.BlockSpec((1, slabs, 2 * chunk), lambda p, s: (p, 0, 0)),
        ),
        ((rows, model + LANES), bf16, whole_spec((rows, model + LANES))),
    ]
    return pl.pallas_call(
        functools.partial(attend_kernel, (slabs, chunk, group, head_dim, rank, half)),
        grid_spec=pltpu.PrefetchScalarGridSpec(
            num_scalar_prefetch=1,
            grid=(pairs,),
            in_specs=in_specs,
            out_specs=[o[2] for o in out],
            scratch_shapes=[
                pltpu.VMEM((LANES, length), bf16),
                pltpu.VMEM((rows, model + LANES), f32),
            ],
        ),
        out_shape=[jax.ShapeDtypeStruct(o[0], o[1]) for o in out],
        compiler_params=params(),
        name="attend",
    )(place, tokens, *pieces, start, w, a, b, cos, sin, scale, wout, ah)


def feed_kernel(
    dims, mine_ref, other_ref, h_ref, bo_ref, rate_ref, a_ref, wgu_ref, bgu_ref, wd_ref, ad_ref,
    scales_ref, mid_ref, u_ref, gate_ref, up_ref, msg_ref, low_ref, acc_ref,
):
    rank, model = dims
    rows = h_ref.shape[0]
    step = pl.program_id(0)

    @pl.when(step == 0)
    def _():
        def mix(sl):
            both = mine_ref[sl, :].astype(f32) + other_ref[sl, :].astype(f32)
            low = both[:, model : model + rank].astype(bf16)
            raw = both[:, :model] + nn(low, bo_ref[...])
            unit = raw * inverse_rms(raw)
            state = h_ref[sl, :].astype(f32)
            mixed = state + rate_ref[0:1, :] * (unit - state)
            mixed = mixed * inverse_rms(mixed)
            mid_ref[sl, :] = mixed
            low_ref[sl, :] = mixed.astype(bf16)

        by_rows(rows, 64, mix)
        u_ref[...] = nt(low_ref[...], a_ref[...]).astype(bf16)
        acc_ref[...] = jnp.zeros_like(acc_ref)

    low = low_ref[...]
    u = u_ref[...]
    gate = nn(low, wgu_ref[0]) + nn(u[:, :rank], bgu_ref[0])
    up = nn(low, wgu_ref[1]) + nn(u[:, rank:], bgu_ref[1])
    gate_ref[...] = gate.astype(bf16)
    up_ref[...] = up.astype(bf16)
    turned = gate * scales_ref[1:2, :]
    hidden = (up * scales_ref[0:1, :] * (turned / (1.0 + jnp.exp(-turned)))).astype(bf16)
    acc_ref[:, :model] += nn(hidden, wd_ref[...])
    acc_ref[:, model:] += nt(hidden, ad_ref[...])

    @pl.when(step == pl.num_programs(0) - 1)
    def _():
        msg_ref[...] = acc_ref[...].astype(bf16)


def run_feed(mine, other, h_own, bo, rates, a, wgu, bgu, wd, ad, scales, block):
    rows, model = h_own.shape
    hidden = wd.shape[0]
    rank = bo.shape[0]
    out = [
        ((rows, model), f32, whole_spec((rows, model))),
        ((rows, 2 * rank), bf16, whole_spec((rows, 2 * rank))),
        ((rows, hidden), bf16, pl.BlockSpec((rows, block), lambda f: (0, f))),
        ((rows, hidden), bf16, pl.BlockSpec((rows, block), lambda f: (0, f))),
        ((rows, model + LANES), bf16, whole_spec((rows, model + LANES))),
    ]
    return pl.pallas_call(
        functools.partial(feed_kernel, (rank, model)),
        grid=(hidden // block,),
        in_specs=[
            whole_spec((rows, model + LANES)),
            whole_spec((rows, model + LANES)),
            whole_spec((rows, model)),
            whole_spec((rank, model)),
            whole_spec((2, model)),
            whole_spec((2 * rank, model)),
            pl.BlockSpec((2, model, block), lambda f: (0, 0, f)),
            pl.BlockSpec((2, rank, block), lambda f: (0, 0, f)),
            pl.BlockSpec((block, model), lambda f: (f, 0)),
            pl.BlockSpec((LANES, block), lambda f: (0, f)),
            pl.BlockSpec((2, block), lambda f: (0, f)),
        ],
        out_specs=[o[2] for o in out],
        out_shape=[jax.ShapeDtypeStruct(o[0], o[1]) for o in out],
        scratch_shapes=[
            pltpu.VMEM((rows, model), bf16),
            pltpu.VMEM((rows, model + LANES), f32),
        ],
        compiler_params=params(),
        name="feed",
    )(mine, other, h_own, bo, rates, a, wgu, bgu, wd, ad, scales)


def owner_index(place, group, slabs, n_seq):
    inner, slab, seq = place
    return seq * slabs * group + slab * group + inner


def pad_lanes(tile):
    return jnp.pad(tile, ((0, 0), (0, LANES - tile.shape[1])))


def feed_back_kernel(
    dims, place, mine_ref, other_ref, mid_ref, g_own_ref, g_mine_ref, g_other_ref, bd_ref,
    rate_ref, a_ref, u_ref, gate_ref, up_ref, wgu_ref, bgu_ref, wd_ref, ad_ref, scales_ref,
    out_ref, res_ref, msg_ref, table_ref,
    gd_ref, gdt_ref, ut_ref, udt_ref, gud_ref, gudt_ref, low_ref, acc_ref, gu_ref, hid_ref,
    g_ref, lo_ref,
):
    slabs, chunk, group, n_seq, rank, model, row_width, hidden_rows = dims
    rows = slabs * chunk
    half = model // 2
    step = pl.program_id(0)
    slab, core = place[1], place[2]
    block = gate_ref.shape[1]

    @pl.when(step == 0)
    def _():
        mine = pl.ds(pl.multiple_of(core * half, half), half)
        other = pl.ds(pl.multiple_of((1 - core) * half, half), half)
        g_ref[at_rows(slab, chunk), :] = g_own_ref[0]
        for shift in range(1, slabs):
            source = at_rows(lax.rem(slab - shift + slabs, slabs), chunk)
            g_ref[source, mine] = g_mine_ref[shift - 1]
            g_ref[source, other] = g_other_ref[shift - 1]

        def mix(sl):
            both = mine_ref[sl, :].astype(f32) + other_ref[sl, :].astype(f32)
            low = both[:, model : model + rank].astype(bf16)
            hid_ref[sl, :] = low
            raw = both[:, :model] + nn(low, bd_ref[...])
            raw_inv = inverse_rms(raw)
            unit = raw * raw_inv
            state = mid_ref[sl, :]
            low_ref[sl, :] = state.astype(bf16)
            rate = rate_ref[1:2, :]
            mixed = state + rate * (unit - state)
            mixed_inv = inverse_rms(mixed)
            out = mixed * mixed_inv
            lo_ref[sl, :] = out.astype(bf16)
            grad = g_ref[sl, :].astype(f32)
            grad_mixed = mixed_inv * (grad - out * row_mean(grad * out))
            res_ref[sl, :] = (1.0 - rate) * grad_mixed
            grad_unit = rate * grad_mixed
            gd_ref[sl, :] = (raw_inv * (grad_unit - unit * row_mean(grad_unit * unit))).astype(bf16)

        by_rows(rows, 64, mix)
        out_ref[...] = lo_ref[:, mine].reshape(slabs, chunk, half)
        ut_ref[...] = u_ref[...].T
        udt_ref[...] = hid_ref[...].T
        low_gud = nt(gd_ref[...], bd_ref[...]).astype(bf16)
        gud_ref[...] = low_gud
        gudt_ref[...] = low_gud.T
        acc_ref[...] = jnp.zeros_like(acc_ref)
        gu_ref[...] = jnp.zeros_like(gu_ref)

    grad_hidden = nt(gd_ref[...], wd_ref[...]) + nn(gud_ref[...], ad_ref[...])
    gate = gate_ref[...].astype(f32)
    up = up_ref[...].astype(f32)
    up_scale = scales_ref[0:1, :]
    gate_scale = scales_ref[1:2, :]
    turned = gate * gate_scale
    sigmoid = 1.0 / (1.0 + jnp.exp(-turned))
    silu = turned * sigmoid
    up_scaled = up * up_scale
    hidden = (up_scaled * silu).astype(bf16)
    grad_up = (grad_hidden * up_scale * silu).astype(bf16)
    slope = sigmoid * (1.0 + turned * (1.0 - sigmoid)) * gate_scale
    grad_gate = (grad_hidden * up_scaled * slope).astype(bf16)
    acc_ref[...] += nt(grad_gate, wgu_ref[0]) + nt(grad_up, wgu_ref[1])
    gu_ref[:, :rank] += nt(grad_gate, bgu_ref[0])
    gu_ref[:, rank:] += nt(grad_up, bgu_ref[1])
    ut = ut_ref[...]
    parts = jnp.concatenate(
        [nn(gudt_ref[...], hidden), nn(ut[:rank], grad_gate), nn(ut[rank:], grad_up)], axis=0
    ).astype(bf16)
    tiles = block // row_width
    for tile in range(tiles):
        gdt_ref[step * tiles + tile] = parts[:, tile * row_width : (tile + 1) * row_width]

    @pl.when(step == pl.num_programs(0) - 1)
    def _():
        low_gu = gu_ref[...].astype(bf16)
        msg_ref[...] = (acc_ref[...] + nn(low_gu, a_ref[...])).astype(bf16)
        low = low_ref[...]
        model_rows = jnp.concatenate(
            [nn(low_gu.T, low), nn(udt_ref[...], gd_ref[...])], axis=0
        ).astype(bf16).astype(f32)
        ranks = 3 * rank
        units = ranks * hidden_rows
        padded = (units + LANES - 1) // LANES * LANES
        flat = gdt_ref[...].reshape(units, row_width)
        lanes = lane_iota((1, padded))
        target = lanes % hidden_rows * ranks + lanes // hidden_rows
        target = jnp.where(lanes < units, target, -1)
        moved = jnp.where(row_iota((units, padded)) == target, 1.0, 0.0).astype(bf16)
        turned_rows = tn(flat, moved)
        owners = n_seq * slabs * group
        cols = model // owners
        units_each = row_width // owners
        for y in range(group):
            for z in range(slabs):
                for x in range(n_seq):
                    d = owner_index((y, z, x), group, slabs, n_seq)
                    head = pad_lanes(model_rows[:, d * cols : (d + 1) * cols])
                    mine = turned_rows[d * units_each : (d + 1) * units_each]
                    tail = [
                        mine[:, t * LANES : (t + 1) * LANES] for t in range(padded // LANES)
                    ]
                    table_ref[y, z, x] = jnp.concatenate([head] + tail, axis=0).astype(bf16)


def run_feed_back(
    place, mine, other, mid, cotangent, g_mine, g_other, bd_model, rates, a, u, gate, up, wgu,
    bgu, wd, ad, scales, block, group, n_seq, row_width,
):
    slabs, chunk, model = cotangent.shape
    rows = slabs * chunk
    half = model // 2
    hidden = wd.shape[0]
    rank = bd_model.shape[0]
    hidden_rows = hidden // row_width
    owners = n_seq * slabs * group
    padded = (3 * rank * hidden_rows + LANES - 1) // LANES * LANES
    table_rows = 3 * rank + row_width // owners * (padded // LANES)
    out = [
        ((slabs, chunk, half), bf16),
        ((rows, model), f32),
        ((rows, model), bf16),
        ((group, slabs, n_seq, table_rows, LANES), bf16),
    ]
    return pl.pallas_call(
        functools.partial(
            feed_back_kernel,
            (slabs, chunk, group, n_seq, rank, model, row_width, hidden_rows),
        ),
        grid_spec=pltpu.PrefetchScalarGridSpec(
            num_scalar_prefetch=1,
            grid=(hidden // block,),
            in_specs=[
                whole_spec((rows, model + LANES)),
                whole_spec((rows, model + LANES)),
                whole_spec((rows, model)),
                pl.BlockSpec((1, chunk, model), lambda f, s: (s[1], 0, 0)),
                whole_spec((slabs - 1, chunk, half)),
                whole_spec((slabs - 1, chunk, half)),
                whole_spec((rank, model)),
                whole_spec((2, model)),
                whole_spec((2 * rank, model)),
                whole_spec((rows, 2 * rank)),
                col_spec(rows, block),
                col_spec(rows, block),
                pl.BlockSpec((2, model, block), lambda f, s: (0, 0, f)),
                pl.BlockSpec((2, rank, block), lambda f, s: (0, 0, f)),
                pl.BlockSpec((block, model), lambda f, s: (f, 0)),
                col_spec(rank, block),
                col_spec(2, block),
            ],
            out_specs=[whole_spec(o[0]) for o in out],
            scratch_shapes=[
                pltpu.VMEM((rows, model), bf16),
                pltpu.VMEM((hidden_rows, 3 * rank, row_width), bf16),
                pltpu.VMEM((2 * rank, rows), bf16),
                pltpu.VMEM((rank, rows), bf16),
                pltpu.VMEM((rows, rank), bf16),
                pltpu.VMEM((rank, rows), bf16),
                pltpu.VMEM((rows, model), bf16),
                pltpu.VMEM((rows, model), f32),
                pltpu.VMEM((rows, 2 * rank), f32),
                pltpu.VMEM((rows, rank), bf16),
                pltpu.VMEM((rows, model), bf16),
                pltpu.VMEM((rows, model), bf16),
            ],
        ),
        out_shape=[jax.ShapeDtypeStruct(o[0], o[1]) for o in out],
        compiler_params=params(),
        name="feed_back",
    )(
        place, mine, other, mid, cotangent, g_mine, g_other, bd_model, rates, a, u, gate, up,
        wgu, bgu, wd, ad, scales,
    )


def attend_back_kernel(
    dims, place, res_ref, gm_ref, go_ref, mid_ref, h_ref, am_ref, ao_ref, rate_ref, bo_ref,
    wout_ref, ah_ref, start_ref, q_ref, k_ref, v_ref, o_ref, of_ref, inv_ref, qi_ref, ki_ref,
    cos_ref, sin_ref, scale_ref,
    gq_ref, gk_ref, gv_ref, gres_ref, gbo_ref, gah_ref,
    kt_ref, gqt_ref, ga_ref, guo_ref, guot_ref, uo_ref,
):
    slabs, chunk, group, head_dim, rank, model = dims
    block = group * chunk
    rows = slabs * chunk
    inner = place[0]
    step = pl.program_id(0)

    @pl.when(step == 0)
    def _():
        def mix(sl):
            grad = res_ref[sl, :] + gm_ref[sl, :].astype(f32) + go_ref[sl, :].astype(f32)
            both = am_ref[sl, :].astype(f32) + ao_ref[sl, :].astype(f32)
            low = both[:, model : model + rank].astype(bf16)
            uo_ref[sl, :] = low
            raw = both[:, :model] + nn(low, bo_ref[...])
            raw_inv = inverse_rms(raw)
            unit = raw * raw_inv
            state = h_ref[sl, :].astype(f32)
            rate = rate_ref[0:1, :]
            mixed = state + rate * (unit - state)
            mixed_inv = inverse_rms(mixed)
            out = mid_ref[sl, :]
            grad_mixed = mixed_inv * (grad - out * row_mean(grad * out))
            gres_ref[sl, :] = (1.0 - rate) * grad_mixed
            grad_unit = rate * grad_mixed
            ga_ref[sl, :] = (raw_inv * (grad_unit - unit * row_mean(grad_unit * unit))).astype(bf16)

        by_rows(rows, 64, mix)
        gbo_ref[...] = nn(uo_ref[...].T, ga_ref[...])
        low_g = nt(ga_ref[...], bo_ref[...]).astype(bf16)
        guo_ref[...] = low_g
        guot_ref[...] = low_g.T

    kt_ref[...] = k_ref[...].T
    scale = scale_ref[...]
    grad_o = (nt(ga_ref[...], wout_ref[...]) + nn(guo_ref[...], ah_ref[...])).astype(bf16)
    gah_ref[...] = nn(guot_ref[...], o_ref[...])
    pairs_q, pairs_g, deltas, bounds = [], [], [], []
    for m in range(slabs):
        own = slice(m * chunk, (m + 1) * chunk)
        pairs_q.append(spread_pair(q_ref[own, :], head_dim))
        grad = grad_o[own]
        pairs_g.append(spread_pair(grad, head_dim))
        products = grad.astype(f32).T * of_ref[0, :, own]
        deltas.append(
            jnp.concatenate(
                [
                    jnp.sum(products[:head_dim], axis=0, keepdims=True),
                    jnp.sum(products[head_dim:], axis=0, keepdims=True),
                ],
                axis=1,
            )
        )
        bounds.append(query_bounds(start_ref, m, inner, group, chunk))
    for b in range(slabs):
        at = slice(b * block, (b + 1) * block)
        grad_key = jnp.zeros((block, LANES), f32)
        grad_value = jnp.zeros((block, LANES), f32)
        for m in range(b, slabs):
            first, last = bounds[m]
            scores = nt(k_ref[at, :], pairs_q[m])
            mask = allowed_mask(first, last, b * block, block, b == m)
            weights = jnp.exp2(scores * (0.125 * log2e)) * inv_ref[0, m : m + 1, :]
            weights = jnp.where(mask, weights, 0.0)
            grad_value = grad_value + nn(weights.astype(bf16), pairs_g[m])
            grad_weights = nt(v_ref[at, :], pairs_g[m])
            grad_scores = (weights * (grad_weights - deltas[m])).astype(bf16)
            grad_key = grad_key + nn(grad_scores, pairs_q[m])
            part = nn(kt_ref[:, at], grad_scores)
            if b == 0:
                gqt_ref[m] = part
            else:
                gqt_ref[m] += part
        gv_ref[at, :] = grad_value.astype(bf16)
        gk_ref[at, :] = prep_tile_back(
            grad_key * 0.125, k_ref[at, :], ki_ref[at, :], cos_ref[at, :], sin_ref[at, :],
            scale, head_dim,
        )
    upper = row_iota((LANES, chunk)) < head_dim
    for m in range(slabs):
        own = slice(m * chunk, (m + 1) * chunk)
        both = gqt_ref[m]
        grad = jnp.where(upper, both[:, :chunk], both[:, chunk:]).T * 0.125
        there = at_rows(m * group + inner, chunk)
        gq_ref[own, :] = prep_tile_back(
            grad, q_ref[own, :], qi_ref[own, :], cos_ref[there, :], sin_ref[there, :],
            scale, head_dim,
        )


def run_attend_back(
    place, res, gm, go, mid, h_own, am, ao, rates, bo, wout, ah, start, q, k, v, o, of, inv,
    qi, ki, cos, sin, scale, slabs, group, head_dim,
):
    rows, model = h_own.shape
    chunk = rows // slabs
    width = q.shape[1]
    length = k.shape[0]
    rank = bo.shape[0]
    pairs = width // LANES
    full = whole_spec((rows, model))
    out = [
        ((rows, width), bf16, col_spec(rows)),
        ((length, width), bf16, col_spec(length)),
        ((length, width), bf16, col_spec(length)),
        ((rows, model), f32, full),
        ((rank, model), f32, whole_spec((rank, model))),
        ((rank, width), f32, col_spec(rank)),
    ]
    return pl.pallas_call(
        functools.partial(attend_back_kernel, (slabs, chunk, group, head_dim, rank, model)),
        grid_spec=pltpu.PrefetchScalarGridSpec(
            num_scalar_prefetch=1,
            grid=(pairs,),
            in_specs=[
                full,
                full,
                full,
                full,
                full,
                whole_spec((rows, model + LANES)),
                whole_spec((rows, model + LANES)),
                whole_spec((2, model)),
                whole_spec((rank, model)),
                pl.BlockSpec((LANES, model), lambda p, s: (p, 0)),
                col_spec(rank),
                whole_spec((1, rows)),
                col_spec(rows),
                col_spec(length),
                col_spec(length),
                col_spec(rows),
                pl.BlockSpec((1, LANES, rows), lambda p, s: (p, 0, 0)),
                pl.BlockSpec((1, slabs, 2 * chunk), lambda p, s: (p, 0, 0)),
                col_spec(rows),
                col_spec(length),
                whole_spec((length, LANES)),
                whole_spec((length, LANES)),
                col_spec(1),
            ],
            out_specs=[o_[2] for o_ in out],
            scratch_shapes=[
                pltpu.VMEM((LANES, length), bf16),
                pltpu.VMEM((slabs, LANES, 2 * chunk), f32),
                pltpu.VMEM((rows, model), bf16),
                pltpu.VMEM((rows, rank), bf16),
                pltpu.VMEM((rank, rows), bf16),
                pltpu.VMEM((rows, rank), bf16),
            ],
        ),
        out_shape=[jax.ShapeDtypeStruct(o_[0], o_[1]) for o_ in out],
        compiler_params=params(),
        name="attend_back",
    )(
        place, res, gm, go, mid, h_own, am, ao, rates, bo, wout, ah, start, q, k, v, o, of,
        inv, qi, ki, cos, sin, scale,
    )


def others_kernel(dims, place, gk_ref, gv_ref, w_ref, a_ref, b_ref, keep_ref, send_ref, acc_ref):
    slabs, chunk, rank, model = dims
    half = model // 2
    core = place[2]
    width = gk_ref.shape[-1]
    gk = gk_ref[...].reshape(slabs * chunk, width)
    gv = gv_ref[...].reshape(slabs * chunk, width)
    low_k = nt(gk, b_ref[1]).astype(bf16)
    low_v = nt(gv, b_ref[2]).astype(bf16)
    acc_ref[...] = (
        nt(gk, w_ref[1])
        + nt(gv, w_ref[2])
        + nn(low_k, a_ref[rank : 2 * rank, :])
        + nn(low_v, a_ref[2 * rank :, :])
    )
    keep_ref[0] = acc_ref[:, pl.ds(pl.multiple_of(core * half, half), half)]
    send_ref[0] = acc_ref[:, pl.ds(pl.multiple_of((1 - core) * half, half), half)].astype(bf16)


def run_others(place, gk, gv, w, a, b, slabs, group):
    length, width = gk.shape
    chunk = length // (slabs * group)
    rows = slabs * chunk
    model = w.shape[1]
    half = model // 2
    rank = b.shape[1]
    shaped = (slabs, group, chunk, width)
    peer = pl.BlockSpec(
        (slabs, 1, chunk, width), lambda g, s: (0, lax.rem(s[0] + 1 + g, group), 0, 0)
    )
    return pl.pallas_call(
        functools.partial(others_kernel, (slabs, chunk, rank, model)),
        grid_spec=pltpu.PrefetchScalarGridSpec(
            num_scalar_prefetch=1,
            grid=(group - 1,),
            in_specs=[
                peer,
                peer,
                whole_spec((3, model, width)),
                whole_spec((3 * rank, model)),
                whole_spec((3, rank, width)),
            ],
            out_specs=[pl.BlockSpec((1, rows, half), lambda g, s: (g, 0, 0))] * 2,
            scratch_shapes=[pltpu.VMEM((rows, model), f32)],
        ),
        out_shape=[
            jax.ShapeDtypeStruct((group - 1, rows, half), f32),
            jax.ShapeDtypeStruct((group - 1, rows, half), bf16),
        ],
        compiler_params=params(),
        name="others",
    )(place, gk.reshape(shaped), gv.reshape(shaped), w, a, b)


def own_kernel(
    dims, place, gq_ref, gk_ref, gv_ref, gko_ref, gvo_ref, w_ref, a_ref, b_ref, u_ref, h_ref,
    hown_ref, res_ref, gbo_ref, gah_ref, keep_ref, send_ref, table_ref, acc_ref, uq_ref,
):
    slabs, chunk, group, n_seq, rank, model, head_dim = dims
    half = model // 2
    rows = slabs * chunk
    inner, core = place[0], place[2]
    width = gq_ref.shape[1]
    heads = width // head_dim
    gq = gq_ref[...]
    gko = gko_ref[...].reshape(rows, width)
    gvo = gvo_ref[...].reshape(rows, width)
    low_q = nt(gq, b_ref[0]).astype(bf16)
    low_k = nt(gk_ref[...], b_ref[1]).astype(bf16)
    low_v = nt(gv_ref[...], b_ref[2]).astype(bf16)
    acc_ref[...] = (
        nt(gq, w_ref[0])
        + nt(gko, w_ref[1])
        + nt(gvo, w_ref[2])
        + nn(low_q, a_ref[:rank, :])
        + nn(nt(gko, b_ref[1]).astype(bf16), a_ref[rank : 2 * rank, :])
        + nn(nt(gvo, b_ref[2]).astype(bf16), a_ref[2 * rank :, :])
    )
    mine = pl.ds(pl.multiple_of(core * half, half), half)
    keep_ref[...] = acc_ref[:, mine] + res_ref[:, mine]
    send_ref[...] = acc_ref[:, pl.ds(pl.multiple_of((1 - core) * half, half), half)].astype(bf16)

    for m in range(slabs):
        uq_ref[m * chunk : (m + 1) * chunk, :] = u_ref[at_rows(m * group + inner, chunk), :]
    h = h_ref[...]
    model_rows = jnp.concatenate(
        [
            nn(low_q.T, hown_ref[...]),
            nn(low_k.T, h),
            nn(low_v.T, h),
            gbo_ref[...],
        ],
        axis=0,
    ).astype(bf16).astype(f32)
    ut = u_ref[...].T
    uqt = uq_ref[...].T
    head_rows = jnp.concatenate(
        [
            gah_ref[...],
            nn(uqt[:rank], gq),
            nn(ut[rank : 2 * rank], gk_ref[...]),
            nn(ut[2 * rank :], gv_ref[...]),
        ],
        axis=0,
    ).astype(bf16)
    owners = n_seq * slabs * group
    cols = model // owners
    each = head_dim // owners
    units = heads * each
    spots = lax.broadcasted_iota(i32, (width, 1), 0)
    owner = spots // units
    inside = spots % units
    source = inside // each * head_dim + owner * each + inside % each
    moved = jnp.where(lane_iota((width, width)) == source, 1.0, 0.0).astype(bf16)
    turned = nt(moved, head_rows)
    gap = table_ref.shape[3] - 4 * rank - units
    for y in range(group):
        for z in range(slabs):
            for x in range(n_seq):
                d = owner_index((y, z, x), group, slabs, n_seq)
                parts = [
                    pad_lanes(model_rows[:, d * cols : (d + 1) * cols]),
                    pad_lanes(turned[d * units : (d + 1) * units]),
                ]
                if gap:
                    parts.append(jnp.zeros((gap, LANES), f32))
                table_ref[y, z, x] = jnp.concatenate(parts, axis=0).astype(bf16)


def run_own(place, gq, gk, gv, w, a, b, u, h, h_own, res, gbo, gah, slabs, group, n_seq, head_dim):
    length, width = gk.shape
    rows, model = h_own.shape
    chunk = rows // slabs
    half = model // 2
    rank = b.shape[1]
    heads = width // head_dim
    owners = n_seq * slabs * group
    units = heads * (head_dim // owners)
    table_rows = (4 * rank + units + 7) // 8 * 8
    shaped = (slabs, group, chunk, width)
    peer = pl.BlockSpec((slabs, 1, chunk, width), lambda g, s: (0, s[0], 0, 0))
    out = [
        ((rows, half), f32),
        ((rows, half), bf16),
        ((group, slabs, n_seq, table_rows, LANES), bf16),
    ]
    return pl.pallas_call(
        functools.partial(own_kernel, (slabs, chunk, group, n_seq, rank, model, head_dim)),
        grid_spec=pltpu.PrefetchScalarGridSpec(
            num_scalar_prefetch=1,
            grid=(1,),
            in_specs=[
                whole_spec((rows, width)),
                whole_spec((length, width)),
                whole_spec((length, width)),
                peer,
                peer,
                whole_spec((3, model, width)),
                whole_spec((3 * rank, model)),
                whole_spec((3, rank, width)),
                whole_spec((length, 3 * rank)),
                whole_spec((length, model)),
                whole_spec((rows, model)),
                whole_spec((rows, model)),
                whole_spec((rank, model)),
                whole_spec((rank, width)),
            ],
            out_specs=[whole_spec(o[0]) for o in out],
            scratch_shapes=[
                pltpu.VMEM((rows, model), f32),
                pltpu.VMEM((rows, 3 * rank), bf16),
            ],
        ),
        out_shape=[jax.ShapeDtypeStruct(o[0], o[1]) for o in out],
        compiler_params=params(),
        name="own",
    )(
        place, gq, gk, gv, gk.reshape(shaped), gv.reshape(shaped), w, a, b, u, h, h_own, res,
        gbo, gah,
    )


def join_kernel(slabs, place, mine_ref, other_ref, out_ref):
    half = mine_ref.shape[-1]
    core, slab = place[2], place[1]
    for shift in range(slabs):
        source = lax.rem(slab - shift + slabs, slabs)
        out_ref[source, :, pl.ds(pl.multiple_of(core * half, half), half)] = mine_ref[
            shift
        ].astype(out_ref.dtype)
        out_ref[source, :, pl.ds(pl.multiple_of((1 - core) * half, half), half)] = other_ref[
            shift
        ].astype(out_ref.dtype)


def run_join(place, mine, other, dtype):
    slabs, chunk, half = mine.shape
    return pl.pallas_call(
        functools.partial(join_kernel, slabs),
        grid_spec=pltpu.PrefetchScalarGridSpec(
            num_scalar_prefetch=1,
            grid=(1,),
            in_specs=[whole_spec(mine.shape)] * 2,
            out_specs=whole_spec((slabs, chunk, 2 * half)),
        ),
        out_shape=jax.ShapeDtypeStruct((slabs, chunk, 2 * half), dtype),
        compiler_params=params(),
        name="join",
    )(place, mine, other)


def unpack_early_kernel(dims, place, index, mine_ref, other_ref, am_ref, bm_ref, ad_ref, bd_ref):
    n_seq, slabs, rank, cols, each, hidden_rows, tiles = dims
    core = place[2]
    for s in range(n_seq):
        for r in range(slabs):
            adapter = index[s, r]
            block = mine_ref[s, r].astype(f32)
            both = block[: 2 * rank] + other_ref[s, r, : 2 * rank].astype(f32)
            left = both[:, : cols // 2]
            right = both[:, cols // 2 : cols]
            am_ref[adapter] = jnp.where(core == 0, left, right).reshape(2, rank, cols // 2)
            bm_ref[adapter] = block[2 * rank : 3 * rank, :cols]
            base = 3 * rank
            wide = jnp.concatenate(
                [block[base + t * each : base + (t + 1) * each] for t in range(tiles)], axis=1
            )
            for k in range(rank):
                ad_ref[adapter, k] = wide[:, k * hidden_rows : (k + 1) * hidden_rows]
            for j in range(2):
                for k in range(rank):
                    at = ((j + 1) * rank + k) * hidden_rows
                    bd_ref[adapter, j, k] = wide[:, at : at + hidden_rows]


def run_unpack_early(place, index, mine, other, adapters, rank, cols, each, hidden_rows):
    n_seq, slabs = mine.shape[:2]
    tiles = (mine.shape[2] - 3 * rank) // each
    shapes = [
        (adapters, 2, rank, cols // 2),
        (adapters, rank, cols),
        (adapters, rank, each, hidden_rows),
        (adapters, 2, rank, each, hidden_rows),
    ]
    return pl.pallas_call(
        functools.partial(
            unpack_early_kernel, (n_seq, slabs, rank, cols, each, hidden_rows, tiles)
        ),
        grid_spec=pltpu.PrefetchScalarGridSpec(
            num_scalar_prefetch=2,
            grid=(1,),
            in_specs=[whole_spec(mine.shape)] * 2,
            out_specs=[whole_spec(s) for s in shapes],
        ),
        out_shape=[jax.ShapeDtypeStruct(s, f32) for s in shapes],
        compiler_params=params(),
        name="unpack_early",
    )(place, index, mine, other)


def unpack_late_kernel(
    dims, place, index, mine_ref, other_ref, am_gu_ref, bm_down_ref, am_ref, bm_ref, ah_ref,
    bh_ref,
):
    n_seq, slabs, rank, cols, heads, each = dims
    core = place[2]
    for s in range(n_seq):
        for r in range(slabs):
            adapter = index[s, r]
            block = mine_ref[s, r].astype(f32)
            both = block[: 3 * rank] + other_ref[s, r, : 3 * rank].astype(f32)
            left = both[:, : cols // 2]
            right = both[:, cols // 2 : cols]
            am_ref[adapter, 0:3] = jnp.where(core == 0, left, right).reshape(3, rank, cols // 2)
            am_ref[adapter, 3:5] = am_gu_ref[adapter]
            bm_ref[adapter, 0] = block[3 * rank : 4 * rank, :cols]
            bm_ref[adapter, 1] = bm_down_ref[adapter]
            units = block[4 * rank : 4 * rank + heads * each]
            for n in range(heads):
                piece = units[n * each : (n + 1) * each]
                ah_ref[adapter, n] = piece[:, :rank]
                for j in range(3):
                    bh_ref[adapter, j, n] = piece[:, (j + 1) * rank : (j + 2) * rank]


def run_unpack_late(place, index, mine, other, am_gu, bm_down, heads, each):
    n_seq, slabs = mine.shape[:2]
    adapters, _, rank, narrow = am_gu.shape
    cols = bm_down.shape[2]
    shapes = [
        (adapters, 5, rank, narrow),
        (adapters, 2, rank, cols),
        (adapters, heads, each, rank),
        (adapters, 3, heads, each, rank),
    ]
    return pl.pallas_call(
        functools.partial(unpack_late_kernel, (n_seq, slabs, rank, cols, heads, each)),
        grid_spec=pltpu.PrefetchScalarGridSpec(
            num_scalar_prefetch=2,
            grid=(1,),
            in_specs=[
                whole_spec(mine.shape),
                whole_spec(other.shape),
                whole_spec(am_gu.shape),
                whole_spec(bm_down.shape),
            ],
            out_specs=[whole_spec(s) for s in shapes],
        ),
        out_shape=[jax.ShapeDtypeStruct(s, f32) for s in shapes],
        compiler_params=params(),
        name="unpack_late",
    )(place, index, mine, other, am_gu, bm_down)


def pick(array, index):
    return lax.dynamic_index_in_dim(array, index, 0, keepdims=False)


def body(
    tokens, segments, adapter_index, w_attn_in, w_attn_out, w_gate_up, w_down, qk_scale,
    mix_rates, mlp_scales, a_model, b_model, a_heads, b_heads, a_hidden, b_hidden, cotangent,
):
    slabs, chunk, model = tokens.shape
    n_seq = lax.axis_size("seq")
    n_ctx = lax.axis_size("ctx")
    group = n_ctx // slabs
    local_width = w_attn_out.shape[0]
    local_hidden = w_down.shape[0]
    head_dim = a_heads.shape[-1]
    local_heads = local_width // head_dim
    rank = a_model.shape[2]
    adapters = a_model.shape[0]
    row_width = a_hidden.shape[-1]
    half = model // 2
    ctx_place = lax.axis_index("ctx")
    slab = ctx_place // group
    inner = ctx_place % group
    core = lax.axis_index("wt")
    seq_place = lax.axis_index("seq")
    owners = n_seq * n_ctx
    rows = slabs * chunk
    length = rows * group
    place = jnp.stack([inner, slab, core, seq_place]).astype(i32)

    def to_slab(array, shift):
        pairs = [(c, (c + shift * group) % n_ctx) for c in range(n_ctx)]
        return lax.ppermute(array, "ctx", pairs)

    def within_slab(array, shift):
        pairs = [(c, c - c % group + (c % group + shift) % group) for c in range(n_ctx)]
        return lax.ppermute(array, "ctx", pairs)

    def to_seq(array, shift):
        return lax.ppermute(array, "seq", [(c, (c + shift) % n_seq) for c in range(n_seq)])

    def other_core(array):
        return lax.ppermute(array, "wt", [(0, 1), (1, 0)])

    def half_piece(array, index, which):
        return lax.dynamic_slice(array, (index, 0, which * half), (1, chunk, half))[0]

    own_piece = half_piece(tokens, slab, core)
    got = [own_piece] + [
        to_slab(half_piece(tokens, (slab + shift) % slabs, core), shift)
        for shift in range(1, slabs)
    ]
    pieces = []
    for shift in range(1, slabs):
        pieces += [got[shift], other_core(got[shift])]
    for turn in range(1, group):
        for shift in range(slabs):
            peer = within_slab(got[shift], turn)
            pieces += [peer, other_core(peer)]

    own_seg = lax.dynamic_update_index_in_dim(segments, pick(segments, slab), slab, 0)
    for shift in range(1, slabs):
        seg = to_slab(pick(segments, (slab + shift) % slabs), shift)
        own_seg = lax.dynamic_update_index_in_dim(own_seg, seg, (slab - shift) % slabs, 0)
    below = lambda seg: jnp.sum(
        (seg.reshape(1, rows) < own_seg.reshape(rows, 1)).astype(i32), axis=1
    )
    start = below(own_seg)
    for turn in range(1, group):
        start = start + below(within_slab(own_seg, turn))
    start = start.reshape(1, rows)

    g_mine = [
        to_slab(half_piece(cotangent, (slab + shift) % slabs, core), shift)
        for shift in range(1, slabs)
    ]
    g_mine = jnp.stack(g_mine)
    g_other = other_core(g_mine)

    adapter = pick(adapter_index, slab)
    am = pick(a_model, adapter)
    bm = pick(b_model, adapter)
    ah = pick(a_heads, adapter).reshape(rank, local_width)
    bh = pick(b_heads, adapter).reshape(3, rank, local_width)
    ad = pick(a_hidden, adapter).reshape(rank, local_hidden)
    bd = pick(b_hidden, adapter).reshape(2, rank, local_hidden)
    am_qkv = am[:3].reshape(3 * rank, model)
    am_gu = am[3:].reshape(2 * rank, model)
    ah_pad = jnp.pad(ah, ((0, LANES - rank), (0, 0)))
    ad_pad = jnp.pad(ad, ((0, LANES - rank), (0, 0)))

    frequency = 10000.0 ** (-jnp.arange(head_dim // 2, dtype=f32) / (head_dim // 2))
    turn = jnp.arange(length, dtype=i32).astype(f32)[:, None] * frequency[None, :]
    cos = jnp.tile(jnp.cos(turn), (1, 2 * LANES // head_dim))
    sine = jnp.sin(turn)
    sin = jnp.tile(jnp.concatenate([-sine, sine], axis=1), (1, LANES // head_dim))
    scale = qk_scale[None, :]

    h_full, h_own, u, q, k, v, qi, ki, o, of, inv, attn_msg = run_attend(
        place, tokens, pieces, start, w_attn_in, am_qkv, bh, cos, sin, scale, w_attn_out,
        ah_pad, group, head_dim,
    )
    attn_other = other_core(attn_msg)
    mid, u_gu, gate, up, down_msg = run_feed(
        attn_msg, attn_other, h_own, bm[0], mix_rates, am_gu, w_gate_up, bd, w_down, ad_pad,
        mlp_scales, 512,
    )
    down_other = other_core(down_msg)
    out_half, mid_res, mid_msg, early = run_feed_back(
        place, down_msg, down_other, mid, cotangent, g_mine, g_other, bm[1], mix_rates, am_gu,
        u_gu, gate, up, w_gate_up, bd, w_down, ad, mlp_scales, 512, group, n_seq, row_width,
    )
    mid_other = other_core(mid_msg)

    out_mine = jnp.stack(
        [pick(out_half, slab)]
        + [
            to_slab(pick(out_half, (slab + shift) % slabs), shift)
            for shift in range(1, slabs)
        ]
    )
    layer_out = run_join(place, out_mine, other_core(out_mine), bf16)

    index = [adapter_index]
    for shift in range(1, n_seq):
        index.append(to_seq(adapter_index, shift))
    order = (slab - jnp.arange(slabs, dtype=i32)) % slabs
    index = jnp.stack(index)[:, order]

    def send_home(table):
        total = pick(table, inner).astype(f32)
        for turn in range(1, group):
            total = total + within_slab(pick(table, (inner + turn) % group), turn).astype(f32)
        total = total.astype(bf16)
        got = [pick(total, slab)]
        for shift in range(1, slabs):
            got.append(to_slab(pick(total, (slab + shift) % slabs), shift))
        got = jnp.stack(got)
        result = [lax.dynamic_index_in_dim(got, seq_place, 1, keepdims=False)]
        for shift in range(1, n_seq):
            sent = lax.dynamic_index_in_dim(
                got, (seq_place + shift) % n_seq, 1, keepdims=False
            )
            result.append(to_seq(sent, shift))
        return jnp.stack(result)

    early = send_home(early)
    grad_am_gu, grad_bm_down, grad_ad, grad_bd = run_unpack_early(
        place, index, early, other_core(early[:, :, : 2 * rank]), adapters, rank,
        model // owners, row_width // owners, local_hidden // row_width,
    )

    gq, gk, gv, h_res, gbo, gah = run_attend_back(
        place, mid_res, mid_msg, mid_other, mid, h_own, attn_msg, attn_other, mix_rates, bm[0],
        w_attn_out, ah, start, q, k, v, o, of, inv, qi, ki, cos, sin, scale, slabs, group,
        head_dim,
    )
    keep, send = run_others(place, gk, gv, w_attn_in, am_qkv, bh, slabs, group)
    others = (keep + other_core(send).astype(f32)).astype(bf16)
    own_keep, own_send, late = run_own(
        place, gq, gk, gv, w_attn_in, am_qkv, bh, u, h_full, h_own, h_res, gbo, gah, slabs,
        group, n_seq, head_dim,
    )
    own_got = other_core(own_send)
    others = others.reshape(group - 1, slabs, chunk, half)
    own_keep = own_keep.reshape(slabs, chunk, half)
    own_got = own_got.reshape(slabs, chunk, half)
    result = [None] * slabs
    for shift in [2, 1, 3, 0] if slabs == 4 else list(range(slabs)):
        target = (slab + shift) % slabs
        total = pick(own_keep, target) + pick(own_got, target).astype(f32)
        for turn in range(1, group):
            got = within_slab(pick(others[turn - 1], target), turn)
            total = total + got.astype(f32)
        total = total.astype(bf16)
        result[shift] = to_slab(total, shift) if shift else total
    result = jnp.stack(result)
    input_grad = run_join(place, result, other_core(result), f32)

    late = send_home(late)
    grad_am, grad_bm, grad_ah, grad_bh = run_unpack_late(
        place, index, late, other_core(late[:, :, : 3 * rank]), grad_am_gu, grad_bm_down,
        local_heads, head_dim // owners,
    )
    return (
        layer_out,
        input_grad,
        grad_am,
        grad_bm,
        jnp.transpose(grad_ah, (0, 3, 1, 2)),
        jnp.transpose(grad_bh, (0, 1, 4, 2, 3)),
        jnp.transpose(grad_ad, (0, 1, 3, 2)),
        jnp.transpose(grad_bd, (0, 1, 2, 4, 3)),
    )


def solution(mesh):
    return jax.shard_map(
        body,
        mesh=mesh,
        in_specs=(
            P("seq", "ctx", None),
            P("seq", "ctx"),
            P("seq"),
            P(None, None, "wt"),
            P("wt", None),
            P(None, None, "wt"),
            P("wt", None),
            P("wt"),
            P(),
            P(None, "wt"),
            P(),
            P(),
            P(None, None, "wt", None),
            P(None, None, None, "wt", None),
            P(None, None, "wt", None),
            P(None, None, None, "wt", None),
            P("seq", "ctx", None),
        ),
        out_specs=(
            P("seq", "ctx", None),
            P("seq", "ctx", None),
            P(None, None, None, ("seq", "ctx", "wt")),
            P(None, None, None, ("seq", "ctx")),
            P(None, None, "wt", ("seq", "ctx")),
            P(None, None, None, "wt", ("seq", "ctx")),
            P(None, None, "wt", ("seq", "ctx")),
            P(None, None, None, "wt", ("seq", "ctx")),
        ),
        check_vma=False,
    )
```

time: 453 us -> 313 us (0.69)
  matrix products: 117 us -> 0 us
  Pallas kernels: 46.9 us -> 158 us
  local copies, waits for them, and re-layouts: 126 us -> 25.4 us
  other arithmetic: 35.9 us -> 4.47 us
  starting transfers between devices: 34.9 us -> 52.9 us
  waiting for transfers between devices: 82.9 us -> 68.3 us
    dot_general x48 -> x0, matrix products: 117 us -> none  [dot(): lax.dot_general(left, right, (contract, ((), ())), preferred_element_type...]
    pallas_call x3 -> x10, Pallas kernels: 46.9 us -> 158 us  [the longest x1 34.3 us: run_attend_back(): pl.pallas_call(functools.partial(attend_back_kernel, (slabs, chunk, group...]
    concatenate x12 -> x0, local copies, waits for them, and re-layouts: 23.4 us -> none  [the longest x7 16.8 us: body(): jnp.concatenate([am_sum, by_owner(jnp.stack([grad_bm_attn, grad_bm_down])...]
    dynamic_update_slice x28 -> x4, local copies, waits for them, and re-layouts: 18.1 us -> 0.14 us  [the longest x3 0.1 us: body(): lax.dynamic_update_index_in_dim(own_seg, seg, (slab - shift) % slabs, 0)]
    transpose x5 -> x0, local copies, waits for them, and re-layouts: 17.9 us -> none  [the longest x4 17.8 us: by_owner(): return jnp.moveaxis(shaped, -2, 0).reshape(owners, -1)]
    ppermute x4 -> x11, waiting for transfers between devices: 35.4 us -> 22.6 us  [within_slab(): return lax.ppermute(array, 'ctx', pairs)]
    reduce_sum x6 -> x1, other arithmetic: 11.9 us -> 0.36 us  [body(): jnp.sum((seg.reshape(1, rows) < own_seg.reshape(rows, 1)).astype(i32), ax...]
    unnamed x166 -> x58, local copies, waits for them, and re-layouts: 17.5 us -> 7.35 us
  transfers between devices with their start and end apart: 36 -> 52, of which waited for: 10 -> 21; matrix products, arithmetic and copies ran while one was open for 31% -> 7% of each run, Pallas kernels for 0% -> 21%
where the time goes in v2:
time: 313 us; the launch traced here: 312 us
  Pallas kernels  158 us (50%)
  waiting for transfers between devices  68.3 us (22%)
  starting transfers between devices  52.9 us (17%)
  local copies, waits for them, and re-layouts  25.4 us (8%)
  other arithmetic  4.47 us (1%)
  between operations  3.15 us (1%)
    ppermute x21, waiting for transfers between devices, to_slab(): return lax.ppermute(array, 'ctx', pairs)  41.3 us
    pallas_call x1, Pallas kernels, run_attend_back(): pl.pallas_call(functools.partial(attend_back_kernel, (slabs, chunk, group...  34.3 us
    ppermute x21, starting transfers between devices, to_slab(): return lax.ppermute(array, 'ctx', pairs)  33.6 us
    pallas_call x1, Pallas kernels, run_attend(): pl.pallas_call(functools.partial(attend_kernel, (slabs, chunk, group, hea...  33.3 us
    pallas_call x1, Pallas kernels, run_feed_back(): pl.pallas_call(functools.partial(feed_back_kernel, (slabs, chunk, group,...  30.9 us
    pallas_call x1, Pallas kernels, run_feed(): pl.pallas_call(functools.partial(feed_kernel, (rank, model)), grid=(hidde...  23.4 us
    ppermute x11, waiting for transfers between devices, within_slab(): return lax.ppermute(array, 'ctx', pairs)  22.6 us
    pallas_call x1, Pallas kernels, run_own(): pl.pallas_call(functools.partial(own_kernel, (slabs, chunk, group, n_seq,...  14.9 us
  transfers between devices with their start and end apart: 52, of which 21 were waited for; matrix products, arithmetic and copies ran while one was open for 7% of the time, Pallas kernels for 21%

profile of v2, /device:TPU:0, one launch (start us, length us, event | category | flops | bytes accessed | tf_op | source)
XLA Modules:
  0.0 312.1 jit_solution(7151082574675310625)
XLA Ops:
  1.5 3.1 collective-permute-start.14
  16.1 6.8 %collective-permute-done.15 = s32[128]{0:T(128)S(1)} collective-permute-done((s32[128]{0:T(128)S(1)}, s32[128]{0:T(128)S(1)}, u32[]{:S(2)}, u32[]{:S(2)}) %collective-permute-start.15) | collective-permute-done | bytes 544 | tf_op jit(solution)/shard_map/ppermute | solution.py:1052
  33.3 5.8 %collective-permute-done.10.refs_11_ = bf16[128,640]{1,0:T(8,128)(2,1)S(1)} collective-permute-done((bf16[128,640]{1,0:T(8,128)(2,1)S(1)}, bf16[128,640]{1,0:T(8,128)(2,1)S(1)}, u32[]{:S(2)}, u32[]{:S(2)}) %collective-permute-start.10) | collective-permute-done | bytes 163872 | tf_op jit(solution)/shard_map/ppermute | solution.py:1056
  48.6 33.3 %attend.1 = (bf16[1024,1280]{1,0:T(8,128)(2,1)}, bf16[512,1280]{1,0:T(8,128)(2,1)}, bf16[1024,48]{1,0:T(8,128)(2,1)}, bf16[512,640]{1,0:T(8,128)(2,1)}, bf16[102...) custom-call(s32[4]{0:T(128)} %pad_add_fusion.1.place, ...), custom_call_target="tpu_custom_call" | custom-call | tf_op jit(solution)/shard_map/attend/pallas_call | solution.py:255
  88.9 23.4 %feed.1 = (f32[512,1280]{1,0:T(8,128)}, bf16[512,32]{1,0:T(8,128)(2,1)}, bf16[512,2560]{1,0:T(8,128)(2,1)}, bf16[512,2560]{1,0:T(8,128)(2,1)}, bf16[512,1408]{1,0:T(8,128)(2,1)}) custom-call(bf16[512,1408]{1,0:T(8,128)(2,1)} %get-tuple-element.48.mine_ref.am_ref, bf16[512,1408]{1,0:T(8,128)(2,1)} %copy-done.2, ...), custom_call_target="tpu_custom_call" | custom-call | tf_op jit(solution)/shard_map/feed/pallas_call | solution.py:325
  114.0 4.7 %collective-permute-start.21 = (bf16[128,640]{1,0:T(8,128)(2,1)S(1)}, bf16[128,640]{1,0:T(8,128)(2,1)S(1)}, u32[]{:S(2)}, u32[]{:S(2)}) collective-permute-start(bf16[128,640]{1,0:T(8,128)(2,1)S(1)} %get-tuple-element.95), channel_id=1, source_target_pairs={{0,8},{2,10},{4,12},{6,14},{8,0},{10,2},{12,4},{14,6},{1,9},{3,11}... | collective-permute-start | bytes 491528 | tf_op jit(solution)/shard_map/ppermute | solution.py:1052
  118.7 4.5 %collective-permute-done.20 = bf16[128,640]{1,0:T(8,128)(2,1)S(1)} collective-permute-done((bf16[128,640]{1,0:T(8,128)(2,1)S(1)}, bf16[128,640]{1,0:T(8,128)(2,1)S(1)}, u32[]{:S(2)}, u32[]{:S(2)}) %collective-permute-start.20) | collective-permute-done | bytes 163872 | tf_op jit(solution)/shard_map/ppermute | solution.py:1052
  123.2 6.4 %collective-permute-done.21 = bf16[128,640]{1,0:T(8,128)(2,1)S(1)} collective-permute-done((bf16[128,640]{1,0:T(8,128)(2,1)S(1)}, bf16[128,640]{1,0:T(8,128)(2,1)S(1)}, u32[]{:S(2)}, u32[]{:S(2)}) %collective-permute-start.21) | collective-permute-done | bytes 163872 | tf_op jit(solution)/shard_map/ppermute | solution.py:1052
  132.9 30.9 %feed_back.1 = (bf16[4,128,640]{2,1,0:T(8,128)(2,1)}, f32[512,1280]{1,0:T(8,128)}, bf16[512,1280]{1,0:T(8,128)(2,1)}, bf16[2,4,2,112,128]{4,3,2,1,0:T(8,128)(2,1)}) custom-call(s32[4]{0:T(128)} %pad_add_fusion.1.place, bf16[512,1408]{1,0:T(8,128)(2,1)} %get-tuple-element.50.mine_ref, bf16[512,1408]{1,0:T(8,128)(2,1)} %copy-done.6, ...), custom_call_target="tpu_custom_call" | custom-call | tf_op jit(solution)/shard_map/feed_back/pallas_call | solution.py:490
  171.6 34.3 %attend_back.1 = (bf16[512,640]{1,0:T(8,128)(2,1)}, bf16[1024,640]{1,0:T(8,128)(2,1)}, bf16[1024,640]{1,0:T(8,128)(2,1)}, f32[512,1280]{1,0:T(8,128)}, f32[16,1280]{1,0:T(8,128)}, /*index=5*/f32[16,640]{1,0:T(8,128)}) custom-call(s32[4]{0:T(128)} %pad_add_fusion.1.place, f32[512,1280]{1,0:T(8,128)} %get-tuple-element.56.res_ref, ...), custom_call_target="tpu_custom_call" | custom-call | tf_op jit(solution)/shard_map/attend_back/pallas_call | solution.py:657
  205.9 8.2 %others.1 = (f32[1,512,640]{2,1,0:T(8,128)}, bf16[1,512,640]{2,1,0:T(8,128)(2,1)}) custom-call(s32[4]{0:T(128)} %pad_add_fusion.1.place, bf16[4,2,128,640]{3,2,1,0:T(8,128)(2,1)} %bitcast.139, bf16[4,2,128,640]{3,2,1,0:T(8,128)(2,1)} %bitcast.141, bf16[3,1280,640]{2,1,0:T(8,128)(2,1)} %w_ref.3, bf16[48,1280]{1,0:T(8,128)(2,1)} %bitcast.147, ...), custom_call_target="tpu_custom_call" | custom-call | tf_op jit(solution)/shard_map/others/pallas_call | solution.py:736
  214.2 4.0 %collective-permute-start.24 = (bf16[128,640]{1,0:T(8,128)(2,1)S(1)}, bf16[128,640]{1,0:T(8,128)(2,1)S(1)}, u32[]{:S(2)}, u32[]{:S(2)}) collective-permute-start(bf16[128,640]{1,0:T(8,128)(2,1)S(1)} %get-tuple-element.108), channel_id=1, source_target_pairs={{0,4},{2,6},{4,8},{6,10},{8,12},{10,14},{12,0},{14,2},{1,5},{3,7},... | collective-permute-start | bytes 491528 | tf_op jit(solution)/shard_map/ppermute | solution.py:1052
  224.7 5.4 %collective-permute-done.25 = bf16[128,640]{1,0:T(8,128)(2,1)S(1)} collective-permute-done((bf16[128,640]{1,0:T(8,128)(2,1)S(1)}, bf16[128,640]{1,0:T(8,128)(2,1)S(1)}, u32[]{:S(2)}, u32[]{:S(2)}) %collective-permute-start.25) | collective-permute-done | bytes 163872 | tf_op jit(solution)/shard_map/ppermute | solution.py:1052
  230.1 7.3 %collective-permute-start.49 = (bf16[2,112,128]{2,1,0:T(8,128)(2,1)S(1)}, bf16[2,112,128]{2,1,0:T(8,128)(2,1)S(1)}, u32[]{:S(2)}, u32[]{:S(2)}) collective-permute-start(bf16[2,112,128]{2,1,0:T(8,128)(2,1)S(1)} %get-tuple-element.114), channel_id=1, source_target_pairs={{0,12},{2,14},{4,0},{6,2},{8,4},{10,6},{12,8},{14,10},{1,13},{3,15... | collective-permute-start | bytes 172040 | tf_op jit(solution)/shard_map/ppermute | solution.py:1052
  237.5 14.9 %own.1 = (f32[512,640]{1,0:T(8,128)}, bf16[512,640]{1,0:T(8,128)(2,1)}, bf16[2,4,2,104,128]{4,3,2,1,0:T(8,128)(2,1)}) custom-call(s32[4]{0:T(128)} %pad_add_fusion.1.place, bf16[512,640]{1,0:T(8,128)(2,1)} %get-tuple-element.66.gq_ref, bf16[1024,640]{1,0:T(8,128)(2,1)} %get-tuple-element.67.gk_ref, bf16[1024,640]{1,0:T(8,128)(2,1)} %get-tuple-element.68.gv_ref, ...), custom_call_target="tpu_custom_call" | custom-call | tf_op jit(solution)/shard_map/own/pallas_call | solution.py:852
  257.0 2.8 collective-permute-done.31
  266.8 3.5 %collective-permute-done.36 = bf16[128,640]{1,0:T(8,128)(2,1)S(1)} collective-permute-done((bf16[128,640]{1,0:T(8,128)(2,1)S(1)}, bf16[128,640]{1,0:T(8,128)(2,1)S(1)}, u32[]{:S(2)}, u32[]{:S(2)}) %collective-permute-start.36) | collective-permute-done | bytes 163872 | tf_op jit(solution)/shard_map/ppermute | solution.py:1056
  271.2 3.3 %collective-permute-done.40 = bf16[4,2,104,128]{3,2,1,0:T(8,128)(2,1)S(1)} collective-permute-done((bf16[4,2,104,128]{3,2,1,0:T(8,128)(2,1)S(1)}, bf16[4,2,104,128]{3,2,1,0:T(8,128)(2,1)S(1)}, u32[]{:S(2)}, u32[]{:S(2)}) %collective-permute-start.40) | collective-permute-done | bytes 213024 | tf_op jit(solution)/shard_map/ppermute | solution.py:1056
  274.6 5.0 %collective-permute-done.33 = bf16[128,640]{1,0:T(8,128)(2,1)S(1)} collective-permute-done((bf16[128,640]{1,0:T(8,128)(2,1)S(1)}, bf16[128,640]{1,0:T(8,128)(2,1)S(1)}, u32[]{:S(2)}, u32[]{:S(2)}) %collective-permute-start.33) | collective-permute-done | bytes 163872 | tf_op jit(solution)/shard_map/ppermute | solution.py:1052
  279.6 6.5 %collective-permute-done.35 = bf16[128,640]{1,0:T(8,128)(2,1)S(1)} collective-permute-done((bf16[128,640]{1,0:T(8,128)(2,1)S(1)}, bf16[128,640]{1,0:T(8,128)(2,1)S(1)}, u32[]{:S(2)}, u32[]{:S(2)}) %collective-permute-start.35) | collective-permute-done | bytes 163872 | tf_op jit(solution)/shard_map/ppermute | solution.py:1052
  295.5 3.1 %unpack_early.1 = (f32[8,2,16,40]{3,2,1,0:T(8,128)}, f32[8,16,80]{2,1,0:T(8,128)}, f32[8,16,8,20]{3,2,1,0:T(8,128)}, f32[8,2,16,8,20]{4,3,2,1,0:T(8,128)}) custom-call(s32[4]{0:T(128)} %pad_add_fusion.1.place, s32[2,4]{1,0:T(2,128)} %bitcast.178, bf16[2,4,112,128]{3,2,1,0:T(8,128)(2,1)} %pad_maximum_fusion.4.mine_ref, bf16[2,4,32,128]{3,2,1,0:T(8,128)(2,1)} %copy-done.25), custom_call_target="tpu_custom_call" | custom-call | tf_op jit(solution)/shard_map/unpack_early/pallas_call | solution.py:950
  299.5 3.1 join.2
  304.6 3.0 unpack_late.1
  308.5 3.6 %join.3 = f32[4,128,1280]{2,1,0:T(8,128)} custom-call(s32[4]{0:T(128)} %pad_add_fusion.1.place, bf16[4,128,640]{2,1,0:T(8,128)(2,1)} %copy-done.4, bf16[4,128,640]{2,1,0:T(8,128)(2,1)} %copy-done.13), custom_call_target="tpu_custom_call" | custom-call | tf_op jit(solution)/shard_map/join/pallas_call | solution.py:903
  (212 shorter events, 81.9 us)
Async XLA Ops:
  1.5 14.3 %collective-permute-start.14 = (s32[128]{0:T(128)S(1)}, s32[128]{0:T(128)S(1)}, u32[]{:S(2)}, u32[]{:S(2)}) collective-permute-start(s32[128]{0:T(128)S(1)} %get-tuple-element.127), channel_id=1, source_target_pairs={{0,4},{2,6},{4,8},{6,10},{8,12},{10,14},{12,0},{14,2},{1,5},{3,7},... | collective-permute-start | bytes 1544 | tf_op jit(solution)/shard_map/ppermute | solution.py:1052
  5.8 24.5 %collective-permute-start.2 = (bf16[128,640]{1,0:T(8,128)(2,1)S(1)}, bf16[128,640]{1,0:T(8,128)(2,1)S(1)}, u32[]{:S(2)}, u32[]{:S(2)}) collective-permute-start(bf16[128,640]{1,0:T(8,128)(2,1)S(1)} %get-tuple-element.99), channel_id=1, source_target_pairs={{0,8},{2,10},{4,12},{6,14},{8,0},{10,2},{12,4},{14,6},{1,9},{3,11}... | collective-permute-start | bytes 491528 | tf_op jit(solution)/shard_map/ppermute | solution.py:1052
  8.4 23.4 %collective-permute-start.4 = (bf16[128,640]{1,0:T(8,128)(2,1)S(1)}, bf16[128,640]{1,0:T(8,128)(2,1)S(1)}, u32[]{:S(2)}, u32[]{:S(2)}) collective-permute-start(bf16[128,640]{1,0:T(8,128)(2,1)S(1)} %get-tuple-element.98), channel_id=1, source_target_pairs={{0,12},{2,14},{4,0},{6,2},{8,4},{10,6},{12,8},{14,10},{1,13},{3,15... | collective-permute-start | bytes 491528 | tf_op jit(solution)/shard_map/ppermute | solution.py:1052
  9.8 19.3 %collective-permute-start = (bf16[128,640]{1,0:T(8,128)(2,1)S(1)}, bf16[128,640]{1,0:T(8,128)(2,1)S(1)}, u32[]{:S(2)}, u32[]{:S(2)}) collective-permute-start(bf16[128,640]{1,0:T(8,128)(2,1)S(1)} %get-tuple-element.100), channel_id=1, source_target_pairs={{0,4},{2,6},{4,8},{6,10},{8,12},{10,14},{12,0},{14,2},{1,5},{3,7},... | collective-permute-start | bytes 491528 | tf_op jit(solution)/shard_map/ppermute | solution.py:1052
  10.5 21.5 %collective-permute-start.6 = (bf16[128,640]{1,0:T(8,128)(2,1)S(1)}, bf16[128,640]{1,0:T(8,128)(2,1)}, u32[]{:S(2)}, u32[]{:S(2)}) collective-permute-start(bf16[128,640]{1,0:T(8,128)(2,1)S(1)} %get-tuple-element.97), channel_id=1, source_target_pairs={{0,2},{2,0},{4,6},{6,4},{8,10},{10,8},{12,14},{14,12},{1,3},{3,1},... | collective-permute-start | bytes 491528 | tf_op jit(solution)/shard_map/ppermute | solution.py:1056
  29.1 12.5 %collective-permute-start.8 = (bf16[128,640]{1,0:T(8,128)(2,1)S(1)}, bf16[128,640]{1,0:T(8,128)(2,1)S(1)}, u32[]{:S(2)}, u32[]{:S(2)}) collective-permute-start(bf16[128,640]{1,0:T(8,128)(2,1)S(1)} %collective-permute-done.refs_1_), channel_id=1, source_target_pairs={{0,2},{2,0},{4,6},{6,4},{8,10},{10,8},{12,14},{14,12},{1,3},{3,1},... | collective-permute-start | bytes 491528 | tf_op jit(solution)/shard_map/ppermute | solution.py:1056
  30.2 11.9 %collective-permute-start.1 = (bf16[128,640]{1,0:T(8,128)(2,1)S(1)}, bf16[128,640]{1,0:T(8,128)(2,1)S(1)}, u32[]{:S(2)}, u32[]{:S(2)}) collective-permute-start(bf16[128,640]{1,0:T(8,128)(2,1)S(1)} %collective-permute-done.refs_1_), channel_id=1, source_target_pairs={{0,1},{1,0},{2,3},{3,2},{4,5},{5,4},{6,7},{7,6},{8,9},{9,8},{10,11... | collective-permute-start | bytes 491528 | tf_op jit(solution)/shard_map/ppermute | solution.py:1062
  112.3 19.3 %collective-permute-start.19 = (bf16[512,1408]{1,0:T(8,128)(2,1)}, bf16[512,1408]{1,0:T(8,128)(2,1)S(1)}, u32[]{:S(2)}, u32[]{:S(2)}) collective-permute-start(bf16[512,1408]{1,0:T(8,128)(2,1)} %get-tuple-element.50.mine_ref), channel_id=1, source_target_pairs={{0,1},{1,0},{2,3},{3,2},{4,5},{5,4},{6,7},{7,6},{8,9},{9,8},{10,11... | collective-permute-start | bytes 4325384 | tf_op jit(solution)/shard_map/ppermute | solution.py:1062
  114.0 15.6 %collective-permute-start.21 = (bf16[128,640]{1,0:T(8,128)(2,1)S(1)}, bf16[128,640]{1,0:T(8,128)(2,1)S(1)}, u32[]{:S(2)}, u32[]{:S(2)}) collective-permute-start(bf16[128,640]{1,0:T(8,128)(2,1)S(1)} %get-tuple-element.95), channel_id=1, source_target_pairs={{0,8},{2,10},{4,12},{6,14},{8,0},{10,2},{12,4},{14,6},{1,9},{3,11}... | collective-permute-start | bytes 491528 | tf_op jit(solution)/shard_map/ppermute | solution.py:1052
  168.6 52.1 %collective-permute-start.46 = (bf16[4,2,112,128]{3,2,1,0:T(8,128)(2,1)S(1)}, bf16[4,2,112,128]{3,2,1,0:T(8,128)(2,1)S(1)}, u32[]{:S(2)}, u32[]{:S(2)}) collective-permute-start(bf16[4,2,112,128]{3,2,1,0:T(8,128)(2,1)S(1)} %dynamic-slice_bitcast_fusion), channel_id=1, source_target_pairs={{0,2},{2,0},{4,6},{6,4},{8,10},{10,8},{12,14},{14,12},{1,3},{3,1},... | collective-permute-start | bytes 688136 | tf_op jit(solution)/shard_map/ppermute | solution.py:1056
  214.1 38.4 %collective-permute-start.30 = (bf16[1,512,640]{2,1,0:T(8,128)(2,1)}, bf16[1,512,640]{2,1,0:T(8,128)(2,1)S(1)}, u32[]{:S(2)}, u32[]{:S(2)}) collective-permute-start(bf16[1,512,640]{2,1,0:T(8,128)(2,1)} %get-tuple-element.77), channel_id=1, source_target_pairs={{0,1},{1,0},{2,3},{3,2},{4,5},{5,4},{6,7},{7,6},{8,9},{9,8},{10,11... | collective-permute-start | bytes 1966088 | tf_op jit(solution)/shard_map/ppermute | solution.py:1062
  218.2 11.9 %collective-permute-start.25 = (bf16[128,640]{1,0:T(8,128)(2,1)S(1)}, bf16[128,640]{1,0:T(8,128)(2,1)S(1)}, u32[]{:S(2)}, u32[]{:S(2)}) collective-permute-start(bf16[128,640]{1,0:T(8,128)(2,1)S(1)} %get-tuple-element.107), channel_id=1, source_target_pairs={{0,8},{2,10},{4,12},{6,14},{8,0},{10,2},{12,4},{14,6},{1,9},{3,11}... | collective-permute-start | bytes 491528 | tf_op jit(solution)/shard_map/ppermute | solution.py:1052
  218.2 19.2 %collective-permute-start.26 = (bf16[128,640]{1,0:T(8,128)(2,1)S(1)}, bf16[128,640]{1,0:T(8,128)(2,1)S(1)}, u32[]{:S(2)}, u32[]{:S(2)}) collective-permute-start(bf16[128,640]{1,0:T(8,128)(2,1)S(1)} %get-tuple-element.106), channel_id=1, source_target_pairs={{0,12},{2,14},{4,0},{6,2},{8,4},{10,6},{12,8},{14,10},{1,13},{3,15... | collective-permute-start | bytes 491528 | tf_op jit(solution)/shard_map/ppermute | solution.py:1052
  220.8 31.7 %collective-permute-start.47 = (bf16[2,112,128]{2,1,0:T(8,128)(2,1)S(1)}, bf16[2,112,128]{2,1,0:T(8,128)(2,1)S(1)}, u32[]{:S(2)}, u32[]{:S(2)}) collective-permute-start(bf16[2,112,128]{2,1,0:T(8,128)(2,1)S(1)} %get-tuple-element.116), channel_id=1, source_target_pairs={{0,4},{2,6},{4,8},{6,10},{8,12},{10,14},{12,0},{14,2},{1,5},{3,7},... | collective-permute-start | bytes 172040 | tf_op jit(solution)/shard_map/ppermute | solution.py:1052
  223.1 29.3 %collective-permute-start.48 = (bf16[2,112,128]{2,1,0:T(8,128)(2,1)S(1)}, bf16[2,112,128]{2,1,0:T(8,128)(2,1)S(1)}, u32[]{:S(2)}, u32[]{:S(2)}) collective-permute-start(bf16[2,112,128]{2,1,0:T(8,128)(2,1)S(1)} %get-tuple-element.115), channel_id=1, source_target_pairs={{0,8},{2,10},{4,12},{6,14},{8,0},{10,2},{12,4},{14,6},{1,9},{3,11}... | collective-permute-start | bytes 172040 | tf_op jit(solution)/shard_map/ppermute | solution.py:1052
  230.1 22.3 %collective-permute-start.49 = (bf16[2,112,128]{2,1,0:T(8,128)(2,1)S(1)}, bf16[2,112,128]{2,1,0:T(8,128)(2,1)S(1)}, u32[]{:S(2)}, u32[]{:S(2)}) collective-permute-start(bf16[2,112,128]{2,1,0:T(8,128)(2,1)S(1)} %get-tuple-element.114), channel_id=1, source_target_pairs={{0,12},{2,14},{4,0},{6,2},{8,4},{10,6},{12,8},{14,10},{1,13},{3,15... | collective-permute-start | bytes 172040 | tf_op jit(solution)/shard_map/ppermute | solution.py:1052
  254.8 12.0 %collective-permute-start.34 = (bf16[128,640]{1,0:T(8,128)(2,1)S(1)}, bf16[128,640]{1,0:T(8,128)(2,1)S(1)}, u32[]{:S(2)}, u32[]{:S(2)}) collective-permute-start(bf16[128,640]{1,0:T(8,128)(2,1)S(1)} %get-tuple-element.103), channel_id=1, source_target_pairs={{0,2},{2,0},{4,6},{6,4},{8,10},{10,8},{12,14},{14,12},{1,3},{3,1},... | collective-permute-start | bytes 491528 | tf_op jit(solution)/shard_map/ppermute | solution.py:1056
  256.3 14.1 %collective-permute-start.36 = (bf16[128,640]{1,0:T(8,128)(2,1)S(1)}, bf16[128,640]{1,0:T(8,128)(2,1)S(1)}, u32[]{:S(2)}, u32[]{:S(2)}) collective-permute-start(bf16[128,640]{1,0:T(8,128)(2,1)S(1)} %get-tuple-element.102), channel_id=1, source_target_pairs={{0,2},{2,0},{4,6},{6,4},{8,10},{10,8},{12,14},{14,12},{1,3},{3,1},... | collective-permute-start | bytes 491528 | tf_op jit(solution)/shard_map/ppermute | solution.py:1056
  257.0 41.7 %collective-permute-start.27 = (bf16[4,128,640]{2,1,0:T(8,128)(2,1)S(1)}, bf16[4,128,640]{2,1,0:T(8,128)(2,1)S(1)}, u32[]{:S(2)}, u32[]{:S(2)}) collective-permute-start(bf16[4,128,640]{2,1,0:T(8,128)(2,1)S(1)} %pad_maximum_fusion.mine_ref), channel_id=1, source_target_pairs={{0,1},{1,0},{2,3},{3,2},{4,5},{5,4},{6,7},{7,6},{8,9},{9,8},{10,11... | collective-permute-start | bytes 1966088 | tf_op jit(solution)/shard_map/ppermute | solution.py:1062
  259.8 28.9 %collective-permute-start.50 = (bf16[4,112,128]{2,1,0:T(8,128)(2,1)S(1)}, bf16[4,112,128]{2,1,0:T(8,128)(2,1)S(1)}, u32[]{:S(2)}, u32[]{:S(2)}) collective-permute-start(bf16[4,112,128]{2,1,0:T(8,128)(2,1)S(1)} %get-tuple-element.112), channel_id=1, source_target_pairs={{0,16},{16,0},{1,17},{17,1},{2,18},{18,2},{3,19},{19,3},{4,20},{20... | collective-permute-start | bytes 344072 | tf_op jit(solution)/shard_map/ppermute | solution.py:1059
  263.3 11.2 %collective-permute-start.40 = (bf16[4,2,104,128]{3,2,1,0:T(8,128)(2,1)S(1)}, bf16[4,2,104,128]{3,2,1,0:T(8,128)(2,1)S(1)}, u32[]{:S(2)}, u32[]{:S(2)}) collective-permute-start(bf16[4,2,104,128]{3,2,1,0:T(8,128)(2,1)S(1)} %dynamic-slice_bitcast_fusion.1), channel_id=1, source_target_pairs={{0,2},{2,0},{4,6},{6,4},{8,10},{10,8},{12,14},{14,12},{1,3},{3,1},... | collective-permute-start | bytes 638984 | tf_op jit(solution)/shard_map/ppermute | solution.py:1056
  270.6 15.5 %collective-permute-start.35 = (bf16[128,640]{1,0:T(8,128)(2,1)S(1)}, bf16[128,640]{1,0:T(8,128)(2,1)S(1)}, u32[]{:S(2)}, u32[]{:S(2)}) collective-permute-start(bf16[128,640]{1,0:T(8,128)(2,1)S(1)} %get-tuple-element.92), channel_id=1, source_target_pairs={{0,8},{2,10},{4,12},{6,14},{8,0},{10,2},{12,4},{14,6},{1,9},{3,11}... | collective-permute-start | bytes 491528 | tf_op jit(solution)/shard_map/ppermute | solution.py:1052
  274.5 11.7 %collective-permute-start.37 = (bf16[128,640]{1,0:T(8,128)(2,1)S(1)}, bf16[128,640]{1,0:T(8,128)(2,1)S(1)}, u32[]{:S(2)}, u32[]{:S(2)}) collective-permute-start(bf16[128,640]{1,0:T(8,128)(2,1)S(1)} %get-tuple-element.91), channel_id=1, source_target_pairs={{0,12},{2,14},{4,0},{6,2},{8,4},{10,6},{12,8},{14,10},{1,13},{3,15... | collective-permute-start | bytes 491528 | tf_op jit(solution)/shard_map/ppermute | solution.py:1052
  288.7 18.9 %collective-permute-start.38 = (bf16[4,128,640]{2,1,0:T(8,128)(2,1)S(1)}, bf16[4,128,640]{2,1,0:T(8,128)(2,1)S(1)}, u32[]{:S(2)}, u32[]{:S(2)}) collective-permute-start(bf16[4,128,640]{2,1,0:T(8,128)(2,1)S(1)} %pad_maximum_fusion.1.mine_ref), channel_id=1, source_target_pairs={{0,1},{1,0},{2,3},{3,2},{4,5},{5,4},{6,7},{7,6},{8,9},{9,8},{10,11... | collective-permute-start | bytes 1966088 | tf_op jit(solution)/shard_map/ppermute | solution.py:1062
  (56 other events, 413.3 us)

commit v3 on v2

--- a/solution.py
+++ b/solution.py
@@ -99,7 +99,7 @@
 
 
 def query_bounds(start_ref, m, place, group, chunk):
-    first = start_ref[:, m * chunk : (m + 1) * chunk]
+    first = start_ref[m : m + 1, :]
     last = (m * group + place) * chunk + lane_iota((1, chunk))
     return jnp.concatenate([first, first], axis=1), jnp.concatenate([last, last], axis=1)
 
@@ -116,14 +116,20 @@
     return pltpu.CompilerParams(vmem_limit_bytes=VMEM_LIMIT)
 
 
+def cost(flops, moved, transcendentals=0):
+    return pl.CostEstimate(
+        flops=int(flops), bytes_accessed=int(moved), transcendentals=int(transcendentals)
+    )
+
+
 def attend_kernel(dims, place, *refs):
     slabs, chunk, group, head_dim, rank, half = dims
-    count = 1 + (slabs - 1) * 2 + (group - 1) * slabs * 2
+    count = 2 + (slabs - 1) * 2 + (group - 1) * slabs * 2
     pieces = refs[:count]
     (
-        start_ref, w_ref, a_ref, b_ref, cos_ref, sin_ref, scale_ref, wout_ref, ah_ref,
+        w_ref, a_ref, b_ref, cos_ref, sin_ref, scale_ref, wout_ref, ah_ref,
         h_ref, own_ref, u_ref, q_ref, k_ref, v_ref, qi_ref, ki_ref, o_ref, of_ref, inv_ref,
-        msg_ref, vt_ref, acc_ref,
+        msg_ref, start_ref, vt_ref, acc_ref, seg_ref,
     ) = refs[count:]
     inner, slab, core = place[0], place[1], place[2]
     block = group * chunk
@@ -138,23 +144,39 @@
         other = pl.ds(pl.multiple_of((1 - core) * half, half), half)
         h_ref[at_rows(slab * group + inner, chunk), :] = pieces[0][0]
         own_ref[at_rows(slab, chunk), :] = pieces[0][0]
-        at = 1
+        seg_ref[...] = jnp.zeros_like(seg_ref)
+
+        def keep_segments(where, piece):
+            tail = piece[chunk:, :chunk].astype(f32)
+            seg_ref[pl.ds(where, 1), :] = tail[0:1]
+
+        keep_segments(slab * group + inner, pieces[1])
+        at = 2
         for shift in range(1, slabs):
             source = lax.rem(slab - shift + slabs, slabs)
             rows_at = at_rows(source * group + inner, chunk)
-            h_ref[rows_at, mine] = pieces[at][...]
-            h_ref[rows_at, other] = pieces[at + 1][...]
-            own_ref[at_rows(source, chunk), mine] = pieces[at][...]
-            own_ref[at_rows(source, chunk), other] = pieces[at + 1][...]
+            h_ref[rows_at, mine] = pieces[at][:chunk, :]
+            h_ref[rows_at, other] = pieces[at + 1][:chunk, :]
+            own_ref[at_rows(source, chunk), mine] = pieces[at][:chunk, :]
+            own_ref[at_rows(source, chunk), other] = pieces[at + 1][:chunk, :]
+            keep_segments(source * group + inner, pieces[at])
             at += 2
         for turn in range(1, group):
             peer = lax.rem(inner - turn + group, group)
             for shift in range(slabs):
                 source = lax.rem(slab - shift + slabs, slabs)
                 rows_at = at_rows(source * group + peer, chunk)
-                h_ref[rows_at, mine] = pieces[at][...]
-                h_ref[rows_at, other] = pieces[at + 1][...]
+                h_ref[rows_at, mine] = pieces[at][:chunk, :]
+                h_ref[rows_at, other] = pieces[at + 1][:chunk, :]
+                keep_segments(source * group + peer, pieces[at])
                 at += 2
+        columns = seg_ref[...].T
+        for m in range(slabs):
+            line = seg_ref[pl.ds(m * group + inner, 1), :]
+            below = jnp.zeros((chunk, chunk), f32)
+            for c in range(slabs * group):
+                below = below + jnp.where(columns[:, c : c + 1] < line, 1.0, 0.0)
+            start_ref[m : m + 1, :] = jnp.sum(below, axis=0, keepdims=True).astype(i32)
 
         def low_rows(sl):
             u_ref[sl, :] = nt(h_ref[sl, :], a_ref[...]).astype(bf16)
@@ -213,7 +235,7 @@
         msg_ref[...] = acc_ref[...].astype(bf16)
 
 
-def run_attend(place, tokens, pieces, start, w, a, b, cos, sin, scale, wout, ah, group, head_dim):
+def run_attend(place, tokens, pieces, w, a, b, cos, sin, scale, wout, ah, group, head_dim):
     slabs, chunk, model = tokens.shape
     width = w.shape[2]
     rank = b.shape[1]
@@ -222,9 +244,8 @@
     length = rows * group
     pairs = width // LANES
     in_specs = [pl.BlockSpec((1, chunk, model), lambda p, s: (s[1], 0, 0))]
-    in_specs += [whole_spec((chunk, half))] * len(pieces)
+    in_specs += [whole_spec(piece.shape) for piece in pieces]
     in_specs += [
-        whole_spec((1, rows)),
         pl.BlockSpec((3, model, LANES), lambda p, s: (0, 0, p)),
         whole_spec((3 * rank, model)),
         pl.BlockSpec((3, rank, LANES), lambda p, s: (0, 0, p)),
@@ -251,6 +272,7 @@
             pl.BlockSpec((1, slabs, 2 * chunk), lambda p, s: (p, 0, 0)),
         ),
         ((rows, model + LANES), bf16, whole_spec((rows, model + LANES))),
+        ((slabs, chunk), i32, whole_spec((slabs, chunk))),
     ]
     return pl.pallas_call(
         functools.partial(attend_kernel, (slabs, chunk, group, head_dim, rank, half)),
@@ -262,12 +284,14 @@
             scratch_shapes=[
                 pltpu.VMEM((LANES, length), bf16),
                 pltpu.VMEM((rows, model + LANES), f32),
+                pltpu.VMEM((chunk, chunk), f32),
             ],
         ),
         out_shape=[jax.ShapeDtypeStruct(o[0], o[1]) for o in out],
         compiler_params=params(),
+        cost_estimate=cost(3e10, 4e7),
         name="attend",
-    )(place, tokens, *pieces, start, w, a, b, cos, sin, scale, wout, ah)
+    )(place, tokens, *pieces, w, a, b, cos, sin, scale, wout, ah)
 
 
 def feed_kernel(
@@ -345,6 +369,7 @@
             pltpu.VMEM((rows, model + LANES), f32),
         ],
         compiler_params=params(),
+        cost_estimate=cost(2.4e10, 3e7),
         name="feed",
     )(mine, other, h_own, bo, rates, a, wgu, bgu, wd, ad, scales)
 
@@ -532,6 +557,7 @@
         ),
         out_shape=[jax.ShapeDtypeStruct(o[0], o[1]) for o in out],
         compiler_params=params(),
+        cost_estimate=cost(3e10, 4e7),
         name="feed_back",
     )(
         place, mine, other, mid, cotangent, g_mine, g_other, bd_model, rates, a, u, gate, up,
@@ -671,7 +697,7 @@
                 whole_spec((rank, model)),
                 pl.BlockSpec((LANES, model), lambda p, s: (p, 0)),
                 col_spec(rank),
-                whole_spec((1, rows)),
+                whole_spec((slabs, chunk)),
                 col_spec(rows),
                 col_spec(length),
                 col_spec(length),
@@ -696,6 +722,7 @@
         ),
         out_shape=[jax.ShapeDtypeStruct(o_[0], o_[1]) for o_ in out],
         compiler_params=params(),
+        cost_estimate=cost(3e10, 4e7),
         name="attend_back",
     )(
         place, res, gm, go, mid, h_own, am, ao, rates, bo, wout, ah, start, q, k, v, o, of,
@@ -753,38 +780,80 @@
             jax.ShapeDtypeStruct((group - 1, rows, half), bf16),
         ],
         compiler_params=params(),
+        cost_estimate=cost(7e9, 1e7),
         name="others",
     )(place, gk.reshape(shaped), gv.reshape(shaped), w, a, b)
 
 
 def own_kernel(
-    dims, place, gq_ref, gk_ref, gv_ref, gko_ref, gvo_ref, w_ref, a_ref, b_ref, u_ref, h_ref,
-    hown_ref, res_ref, gbo_ref, gah_ref, keep_ref, send_ref, table_ref, acc_ref, uq_ref,
+    dims, place, gq_ref, gk_ref, gv_ref, w_ref, a_ref, b_ref, res_ref, keep_ref, send_ref, acc_ref
+):
+    slabs, chunk, rank, model = dims
+    half = model // 2
+    rows = slabs * chunk
+    core = place[2]
+    width = gq_ref.shape[1]
+    gq = gq_ref[...]
+    gk = gk_ref[...].reshape(rows, width)
+    gv = gv_ref[...].reshape(rows, width)
+    acc_ref[...] = (
+        nt(gq, w_ref[0])
+        + nt(gk, w_ref[1])
+        + nt(gv, w_ref[2])
+        + nn(nt(gq, b_ref[0]).astype(bf16), a_ref[:rank, :])
+        + nn(nt(gk, b_ref[1]).astype(bf16), a_ref[rank : 2 * rank, :])
+        + nn(nt(gv, b_ref[2]).astype(bf16), a_ref[2 * rank :, :])
+    )
+    mine = pl.ds(pl.multiple_of(core * half, half), half)
+    keep_ref[...] = acc_ref[:, mine] + res_ref[:, mine]
+    send_ref[...] = acc_ref[:, pl.ds(pl.multiple_of((1 - core) * half, half), half)].astype(bf16)
+
+
+def run_own(place, gq, gk, gv, w, a, b, res, slabs, group):
+    length, width = gk.shape
+    rows, model = res.shape
+    chunk = rows // slabs
+    half = model // 2
+    rank = b.shape[1]
+    shaped = (slabs, group, chunk, width)
+    peer = pl.BlockSpec((slabs, 1, chunk, width), lambda g, s: (0, s[0], 0, 0))
+    out = [((rows, half), f32), ((rows, half), bf16)]
+    return pl.pallas_call(
+        functools.partial(own_kernel, (slabs, chunk, rank, model)),
+        grid_spec=pltpu.PrefetchScalarGridSpec(
+            num_scalar_prefetch=1,
+            grid=(1,),
+            in_specs=[
+                whole_spec((rows, width)),
+                peer,
+                peer,
+                whole_spec((3, model, width)),
+                whole_spec((3 * rank, model)),
+                whole_spec((3, rank, width)),
+                whole_spec((rows, model)),
+            ],
+            out_specs=[whole_spec(o[0]) for o in out],
+            scratch_shapes=[pltpu.VMEM((rows, model), f32)],
+        ),
+        out_shape=[jax.ShapeDtypeStruct(o[0], o[1]) for o in out],
+        compiler_params=params(),
+        cost_estimate=cost(7e9, 1e7),
+        name="own",
+    )(place, gq, gk.reshape(shaped), gv.reshape(shaped), w, a, b, res)
+
+
+def grads_kernel(
+    dims, place, gq_ref, gk_ref, gv_ref, b_ref, u_ref, h_ref, hown_ref, gbo_ref, gah_ref,
+    table_ref, uq_ref,
 ):
     slabs, chunk, group, n_seq, rank, model, head_dim = dims
-    half = model // 2
-    rows = slabs * chunk
-    inner, core = place[0], place[2]
+    inner = place[0]
     width = gq_ref.shape[1]
     heads = width // head_dim
     gq = gq_ref[...]
-    gko = gko_ref[...].reshape(rows, width)
-    gvo = gvo_ref[...].reshape(rows, width)
     low_q = nt(gq, b_ref[0]).astype(bf16)
     low_k = nt(gk_ref[...], b_ref[1]).astype(bf16)
     low_v = nt(gv_ref[...], b_ref[2]).astype(bf16)
-    acc_ref[...] = (
-        nt(gq, w_ref[0])
-        + nt(gko, w_ref[1])
-        + nt(gvo, w_ref[2])
-        + nn(low_q, a_ref[:rank, :])
-        + nn(nt(gko, b_ref[1]).astype(bf16), a_ref[rank : 2 * rank, :])
-        + nn(nt(gvo, b_ref[2]).astype(bf16), a_ref[2 * rank :, :])
-    )
-    mine = pl.ds(pl.multiple_of(core * half, half), half)
-    keep_ref[...] = acc_ref[:, mine] + res_ref[:, mine]
-    send_ref[...] = acc_ref[:, pl.ds(pl.multiple_of((1 - core) * half, half), half)].astype(bf16)
-
     for m in range(slabs):
         uq_ref[m * chunk : (m + 1) * chunk, :] = u_ref[at_rows(m * group + inner, chunk), :]
     h = h_ref[...]
@@ -832,86 +901,61 @@
                 table_ref[y, z, x] = jnp.concatenate(parts, axis=0).astype(bf16)
 
 
-def run_own(place, gq, gk, gv, w, a, b, u, h, h_own, res, gbo, gah, slabs, group, n_seq, head_dim):
+def run_grads(place, gq, gk, gv, b, u, h, h_own, gbo, gah, slabs, group, n_seq, head_dim):
     length, width = gk.shape
     rows, model = h_own.shape
     chunk = rows // slabs
-    half = model // 2
     rank = b.shape[1]
     heads = width // head_dim
     owners = n_seq * slabs * group
     units = heads * (head_dim // owners)
     table_rows = (4 * rank + units + 7) // 8 * 8
-    shaped = (slabs, group, chunk, width)
-    peer = pl.BlockSpec((slabs, 1, chunk, width), lambda g, s: (0, s[0], 0, 0))
-    out = [
-        ((rows, half), f32),
-        ((rows, half), bf16),
-        ((group, slabs, n_seq, table_rows, LANES), bf16),
-    ]
+    shape = (group, slabs, n_seq, table_rows, LANES)
+    operands = (gq, gk, gv, b, u, h, h_own, gbo, gah)
     return pl.pallas_call(
-        functools.partial(own_kernel, (slabs, chunk, group, n_seq, rank, model, head_dim)),
+        functools.partial(grads_kernel, (slabs, chunk, group, n_seq, rank, model, head_dim)),
         grid_spec=pltpu.PrefetchScalarGridSpec(
             num_scalar_prefetch=1,
             grid=(1,),
-            in_specs=[
-                whole_spec((rows, width)),
-                whole_spec((length, width)),
-                whole_spec((length, width)),
-                peer,
-                peer,
-                whole_spec((3, model, width)),
-                whole_spec((3 * rank, model)),
-                whole_spec((3, rank, width)),
-                whole_spec((length, 3 * rank)),
-                whole_spec((length, model)),
-                whole_spec((rows, model)),
-                whole_spec((rows, model)),
-                whole_spec((rank, model)),
-                whole_spec((rank, width)),
-            ],
-            out_specs=[whole_spec(o[0]) for o in out],
-            scratch_shapes=[
-                pltpu.VMEM((rows, model), f32),
-                pltpu.VMEM((rows, 3 * rank), bf16),
-            ],
+            in_specs=[whole_spec(operand.shape) for operand in operands],
+            out_specs=whole_spec(shape),
+            scratch_shapes=[pltpu.VMEM((rows, 3 * rank), bf16)],
         ),
-        out_shape=[jax.ShapeDtypeStruct(o[0], o[1]) for o in out],
+        out_shape=jax.ShapeDtypeStruct(shape, bf16),
         compiler_params=params(),
-        name="own",
-    )(
-        place, gq, gk, gv, gk.reshape(shaped), gv.reshape(shaped), w, a, b, u, h, h_own, res,
-        gbo, gah,
-    )
-
-
-def join_kernel(slabs, place, mine_ref, other_ref, out_ref):
-    half = mine_ref.shape[-1]
+        cost_estimate=cost(1e10, 1e7),
+        name="grads",
+    )(place, *operands)
+
+
+def join_kernel(slabs, place, *refs):
+    out_ref = refs[-1]
+    half = refs[0].shape[-1]
     core, slab = place[2], place[1]
     for shift in range(slabs):
         source = lax.rem(slab - shift + slabs, slabs)
-        out_ref[source, :, pl.ds(pl.multiple_of(core * half, half), half)] = mine_ref[
-            shift
-        ].astype(out_ref.dtype)
-        out_ref[source, :, pl.ds(pl.multiple_of((1 - core) * half, half), half)] = other_ref[
-            shift
-        ].astype(out_ref.dtype)
+        for which, ref in ((core, refs[shift]), (1 - core, refs[slabs + shift])):
+            out_ref[source, :, pl.ds(pl.multiple_of(which * half, half), half)] = ref[
+                ...
+            ].astype(out_ref.dtype)
 
 
 def run_join(place, mine, other, dtype):
-    slabs, chunk, half = mine.shape
+    slabs = len(mine)
+    chunk, half = mine[0].shape
     return pl.pallas_call(
         functools.partial(join_kernel, slabs),
         grid_spec=pltpu.PrefetchScalarGridSpec(
             num_scalar_prefetch=1,
             grid=(1,),
-            in_specs=[whole_spec(mine.shape)] * 2,
+            in_specs=[whole_spec((chunk, half))] * (2 * slabs),
             out_specs=whole_spec((slabs, chunk, 2 * half)),
         ),
         out_shape=jax.ShapeDtypeStruct((slabs, chunk, 2 * half), dtype),
         compiler_params=params(),
+        cost_estimate=cost(1e6, 8e6),
         name="join",
-    )(place, mine, other)
+    )(place, *mine, *other)
 
 
 def unpack_early_kernel(dims, place, index, mine_ref, other_ref, am_ref, bm_ref, ad_ref, bd_ref):
@@ -959,6 +1003,7 @@
         ),
         out_shape=[jax.ShapeDtypeStruct(s, f32) for s in shapes],
         compiler_params=params(),
+        cost_estimate=cost(1e6, 8e6),
         name="unpack_early",
     )(place, index, mine, other)
 
@@ -1013,6 +1058,7 @@
         ),
         out_shape=[jax.ShapeDtypeStruct(s, f32) for s in shapes],
         compiler_params=params(),
+        cost_estimate=cost(1e6, 8e6),
         name="unpack_late",
     )(place, index, mine, other, am_gu, bm_down)
 
@@ -1064,37 +1110,13 @@
     def half_piece(array, index, which):
         return lax.dynamic_slice(array, (index, 0, which * half), (1, chunk, half))[0]
 
-    own_piece = half_piece(tokens, slab, core)
-    got = [own_piece] + [
-        to_slab(half_piece(tokens, (slab + shift) % slabs, core), shift)
-        for shift in range(1, slabs)
-    ]
-    pieces = []
-    for shift in range(1, slabs):
-        pieces += [got[shift], other_core(got[shift])]
-    for turn in range(1, group):
-        for shift in range(slabs):
-            peer = within_slab(got[shift], turn)
-            pieces += [peer, other_core(peer)]
-
-    own_seg = lax.dynamic_update_index_in_dim(segments, pick(segments, slab), slab, 0)
-    for shift in range(1, slabs):
-        seg = to_slab(pick(segments, (slab + shift) % slabs), shift)
-        own_seg = lax.dynamic_update_index_in_dim(own_seg, seg, (slab - shift) % slabs, 0)
-    below = lambda seg: jnp.sum(
-        (seg.reshape(1, rows) < own_seg.reshape(rows, 1)).astype(i32), axis=1
-    )
-    start = below(own_seg)
-    for turn in range(1, group):
-        start = start + below(within_slab(own_seg, turn))
-    start = start.reshape(1, rows)
-
-    g_mine = [
-        to_slab(half_piece(cotangent, (slab + shift) % slabs, core), shift)
-        for shift in range(1, slabs)
-    ]
-    g_mine = jnp.stack(g_mine)
-    g_other = other_core(g_mine)
+    def token_piece(index):
+        seg = jnp.pad(pick(segments, index).astype(bf16), (0, half - chunk))
+        return jnp.concatenate(
+            [half_piece(tokens, index, core), jnp.broadcast_to(seg, (8, half))], axis=0
+        )
+
+    tie = lax.optimization_barrier
 
     adapter = pick(adapter_index, slab)
     am = pick(a_model, adapter)
@@ -1115,11 +1137,40 @@
     sin = jnp.tile(jnp.concatenate([-sine, sine], axis=1), (1, LANES // head_dim))
     scale = qk_scale[None, :]
 
-    h_full, h_own, u, q, k, v, qi, ki, o, of, inv, attn_msg = run_attend(
-        place, tokens, pieces, start, w_attn_in, am_qkv, bh, cos, sin, scale, w_attn_out,
+    own_piece = token_piece(slab)
+    got = [own_piece] + [
+        to_slab(token_piece((slab + shift) % slabs), shift) for shift in range(1, slabs)
+    ]
+    index = [adapter_index]
+    for shift in range(1, n_seq):
+        index.append(to_seq(adapter_index, shift))
+    got[2], cos, sin, am_qkv, am_gu, bh, ah_pad, ad_pad, ad, ah, bd, bm = tie(
+        (got[2], cos, sin, am_qkv, am_gu, bh, ah_pad, ad_pad, ad, ah, bd, bm)
+    )
+    pieces = [own_piece]
+    for shift in range(1, slabs):
+        pieces += [got[shift], other_core(got[shift])]
+    for turn in range(1, group):
+        for shift in range(slabs):
+            peer = within_slab(got[shift], turn)
+            pieces += [peer, other_core(peer)]
+    got, g_send = tie(
+        (
+            got,
+            [half_piece(cotangent, (slab + shift) % slabs, core) for shift in range(1, slabs)],
+        )
+    )
+    g_mine = [to_slab(g_send[shift - 1], shift) for shift in range(1, slabs)]
+    pieces, index = tie((pieces, index))
+
+    h_full, h_own, u, q, k, v, qi, ki, o, of, inv, attn_msg, start = run_attend(
+        place, tokens, pieces, w_attn_in, am_qkv, bh, cos, sin, scale, w_attn_out,
         ah_pad, group, head_dim,
     )
+    g_mine, attn_msg = tie((g_mine, attn_msg))
     attn_other = other_core(attn_msg)
+    g_mine = jnp.stack(g_mine)
+    attn_other, g_other = tie((attn_other, other_core(g_mine)))
     mid, u_gu, gate, up, down_msg = run_feed(
         attn_msg, attn_other, h_own, bm[0], mix_rates, am_gu, w_gate_up, bd, w_down, ad_pad,
         mlp_scales, 512,
@@ -1131,29 +1182,30 @@
     )
     mid_other = other_core(mid_msg)
 
-    out_mine = jnp.stack(
-        [pick(out_half, slab)]
-        + [
-            to_slab(pick(out_half, (slab + shift) % slabs), shift)
-            for shift in range(1, slabs)
-        ]
-    )
-    layer_out = run_join(place, out_mine, other_core(out_mine), bf16)
-
-    index = [adapter_index]
-    for shift in range(1, n_seq):
-        index.append(to_seq(adapter_index, shift))
     order = (slab - jnp.arange(slabs, dtype=i32)) % slabs
     index = jnp.stack(index)[:, order]
 
-    def send_home(table):
-        total = pick(table, inner).astype(f32)
-        for turn in range(1, group):
-            total = total + within_slab(pick(table, (inner + turn) % group), turn).astype(f32)
-        total = total.astype(bf16)
-        got = [pick(total, slab)]
-        for shift in range(1, slabs):
-            got.append(to_slab(pick(total, (slab + shift) % slabs), shift))
+    out_mine = [pick(out_half, slab)] + [
+        to_slab(pick(out_half, (slab + shift) % slabs), shift) for shift in range(1, slabs)
+    ]
+
+    def sum_inner(table):
+        return pick(table, inner), [
+            within_slab(pick(table, (inner + turn) % group), turn) for turn in range(1, group)
+        ]
+
+    def add_inner(own, got):
+        total = own.astype(f32)
+        for piece in got:
+            total = total + piece.astype(f32)
+        return total.astype(bf16)
+
+    def over_slabs(total):
+        return [pick(total, slab)] + [
+            to_slab(pick(total, (slab + shift) % slabs), shift) for shift in range(1, slabs)
+        ]
+
+    def over_seqs(got):
         got = jnp.stack(got)
         result = [lax.dynamic_index_in_dim(got, seq_place, 1, keepdims=False)]
         for shift in range(1, n_seq):
@@ -1161,42 +1213,47 @@
                 got, (seq_place + shift) % n_seq, 1, keepdims=False
             )
             result.append(to_seq(sent, shift))
-        return jnp.stack(result)
-
-    early = send_home(early)
-    grad_am_gu, grad_bm_down, grad_ad, grad_bd = run_unpack_early(
-        place, index, early, other_core(early[:, :, : 2 * rank]), adapters, rank,
-        model // owners, row_width // owners, local_hidden // row_width,
-    )
-
+        return result
+
+    early_own, early_got = sum_inner(early)
     gq, gk, gv, h_res, gbo, gah = run_attend_back(
         place, mid_res, mid_msg, mid_other, mid, h_own, attn_msg, attn_other, mix_rates, bm[0],
         w_attn_out, ah, start, q, k, v, o, of, inv, qi, ki, cos, sin, scale, slabs, group,
         head_dim,
     )
+    early_got, out_mine, gk, gv = tie((early_got, out_mine, gk, gv))
+    early = over_slabs(add_inner(early_own, early_got))
+    out_other = [other_core(piece) for piece in out_mine]
     keep, send = run_others(place, gk, gv, w_attn_in, am_qkv, bh, slabs, group)
     others = (keep + other_core(send).astype(f32)).astype(bf16)
-    own_keep, own_send, late = run_own(
-        place, gq, gk, gv, w_attn_in, am_qkv, bh, u, h_full, h_own, h_res, gbo, gah, slabs,
-        group, n_seq, head_dim,
-    )
+    early, out_other, others, gq = tie((early, out_other, others, gq))
+    others_got = [within_slab(others[turn - 1], turn) for turn in range(1, group)]
+    early = over_seqs(early)
+    late = run_grads(
+        place, gq, gk, gv, bh, u, h_full, h_own, gbo, gah, slabs, group, n_seq, head_dim
+    )
+    early, late = tie((early, late))
+    late_own, late_got = sum_inner(late)
+    early_other = other_core(jnp.stack(early)[:, :, : 2 * rank])
+    late_own, gq = tie((late_own, gq))
+    own_keep, own_send = run_own(
+        place, gq, gk, gv, w_attn_in, am_qkv, bh, h_res, slabs, group
+    )
+    late_got, own_send = tie((late_got, own_send))
     own_got = other_core(own_send)
-    others = others.reshape(group - 1, slabs, chunk, half)
-    own_keep = own_keep.reshape(slabs, chunk, half)
-    own_got = own_got.reshape(slabs, chunk, half)
-    result = [None] * slabs
-    for shift in [2, 1, 3, 0] if slabs == 4 else list(range(slabs)):
-        target = (slab + shift) % slabs
-        total = pick(own_keep, target) + pick(own_got, target).astype(f32)
-        for turn in range(1, group):
-            got = within_slab(pick(others[turn - 1], target), turn)
-            total = total + got.astype(f32)
-        total = total.astype(bf16)
-        result[shift] = to_slab(total, shift) if shift else total
-    result = jnp.stack(result)
-    input_grad = run_join(place, result, other_core(result), f32)
-
-    late = send_home(late)
+    total = own_keep + own_got.astype(f32)
+    for got_part in others_got:
+        total = total + got_part.astype(f32)
+    total = total.astype(bf16).reshape(slabs, chunk, half)
+    result = over_slabs(total)
+    late = over_slabs(add_inner(late_own, late_got))
+    layer_out = run_join(place, out_mine, out_other, bf16)
+    grad_am_gu, grad_bm_down, grad_ad, grad_bd = run_unpack_early(
+        place, index, jnp.stack(early), early_other, adapters, rank, model // owners,
+        row_width // owners, local_hidden // row_width,
+    )
+    late = jnp.stack(over_seqs(late))
+    input_grad = run_join(place, result, [other_core(piece) for piece in result], f32)
     grad_am, grad_bm, grad_ah, grad_bh = run_unpack_late(
         place, index, late, other_core(late[:, :, : 3 * rank]), grad_am_gu, grad_bm_down,
         local_heads, head_dim // owners,

time: 313 us -> 269 us (0.86)
  waiting for transfers between devices: 68.3 us -> 28.1 us
  starting transfers between devices: 52.9 us -> 43.2 us
  Pallas kernels: 158 us -> 162 us
    ppermute x21 -> x18, waiting for transfers between devices: 41.3 us -> 11.9 us  [to_slab(): return lax.ppermute(array, 'ctx', pairs)]
    ppermute x11 -> x7, waiting for transfers between devices: 22.6 us -> 9.72 us  [within_slab(): return lax.ppermute(array, 'ctx', pairs)]
    ppermute x11 -> x7, starting transfers between devices: 11.9 us -> 6.91 us  [within_slab(): return lax.ppermute(array, 'ctx', pairs)]
    ppermute x21 -> x18, starting transfers between devices: 33.6 us -> 28.9 us  [to_slab(): return lax.ppermute(array, 'ctx', pairs)]
    ppermute x17 -> x23, waiting for transfers between devices: 2.47 us -> 6.48 us  [other_core(): return lax.ppermute(array, 'wt', [(0, 1), (1, 0)])]
    pallas_call x1 -> x2, Pallas kernels: 14.9 us -> 18.4 us  [the longest x1 11 us: run_own(): pl.pallas_call(functools.partial(own_kernel, (slabs, chunk, rank, model))...]
    unnamed x58 -> x79, local copies, waits for them, and re-layouts: 7.35 us -> 5.73 us
  transfers between devices with their start and end apart: 52 -> 51, of which waited for: 21 -> 11; matrix products, arithmetic and copies ran while one was open for 7% -> 8% of each run, Pallas kernels for 21% -> 36%
where the time goes in v3:
time: 269 us; the launch traced here: 268 us
  Pallas kernels  162 us (60%)
  starting transfers between devices  43.2 us (16%)
  waiting for transfers between devices  28.1 us (10%)
  local copies, waits for them, and re-layouts  25 us (9%)
  other arithmetic  5.56 us (2%)
  between operations  3.46 us (1%)
    pallas_call x1, Pallas kernels, run_attend_back(): pl.pallas_call(functools.partial(attend_back_kernel, (slabs, chunk, group...  34.3 us
    pallas_call x1, Pallas kernels, run_attend(): pl.pallas_call(functools.partial(attend_kernel, (slabs, chunk, group, hea...  34.1 us
    pallas_call x1, Pallas kernels, run_feed_back(): pl.pallas_call(functools.partial(feed_back_kernel, (slabs, chunk, group,...  30.8 us
    ppermute x18, starting transfers between devices, to_slab(): return lax.ppermute(array, 'ctx', pairs)  28.9 us
    pallas_call x1, Pallas kernels, run_feed(): pl.pallas_call(functools.partial(feed_kernel, (rank, model)), grid=(hidde...  23.4 us
    ppermute x18, waiting for transfers between devices, to_slab(): return lax.ppermute(array, 'ctx', pairs)  11.9 us
    pallas_call x1, Pallas kernels, run_own(): pl.pallas_call(functools.partial(own_kernel, (slabs, chunk, rank, model))...  11 us
    ppermute x7, waiting for transfers between devices, within_slab(): return lax.ppermute(array, 'ctx', pairs)  9.72 us
  transfers between devices with their start and end apart: 51, of which 11 were waited for; matrix products, arithmetic and copies ran while one was open for 8% of the time, Pallas kernels for 36%

profile of v3, /device:TPU:0, one launch (start us, length us, event | category | flops | bytes accessed | tf_op | source)
XLA Modules:
  0.0 267.5 jit_solution(14312779667280263774)
XLA Ops:
  2.9 4.1 %collective-permute-start.1 = (bf16[136,640]{1,0:T(8,128)(2,1)S(1)}, bf16[136,640]{1,0:T(8,128)(2,1)S(1)}, u32[]{:S(2)}, u32[]{:S(2)}) collective-permute-start(bf16[136,640]{1,0:T(8,128)(2,1)S(1)} %pad_maximum_fusion.8), channel_id=1, source_target_pairs={{0,8},{2,10},{4,12},{6,14},{8,0},{10,2},{12,4},{14,6},{1,9},{3,11}... | collective-permute-start | bytes 522248 | tf_op jit(solution)/shard_map/ppermute | solution.py:1098
  8.7 2.3 collective-permute-start.2
  29.3 4.6 %collective-permute-done.13.refs_12_ = bf16[136,640]{1,0:T(8,128)(2,1)S(1)} collective-permute-done((bf16[136,640]{1,0:T(8,128)(2,1)S(1)}, bf16[136,640]{1,0:T(8,128)(2,1)S(1)}, u32[]{:S(2)}, u32[]{:S(2)}) %collective-permute-start.13) | collective-permute-done | bytes 174112 | tf_op jit(solution)/shard_map/ppermute | solution.py:1102
  34.3 3.3 %collective-permute-done.11.refs_10_ = bf16[136,640]{1,0:T(8,128)(2,1)} collective-permute-done((bf16[136,640]{1,0:T(8,128)(2,1)S(1)}, bf16[136,640]{1,0:T(8,128)(2,1)}, u32[]{:S(2)}, u32[]{:S(2)}) %collective-permute-start.11) | collective-permute-done | bytes 174112 | tf_op jit(solution)/shard_map/ppermute | solution.py:1102
  45.0 3.3 %collective-permute-start.5 = (bf16[128,640]{1,0:T(8,128)(2,1)S(1)}, bf16[128,640]{1,0:T(8,128)(2,1)S(1)}, u32[]{:S(2)}, u32[]{:S(2)}) collective-permute-start(bf16[128,640]{1,0:T(8,128)(2,1)S(1)} %get-tuple-element.113), channel_id=1, source_target_pairs={{0,12},{2,14},{4,0},{6,2},{8,4},{10,6},{12,8},{14,10},{1,13},{3,15... | collective-permute-start | bytes 491528 | tf_op jit(solution)/shard_map/ppermute | solution.py:1098
  48.3 34.1 %attend.1 = (bf16[1024,1280]{1,0:T(8,128)(2,1)}, bf16[512,1280]{1,0:T(8,128)(2,1)}, bf16[1024,48]{1,0:T(8,128)(2,1)}, bf16[512,640]{1,0:T(8,128)(2,1)}, bf16[102...) custom-call(s32[4]{0:T(128)} %pad_add_fusion.1.place, ...), custom_call_target="tpu_custom_call" | custom-call | flops 30000001024 | bytes 40000000 | tf_op jit(solution)/shard_map/attend/pallas_call | solution.py:277
  83.9 2.6 collective-permute-done.19.g_other_ref
  87.6 23.4 %feed.1 = (f32[512,1280]{1,0:T(8,128)}, bf16[512,32]{1,0:T(8,128)(2,1)}, bf16[512,2560]{1,0:T(8,128)(2,1)}, bf16[512,2560]{1,0:T(8,128)(2,1)}, bf16[512,1408]{1,0:T(8,128)(2,1)}) custom-call(bf16[512,1408]{1,0:T(8,128)(2,1)} %get-tuple-element.135.mine_ref.am_ref, bf16[512,1408]{1,0:T(8,128)(2,1)} %copy-done.28, ...), custom_call_target="tpu_custom_call" | custom-call | flops 24000000000 | bytes 30000000 | tf_op jit(solution)/shard_map/feed/pallas_call | solution.py:349
  111.3 3.3 %collective-permute-done.20.other_ref = bf16[512,1408]{1,0:T(8,128)(2,1)S(1)} collective-permute-done((bf16[512,1408]{1,0:T(8,128)(2,1)}, bf16[512,1408]{1,0:T(8,128)(2,1)S(1)}, u32[]{:S(2)}, u32[]{:S(2)}) %collective-permute-start.20) | collective-permute-done | bytes 1441824 | tf_op jit(solution)/shard_map/ppermute | solution.py:1108
  115.7 30.8 %feed_back.1 = (bf16[4,128,640]{2,1,0:T(8,128)(2,1)}, f32[512,1280]{1,0:T(8,128)}, bf16[512,1280]{1,0:T(8,128)(2,1)}, bf16[2,4,2,112,128]{4,3,2,1,0:T(8,128)(2,1)}) custom-call(s32[4]{0:T(128)} %pad_add_fusion.1.place, bf16[512,1408]{1,0:T(8,128)(2,1)} %get-tuple-element.145.mine_ref, bf16[512,1408]{1,0:T(8,128)(2,1)} %copy-done.29, ...), custom_call_target="tpu_custom_call" | custom-call | flops 30000001024 | bytes 40000000 | tf_op jit(solution)/shard_map/feed_back/pallas_call | solution.py:515
  150.1 2.8 %collective-permute-start.24 = (bf16[128,640]{1,0:T(8,128)(2,1)S(1)}, bf16[128,640]{1,0:T(8,128)(2,1)S(1)}, u32[]{:S(2)}, u32[]{:S(2)}) collective-permute-start(bf16[128,640]{1,0:T(8,128)(2,1)S(1)} %get-tuple-element.223), channel_id=1, source_target_pairs={{0,12},{2,14},{4,0},{6,2},{8,4},{10,6},{12,8},{14,10},{1,13},{3,15... | collective-permute-start | bytes 491528 | tf_op jit(solution)/shard_map/ppermute | solution.py:1098
  153.6 34.3 %attend_back.1 = (bf16[512,640]{1,0:T(8,128)(2,1)}, bf16[1024,640]{1,0:T(8,128)(2,1)}, bf16[1024,640]{1,0:T(8,128)(2,1)}, f32[512,1280]{1,0:T(8,128)}, f32[16,1280]{1,0:T(8,128)}, /*index=5*/f32[16,640]{1,0:T(8,128)}) custom-call(s32[4]{0:T(128)} %pad_add_fusion.1.place, f32[512,1280]{1,0:T(8,128)} %get-tuple-element.154.res_ref, ...), custom_call_target="tpu_custom_call" | custom-call | flops 30000001024 | bytes 40000000 | tf_op jit(solution)/shard_map/attend_back/pallas_call | solution.py:683
  187.9 8.1 %others.1 = (f32[1,512,640]{2,1,0:T(8,128)}, bf16[1,512,640]{2,1,0:T(8,128)(2,1)}) custom-call(s32[4]{0:T(128)} %pad_add_fusion.1.place, bf16[4,2,128,640]{3,2,1,0:T(8,128)(2,1)} %bitcast.151, bf16[4,2,128,640]{3,2,1,0:T(8,128)(2,1)} %bitcast.153, bf16[3,1280,640]{2,1,0:T(8,128)(2,1)} %w_ref.3, bf16[48,1280]{1,0:T(8,128)(2,1)} %bitcast.133, ...), custom_call_target="tpu_custom_call" | custom-call | flops 7000000000 | bytes 10000000 | tf_op jit(solution)/shard_map/others/pallas_call | solution.py:763
  197.4 3.1 %collective-permute-start.28 = (bf16[2,112,128]{2,1,0:T(8,128)(2,1)S(1)}, bf16[2,112,128]{2,1,0:T(8,128)(2,1)S(1)}, u32[]{:S(2)}, u32[]{:S(2)}) collective-permute-start(bf16[2,112,128]{2,1,0:T(8,128)(2,1)S(1)} %get-tuple-element.231), channel_id=1, source_target_pairs={{0,12},{2,14},{4,0},{6,2},{8,4},{10,6},{12,8},{14,10},{1,13},{3,15... | collective-permute-start | bytes 172040 | tf_op jit(solution)/shard_map/ppermute | solution.py:1098
  200.5 2.3 collective-permute-done.26
  209.2 7.4 %grads.1 = bf16[2,4,2,104,128]{4,3,2,1,0:T(8,128)(2,1)} custom-call(s32[4]{0:T(128)} %pad_add_fusion.1.place, bf16[512,640]{1,0:T(8,128)(2,1)} %get-tuple-element.192.gq_ref, bf16[1024,640]{1,0:T(8,128)(2,1)} %get-tuple-element.173.gk_ref, bf16[1024,640]{1,0:T(8,128)(2,1)} %get-tuple-element.174.gv_ref, bf16[3,16,640]{2,1,0:T(8,128)(2,1)} %reshape.155.refs_18_.b_ref, ...), custom_call_target="tpu_custom_call" | custom-call | flops 10000000000 | bytes 10000000 | tf_op jit(solution)/shard_map/grads/pallas_call | solution.py:915
  218.3 11.0 %own.1 = (f32[512,640]{1,0:T(8,128)}, bf16[512,640]{1,0:T(8,128)(2,1)}) custom-call(s32[4]{0:T(128)} %pad_add_fusion.1.place, bf16[512,640]{1,0:T(8,128)(2,1)} %get-tuple-element.192.gq_ref, bf16[4,2,128,640]{3,2,1,0:T(8,128)(2,1)} %bitcast.152, bf16[4,2,128,640]{3,2,1,0:T(8,128)(2,1)} %bitcast.154, bf16[3,1280,640]{2,1,0:T(8,128)(2,1)} %w_ref.3, ...), custom_call_target="tpu_custom_call" | custom-call | flops 7000000000 | bytes 10000000 | tf_op jit(solution)/shard_map/own/pallas_call | solution.py:821
  230.6 3.2 %join.2 = bf16[4,128,1280]{2,1,0:T(8,128)(2,1)} custom-call(s32[4]{0:T(128)} %pad_add_fusion.1.place, bf16[128,640]{1,0:T(8,128)(2,1)} %copy-done.3, bf16[128,640]{1,0:T(8,128)(2,1)} %copy-done.9, bf16[128,640]{1,0:T(8,128)(2,1)} %copy-done.10, bf16[128,640]{1,0:T(8,128)(2,1)} %copy-done.11, bf16[128,640]{1,0:T(8,128)(2,1)} %copy-done.12, ...), custom_call_target="tpu_custom_call" | custom-call | flops 1000000 | bytes 8000000 | tf_op jit(solution)/shard_map/join/pallas_call | solution.py:946
  235.3 2.4 collective-permute-start.47
  237.8 2.7 %collective-permute-done.45 = bf16[2,104,128]{2,1,0:T(8,128)(2,1)S(1)} collective-permute-done((bf16[2,104,128]{2,1,0:T(8,128)(2,1)S(1)}, bf16[2,104,128]{2,1,0:T(8,128)(2,1)S(1)}, u32[]{:S(2)}, u32[]{:S(2)}) %collective-permute-start.45) | collective-permute-done | bytes 53280 | tf_op jit(solution)/shard_map/ppermute | solution.py:1098
  249.2 3.1 %unpack_early.1 = (f32[8,2,16,40]{3,2,1,0:T(8,128)}, f32[8,16,80]{2,1,0:T(8,128)}, f32[8,16,8,20]{3,2,1,0:T(8,128)}, f32[8,2,16,8,20]{4,3,2,1,0:T(8,128)}) custom-call(s32[4]{0:T(128)} %pad_add_fusion.1.place, s32[2,4]{1,0:T(2,128)} %bitcast.143, bf16[2,4,112,128]{3,2,1,0:T(8,128)(2,1)} %pad_maximum_fusion.2.mine_ref, bf16[2,4,32,128]{3,2,1,0:T(8,128)(2,1)} %copy-done.25), custom_call_target="tpu_custom_call" | custom-call | flops 1000000 | bytes 8000000 | tf_op jit(solution)/shard_map/unpack_early/pallas_call | solution.py:994
  252.8 4.0 %collective-permute-done.39.refs_2_ = bf16[128,640]{1,0:T(8,128)(2,1)S(1)} collective-permute-done((bf16[128,640]{1,0:T(8,128)(2,1)S(1)}, bf16[128,640]{1,0:T(8,128)(2,1)S(1)}, u32[]{:S(2)}, u32[]{:S(2)}) %collective-permute-start.39) | collective-permute-done | bytes 163872 | tf_op jit(solution)/shard_map/ppermute | solution.py:1098
  259.4 3.0 %unpack_late.1 = (f32[8,5,16,40]{3,2,1,0:T(8,128)}, f32[8,2,16,80]{3,2,1,0:T(8,128)}, f32[8,10,4,16]{3,2,1,0:T(4,128)}, f32[8,3,10,4,16]{4,3,2,1,0:T(4,128)}) custom-call(s32[4]{0:T(128)} %pad_add_fusion.1.place, s32[2,4]{1,0:T(2,128)} %bitcast.144, bf16[2,4,104,128]{3,2,1,0:T(8,128)(2,1)} %pad_maximum_fusion.3.mine_ref, bf16[2,4,48,128]{3,2,1,0:T(8,128)(2,1)} %copy-done.23, ...), custom_call_target="tpu_custom_call" | custom-call | flops 1000000 | bytes 8000000 | tf_op jit(solution)/shard_map/unpack_late/pallas_call | solution.py:1046
  263.8 3.7 %join.3 = f32[4,128,1280]{2,1,0:T(8,128)} custom-call(s32[4]{0:T(128)} %pad_add_fusion.1.place, bf16[128,640]{1,0:T(8,128)(2,1)} %copy-done.4, bf16[128,640]{1,0:T(8,128)(2,1)} %copy-done.14, bf16[128,640]{1,0:T(8,128)(2,1)} %copy-done.16, bf16[128,640]{1,0:T(8,128)(2,1)} %copy-done.17, bf16[128,640]{1,0:T(8,128)(2,1)} %copy-done.19, ...), custom_call_target="tpu_custom_call" | custom-call | flops 1000000 | bytes 8000000 | tf_op jit(solution)/shard_map/join/pallas_call | solution.py:946
  (237 shorter events, 61.1 us)
Async XLA Ops:
  2.9 23.5 %collective-permute-start.1 = (bf16[136,640]{1,0:T(8,128)(2,1)S(1)}, bf16[136,640]{1,0:T(8,128)(2,1)S(1)}, u32[]{:S(2)}, u32[]{:S(2)}) collective-permute-start(bf16[136,640]{1,0:T(8,128)(2,1)S(1)} %pad_maximum_fusion.8), channel_id=1, source_target_pairs={{0,8},{2,10},{4,12},{6,14},{8,0},{10,2},{12,4},{14,6},{1,9},{3,11}... | collective-permute-start | bytes 522248 | tf_op jit(solution)/shard_map/ppermute | solution.py:1098
  7.0 20.1 %collective-permute-start = (bf16[136,640]{1,0:T(8,128)(2,1)S(1)}, bf16[136,640]{1,0:T(8,128)(2,1)S(1)}, u32[]{:S(2)}, u32[]{:S(2)}) collective-permute-start(bf16[136,640]{1,0:T(8,128)(2,1)S(1)} %pad_maximum_fusion.7), channel_id=1, source_target_pairs={{0,4},{2,6},{4,8},{6,10},{8,12},{10,14},{12,0},{14,2},{1,5},{3,7},... | collective-permute-start | bytes 522248 | tf_op jit(solution)/shard_map/ppermute | solution.py:1098
  8.7 20.1 %collective-permute-start.2 = (bf16[136,640]{1,0:T(8,128)(2,1)S(1)}, bf16[136,640]{1,0:T(8,128)(2,1)S(1)}, u32[]{:S(2)}, u32[]{:S(2)}) collective-permute-start(bf16[136,640]{1,0:T(8,128)(2,1)S(1)} %pad_maximum_fusion.9), channel_id=1, source_target_pairs={{0,12},{2,14},{4,0},{6,2},{8,4},{10,6},{12,8},{14,10},{1,13},{3,15... | collective-permute-start | bytes 522248 | tf_op jit(solution)/shard_map/ppermute | solution.py:1098
  11.0 18.2 %collective-permute-start.9 = (bf16[136,640]{1,0:T(8,128)(2,1)S(1)}, bf16[136,640]{1,0:T(8,128)(2,1)S(1)}, u32[]{:S(2)}, u32[]{:S(2)}) collective-permute-start(bf16[136,640]{1,0:T(8,128)(2,1)S(1)} %pad_maximum_fusion.6.refs_1_), channel_id=1, source_target_pairs={{0,2},{2,0},{4,6},{6,4},{8,10},{10,8},{12,14},{14,12},{1,3},{3,1},... | collective-permute-start | bytes 522248 | tf_op jit(solution)/shard_map/ppermute | solution.py:1102
  12.6 14.5 %collective-permute-start.17 = (s32[4]{0:T(128)S(1)}, s32[4]{0:T(128)S(1)}, u32[]{:S(2)}, u32[]{:S(2)}) collective-permute-start(s32[4]{0:T(128)S(1)} %copy-done.27), channel_id=1, source_target_pairs={{0,16},{16,0},{1,17},{17,1},{2,18},{18,2},{3,19},{19,3},{4,20},{20... | collective-permute-start | bytes 56 | tf_op jit(solution)/shard_map/ppermute | solution.py:1105
  27.1 10.5 %collective-permute-start.11 = (bf16[136,640]{1,0:T(8,128)(2,1)S(1)}, bf16[136,640]{1,0:T(8,128)(2,1)}, u32[]{:S(2)}, u32[]{:S(2)}) collective-permute-start(bf16[136,640]{1,0:T(8,128)(2,1)S(1)} %collective-permute-done.refs_2_), channel_id=1, source_target_pairs={{0,2},{2,0},{4,6},{6,4},{8,10},{10,8},{12,14},{14,12},{1,3},{3,1},... | collective-permute-start | bytes 522248 | tf_op jit(solution)/shard_map/ppermute | solution.py:1102
  28.7 10.8 %collective-permute-start.15 = (bf16[136,640]{1,0:T(8,128)(2,1)S(1)}, bf16[136,640]{1,0:T(8,128)(2,1)S(1)}, u32[]{:S(2)}, u32[]{:S(2)}) collective-permute-start(bf16[136,640]{1,0:T(8,128)(2,1)S(1)} %collective-permute-done.2.refs_6_), channel_id=1, source_target_pairs={{0,2},{2,0},{4,6},{6,4},{8,10},{10,8},{12,14},{14,12},{1,3},{3,1},... | collective-permute-start | bytes 522248 | tf_op jit(solution)/shard_map/ppermute | solution.py:1102
  29.2 10.3 %collective-permute-start.6 = (bf16[136,640]{1,0:T(8,128)(2,1)S(1)}, bf16[136,640]{1,0:T(8,128)(2,1)S(1)}, u32[]{:S(2)}, u32[]{:S(2)}) collective-permute-start(bf16[136,640]{1,0:T(8,128)(2,1)S(1)} %collective-permute-done.refs_2_), channel_id=1, source_target_pairs={{0,1},{1,0},{2,3},{3,2},{4,5},{5,4},{6,7},{7,6},{8,9},{9,8},{10,11... | collective-permute-start | bytes 522248 | tf_op jit(solution)/shard_map/ppermute | solution.py:1108
  33.8 10.5 %collective-permute-start.8 = (bf16[136,640]{1,0:T(8,128)(2,1)S(1)}, bf16[136,640]{1,0:T(8,128)(2,1)}, u32[]{:S(2)}, u32[]{:S(2)}) collective-permute-start(bf16[136,640]{1,0:T(8,128)(2,1)S(1)} %collective-permute-done.2.refs_6_), channel_id=1, source_target_pairs={{0,1},{1,0},{2,3},{3,2},{4,5},{5,4},{6,7},{7,6},{8,9},{9,8},{10,11... | collective-permute-start | bytes 522248 | tf_op jit(solution)/shard_map/ppermute | solution.py:1108
  33.8 10.6 %collective-permute-start.10 = (bf16[136,640]{1,0:T(8,128)(2,1)S(1)}, bf16[136,640]{1,0:T(8,128)(2,1)}, u32[]{:S(2)}, u32[]{:S(2)}) collective-permute-start(bf16[136,640]{1,0:T(8,128)(2,1)S(1)} %collective-permute-done.9.refs_8_), channel_id=1, source_target_pairs={{0,1},{1,0},{2,3},{3,2},{4,5},{5,4},{6,7},{7,6},{8,9},{9,8},{10,11... | collective-permute-start | bytes 522248 | tf_op jit(solution)/shard_map/ppermute | solution.py:1108
  44.4 38.1 %collective-permute-start.3 = (bf16[128,640]{1,0:T(8,128)(2,1)S(1)}, bf16[128,640]{1,0:T(8,128)(2,1)S(1)}, u32[]{:S(2)}, u32[]{:S(2)}) collective-permute-start(bf16[128,640]{1,0:T(8,128)(2,1)S(1)} %get-tuple-element.111), channel_id=1, source_target_pairs={{0,4},{2,6},{4,8},{6,10},{8,12},{10,14},{12,0},{14,2},{1,5},{3,7},... | collective-permute-start | bytes 491528 | tf_op jit(solution)/shard_map/ppermute | solution.py:1098
  44.5 38.0 %collective-permute-start.4 = (bf16[128,640]{1,0:T(8,128)(2,1)S(1)}, bf16[128,640]{1,0:T(8,128)(2,1)S(1)}, u32[]{:S(2)}, u32[]{:S(2)}) collective-permute-start(bf16[128,640]{1,0:T(8,128)(2,1)S(1)} %get-tuple-element.112), channel_id=1, source_target_pairs={{0,8},{2,10},{4,12},{6,14},{8,0},{10,2},{12,4},{14,6},{1,9},{3,11}... | collective-permute-start | bytes 491528 | tf_op jit(solution)/shard_map/ppermute | solution.py:1098
  45.0 37.5 %collective-permute-start.5 = (bf16[128,640]{1,0:T(8,128)(2,1)S(1)}, bf16[128,640]{1,0:T(8,128)(2,1)S(1)}, u32[]{:S(2)}, u32[]{:S(2)}) collective-permute-start(bf16[128,640]{1,0:T(8,128)(2,1)S(1)} %get-tuple-element.113), channel_id=1, source_target_pairs={{0,12},{2,14},{4,0},{6,2},{8,4},{10,6},{12,8},{14,10},{1,13},{3,15... | collective-permute-start | bytes 491528 | tf_op jit(solution)/shard_map/ppermute | solution.py:1098
  148.0 39.8 %collective-permute-start.22 = (bf16[128,640]{1,0:T(8,128)(2,1)S(1)}, bf16[128,640]{1,0:T(8,128)(2,1)S(1)}, u32[]{:S(2)}, u32[]{:S(2)}) collective-permute-start(bf16[128,640]{1,0:T(8,128)(2,1)S(1)} %get-tuple-element.225), channel_id=1, source_target_pairs={{0,4},{2,6},{4,8},{6,10},{8,12},{10,14},{12,0},{14,2},{1,5},{3,7},... | collective-permute-start | bytes 491528 | tf_op jit(solution)/shard_map/ppermute | solution.py:1098
  148.7 39.2 %collective-permute-start.23 = (bf16[128,640]{1,0:T(8,128)(2,1)S(1)}, bf16[128,640]{1,0:T(8,128)(2,1)S(1)}, u32[]{:S(2)}, u32[]{:S(2)}) collective-permute-start(bf16[128,640]{1,0:T(8,128)(2,1)S(1)} %get-tuple-element.224), channel_id=1, source_target_pairs={{0,8},{2,10},{4,12},{6,14},{8,0},{10,2},{12,4},{14,6},{1,9},{3,11}... | collective-permute-start | bytes 491528 | tf_op jit(solution)/shard_map/ppermute | solution.py:1098
  150.1 37.8 %collective-permute-start.24 = (bf16[128,640]{1,0:T(8,128)(2,1)S(1)}, bf16[128,640]{1,0:T(8,128)(2,1)S(1)}, u32[]{:S(2)}, u32[]{:S(2)}) collective-permute-start(bf16[128,640]{1,0:T(8,128)(2,1)S(1)} %get-tuple-element.223), channel_id=1, source_target_pairs={{0,12},{2,14},{4,0},{6,2},{8,4},{10,6},{12,8},{14,10},{1,13},{3,15... | collective-permute-start | bytes 491528 | tf_op jit(solution)/shard_map/ppermute | solution.py:1098
  153.0 34.9 %collective-permute-start.21 = (bf16[4,2,112,128]{3,2,1,0:T(8,128)(2,1)S(1)}, bf16[4,2,112,128]{3,2,1,0:T(8,128)(2,1)S(1)}, u32[]{:S(2)}, u32[]{:S(2)}) collective-permute-start(bf16[4,2,112,128]{3,2,1,0:T(8,128)(2,1)S(1)} %dynamic-slice_bitcast_fusion), channel_id=1, source_target_pairs={{0,2},{2,0},{4,6},{6,4},{8,10},{10,8},{12,14},{14,12},{1,3},{3,1},... | collective-permute-start | bytes 688136 | tf_op jit(solution)/shard_map/ppermute | solution.py:1102
  207.6 34.2 %collective-permute-start.37 = (bf16[512,640]{1,0:T(8,128)(2,1)S(1)}, bf16[512,640]{1,0:T(8,128)(2,1)S(1)}, u32[]{:S(2)}, u32[]{:S(2)}) collective-permute-start(bf16[512,640]{1,0:T(8,128)(2,1)S(1)} %bitcast.120), channel_id=1, source_target_pairs={{0,2},{2,0},{4,6},{6,4},{8,10},{10,8},{12,14},{14,12},{1,3},{3,1},... | collective-permute-start | bytes 1966088 | tf_op jit(solution)/shard_map/ppermute | solution.py:1102
  217.7 11.5 %collective-permute-start.35 = (bf16[4,2,104,128]{3,2,1,0:T(8,128)(2,1)S(1)}, bf16[4,2,104,128]{3,2,1,0:T(8,128)(2,1)S(1)}, u32[]{:S(2)}, u32[]{:S(2)}) collective-permute-start(bf16[4,2,104,128]{3,2,1,0:T(8,128)(2,1)S(1)} %get-tuple-element.227), channel_id=1, source_target_pairs={{0,2},{2,0},{4,6},{6,4},{8,10},{10,8},{12,14},{14,12},{1,3},{3,1},... | collective-permute-start | bytes 638984 | tf_op jit(solution)/shard_map/ppermute | solution.py:1102
  229.3 12.7 %collective-permute-start.36 = (bf16[512,640]{1,0:T(8,128)(2,1)}, bf16[512,640]{1,0:T(8,128)(2,1)S(1)}, u32[]{:S(2)}, u32[]{:S(2)}) collective-permute-start(bf16[512,640]{1,0:T(8,128)(2,1)} %get-tuple-element.196), channel_id=1, source_target_pairs={{0,1},{1,0},{2,3},{3,2},{4,5},{5,4},{6,7},{7,6},{8,9},{9,8},{10,11... | collective-permute-start | bytes 1966088 | tf_op jit(solution)/shard_map/ppermute | solution.py:1108
  242.3 10.0 %collective-permute-start.38 = (bf16[128,640]{1,0:T(8,128)(2,1)S(1)}, bf16[128,640]{1,0:T(8,128)(2,1)S(1)}, u32[]{:S(2)}, u32[]{:S(2)}) collective-permute-start(bf16[128,640]{1,0:T(8,128)(2,1)S(1)} %get-tuple-element.221), channel_id=1, source_target_pairs={{0,4},{2,6},{4,8},{6,10},{8,12},{10,14},{12,0},{14,2},{1,5},{3,7},... | collective-permute-start | bytes 491528 | tf_op jit(solution)/shard_map/ppermute | solution.py:1098
  243.7 13.1 %collective-permute-start.39 = (bf16[128,640]{1,0:T(8,128)(2,1)S(1)}, bf16[128,640]{1,0:T(8,128)(2,1)S(1)}, u32[]{:S(2)}, u32[]{:S(2)}) collective-permute-start(bf16[128,640]{1,0:T(8,128)(2,1)S(1)} %get-tuple-element.220), channel_id=1, source_target_pairs={{0,8},{2,10},{4,12},{6,14},{8,0},{10,2},{12,4},{14,6},{1,9},{3,11}... | collective-permute-start | bytes 491528 | tf_op jit(solution)/shard_map/ppermute | solution.py:1098
  245.0 11.9 %collective-permute-start.40 = (bf16[128,640]{1,0:T(8,128)(2,1)S(1)}, bf16[128,640]{1,0:T(8,128)(2,1)S(1)}, u32[]{:S(2)}, u32[]{:S(2)}) collective-permute-start(bf16[128,640]{1,0:T(8,128)(2,1)S(1)} %get-tuple-element.219), channel_id=1, source_target_pairs={{0,12},{2,14},{4,0},{6,2},{8,4},{10,6},{12,8},{14,10},{1,13},{3,15... | collective-permute-start | bytes 491528 | tf_op jit(solution)/shard_map/ppermute | solution.py:1098
  246.3 11.1 %collective-permute-start.48 = (bf16[4,104,128]{2,1,0:T(8,128)(2,1)S(1)}, bf16[4,104,128]{2,1,0:T(8,128)(2,1)S(1)}, u32[]{:S(2)}, u32[]{:S(2)}) collective-permute-start(bf16[4,104,128]{2,1,0:T(8,128)(2,1)S(1)} %get-tuple-element.236), channel_id=1, source_target_pairs={{0,16},{16,0},{1,17},{17,1},{2,18},{18,2},{3,19},{19,3},{4,20},{20... | collective-permute-start | bytes 319496 | tf_op jit(solution)/shard_map/ppermute | solution.py:1105
  (66 other events, 593.0 us)

commit v4 on v3

--- a/solution.py
+++ b/solution.py
@@ -12,6 +12,7 @@
 bf16 = jnp.bfloat16
 i32 = jnp.int32
 VMEM_LIMIT = 58 * 1024 * 1024
+SMALL_LIMIT = 24 * 1024 * 1024
 log2e = 1.4426950408889634
 LANES = 128
 
@@ -64,23 +65,21 @@
 def head_sums(tile, head_dim):
     same = row_iota((LANES, LANES)) // head_dim == lane_iota((LANES, LANES)) // head_dim
     ones = jnp.where(same, 1.0, 0.0).astype(bf16)
-    high = tile.astype(bf16)
-    rest = (tile - high.astype(f32)).astype(bf16)
-    return nn(high, ones) + nn(rest, ones)
+    return nn(tile.astype(bf16), ones)
 
 
 def prep_tile(raw, cosine, sine, scale, head_dim):
     mean = head_sums(raw * raw, head_dim) * (1.0 / head_dim)
     inverse = lax.rsqrt(mean + epsilon)
     turned = raw * cosine + swap_halves(raw, head_dim // 2) * sine
-    return (turned * inverse * scale).astype(bf16), inverse
+    return (turned * inverse * scale).astype(bf16), inverse.astype(bf16)
 
 
 def prep_tile_back(grad, low, inverse, cosine, sine, scale, head_dim):
     unit = low.astype(f32) / scale
     grad_unit = grad * scale
     mean = head_sums(grad_unit * unit, head_dim) * (1.0 / head_dim)
-    grad_turned = inverse * (grad_unit - unit * mean)
+    grad_turned = inverse.astype(f32) * (grad_unit - unit * mean)
     return (grad_turned * cosine - swap_halves(grad_turned, head_dim // 2) * sine).astype(bf16)
 
 
@@ -112,8 +111,9 @@
     return pl.BlockSpec((size, width), lambda p, s: (0, p))
 
 
-def params():
-    return pltpu.CompilerParams(vmem_limit_bytes=VMEM_LIMIT)
+def params(small=False):
+    limit = SMALL_LIMIT if small else VMEM_LIMIT
+    return pltpu.CompilerParams(vmem_limit_bytes=limit)
 
 
 def cost(flops, moved, transcendentals=0):
@@ -127,9 +127,9 @@
     count = 2 + (slabs - 1) * 2 + (group - 1) * slabs * 2
     pieces = refs[:count]
     (
-        w_ref, a_ref, b_ref, cos_ref, sin_ref, scale_ref, wout_ref, ah_ref,
-        h_ref, own_ref, u_ref, q_ref, k_ref, v_ref, qi_ref, ki_ref, o_ref, of_ref, inv_ref,
-        msg_ref, start_ref, vt_ref, acc_ref, seg_ref,
+        wq_ref, w_ref, a_ref, b_ref, bq_ref, cos_ref, sin_ref, scale_ref, wout_ref, ah_ref,
+        hout_ref, ownout_ref, u_ref, q_ref, k_ref, v_ref, qi_ref, ki_ref, o_ref, inv_ref,
+        msg_ref, start_ref, vt_ref, all_ref, seg_ref, h_ref, own_ref, raw_ref,
     ) = refs[count:]
     inner, slab, core = place[0], place[1], place[2]
     block = group * chunk
@@ -182,28 +182,41 @@
             u_ref[sl, :] = nt(h_ref[sl, :], a_ref[...]).astype(bf16)
 
         by_rows(length, 512, low_rows)
-        acc_ref[...] = jnp.zeros_like(acc_ref)
-
+        for m in range(slabs):
+            low = u_ref[at_rows(m * group + inner, chunk), :rank]
+            own = slice(m * chunk, (m + 1) * chunk)
+            raw_ref[own, :] = nn(low, bq_ref[0])
+        raw_ref[...] += nn(own_ref[...], wq_ref[0])
+
+    last_block = lax.min(step, slabs - 1)
+    hout_ref[...] = h_ref[at_rows(last_block, block), :]
+    ownout_ref[...] = own_ref[at_rows(last_block, chunk), :]
+    here = pl.ds(pl.multiple_of(step * LANES, LANES), LANES)
     scale = scale_ref[...]
-    w_kv = jnp.concatenate([w_ref[1], w_ref[2]], axis=1)
+    w_kv = jnp.concatenate([w_ref[0], w_ref[1]], axis=1)
+    none = jnp.zeros((rank, LANES), bf16)
+    b_kv = jnp.concatenate(
+        [
+            jnp.zeros((rank, 2 * LANES), bf16),
+            jnp.concatenate([b_ref[0], none], axis=1),
+            jnp.concatenate([none, b_ref[1]], axis=1),
+        ],
+        axis=0,
+    )
 
     def keys_rows(sl):
-        both = nn(h_ref[sl, :], w_kv)
-        low = u_ref[sl, :]
-        raw = both[:, :LANES] + nn(low[:, rank : 2 * rank], b_ref[1])
+        both = nn(h_ref[sl, :], w_kv) + nn(u_ref[sl, :], b_kv)
         k_ref[sl, :], ki_ref[sl, :] = prep_tile(
-            raw, cos_ref[sl, :], sin_ref[sl, :], scale, head_dim
+            both[:, :LANES], cos_ref[sl, :], sin_ref[sl, :], scale, head_dim
         )
-        v_ref[sl, :] = (both[:, LANES:] + nn(low[:, 2 * rank :], b_ref[2])).astype(bf16)
+        v_ref[sl, :] = both[:, LANES:].astype(bf16)
 
     by_rows(length, 512, keys_rows)
-    queries = nn(own_ref[...], w_ref[0])
     for m in range(slabs):
         own = slice(m * chunk, (m + 1) * chunk)
         there = at_rows(m * group + inner, chunk)
-        raw = queries[own] + nn(u_ref[there, :rank], b_ref[0])
         q_ref[own, :], qi_ref[own, :] = prep_tile(
-            raw, cos_ref[there, :], sin_ref[there, :], scale, head_dim
+            raw_ref[own, here], cos_ref[there, :], sin_ref[there, :], scale, head_dim
         )
     vt_ref[...] = v_ref[...].T
     for m in range(slabs):
@@ -223,16 +236,16 @@
         gathered = gathered * inverse
         upper = row_iota((LANES, chunk)) < head_dim
         final = jnp.where(upper, gathered[:, :chunk], gathered[:, chunk:])
-        of_ref[0, :, own] = final
-        o_ref[own, :] = final.T.astype(bf16)
+        final = final.T.astype(bf16)
+        o_ref[own, :] = final
+        all_ref[own, here] = final
         inv_ref[0, m : m + 1, :] = inverse
-    low_o = o_ref[...]
-    acc_ref[:, :model] += nn(low_o, wout_ref[...])
-    acc_ref[:, model:] += nt(low_o, ah_ref[...])
 
     @pl.when(step == pl.num_programs(0) - 1)
     def _():
-        msg_ref[...] = acc_ref[...].astype(bf16)
+        low_o = all_ref[...]
+        msg_ref[:, :model] = nn(low_o, wout_ref[...]).astype(bf16)
+        msg_ref[:, model:] = nt(low_o, ah_ref[...]).astype(bf16)
 
 
 def run_attend(place, tokens, pieces, w, a, b, cos, sin, scale, wout, ah, group, head_dim):
@@ -246,26 +259,36 @@
     in_specs = [pl.BlockSpec((1, chunk, model), lambda p, s: (s[1], 0, 0))]
     in_specs += [whole_spec(piece.shape) for piece in pieces]
     in_specs += [
-        pl.BlockSpec((3, model, LANES), lambda p, s: (0, 0, p)),
+        whole_spec((1, model, width)),
+        pl.BlockSpec(
+            (pl.Element(2), pl.Element(model), pl.Element(LANES)),
+            lambda p, s: (1, 0, p * LANES),
+        ),
         whole_spec((3 * rank, model)),
-        pl.BlockSpec((3, rank, LANES), lambda p, s: (0, 0, p)),
+        pl.BlockSpec(
+            (pl.Element(2), pl.Element(rank), pl.Element(LANES)),
+            lambda p, s: (1, 0, p * LANES),
+        ),
+        whole_spec((1, rank, width)),
         whole_spec((length, LANES)),
         whole_spec((length, LANES)),
         col_spec(1),
-        pl.BlockSpec((LANES, model), lambda p, s: (p, 0)),
-        col_spec(LANES),
+        whole_spec((width, model)),
+        whole_spec((LANES, width)),
     ]
+    def step_rows(size):
+        return pl.BlockSpec((size, model), lambda p, s: (lax.min(p, slabs - 1), 0))
+
     out = [
-        ((length, model), bf16, whole_spec((length, model))),
-        ((rows, model), bf16, whole_spec((rows, model))),
+        ((length, model), bf16, step_rows(group * chunk)),
+        ((rows, model), bf16, step_rows(chunk)),
         ((length, 3 * rank), bf16, whole_spec((length, 3 * rank))),
         ((rows, width), bf16, col_spec(rows)),
         ((length, width), bf16, col_spec(length)),
         ((length, width), bf16, col_spec(length)),
-        ((rows, width), f32, col_spec(rows)),
-        ((length, width), f32, col_spec(length)),
         ((rows, width), bf16, col_spec(rows)),
-        ((pairs, LANES, rows), f32, pl.BlockSpec((1, LANES, rows), lambda p, s: (p, 0, 0))),
+        ((length, width), bf16, col_spec(length)),
+        ((rows, width), bf16, col_spec(rows)),
         (
             (pairs, slabs, 2 * chunk),
             f32,
@@ -283,15 +306,18 @@
             out_specs=[o[2] for o in out],
             scratch_shapes=[
                 pltpu.VMEM((LANES, length), bf16),
-                pltpu.VMEM((rows, model + LANES), f32),
+                pltpu.VMEM((rows, width), bf16),
                 pltpu.VMEM((chunk, chunk), f32),
+                pltpu.VMEM((length, model), bf16),
+                pltpu.VMEM((rows, model), bf16),
+                pltpu.VMEM((rows, width), f32),
             ],
         ),
         out_shape=[jax.ShapeDtypeStruct(o[0], o[1]) for o in out],
         compiler_params=params(),
         cost_estimate=cost(3e10, 4e7),
         name="attend",
-    )(place, tokens, *pieces, w, a, b, cos, sin, scale, wout, ah)
+    )(place, tokens, *pieces, w, w, a, b, b, cos, sin, scale, wout, ah)
 
 
 def feed_kernel(
@@ -315,7 +341,7 @@
             mid_ref[sl, :] = mixed
             low_ref[sl, :] = mixed.astype(bf16)
 
-        by_rows(rows, 64, mix)
+        by_rows(rows, 256, mix)
         u_ref[...] = nt(low_ref[...], a_ref[...]).astype(bf16)
         acc_ref[...] = jnp.zeros_like(acc_ref)
 
@@ -383,6 +409,23 @@
     return jnp.pad(tile, ((0, 0), (0, LANES - tile.shape[1])))
 
 
+def folded_rows(rows, groups):
+    return (rows + groups * 8 - 1) // (groups * 8) * 8
+
+
+def fold(tile, groups):
+    size = folded_rows(tile.shape[0], groups)
+    tile = jnp.pad(tile, ((0, size * groups - tile.shape[0]), (0, 0)))
+    return jnp.concatenate([tile[g * size : (g + 1) * size] for g in range(groups)], axis=1)
+
+
+def unfold(block):
+    groups = block.shape[1] // LANES
+    return jnp.concatenate(
+        [block[:, g * LANES : (g + 1) * LANES] for g in range(groups)], axis=0
+    ).astype(f32)
+
+
 def feed_back_kernel(
     dims, place, mine_ref, other_ref, mid_ref, g_own_ref, g_mine_ref, g_other_ref, bd_ref,
     rate_ref, a_ref, u_ref, gate_ref, up_ref, wgu_ref, bgu_ref, wd_ref, ad_ref, scales_ref,
@@ -427,7 +470,7 @@
             grad_unit = rate * grad_mixed
             gd_ref[sl, :] = (raw_inv * (grad_unit - unit * row_mean(grad_unit * unit))).astype(bf16)
 
-        by_rows(rows, 64, mix)
+        by_rows(rows, 256, mix)
         out_ref[...] = lo_ref[:, mine].reshape(slabs, chunk, half)
         ut_ref[...] = u_ref[...].T
         udt_ref[...] = hid_ref[...].T
@@ -490,7 +533,8 @@
                     tail = [
                         mine[:, t * LANES : (t + 1) * LANES] for t in range(padded // LANES)
                     ]
-                    table_ref[y, z, x] = jnp.concatenate([head] + tail, axis=0).astype(bf16)
+                    packed = jnp.concatenate([head] + tail, axis=0)
+                    table_ref[y, z, x] = fold(packed, half // LANES).astype(bf16)
 
 
 def run_feed_back(
@@ -510,7 +554,7 @@
         ((slabs, chunk, half), bf16),
         ((rows, model), f32),
         ((rows, model), bf16),
-        ((group, slabs, n_seq, table_rows, LANES), bf16),
+        ((group, slabs, n_seq, folded_rows(table_rows, half // LANES), half), bf16),
     ]
     return pl.pallas_call(
         functools.partial(
@@ -567,7 +611,7 @@
 
 def attend_back_kernel(
     dims, place, res_ref, gm_ref, go_ref, mid_ref, h_ref, am_ref, ao_ref, rate_ref, bo_ref,
-    wout_ref, ah_ref, start_ref, q_ref, k_ref, v_ref, o_ref, of_ref, inv_ref, qi_ref, ki_ref,
+    wout_ref, ah_ref, start_ref, q_ref, k_ref, v_ref, o_ref, inv_ref, qi_ref, ki_ref,
     cos_ref, sin_ref, scale_ref,
     gq_ref, gk_ref, gv_ref, gres_ref, gbo_ref, gah_ref,
     kt_ref, gqt_ref, ga_ref, guo_ref, guot_ref, uo_ref,
@@ -598,7 +642,7 @@
             grad_unit = rate * grad_mixed
             ga_ref[sl, :] = (raw_inv * (grad_unit - unit * row_mean(grad_unit * unit))).astype(bf16)
 
-        by_rows(rows, 64, mix)
+        by_rows(rows, 256, mix)
         gbo_ref[...] = nn(uo_ref[...].T, ga_ref[...])
         low_g = nt(ga_ref[...], bo_ref[...]).astype(bf16)
         guo_ref[...] = low_g
@@ -614,7 +658,7 @@
         pairs_q.append(spread_pair(q_ref[own, :], head_dim))
         grad = grad_o[own]
         pairs_g.append(spread_pair(grad, head_dim))
-        products = grad.astype(f32).T * of_ref[0, :, own]
+        products = (grad.astype(f32) * o_ref[own, :].astype(f32)).T
         deltas.append(
             jnp.concatenate(
                 [
@@ -662,7 +706,7 @@
 
 
 def run_attend_back(
-    place, res, gm, go, mid, h_own, am, ao, rates, bo, wout, ah, start, q, k, v, o, of, inv,
+    place, res, gm, go, mid, h_own, am, ao, rates, bo, wout, ah, start, q, k, v, o, inv,
     qi, ki, cos, sin, scale, slabs, group, head_dim,
 ):
     rows, model = h_own.shape
@@ -702,7 +746,6 @@
                 col_spec(length),
                 col_spec(length),
                 col_spec(rows),
-                pl.BlockSpec((1, LANES, rows), lambda p, s: (p, 0, 0)),
                 pl.BlockSpec((1, slabs, 2 * chunk), lambda p, s: (p, 0, 0)),
                 col_spec(rows),
                 col_spec(length),
@@ -725,7 +768,7 @@
         cost_estimate=cost(3e10, 4e7),
         name="attend_back",
     )(
-        place, res, gm, go, mid, h_own, am, ao, rates, bo, wout, ah, start, q, k, v, o, of,
+        place, res, gm, go, mid, h_own, am, ao, rates, bo, wout, ah, start, q, k, v, o,
         inv, qi, ki, cos, sin, scale,
     )
 
@@ -779,7 +822,7 @@
             jax.ShapeDtypeStruct((group - 1, rows, half), f32),
             jax.ShapeDtypeStruct((group - 1, rows, half), bf16),
         ],
-        compiler_params=params(),
+        compiler_params=params(True),
         cost_estimate=cost(7e9, 1e7),
         name="others",
     )(place, gk.reshape(shaped), gv.reshape(shaped), w, a, b)
@@ -836,7 +879,7 @@
             scratch_shapes=[pltpu.VMEM((rows, model), f32)],
         ),
         out_shape=[jax.ShapeDtypeStruct(o[0], o[1]) for o in out],
-        compiler_params=params(),
+        compiler_params=params(True),
         cost_estimate=cost(7e9, 1e7),
         name="own",
     )(place, gq, gk.reshape(shaped), gv.reshape(shaped), w, a, b, res)
@@ -887,7 +930,6 @@
     source = inside // each * head_dim + owner * each + inside % each
     moved = jnp.where(lane_iota((width, width)) == source, 1.0, 0.0).astype(bf16)
     turned = nt(moved, head_rows)
-    gap = table_ref.shape[3] - 4 * rank - units
     for y in range(group):
         for z in range(slabs):
             for x in range(n_seq):
@@ -896,9 +938,8 @@
                     pad_lanes(model_rows[:, d * cols : (d + 1) * cols]),
                     pad_lanes(turned[d * units : (d + 1) * units]),
                 ]
-                if gap:
-                    parts.append(jnp.zeros((gap, LANES), f32))
-                table_ref[y, z, x] = jnp.concatenate(parts, axis=0).astype(bf16)
+                packed = jnp.concatenate(parts, axis=0)
+                table_ref[y, z, x] = fold(packed, table_ref.shape[4] // LANES).astype(bf16)
 
 
 def run_grads(place, gq, gk, gv, b, u, h, h_own, gbo, gah, slabs, group, n_seq, head_dim):
@@ -909,8 +950,8 @@
     heads = width // head_dim
     owners = n_seq * slabs * group
     units = heads * (head_dim // owners)
-    table_rows = (4 * rank + units + 7) // 8 * 8
-    shape = (group, slabs, n_seq, table_rows, LANES)
+    half = model // 2
+    shape = (group, slabs, n_seq, folded_rows(4 * rank + units, half // LANES), half)
     operands = (gq, gk, gv, b, u, h, h_own, gbo, gah)
     return pl.pallas_call(
         functools.partial(grads_kernel, (slabs, chunk, group, n_seq, rank, model, head_dim)),
@@ -922,7 +963,7 @@
             scratch_shapes=[pltpu.VMEM((rows, 3 * rank), bf16)],
         ),
         out_shape=jax.ShapeDtypeStruct(shape, bf16),
-        compiler_params=params(),
+        compiler_params=params(True),
         cost_estimate=cost(1e10, 1e7),
         name="grads",
     )(place, *operands)
@@ -930,137 +971,102 @@
 
 def join_kernel(slabs, place, *refs):
     out_ref = refs[-1]
-    half = refs[0].shape[-1]
+    chunk, half = out_ref.shape[1], refs[0].shape[-1]
     core, slab = place[2], place[1]
     for shift in range(slabs):
         source = lax.rem(slab - shift + slabs, slabs)
         for which, ref in ((core, refs[shift]), (1 - core, refs[slabs + shift])):
             out_ref[source, :, pl.ds(pl.multiple_of(which * half, half), half)] = ref[
-                ...
+                :chunk, :
             ].astype(out_ref.dtype)
 
 
-def run_join(place, mine, other, dtype):
+def run_join(place, mine, other, chunk, dtype):
     slabs = len(mine)
-    chunk, half = mine[0].shape
+    half = mine[0].shape[1]
     return pl.pallas_call(
         functools.partial(join_kernel, slabs),
         grid_spec=pltpu.PrefetchScalarGridSpec(
             num_scalar_prefetch=1,
             grid=(1,),
-            in_specs=[whole_spec((chunk, half))] * (2 * slabs),
+            in_specs=[whole_spec(piece.shape) for piece in (*mine, *other)],
             out_specs=whole_spec((slabs, chunk, 2 * half)),
         ),
         out_shape=jax.ShapeDtypeStruct((slabs, chunk, 2 * half), dtype),
-        compiler_params=params(),
+        compiler_params=params(True),
         cost_estimate=cost(1e6, 8e6),
         name="join",
     )(place, *mine, *other)
 
 
-def unpack_early_kernel(dims, place, index, mine_ref, other_ref, am_ref, bm_ref, ad_ref, bd_ref):
-    n_seq, slabs, rank, cols, each, hidden_rows, tiles = dims
+def tables_of(dims, place, index, refs):
+    n_seq, slabs, chunk, size = dims
+    home, home_other = refs[:slabs], refs[slabs : 2 * slabs]
+    far, far_other = refs[2 * slabs : 2 * slabs + n_seq - 1], refs[2 * slabs + n_seq - 1 :]
+    for r in range(slabs):
+        at = pl.ds(pl.multiple_of(chunk + place[3] * size, 8), size)
+        yield index[0, r], unfold(home[r][at, :]), unfold(home_other[r][at, :])
+    for s in range(1, n_seq):
+        for r in range(slabs):
+            yield index[s, r], unfold(far[s - 1][r]), unfold(far_other[s - 1][r])
+
+
+def unpack_early_kernel(dims, where, place, index, *refs):
+    rank, cols, each, hidden_rows, tiles = dims
+    am_ref, bm_ref, ad_ref, bd_ref = refs[-4:]
     core = place[2]
-    for s in range(n_seq):
-        for r in range(slabs):
-            adapter = index[s, r]
-            block = mine_ref[s, r].astype(f32)
-            both = block[: 2 * rank] + other_ref[s, r, : 2 * rank].astype(f32)
-            left = both[:, : cols // 2]
-            right = both[:, cols // 2 : cols]
-            am_ref[adapter] = jnp.where(core == 0, left, right).reshape(2, rank, cols // 2)
-            bm_ref[adapter] = block[2 * rank : 3 * rank, :cols]
-            base = 3 * rank
-            wide = jnp.concatenate(
-                [block[base + t * each : base + (t + 1) * each] for t in range(tiles)], axis=1
-            )
+    for adapter, block, other in tables_of(where, place, index, refs[:-4]):
+        both = block[: 2 * rank] + other[: 2 * rank]
+        am = jnp.where(core == 0, both[:, : cols // 2], both[:, cols // 2 : cols])
+        am_ref[adapter] = am.reshape(2, rank, cols // 2)
+        bm_ref[adapter] = block[2 * rank : 3 * rank, :cols]
+        base = 3 * rank
+        wide = jnp.concatenate(
+            [block[base + t * each : base + (t + 1) * each] for t in range(tiles)], axis=1
+        )
+        for k in range(rank):
+            ad_ref[adapter, k] = wide[:, k * hidden_rows : (k + 1) * hidden_rows]
+        for j in range(2):
             for k in range(rank):
-                ad_ref[adapter, k] = wide[:, k * hidden_rows : (k + 1) * hidden_rows]
-            for j in range(2):
-                for k in range(rank):
-                    at = ((j + 1) * rank + k) * hidden_rows
-                    bd_ref[adapter, j, k] = wide[:, at : at + hidden_rows]
-
-
-def run_unpack_early(place, index, mine, other, adapters, rank, cols, each, hidden_rows):
-    n_seq, slabs = mine.shape[:2]
-    tiles = (mine.shape[2] - 3 * rank) // each
-    shapes = [
-        (adapters, 2, rank, cols // 2),
-        (adapters, rank, cols),
-        (adapters, rank, each, hidden_rows),
-        (adapters, 2, rank, each, hidden_rows),
-    ]
+                at = ((j + 1) * rank + k) * hidden_rows
+                bd_ref[adapter, j, k] = wide[:, at : at + hidden_rows]
+
+
+def unpack_late_kernel(dims, where, place, index, *refs):
+    rank, cols, heads, each = dims
+    am_gu_ref, bm_down_ref, am_ref, bm_ref, ah_ref, bh_ref = refs[-6:]
+    core = place[2]
+    for adapter, block, other in tables_of(where, place, index, refs[:-6]):
+        both = block[: 3 * rank] + other[: 3 * rank]
+        am = jnp.where(core == 0, both[:, : cols // 2], both[:, cols // 2 : cols])
+        am_ref[adapter, 0:3] = am.reshape(3, rank, cols // 2)
+        am_ref[adapter, 3:5] = am_gu_ref[adapter]
+        bm_ref[adapter, 0] = block[3 * rank : 4 * rank, :cols]
+        bm_ref[adapter, 1] = bm_down_ref[adapter]
+        units = block[4 * rank : 4 * rank + heads * each]
+        for n in range(heads):
+            piece = units[n * each : (n + 1) * each]
+            ah_ref[adapter, n] = piece[:, :rank]
+            for j in range(3):
+                bh_ref[adapter, j, n] = piece[:, (j + 1) * rank : (j + 2) * rank]
+
+
+def run_unpack(kernel, dims, where, place, index, tables, extra, shapes, name):
+    home, home_other, far, far_other = tables
+    operands = [*home, *home_other, *far, *far_other, *extra]
     return pl.pallas_call(
-        functools.partial(
-            unpack_early_kernel, (n_seq, slabs, rank, cols, each, hidden_rows, tiles)
-        ),
+        functools.partial(kernel, dims, where),
         grid_spec=pltpu.PrefetchScalarGridSpec(
             num_scalar_prefetch=2,
             grid=(1,),
-            in_specs=[whole_spec(mine.shape)] * 2,
-            out_specs=[whole_spec(s) for s in shapes],
+            in_specs=[whole_spec(operand.shape) for operand in operands],
+            out_specs=[whole_spec(shape) for shape in shapes],
         ),
-        out_shape=[jax.ShapeDtypeStruct(s, f32) for s in shapes],
-        compiler_params=params(),
+        out_shape=[jax.ShapeDtypeStruct(shape, f32) for shape in shapes],
+        compiler_params=params(True),
         cost_estimate=cost(1e6, 8e6),
-        name="unpack_early",
-    )(place, index, mine, other)
-
-
-def unpack_late_kernel(
-    dims, place, index, mine_ref, other_ref, am_gu_ref, bm_down_ref, am_ref, bm_ref, ah_ref,
-    bh_ref,
-):
-    n_seq, slabs, rank, cols, heads, each = dims
-    core = place[2]
-    for s in range(n_seq):
-        for r in range(slabs):
-            adapter = index[s, r]
-            block = mine_ref[s, r].astype(f32)
-            both = block[: 3 * rank] + other_ref[s, r, : 3 * rank].astype(f32)
-            left = both[:, : cols // 2]
-            right = both[:, cols // 2 : cols]
-            am_ref[adapter, 0:3] = jnp.where(core == 0, left, right).reshape(3, rank, cols // 2)
-            am_ref[adapter, 3:5] = am_gu_ref[adapter]
-            bm_ref[adapter, 0] = block[3 * rank : 4 * rank, :cols]
-            bm_ref[adapter, 1] = bm_down_ref[adapter]
-            units = block[4 * rank : 4 * rank + heads * each]
-            for n in range(heads):
-                piece = units[n * each : (n + 1) * each]
-                ah_ref[adapter, n] = piece[:, :rank]
-                for j in range(3):
-                    bh_ref[adapter, j, n] = piece[:, (j + 1) * rank : (j + 2) * rank]
-
-
-def run_unpack_late(place, index, mine, other, am_gu, bm_down, heads, each):
-    n_seq, slabs = mine.shape[:2]
-    adapters, _, rank, narrow = am_gu.shape
-    cols = bm_down.shape[2]
-    shapes = [
-        (adapters, 5, rank, narrow),
-        (adapters, 2, rank, cols),
-        (adapters, heads, each, rank),
-        (adapters, 3, heads, each, rank),
-    ]
-    return pl.pallas_call(
-        functools.partial(unpack_late_kernel, (n_seq, slabs, rank, cols, heads, each)),
-        grid_spec=pltpu.PrefetchScalarGridSpec(
-            num_scalar_prefetch=2,
-            grid=(1,),
-            in_specs=[
-                whole_spec(mine.shape),
-                whole_spec(other.shape),
-                whole_spec(am_gu.shape),
-                whole_spec(bm_down.shape),
-            ],
-            out_specs=[whole_spec(s) for s in shapes],
-        ),
-        out_shape=[jax.ShapeDtypeStruct(s, f32) for s in shapes],
-        compiler_params=params(),
-        cost_estimate=cost(1e6, 8e6),
-        name="unpack_late",
-    )(place, index, mine, other, am_gu, bm_down)
+        name=name,
+    )(place, index, *operands)
 
 
 def pick(array, index):
@@ -1130,11 +1136,12 @@
     ah_pad = jnp.pad(ah, ((0, LANES - rank), (0, 0)))
     ad_pad = jnp.pad(ad, ((0, LANES - rank), (0, 0)))
 
-    frequency = 10000.0 ** (-jnp.arange(head_dim // 2, dtype=f32) / (head_dim // 2))
+    spot = (jnp.arange(LANES, dtype=i32) % (head_dim // 2)).astype(f32)
+    frequency = 10000.0 ** (-spot / (head_dim // 2))
     turn = jnp.arange(length, dtype=i32).astype(f32)[:, None] * frequency[None, :]
-    cos = jnp.tile(jnp.cos(turn), (1, 2 * LANES // head_dim))
-    sine = jnp.sin(turn)
-    sin = jnp.tile(jnp.concatenate([-sine, sine], axis=1), (1, LANES // head_dim))
+    cos = jnp.cos(turn)
+    lower = jnp.arange(LANES) % head_dim < head_dim // 2
+    sin = jnp.sin(turn) * jnp.where(lower, -1.0, 1.0)[None, :]
     scale = qk_scale[None, :]
 
     own_piece = token_piece(slab)
@@ -1144,26 +1151,27 @@
     index = [adapter_index]
     for shift in range(1, n_seq):
         index.append(to_seq(adapter_index, shift))
-    got[2], cos, sin, am_qkv, am_gu, bh, ah_pad, ad_pad, ad, ah, bd, bm = tie(
-        (got[2], cos, sin, am_qkv, am_gu, bh, ah_pad, ad_pad, ad, ah, bd, bm)
-    )
+    received = {}
+    for turn in range(1, group):
+        for shift in range(slabs):
+            received[turn, shift] = within_slab(got[shift], turn)
+    got, g_send, cos, sin, am_qkv, am_gu, bh, ah_pad, ad_pad, ad, ah, bd, bm, index = tie(
+        (
+            got,
+            [half_piece(cotangent, (slab + shift) % slabs, core) for shift in range(1, slabs)],
+            cos, sin, am_qkv, am_gu, bh, ah_pad, ad_pad, ad, ah, bd, bm, index,
+        )
+    )
+    g_mine = [to_slab(g_send[shift - 1], shift) for shift in range(1, slabs)]
     pieces = [own_piece]
     for shift in range(1, slabs):
         pieces += [got[shift], other_core(got[shift])]
     for turn in range(1, group):
         for shift in range(slabs):
-            peer = within_slab(got[shift], turn)
+            peer = received[turn, shift]
             pieces += [peer, other_core(peer)]
-    got, g_send = tie(
-        (
-            got,
-            [half_piece(cotangent, (slab + shift) % slabs, core) for shift in range(1, slabs)],
-        )
-    )
-    g_mine = [to_slab(g_send[shift - 1], shift) for shift in range(1, slabs)]
-    pieces, index = tie((pieces, index))
-
-    h_full, h_own, u, q, k, v, qi, ki, o, of, inv, attn_msg, start = run_attend(
+
+    h_full, h_own, u, q, k, v, qi, ki, o, inv, attn_msg, start = run_attend(
         place, tokens, pieces, w_attn_in, am_qkv, bh, cos, sin, scale, w_attn_out,
         ah_pad, group, head_dim,
     )
@@ -1185,10 +1193,6 @@
     order = (slab - jnp.arange(slabs, dtype=i32)) % slabs
     index = jnp.stack(index)[:, order]
 
-    out_mine = [pick(out_half, slab)] + [
-        to_slab(pick(out_half, (slab + shift) % slabs), shift) for shift in range(1, slabs)
-    ]
-
     def sum_inner(table):
         return pick(table, inner), [
             within_slab(pick(table, (inner + turn) % group), turn) for turn in range(1, group)
@@ -1205,36 +1209,38 @@
             to_slab(pick(total, (slab + shift) % slabs), shift) for shift in range(1, slabs)
         ]
 
-    def over_seqs(got):
-        got = jnp.stack(got)
-        result = [lax.dynamic_index_in_dim(got, seq_place, 1, keepdims=False)]
+    def pack(rows_part, table):
+        return jnp.concatenate([rows_part, table.reshape(slabs, -1, half)], axis=1)
+
+    def over_seqs(home):
+        result = []
         for shift in range(1, n_seq):
-            sent = lax.dynamic_index_in_dim(
-                got, (seq_place + shift) % n_seq, 1, keepdims=False
-            )
-            result.append(to_seq(sent, shift))
+            at = chunk + (seq_place + shift) % n_seq * size
+            sent = [lax.dynamic_slice_in_dim(piece, at, size, 0) for piece in home]
+            result.append(to_seq(jnp.stack(sent), shift))
         return result
 
     early_own, early_got = sum_inner(early)
+    size = early.shape[3]
     gq, gk, gv, h_res, gbo, gah = run_attend_back(
         place, mid_res, mid_msg, mid_other, mid, h_own, attn_msg, attn_other, mix_rates, bm[0],
-        w_attn_out, ah, start, q, k, v, o, of, inv, qi, ki, cos, sin, scale, slabs, group,
+        w_attn_out, ah, start, q, k, v, o, inv, qi, ki, cos, sin, scale, slabs, group,
         head_dim,
     )
-    early_got, out_mine, gk, gv = tie((early_got, out_mine, gk, gv))
-    early = over_slabs(add_inner(early_own, early_got))
-    out_other = [other_core(piece) for piece in out_mine]
+    early_got, gk, gv = tie((early_got, gk, gv))
+    home = over_slabs(pack(out_half, add_inner(early_own, early_got)))
     keep, send = run_others(place, gk, gv, w_attn_in, am_qkv, bh, slabs, group)
     others = (keep + other_core(send).astype(f32)).astype(bf16)
-    early, out_other, others, gq = tie((early, out_other, others, gq))
+    home, others, gq = tie((home, others, gq))
     others_got = [within_slab(others[turn - 1], turn) for turn in range(1, group)]
-    early = over_seqs(early)
+    home_other = [other_core(piece) for piece in home]
+    far = over_seqs(home)
     late = run_grads(
         place, gq, gk, gv, bh, u, h_full, h_own, gbo, gah, slabs, group, n_seq, head_dim
     )
-    early, late = tie((early, late))
+    far, late = tie((far, late))
     late_own, late_got = sum_inner(late)
-    early_other = other_core(jnp.stack(early)[:, :, : 2 * rank])
+    far_other = [other_core(piece) for piece in far]
     late_own, gq = tie((late_own, gq))
     own_keep, own_send = run_own(
         place, gq, gk, gv, w_attn_in, am_qkv, bh, h_res, slabs, group
@@ -1245,18 +1251,48 @@
     for got_part in others_got:
         total = total + got_part.astype(f32)
     total = total.astype(bf16).reshape(slabs, chunk, half)
+    total = pack(total, add_inner(late_own, late_got))
+    total, home, far = tie((total, home, far))
     result = over_slabs(total)
-    late = over_slabs(add_inner(late_own, late_got))
-    layer_out = run_join(place, out_mine, out_other, bf16)
-    grad_am_gu, grad_bm_down, grad_ad, grad_bd = run_unpack_early(
-        place, index, jnp.stack(early), early_other, adapters, rank, model // owners,
-        row_width // owners, local_hidden // row_width,
-    )
-    late = jnp.stack(over_seqs(late))
-    input_grad = run_join(place, result, [other_core(piece) for piece in result], f32)
-    grad_am, grad_bm, grad_ah, grad_bh = run_unpack_late(
-        place, index, late, other_core(late[:, :, : 3 * rank]), grad_am_gu, grad_bm_down,
-        local_heads, head_dim // owners,
+    layer_out = run_join(place, home, home_other, chunk, bf16)
+    cols = model // owners
+    each = row_width // owners
+    hidden_rows = local_hidden // row_width
+    grad_am_gu, grad_bm_down, grad_ad, grad_bd = run_unpack(
+        unpack_early_kernel,
+        (rank, cols, each, hidden_rows, (3 * rank * hidden_rows + LANES - 1) // LANES),
+        (n_seq, slabs, chunk, size),
+        place, index, (home, home_other, far, far_other), [],
+        [
+            (adapters, 2, rank, cols // 2),
+            (adapters, rank, cols),
+            (adapters, rank, each, hidden_rows),
+            (adapters, 2, rank, each, hidden_rows),
+        ],
+        "unpack_early",
+    )
+    size = late.shape[3]
+    result, layer_out, grad_am_gu, grad_bm_down = tie(
+        (result, layer_out, grad_am_gu, grad_bm_down)
+    )
+    result_other = [other_core(piece) for piece in result]
+    far = over_seqs(result)
+    input_grad = run_join(place, result, result_other, chunk, f32)
+    far, input_grad = tie((far, input_grad))
+    each = head_dim // owners
+    grad_am, grad_bm, grad_ah, grad_bh = run_unpack(
+        unpack_late_kernel,
+        (rank, cols, local_heads, each),
+        (n_seq, slabs, chunk, size),
+        place, index, (result, result_other, far, [other_core(piece) for piece in far]),
+        [grad_am_gu, grad_bm_down],
+        [
+            (adapters, 5, rank, cols // 2),
+            (adapters, 2, rank, cols),
+            (adapters, local_heads, each, rank),
+            (adapters, 3, local_heads, each, rank),
+        ],
+        "unpack_late",
     )
     return (
         layer_out,

time: 269 us -> 270 us (level)
  the two profiles are of different devices: /device:TPU:0 before, /device:TPU:11 now
where the time goes in v4:
time: 270 us; the launch traced here: 266 us
  Pallas kernels  132 us (49%)
  waiting for transfers between devices  52.5 us (19%)
  starting transfers between devices  37.9 us (14%)
  local copies, waits for them, and re-layouts  31.2 us (12%)
  other arithmetic  9.04 us (3%)
  between operations  3.79 us (1%)
    pallas_call x1, Pallas kernels, run_attend_back(): pl.pallas_call(functools.partial(attend_back_kernel, (slabs, chunk, group...  34 us
    ppermute x12, waiting for transfers between devices, to_slab(): return lax.ppermute(array, 'ctx', pairs)  32.3 us
    pallas_call x1, Pallas kernels, run_feed_back(): pl.pallas_call(functools.partial(feed_back_kernel, (slabs, chunk, group,...  29.1 us
    pallas_call x1, Pallas kernels, run_attend(): pl.pallas_call(functools.partial(attend_kernel, (slabs, chunk, group, hea...  26.3 us
    pallas_call x1, Pallas kernels, run_feed(): pl.pallas_call(functools.partial(feed_kernel, (rank, model)), grid=(hidde...  21.6 us
    ppermute x23, starting transfers between devices, other_core(): return lax.ppermute(array, 'wt', [(0, 1), (1, 0)])  17.5 us
    unnamed x91, local copies, waits for them, and re-layouts  15.2 us
    ppermute x12, starting transfers between devices, to_slab(): return lax.ppermute(array, 'ctx', pairs)  13.8 us
  transfers between devices with their start and end apart: 45, of which 19 were waited for; matrix products, arithmetic and copies ran while one was open for 9% of the time, Pallas kernels for 28%

profile of v4, /device:TPU:11, one launch (start us, length us, event | category | flops | bytes accessed | tf_op | source)
XLA Modules:
  0.0 266.1 jit_solution(1100008480145601945)
XLA Ops:
  16.0 3.0 %fusion = (f32[1024,128]{1,0:T(8,128)}, f32[1024,128]{1,0:T(8,128)}) fusion(f32[128]{0:T(128)S(1)} %get-tuple-element.221, f32[128]{0:T(128)S(1)} %get-tuple-element.222, f32[1024]{0:T(1024)S(1)} %iota_convert_fusion), kind=kLoop, calls=%fused_computation.14 | loop fusion | flops 262144 | bytes 1053696 | tf_op jit(solution)/shard_map/mul | solution.py:1144
  24.5 2.1 collective-permute-start.7
  29.8 2.5 collective-permute-done.12.refs_10_
  32.3 2.1 collective-permute-start.13
  36.0 2.1 collective-permute-start.15
  42.2 3.1 %collective-permute-start.5 = (bf16[128,640]{1,0:T(8,128)(2,1)S(1)}, bf16[128,640]{1,0:T(8,128)(2,1)S(1)}, u32[]{:S(2)}, u32[]{:S(2)}) collective-permute-start(bf16[128,640]{1,0:T(8,128)(2,1)S(1)} %get-tuple-element.103), channel_id=1, source_target_pairs={{0,8},{2,10},{4,12},{6,14},{8,0},{10,2},{12,4},{14,6},{1,9},{3,11}... | collective-permute-start | bytes 491528 | tf_op jit(solution)/shard_map/ppermute | solution.py:1104
  46.8 26.3 %attend.1 = (bf16[1024,1280]{1,0:T(8,128)(2,1)}, bf16[512,1280]{1,0:T(8,128)(2,1)}, bf16[1024,48]{1,0:T(8,128)(2,1)}, bf16[512,640]{1,0:T(8,128)(2,1)}, bf16[102...) custom-call(s32[4]{0:T(128)} %pad_add_fusion.1.place, ...), custom_call_target="tpu_custom_call" | custom-call | flops 30000001024 | bytes 40000000 | tf_op jit(solution)/shard_map/attend/pallas_call | solution.py:300
  74.7 2.7 %collective-permute-done.19.g_other_ref = bf16[3,128,640]{2,1,0:T(8,128)(2,1)S(1)} collective-permute-done((bf16[3,128,640]{2,1,0:T(8,128)(2,1)S(1)}, bf16[3,128,640]{2,1,0:T(8,128)(2,1)S(1)}, u32[]{:S(2)}, u32[]{:S(2)}) %collective-permute-start.19) | collective-permute-done | bytes 491552 | tf_op jit(solution)/shard_map/ppermute | solution.py:1114
  78.5 21.6 %feed.1 = (f32[512,1280]{1,0:T(8,128)}, bf16[512,32]{1,0:T(8,128)(2,1)}, bf16[512,2560]{1,0:T(8,128)(2,1)}, bf16[512,2560]{1,0:T(8,128)(2,1)}, bf16[512,1408]{1,0:T(8,128)(2,1)}) custom-call(bf16[512,1408]{1,0:T(8,128)(2,1)} %get-tuple-element.114.mine_ref.am_ref, bf16[512,1408]{1,0:T(8,128)(2,1)} %copy-done.25, ...), custom_call_target="tpu_custom_call" | custom-call | flops 24000000000 | bytes 30000000 | tf_op jit(solution)/shard_map/feed/pallas_call | solution.py:375
  100.5 3.1 %collective-permute-done.20.other_ref = bf16[512,1408]{1,0:T(8,128)(2,1)S(1)} collective-permute-done((bf16[512,1408]{1,0:T(8,128)(2,1)}, bf16[512,1408]{1,0:T(8,128)(2,1)S(1)}, u32[]{:S(2)}, u32[]{:S(2)}) %collective-permute-start.20) | collective-permute-done | bytes 1441824 | tf_op jit(solution)/shard_map/ppermute | solution.py:1114
  104.7 29.1 %feed_back.1 = (bf16[4,128,640]{2,1,0:T(8,128)(2,1)}, f32[512,1280]{1,0:T(8,128)}, bf16[512,1280]{1,0:T(8,128)(2,1)}, bf16[2,4,2,24,640]{4,3,2,1,0:T(8,128)(2,1)}) custom-call(s32[4]{0:T(128)} %pad_add_fusion.1.place, bf16[512,1408]{1,0:T(8,128)(2,1)} %get-tuple-element.124.mine_ref, bf16[512,1408]{1,0:T(8,128)(2,1)} %copy-done.26, ...), custom_call_target="tpu_custom_call" | custom-call | flops 30000001024 | bytes 40000000 | tf_op jit(solution)/shard_map/feed_back/pallas_call | solution.py:559
  138.2 34.0 %attend_back.1 = (bf16[512,640]{1,0:T(8,128)(2,1)}, bf16[1024,640]{1,0:T(8,128)(2,1)}, bf16[1024,640]{1,0:T(8,128)(2,1)}, f32[512,1280]{1,0:T(8,128)}, f32[16,1280]{1,0:T(8,128)}, /*index=5*/f32[16,640]{1,0:T(8,128)}) custom-call(s32[4]{0:T(128)} %pad_add_fusion.1.place, f32[512,1280]{1,0:T(8,128)} %get-tuple-element.133.res_ref, ...), custom_call_target="tpu_custom_call" | custom-call | flops 30000001024 | bytes 40000000 | tf_op jit(solution)/shard_map/attend_back/pallas_call | solution.py:727
  172.3 2.4 copy-done.5
  177.3 3.9 %others.1 = (f32[1,512,640]{2,1,0:T(8,128)S(1)}, bf16[1,512,640]{2,1,0:T(8,128)(2,1)S(1)}) custom-call(s32[4]{0:T(128)S(1)} %copy-done.4, bf16[4,2,128,640]{3,2,1,0:T(8,128)(2,1)S(1)} %bitcast.106, bf16[4,2,128,640]{3,2,1,0:T(8,128)(2,1)S(1)} %bitcast.108, bf16[3,1280,640]{2,1,0:T(8,128)(2,1)S(1)} %copy-done.5, bf16[48,1280]{1,0:T(8,128)(2,1)S(1)} %bitcast.100, ...), custom_call_target="tpu_custom_call" | custom-call | flops 7000000000 | bytes 10000000 | tf_op jit(solution)/shard_map/others/pallas_call | solution.py:806
  189.0 2.2 collective-permute-done.23.refs_1_
  191.3 14.0 %collective-permute-done.24.refs_2_ = bf16[176,640]{1,0:T(8,128)(2,1)S(1)} collective-permute-done((bf16[176,640]{1,0:T(8,128)(2,1)S(1)}, bf16[176,640]{1,0:T(8,128)(2,1)S(1)}, u32[]{:S(2)}, u32[]{:S(2)}) %collective-permute-start.24) | collective-permute-done | bytes 225312 | tf_op jit(solution)/shard_map/ppermute | solution.py:1104
  213.8 3.4 %grads.1 = bf16[2,4,2,24,640]{4,3,2,1,0:T(8,128)(2,1)S(1)} custom-call(s32[4]{0:T(128)S(1)} %copy-done.4, bf16[512,640]{1,0:T(8,128)(2,1)S(1)} %copy-done.13, bf16[1024,640]{1,0:T(8,128)(2,1)S(1)} %copy-done.7, bf16[1024,640]{1,0:T(8,128)(2,1)S(1)} %copy-done.9, bf16[3,16,640]{2,1,0:T(8,128)(2,1)S(1)} %copy-done.3, bf16[1024,48]{1,0:T(8,128)(2,1)S(1)} %copy-done.15, ...), custom_call_target="tpu_custom_call" | custom-call | flops 10000000000 | bytes 10000000 | tf_op jit(solution)/shard_map/grads/pallas_call | solution.py:956
  218.6 5.9 %own.1 = (f32[512,640]{1,0:T(8,128)S(1)}, bf16[512,640]{1,0:T(8,128)(2,1)S(1)}) custom-call(s32[4]{0:T(128)S(1)} %copy-done.4, bf16[512,640]{1,0:T(8,128)(2,1)S(1)} %copy-done.13, bf16[4,2,128,640]{3,2,1,0:T(8,128)(2,1)S(1)} %bitcast.107, bf16[4,2,128,640]{3,2,1,0:T(8,128)(2,1)S(1)} %bitcast.109, bf16[3,1280,640]{2,1,0:T(8,128)(2,1)S(1)} %bitcast.105, ...), custom_call_target="tpu_custom_call" | custom-call | flops 7000000000 | bytes 10000000 | tf_op jit(solution)/shard_map/own/pallas_call | solution.py:864
  224.4 3.6 %collective-permute-done.28 = bf16[4,2,24,640]{3,2,1,0:T(8,128)(2,1)S(1)} collective-permute-done((bf16[4,2,24,640]{3,2,1,0:T(8,128)(2,1)S(1)}, bf16[4,2,24,640]{3,2,1,0:T(8,128)(2,1)S(1)}, u32[]{:S(2)}, u32[]{:S(2)}) %collective-permute-start.28) | collective-permute-done | bytes 245792 | tf_op jit(solution)/shard_map/ppermute | solution.py:1108
  228.1 2.4 collective-permute-start.29
  239.5 2.0 unpack_early.1
  241.5 11.9 %collective-permute-done.32.refs_2_ = bf16[176,640]{1,0:T(8,128)(2,1)S(1)} collective-permute-done((bf16[176,640]{1,0:T(8,128)(2,1)S(1)}, bf16[176,640]{1,0:T(8,128)(2,1)S(1)}, u32[]{:S(2)}, u32[]{:S(2)}) %collective-permute-start.32) | collective-permute-done | bytes 225312 | tf_op jit(solution)/shard_map/ppermute | solution.py:1104
  253.4 2.7 %collective-permute-done.33.refs_3_ = bf16[176,640]{1,0:T(8,128)(2,1)S(1)} collective-permute-done((bf16[176,640]{1,0:T(8,128)(2,1)S(1)}, bf16[176,640]{1,0:T(8,128)(2,1)S(1)}, u32[]{:S(2)}, u32[]{:S(2)}) %collective-permute-start.33) | collective-permute-done | bytes 225312 | tf_op jit(solution)/shard_map/ppermute | solution.py:1104
  258.7 2.2 join.3
  (234 shorter events, 73.9 us)
Async XLA Ops:
  2.9 21.6 %collective-permute-start = (bf16[136,640]{1,0:T(8,128)(2,1)S(1)}, bf16[136,640]{1,0:T(8,128)(2,1)S(1)}, u32[]{:S(2)}, u32[]{:S(2)}) collective-permute-start(bf16[136,640]{1,0:T(8,128)(2,1)S(1)} %pad_maximum_fusion.3), channel_id=1, source_target_pairs={{0,4},{2,6},{4,8},{6,10},{8,12},{10,14},{12,0},{14,2},{1,5},{3,7},... | collective-permute-start | bytes 522248 | tf_op jit(solution)/shard_map/ppermute | solution.py:1104
  4.2 20.2 %collective-permute-start.1 = (bf16[136,640]{1,0:T(8,128)(2,1)S(1)}, bf16[136,640]{1,0:T(8,128)(2,1)S(1)}, u32[]{:S(2)}, u32[]{:S(2)}) collective-permute-start(bf16[136,640]{1,0:T(8,128)(2,1)S(1)} %pad_maximum_fusion.4), channel_id=1, source_target_pairs={{0,8},{2,10},{4,12},{6,14},{8,0},{10,2},{12,4},{14,6},{1,9},{3,11}... | collective-permute-start | bytes 522248 | tf_op jit(solution)/shard_map/ppermute | solution.py:1104
  5.4 19.1 %collective-permute-start.2 = (bf16[136,640]{1,0:T(8,128)(2,1)S(1)}, bf16[136,640]{1,0:T(8,128)(2,1)S(1)}, u32[]{:S(2)}, u32[]{:S(2)}) collective-permute-start(bf16[136,640]{1,0:T(8,128)(2,1)S(1)} %pad_maximum_fusion.5), channel_id=1, source_target_pairs={{0,12},{2,14},{4,0},{6,2},{8,4},{10,6},{12,8},{14,10},{1,13},{3,15... | collective-permute-start | bytes 522248 | tf_op jit(solution)/shard_map/ppermute | solution.py:1104
  6.9 17.5 %collective-permute-start.3 = (s32[4]{0:T(128)S(1)}, s32[4]{0:T(128)S(1)}, u32[]{:S(2)}, u32[]{:S(2)}) collective-permute-start(s32[4]{0:T(128)S(1)} %copy-done.24), channel_id=1, source_target_pairs={{0,16},{16,0},{1,17},{17,1},{2,18},{18,2},{3,19},{19,3},{4,20},{20... | collective-permute-start | bytes 56 | tf_op jit(solution)/shard_map/ppermute | solution.py:1111
  7.2 21.0 %collective-permute-start.10 = (bf16[136,640]{1,0:T(8,128)(2,1)S(1)}, bf16[136,640]{1,0:T(8,128)(2,1)S(1)}, u32[]{:S(2)}, u32[]{:S(2)}) collective-permute-start(bf16[136,640]{1,0:T(8,128)(2,1)S(1)} %pad_maximum_fusion.2.refs_1_), channel_id=1, source_target_pairs={{0,2},{2,0},{4,6},{6,4},{8,10},{10,8},{12,14},{14,12},{1,3},{3,1},... | collective-permute-start | bytes 522248 | tf_op jit(solution)/shard_map/ppermute | solution.py:1108
  26.9 9.1 %collective-permute-start.14 = (bf16[136,640]{1,0:T(8,128)(2,1)S(1)}, bf16[136,640]{1,0:T(8,128)(2,1)S(1)}, u32[]{:S(2)}, u32[]{:S(2)}) collective-permute-start(bf16[136,640]{1,0:T(8,128)(2,1)S(1)} %collective-permute-done.1.refs_4_), channel_id=1, source_target_pairs={{0,2},{2,0},{4,6},{6,4},{8,10},{10,8},{12,14},{14,12},{1,3},{3,1},... | collective-permute-start | bytes 522248 | tf_op jit(solution)/shard_map/ppermute | solution.py:1108
  28.2 11.6 %collective-permute-start.16 = (bf16[136,640]{1,0:T(8,128)(2,1)S(1)}, bf16[136,640]{1,0:T(8,128)(2,1)S(1)}, u32[]{:S(2)}, u32[]{:S(2)}) collective-permute-start(bf16[136,640]{1,0:T(8,128)(2,1)S(1)} %collective-permute-done.2.refs_6_), channel_id=1, source_target_pairs={{0,2},{2,0},{4,6},{6,4},{8,10},{10,8},{12,14},{14,12},{1,3},{3,1},... | collective-permute-start | bytes 522248 | tf_op jit(solution)/shard_map/ppermute | solution.py:1108
  28.4 13.7 %collective-permute-start.9 = (bf16[136,640]{1,0:T(8,128)(2,1)S(1)}, bf16[136,640]{1,0:T(8,128)(2,1)S(1)}, u32[]{:S(2)}, u32[]{:S(2)}) collective-permute-start(bf16[136,640]{1,0:T(8,128)(2,1)S(1)} %collective-permute-done.2.refs_6_), channel_id=1, source_target_pairs={{0,1},{1,0},{2,3},{3,2},{4,5},{5,4},{6,7},{7,6},{8,9},{9,8},{10,11... | collective-permute-start | bytes 522248 | tf_op jit(solution)/shard_map/ppermute | solution.py:1114
  29.7 12.5 %collective-permute-start.11 = (bf16[136,640]{1,0:T(8,128)(2,1)S(1)}, bf16[136,640]{1,0:T(8,128)(2,1)S(1)}, u32[]{:S(2)}, u32[]{:S(2)}) collective-permute-start(bf16[136,640]{1,0:T(8,128)(2,1)S(1)} %collective-permute-done.10.refs_8_), channel_id=1, source_target_pairs={{0,1},{1,0},{2,3},{3,2},{4,5},{5,4},{6,7},{7,6},{8,9},{9,8},{10,11... | collective-permute-start | bytes 522248 | tf_op jit(solution)/shard_map/ppermute | solution.py:1114
  32.3 13.1 %collective-permute-start.13 = (bf16[136,640]{1,0:T(8,128)(2,1)S(1)}, bf16[136,640]{1,0:T(8,128)(2,1)S(1)}, u32[]{:S(2)}, u32[]{:S(2)}) collective-permute-start(bf16[136,640]{1,0:T(8,128)(2,1)S(1)} %collective-permute-done.12.refs_10_), channel_id=1, source_target_pairs={{0,1},{1,0},{2,3},{3,2},{4,5},{5,4},{6,7},{7,6},{8,9},{9,8},{10,11... | collective-permute-start | bytes 522248 | tf_op jit(solution)/shard_map/ppermute | solution.py:1114
  36.0 9.5 %collective-permute-start.15 = (bf16[136,640]{1,0:T(8,128)(2,1)S(1)}, bf16[136,640]{1,0:T(8,128)(2,1)S(1)}, u32[]{:S(2)}, u32[]{:S(2)}) collective-permute-start(bf16[136,640]{1,0:T(8,128)(2,1)S(1)} %collective-permute-done.14.refs_12_), channel_id=1, source_target_pairs={{0,1},{1,0},{2,3},{3,2},{4,5},{5,4},{6,7},{7,6},{8,9},{9,8},{10,11... | collective-permute-start | bytes 522248 | tf_op jit(solution)/shard_map/ppermute | solution.py:1114
  42.1 31.0 %collective-permute-start.4 = (bf16[128,640]{1,0:T(8,128)(2,1)S(1)}, bf16[128,640]{1,0:T(8,128)(2,1)S(1)}, u32[]{:S(2)}, u32[]{:S(2)}) collective-permute-start(bf16[128,640]{1,0:T(8,128)(2,1)S(1)} %get-tuple-element.102), channel_id=1, source_target_pairs={{0,4},{2,6},{4,8},{6,10},{8,12},{10,14},{12,0},{14,2},{1,5},{3,7},... | collective-permute-start | bytes 491528 | tf_op jit(solution)/shard_map/ppermute | solution.py:1104
  42.2 31.0 %collective-permute-start.5 = (bf16[128,640]{1,0:T(8,128)(2,1)S(1)}, bf16[128,640]{1,0:T(8,128)(2,1)S(1)}, u32[]{:S(2)}, u32[]{:S(2)}) collective-permute-start(bf16[128,640]{1,0:T(8,128)(2,1)S(1)} %get-tuple-element.103), channel_id=1, source_target_pairs={{0,8},{2,10},{4,12},{6,14},{8,0},{10,2},{12,4},{14,6},{1,9},{3,11}... | collective-permute-start | bytes 491528 | tf_op jit(solution)/shard_map/ppermute | solution.py:1104
  45.3 27.8 %collective-permute-start.6 = (bf16[128,640]{1,0:T(8,128)(2,1)S(1)}, bf16[128,640]{1,0:T(8,128)(2,1)S(1)}, u32[]{:S(2)}, u32[]{:S(2)}) collective-permute-start(bf16[128,640]{1,0:T(8,128)(2,1)S(1)} %get-tuple-element.104), channel_id=1, source_target_pairs={{0,12},{2,14},{4,0},{6,2},{8,4},{10,6},{12,8},{14,10},{1,13},{3,15... | collective-permute-start | bytes 491528 | tf_op jit(solution)/shard_map/ppermute | solution.py:1104
  135.2 37.0 %collective-permute-start.21 = (bf16[4,2,24,640]{3,2,1,0:T(8,128)(2,1)S(1)}, bf16[4,2,24,640]{3,2,1,0:T(8,128)(2,1)}, u32[]{:S(2)}, u32[]{:S(2)}) collective-permute-start(bf16[4,2,24,640]{3,2,1,0:T(8,128)(2,1)S(1)} %dynamic-slice_bitcast_fusion.2), channel_id=1, source_target_pairs={{0,2},{2,0},{4,6},{6,4},{8,10},{10,8},{12,14},{14,12},{1,3},{3,1},... | collective-permute-start | bytes 737288 | tf_op jit(solution)/shard_map/ppermute | solution.py:1108
  186.0 19.3 %collective-permute-start.24 = (bf16[176,640]{1,0:T(8,128)(2,1)S(1)}, bf16[176,640]{1,0:T(8,128)(2,1)S(1)}, u32[]{:S(2)}, u32[]{:S(2)}) collective-permute-start(bf16[176,640]{1,0:T(8,128)(2,1)S(1)} %get-tuple-element.210), channel_id=1, source_target_pairs={{0,8},{2,10},{4,12},{6,14},{8,0},{10,2},{12,4},{14,6},{1,9},{3,11}... | collective-permute-start | bytes 675848 | tf_op jit(solution)/shard_map/ppermute | solution.py:1104
  187.7 19.1 %collective-permute-start.25 = (bf16[176,640]{1,0:T(8,128)(2,1)S(1)}, bf16[176,640]{1,0:T(8,128)(2,1)S(1)}, u32[]{:S(2)}, u32[]{:S(2)}) collective-permute-start(bf16[176,640]{1,0:T(8,128)(2,1)S(1)} %get-tuple-element.207), channel_id=1, source_target_pairs={{0,12},{2,14},{4,0},{6,2},{8,4},{10,6},{12,8},{14,10},{1,13},{3,15... | collective-permute-start | bytes 675848 | tf_op jit(solution)/shard_map/ppermute | solution.py:1104
  206.8 10.4 %collective-permute-start.27 = (bf16[4,24,640]{2,1,0:T(8,128)(2,1)S(1)}, bf16[4,24,640]{2,1,0:T(8,128)(2,1)S(1)}, u32[]{:S(2)}, u32[]{:S(2)}) collective-permute-start(bf16[4,24,640]{2,1,0:T(8,128)(2,1)S(1)} %pad_maximum_fusion.6), channel_id=1, source_target_pairs={{0,16},{16,0},{1,17},{17,1},{2,18},{18,2},{3,19},{19,3},{4,20},{20... | collective-permute-start | bytes 368648 | tf_op jit(solution)/shard_map/ppermute | solution.py:1111
  208.1 23.1 %collective-permute-start.30 = (bf16[512,640]{1,0:T(8,128)(2,1)S(1)}, bf16[512,640]{1,0:T(8,128)(2,1)S(1)}, u32[]{:S(2)}, u32[]{:S(2)}) collective-permute-start(bf16[512,640]{1,0:T(8,128)(2,1)S(1)} %bitcast.113), channel_id=1, source_target_pairs={{0,2},{2,0},{4,6},{6,4},{8,10},{10,8},{12,14},{14,12},{1,3},{3,1},... | collective-permute-start | bytes 1966088 | tf_op jit(solution)/shard_map/ppermute | solution.py:1108
  217.3 10.8 %collective-permute-start.28 = (bf16[4,2,24,640]{3,2,1,0:T(8,128)(2,1)S(1)}, bf16[4,2,24,640]{3,2,1,0:T(8,128)(2,1)S(1)}, u32[]{:S(2)}, u32[]{:S(2)}) collective-permute-start(bf16[4,2,24,640]{3,2,1,0:T(8,128)(2,1)S(1)} %get-tuple-element.212), channel_id=1, source_target_pairs={{0,2},{2,0},{4,6},{6,4},{8,10},{10,8},{12,14},{14,12},{1,3},{3,1},... | collective-permute-start | bytes 737288 | tf_op jit(solution)/shard_map/ppermute | solution.py:1108
  232.2 7.3 %collective-permute-start.38 = (bf16[4,24,640]{2,1,0:T(8,128)(2,1)S(1)}, bf16[4,24,640]{2,1,0:T(8,128)(2,1)S(1)}, u32[]{:S(2)}, u32[]{:S(2)}) collective-permute-start(bf16[4,24,640]{2,1,0:T(8,128)(2,1)S(1)} %collective-permute-done.27.refs_8_), channel_id=1, source_target_pairs={{0,1},{1,0},{2,3},{3,2},{4,5},{5,4},{6,7},{7,6},{8,9},{9,8},{10,11... | collective-permute-start | bytes 368648 | tf_op jit(solution)/shard_map/ppermute | solution.py:1114
  233.7 7.8 %collective-permute-start.31 = (bf16[176,640]{1,0:T(8,128)(2,1)}, bf16[176,640]{1,0:T(8,128)(2,1)S(1)}, u32[]{:S(2)}, u32[]{:S(2)}) collective-permute-start(bf16[176,640]{1,0:T(8,128)(2,1)} %get-tuple-element.205), channel_id=1, source_target_pairs={{0,4},{2,6},{4,8},{6,10},{8,12},{10,14},{12,0},{14,2},{1,5},{3,7},... | collective-permute-start | bytes 675848 | tf_op jit(solution)/shard_map/ppermute | solution.py:1104
  233.7 19.7 %collective-permute-start.32 = (bf16[176,640]{1,0:T(8,128)(2,1)S(1)}, bf16[176,640]{1,0:T(8,128)(2,1)S(1)}, u32[]{:S(2)}, u32[]{:S(2)}) collective-permute-start(bf16[176,640]{1,0:T(8,128)(2,1)S(1)} %get-tuple-element.204), channel_id=1, source_target_pairs={{0,8},{2,10},{4,12},{6,14},{8,0},{10,2},{12,4},{14,6},{1,9},{3,11}... | collective-permute-start | bytes 675848 | tf_op jit(solution)/shard_map/ppermute | solution.py:1104
  235.5 20.6 %collective-permute-start.33 = (bf16[176,640]{1,0:T(8,128)(2,1)S(1)}, bf16[176,640]{1,0:T(8,128)(2,1)S(1)}, u32[]{:S(2)}, u32[]{:S(2)}) collective-permute-start(bf16[176,640]{1,0:T(8,128)(2,1)S(1)} %get-tuple-element.203), channel_id=1, source_target_pairs={{0,12},{2,14},{4,0},{6,2},{8,4},{10,6},{12,8},{14,10},{1,13},{3,15... | collective-permute-start | bytes 675848 | tf_op jit(solution)/shard_map/ppermute | solution.py:1104
  (66 other events, 659.8 us)

commit v5 on v4

--- a/solution.py
+++ b/solution.py
@@ -103,8 +103,10 @@
     return jnp.concatenate([first, first], axis=1), jnp.concatenate([last, last], axis=1)
 
 
-def whole_spec(shape):
-    return pl.BlockSpec(shape, lambda *a: (0,) * len(shape))
+def whole_spec(shape, buffers=1):
+    return pl.BlockSpec(
+        shape, lambda *a: (0,) * len(shape), pipeline_mode=pl.Buffered(buffers)
+    )
 
 
 def col_spec(size, width=LANES):
@@ -341,7 +343,7 @@
             mid_ref[sl, :] = mixed
             low_ref[sl, :] = mixed.astype(bf16)
 
-        by_rows(rows, 256, mix)
+        by_rows(rows, 128, mix)
         u_ref[...] = nt(low_ref[...], a_ref[...]).astype(bf16)
         acc_ref[...] = jnp.zeros_like(acc_ref)
 
@@ -405,8 +407,12 @@
     return seq * slabs * group + slab * group + inner
 
 
-def pad_lanes(tile):
-    return jnp.pad(tile, ((0, 0), (0, LANES - tile.shape[1])))
+def pad_to(tile, lanes):
+    return jnp.pad(tile, ((0, 0), (0, lanes - tile.shape[1])))
+
+
+def late_rows(rank, units):
+    return max(4 * rank, 2 * units)
 
 
 def folded_rows(rows, groups):
@@ -470,7 +476,7 @@
             grad_unit = rate * grad_mixed
             gd_ref[sl, :] = (raw_inv * (grad_unit - unit * row_mean(grad_unit * unit))).astype(bf16)
 
-        by_rows(rows, 256, mix)
+        by_rows(rows, 128, mix)
         out_ref[...] = lo_ref[:, mine].reshape(slabs, chunk, half)
         ut_ref[...] = u_ref[...].T
         udt_ref[...] = hid_ref[...].T
@@ -528,13 +534,13 @@
             for z in range(slabs):
                 for x in range(n_seq):
                     d = owner_index((y, z, x), group, slabs, n_seq)
-                    head = pad_lanes(model_rows[:, d * cols : (d + 1) * cols])
+                    head = pad_to(model_rows[:, d * cols : (d + 1) * cols], LANES)
                     mine = turned_rows[d * units_each : (d + 1) * units_each]
                     tail = [
                         mine[:, t * LANES : (t + 1) * LANES] for t in range(padded // LANES)
                     ]
                     packed = jnp.concatenate([head] + tail, axis=0)
-                    table_ref[y, z, x] = fold(packed, half // LANES).astype(bf16)
+                    table_ref[z, y, x] = fold(packed, half // LANES).astype(bf16)
 
 
 def run_feed_back(
@@ -554,7 +560,7 @@
         ((slabs, chunk, half), bf16),
         ((rows, model), f32),
         ((rows, model), bf16),
-        ((group, slabs, n_seq, folded_rows(table_rows, half // LANES), half), bf16),
+        ((slabs, group, n_seq, folded_rows(table_rows, half // LANES), half), bf16),
     ]
     return pl.pallas_call(
         functools.partial(
@@ -642,7 +648,7 @@
             grad_unit = rate * grad_mixed
             ga_ref[sl, :] = (raw_inv * (grad_unit - unit * row_mean(grad_unit * unit))).astype(bf16)
 
-        by_rows(rows, 256, mix)
+        by_rows(rows, 128, mix)
         gbo_ref[...] = nn(uo_ref[...].T, ga_ref[...])
         low_g = nt(ga_ref[...], bo_ref[...]).astype(bf16)
         guo_ref[...] = low_g
@@ -934,11 +940,20 @@
         for z in range(slabs):
             for x in range(n_seq):
                 d = owner_index((y, z, x), group, slabs, n_seq)
-                parts = [
-                    pad_lanes(model_rows[:, d * cols : (d + 1) * cols]),
-                    pad_lanes(turned[d * units : (d + 1) * units]),
-                ]
-                packed = jnp.concatenate(parts, axis=0)
+                left = model_rows[:, d * cols : (d + 1) * cols]
+                heads_part = turned[d * units : (d + 1) * units]
+                right = jnp.concatenate(
+                    [heads_part[:, rank:], pad_to(heads_part[:, :rank], 3 * rank)], axis=0
+                )
+                tall = late_rows(rank, units)
+                packed = jnp.concatenate(
+                    [
+                        jnp.pad(left, ((0, tall - left.shape[0]), (0, 0))),
+                        jnp.pad(right, ((0, tall - right.shape[0]), (0, 0))),
+                    ],
+                    axis=1,
+                )
+                packed = pad_to(packed, LANES)
                 table_ref[y, z, x] = fold(packed, table_ref.shape[4] // LANES).astype(bf16)
 
 
@@ -951,7 +966,7 @@
     owners = n_seq * slabs * group
     units = heads * (head_dim // owners)
     half = model // 2
-    shape = (group, slabs, n_seq, folded_rows(4 * rank + units, half // LANES), half)
+    shape = (group, slabs, n_seq, folded_rows(late_rows(rank, units), half // LANES), half)
     operands = (gq, gk, gv, b, u, h, h_own, gbo, gah)
     return pl.pallas_call(
         functools.partial(grads_kernel, (slabs, chunk, group, n_seq, rank, model, head_dim)),
@@ -999,23 +1014,15 @@
     )(place, *mine, *other)
 
 
-def tables_of(dims, place, index, refs):
-    n_seq, slabs, chunk, size = dims
-    home, home_other = refs[:slabs], refs[slabs : 2 * slabs]
-    far, far_other = refs[2 * slabs : 2 * slabs + n_seq - 1], refs[2 * slabs + n_seq - 1 :]
-    for r in range(slabs):
-        at = pl.ds(pl.multiple_of(chunk + place[3] * size, 8), size)
-        yield index[0, r], unfold(home[r][at, :]), unfold(home_other[r][at, :])
-    for s in range(1, n_seq):
-        for r in range(slabs):
-            yield index[s, r], unfold(far[s - 1][r]), unfold(far_other[s - 1][r])
-
-
 def unpack_early_kernel(dims, where, place, index, *refs):
     rank, cols, each, hidden_rows, tiles = dims
+    n_seq, slabs = where
     am_ref, bm_ref, ad_ref, bd_ref = refs[-4:]
     core = place[2]
-    for adapter, block, other in tables_of(where, place, index, refs[:-4]):
+
+    def put(s, r):
+        adapter = index[s, r]
+        block, other = unfold(refs[s][r]), unfold(refs[n_seq + s][r])
         both = block[: 2 * rank] + other[: 2 * rank]
         am = jnp.where(core == 0, both[:, : cols // 2], both[:, cols // 2 : cols])
         am_ref[adapter] = am.reshape(2, rank, cols // 2)
@@ -1031,29 +1038,50 @@
                 at = ((j + 1) * rank + k) * hidden_rows
                 bd_ref[adapter, j, k] = wide[:, at : at + hidden_rows]
 
+    for s in range(n_seq):
+        lax.fori_loop(0, slabs, lambda r, c, s=s: (put(s, r), c)[1], 0)
+
 
 def unpack_late_kernel(dims, where, place, index, *refs):
     rank, cols, heads, each = dims
+    n_seq, slabs, chunk, size = where
     am_gu_ref, bm_down_ref, am_ref, bm_ref, ah_ref, bh_ref = refs[-6:]
+    home, home_other = refs[:slabs], refs[slabs : 2 * slabs]
+    far, far_other = refs[2 * slabs : 2 * slabs + n_seq - 1], refs[2 * slabs + n_seq - 1 : -6]
     core = place[2]
-    for adapter, block, other in tables_of(where, place, index, refs[:-6]):
+
+    def put(adapter, block, other):
         both = block[: 3 * rank] + other[: 3 * rank]
         am = jnp.where(core == 0, both[:, : cols // 2], both[:, cols // 2 : cols])
         am_ref[adapter, 0:3] = am.reshape(3, rank, cols // 2)
         am_ref[adapter, 3:5] = am_gu_ref[adapter]
         bm_ref[adapter, 0] = block[3 * rank : 4 * rank, :cols]
         bm_ref[adapter, 1] = bm_down_ref[adapter]
-        units = block[4 * rank : 4 * rank + heads * each]
+        units = heads * each
         for n in range(heads):
-            piece = units[n * each : (n + 1) * each]
-            ah_ref[adapter, n] = piece[:, :rank]
+            at = n * each
+            ah_ref[adapter, n] = block[units + at : units + at + each, cols : cols + rank]
             for j in range(3):
-                bh_ref[adapter, j, n] = piece[:, (j + 1) * rank : (j + 2) * rank]
+                lanes = slice(cols + j * rank, cols + (j + 1) * rank)
+                bh_ref[adapter, j, n] = block[at : at + each, lanes]
+
+    for r in range(slabs):
+        at = pl.ds(pl.multiple_of(chunk + place[3] * size, 8), size)
+        put(index[0, r], unfold(home[r][at, :]), unfold(home_other[r][at, :]))
+    for s in range(1, n_seq):
+        lax.fori_loop(
+            0,
+            slabs,
+            lambda r, c, s=s: (
+                put(index[s, r], unfold(far[s - 1][r]), unfold(far_other[s - 1][r])),
+                c,
+            )[1],
+            0,
+        )
 
 
 def run_unpack(kernel, dims, where, place, index, tables, extra, shapes, name):
-    home, home_other, far, far_other = tables
-    operands = [*home, *home_other, *far, *far_other, *extra]
+    operands = [*tables, *extra]
     return pl.pallas_call(
         functools.partial(kernel, dims, where),
         grid_spec=pltpu.PrefetchScalarGridSpec(
@@ -1155,14 +1183,18 @@
     for turn in range(1, group):
         for shift in range(slabs):
             received[turn, shift] = within_slab(got[shift], turn)
-    got, g_send, cos, sin, am_qkv, am_gu, bh, ah_pad, ad_pad, ad, ah, bd, bm, index = tie(
+    late_turns = {key: received[key] for key in received if key[1] == 2 % slabs}
+    late_turns, g_send = tie(
         (
-            got,
+            late_turns,
             [half_piece(cotangent, (slab + shift) % slabs, core) for shift in range(1, slabs)],
-            cos, sin, am_qkv, am_gu, bh, ah_pad, ad_pad, ad, ah, bd, bm, index,
         )
     )
+    received.update(late_turns)
     g_mine = [to_slab(g_send[shift - 1], shift) for shift in range(1, slabs)]
+    received, cos, sin, am_qkv, am_gu, bh, ah_pad, ad_pad, ad, ah, bd, bm, index = tie(
+        (received, cos, sin, am_qkv, am_gu, bh, ah_pad, ad_pad, ad, ah, bd, bm, index)
+    )
     pieces = [own_piece]
     for shift in range(1, slabs):
         pieces += [got[shift], other_core(got[shift])]
@@ -1178,11 +1210,13 @@
     g_mine, attn_msg = tie((g_mine, attn_msg))
     attn_other = other_core(attn_msg)
     g_mine = jnp.stack(g_mine)
-    attn_other, g_other = tie((attn_other, other_core(g_mine)))
+    g_mine, attn_other = tie((g_mine, attn_other))
+    g_other = other_core(g_mine)
     mid, u_gu, gate, up, down_msg = run_feed(
         attn_msg, attn_other, h_own, bm[0], mix_rates, am_gu, w_gate_up, bd, w_down, ad_pad,
         mlp_scales, 512,
     )
+    g_other, down_msg = tie((g_other, down_msg))
     down_other = other_core(down_msg)
     out_half, mid_res, mid_msg, early = run_feed_back(
         place, down_msg, down_other, mid, cotangent, g_mine, g_other, bm[1], mix_rates, am_gu,
@@ -1212,48 +1246,71 @@
     def pack(rows_part, table):
         return jnp.concatenate([rows_part, table.reshape(slabs, -1, half)], axis=1)
 
-    def over_seqs(home):
-        result = []
-        for shift in range(1, n_seq):
-            at = chunk + (seq_place + shift) % n_seq * size
-            sent = [lax.dynamic_slice_in_dim(piece, at, size, 0) for piece in home]
-            result.append(to_seq(jnp.stack(sent), shift))
-        return result
-
-    early_own, early_got = sum_inner(early)
+    def over_seqs(table):
+        return [
+            to_seq(pick(table, (seq_place + shift) % n_seq), shift) for shift in range(1, n_seq)
+        ]
+
     size = early.shape[3]
+    home = over_slabs(pack(out_half, early))
     gq, gk, gv, h_res, gbo, gah = run_attend_back(
         place, mid_res, mid_msg, mid_other, mid, h_own, attn_msg, attn_other, mix_rates, bm[0],
         w_attn_out, ah, start, q, k, v, o, inv, qi, ki, cos, sin, scale, slabs, group,
         head_dim,
     )
-    early_got, gk, gv = tie((early_got, gk, gv))
-    home = over_slabs(pack(out_half, add_inner(early_own, early_got)))
+    home, gk, gv = tie((home, gk, gv))
     keep, send = run_others(place, gk, gv, w_attn_in, am_qkv, bh, slabs, group)
     others = (keep + other_core(send).astype(f32)).astype(bf16)
-    home, others, gq = tie((home, others, gq))
-    others_got = [within_slab(others[turn - 1], turn) for turn in range(1, group)]
-    home_other = [other_core(piece) for piece in home]
-    far = over_seqs(home)
+    others, gq, gk, gv = tie((others, gq, gk, gv))
+    waves = [[2, 1], [3, 0]] if slabs == 4 else [list(range(slabs))]
+    others = others.reshape(group - 1, slabs, chunk, half)
+    others_got = [
+        [
+            within_slab(
+                jnp.stack([pick(others[turn - 1], (slab + shift) % slabs) for shift in wave]),
+                turn,
+            )
+            for turn in range(1, group)
+        ]
+        for wave in waves
+    ]
+    tables = jnp.stack([piece[chunk:] for piece in home])
+    tables = jnp.moveaxis(tables.reshape(slabs, group, n_seq, size, half), 0, 2)
+    early_own, early_got = sum_inner(tables)
     late = run_grads(
         place, gq, gk, gv, bh, u, h_full, h_own, gbo, gah, slabs, group, n_seq, head_dim
     )
-    far, late = tie((far, late))
+    early_got, late = tie((early_got, late))
+    early = add_inner(early_own, early_got)
     late_own, late_got = sum_inner(late)
-    far_other = [other_core(piece) for piece in far]
-    late_own, gq = tie((late_own, gq))
+    early_far = over_seqs(early)
+    early_mine = pick(early, seq_place)
+    home_other = [other_core(piece[:chunk]) for piece in home]
+    late_own, gq, others_got[0] = tie((late_own, gq, others_got[0]))
     own_keep, own_send = run_own(
         place, gq, gk, gv, w_attn_in, am_qkv, bh, h_res, slabs, group
     )
-    late_got, own_send = tie((late_got, own_send))
+    late_got, early_far, own_send, others_got = tie(
+        (late_got, early_far, own_send, others_got)
+    )
     own_got = other_core(own_send)
-    total = own_keep + own_got.astype(f32)
-    for got_part in others_got:
-        total = total + got_part.astype(f32)
-    total = total.astype(bf16).reshape(slabs, chunk, half)
-    total = pack(total, add_inner(late_own, late_got))
-    total, home, far = tie((total, home, far))
-    result = over_slabs(total)
+    late_total = add_inner(late_own, late_got)
+    own_sum = (own_keep + own_got.astype(f32)).reshape(slabs, chunk, half)
+    size = late.shape[3]
+    result = [None] * slabs
+    for wave, got_wave in zip(waves, others_got):
+        for n, shift in enumerate(wave):
+            target = (slab + shift) % slabs
+            total = pick(own_sum, target)
+            for got_part in got_wave:
+                total = total + got_part[n].astype(f32)
+            total = jnp.concatenate(
+                [total.astype(bf16), pick(late_total, target).reshape(n_seq * size, half)],
+                axis=0,
+            )
+            result[shift] = to_slab(total, shift) if shift else total
+    early_tables = [early_mine, *early_far]
+    early_tables += [other_core(table) for table in early_tables]
     layer_out = run_join(place, home, home_other, chunk, bf16)
     cols = model // owners
     each = row_width // owners
@@ -1261,8 +1318,8 @@
     grad_am_gu, grad_bm_down, grad_ad, grad_bd = run_unpack(
         unpack_early_kernel,
         (rank, cols, each, hidden_rows, (3 * rank * hidden_rows + LANES - 1) // LANES),
-        (n_seq, slabs, chunk, size),
-        place, index, (home, home_other, far, far_other), [],
+        (n_seq, slabs),
+        place, index, early_tables, [],
         [
             (adapters, 2, rank, cols // 2),
             (adapters, rank, cols),
@@ -1271,12 +1328,15 @@
         ],
         "unpack_early",
     )
-    size = late.shape[3]
     result, layer_out, grad_am_gu, grad_bm_down = tie(
         (result, layer_out, grad_am_gu, grad_bm_down)
     )
     result_other = [other_core(piece) for piece in result]
-    far = over_seqs(result)
+    far = []
+    for shift in range(1, n_seq):
+        at = chunk + (seq_place + shift) % n_seq * size
+        sent = [lax.dynamic_slice_in_dim(piece, at, size, 0) for piece in result]
+        far.append(to_seq(jnp.stack(sent), shift))
     input_grad = run_join(place, result, result_other, chunk, f32)
     far, input_grad = tie((far, input_grad))
     each = head_dim // owners
@@ -1284,7 +1344,7 @@
         unpack_late_kernel,
         (rank, cols, local_heads, each),
         (n_seq, slabs, chunk, size),
-        place, index, (result, result_other, far, [other_core(piece) for piece in far]),
+        place, index, [*result, *result_other, *far, *(other_core(piece) for piece in far)],
         [grad_am_gu, grad_bm_down],
         [
             (adapters, 5, rank, cols // 2),

time: 270 us -> 250 us (0.926)
  the two profiles are of different devices: /device:TPU:11 before, /device:TPU:0 now
where the time goes in v5:
time: 250 us; the launch traced here: 249 us
  Pallas kernels  137 us (55%)
  starting transfers between devices  35.9 us (14%)
  waiting for transfers between devices  32.3 us (13%)
  local copies, waits for them, and re-layouts  29.3 us (12%)
  other arithmetic  11.2 us (4%)
  between operations  3.51 us (1%)
    pallas_call x1, Pallas kernels, run_attend_back(): pl.pallas_call(functools.partial(attend_back_kernel, (slabs, chunk, group...  34.2 us
    pallas_call x1, Pallas kernels, run_feed_back(): pl.pallas_call(functools.partial(feed_back_kernel, (slabs, chunk, group,...  29.5 us
    pallas_call x1, Pallas kernels, run_attend(): pl.pallas_call(functools.partial(attend_kernel, (slabs, chunk, group, hea...  26.3 us
    pallas_call x1, Pallas kernels, run_feed(): pl.pallas_call(functools.partial(feed_kernel, (rank, model)), grid=(hidde...  22.1 us
    ppermute x12, starting transfers between devices, to_slab(): return lax.ppermute(array, 'ctx', pairs)  20.1 us
    ppermute x8, waiting for transfers between devices, within_slab(): return lax.ppermute(array, 'ctx', pairs)  14.2 us
    unnamed x105, local copies, waits for them, and re-layouts  13.5 us
    ppermute x24, waiting for transfers between devices, other_core(): return lax.ppermute(array, 'wt', [(0, 1), (1, 0)])  9.37 us
  transfers between devices with their start and end apart: 47, of which 11 were waited for; matrix products, arithmetic and copies ran while one was open for 10% of the time, Pallas kernels for 40%

profile of v5, /device:TPU:0, one launch (start us, length us, event | category | flops | bytes accessed | tf_op | source)
XLA Modules:
  0.0 249.0 jit_solution(2069036715107551032)
XLA Ops:
  2.9 4.1 %collective-permute-start = (bf16[136,640]{1,0:T(8,128)(2,1)S(1)}, bf16[136,640]{1,0:T(8,128)(2,1)S(1)}, u32[]{:S(2)}, u32[]{:S(2)}) collective-permute-start(bf16[136,640]{1,0:T(8,128)(2,1)S(1)} %pad_maximum_fusion.8), channel_id=1, source_target_pairs={{0,8},{2,10},{4,12},{6,14},{8,0},{10,2},{12,4},{14,6},{1,9},{3,11}... | collective-permute-start | bytes 522248 | tf_op jit(solution)/shard_map/ppermute | solution.py:1132
  7.0 1.6 collective-permute-start.5
  8.7 2.3 collective-permute-start.8
  20.1 3.0 %fusion = (f32[1024,128]{1,0:T(8,128)}, f32[1024,128]{1,0:T(8,128)}) fusion(f32[128]{0:T(128)S(1)} %get-tuple-element.239, f32[128]{0:T(128)S(1)} %get-tuple-element.240, f32[1024]{0:T(1024)S(1)} %iota_convert_fusion), kind=kLoop, calls=%fused_computation.13 | loop fusion | flops 262144 | bytes 1053696 | tf_op jit(solution)/shard_map/mul | solution.py:1172
  27.3 3.5 %collective-permute-done.1.refs_12_ = bf16[136,640]{1,0:T(8,128)(2,1)S(1)} collective-permute-done((bf16[136,640]{1,0:T(8,128)(2,1)S(1)}, bf16[136,640]{1,0:T(8,128)(2,1)S(1)}, u32[]{:S(2)}, u32[]{:S(2)}) %collective-permute-start.1) | collective-permute-done | bytes 174112 | tf_op jit(solution)/shard_map/ppermute | solution.py:1136
  40.0 3.2 %collective-permute-start.4 = (bf16[128,640]{1,0:T(8,128)(2,1)S(1)}, bf16[128,640]{1,0:T(8,128)(2,1)S(1)}, u32[]{:S(2)}, u32[]{:S(2)}) collective-permute-start(bf16[128,640]{1,0:T(8,128)(2,1)S(1)} %get-tuple-element.107), channel_id=1, source_target_pairs={{0,12},{2,14},{4,0},{6,2},{8,4},{10,6},{12,8},{14,10},{1,13},{3,15... | collective-permute-start | bytes 491528 | tf_op jit(solution)/shard_map/ppermute | solution.py:1132
  44.6 26.3 %attend.1 = (bf16[1024,1280]{1,0:T(8,128)(2,1)}, bf16[512,1280]{1,0:T(8,128)(2,1)}, bf16[1024,48]{1,0:T(8,128)(2,1)}, bf16[512,640]{1,0:T(8,128)(2,1)}, bf16[102...) custom-call(s32[4]{0:T(128)} %pad_add_fusion.1.place, ...), custom_call_target="tpu_custom_call" | custom-call | flops 30000001024 | bytes 40000000 | tf_op jit(solution)/shard_map/attend/pallas_call | solution.py:302
  71.7 2.7 %collective-permute-done.18.other_ref.ao_ref = bf16[512,1408]{1,0:T(8,128)(2,1)S(1)} collective-permute-done((bf16[512,1408]{1,0:T(8,128)(2,1)}, bf16[512,1408]{1,0:T(8,128)(2,1)S(1)}, u32[]{:S(2)}, u32[]{:S(2)}) %collective-permute-start.18) | collective-permute-done | bytes 1441824 | tf_op jit(solution)/shard_map/ppermute | solution.py:1142
  75.5 22.1 %feed.1 = (f32[512,1280]{1,0:T(8,128)}, bf16[512,32]{1,0:T(8,128)(2,1)}, bf16[512,2560]{1,0:T(8,128)(2,1)}, bf16[512,2560]{1,0:T(8,128)(2,1)}, bf16[512,1408]{1,0:T(8,128)(2,1)}) custom-call(bf16[512,1408]{1,0:T(8,128)(2,1)} %get-tuple-element.122.mine_ref.am_ref, bf16[512,1408]{1,0:T(8,128)(2,1)} %copy-done.32, ...), custom_call_target="tpu_custom_call" | custom-call | flops 24000000000 | bytes 30000000 | tf_op jit(solution)/shard_map/feed/pallas_call | solution.py:377
  97.8 3.3 %collective-permute-done.20.other_ref = bf16[512,1408]{1,0:T(8,128)(2,1)S(1)} collective-permute-done((bf16[512,1408]{1,0:T(8,128)(2,1)}, bf16[512,1408]{1,0:T(8,128)(2,1)S(1)}, u32[]{:S(2)}, u32[]{:S(2)}) %collective-permute-start.20) | collective-permute-done | bytes 1441824 | tf_op jit(solution)/shard_map/ppermute | solution.py:1142
  102.3 29.5 %feed_back.1 = (bf16[4,128,640]{2,1,0:T(8,128)(2,1)}, f32[512,1280]{1,0:T(8,128)}, bf16[512,1280]{1,0:T(8,128)(2,1)}, bf16[4,2,2,24,640]{4,3,2,1,0:T(8,128)(2,1)}) custom-call(s32[4]{0:T(128)} %pad_add_fusion.1.place, bf16[512,1408]{1,0:T(8,128)(2,1)} %get-tuple-element.131.mine_ref, bf16[512,1408]{1,0:T(8,128)(2,1)} %copy-done.33, ...), custom_call_target="tpu_custom_call" | custom-call | flops 30000001024 | bytes 40000000 | tf_op jit(solution)/shard_map/feed_back/pallas_call | solution.py:565
  135.3 2.8 %collective-permute-start.23 = (bf16[224,640]{1,0:T(8,128)(2,1)S(1)}, bf16[224,640]{1,0:T(8,128)(2,1)S(1)}, u32[]{:S(2)}, u32[]{:S(2)}) collective-permute-start(bf16[224,640]{1,0:T(8,128)(2,1)S(1)} %get-tuple-element.215), channel_id=1, source_target_pairs={{0,12},{2,14},{4,0},{6,2},{8,4},{10,6},{12,8},{14,10},{1,13},{3,15... | collective-permute-start | bytes 860168 | tf_op jit(solution)/shard_map/ppermute | solution.py:1132
  139.3 34.2 %attend_back.1 = (bf16[512,640]{1,0:T(8,128)(2,1)}, bf16[1024,640]{1,0:T(8,128)(2,1)}, bf16[1024,640]{1,0:T(8,128)(2,1)}, f32[512,1280]{1,0:T(8,128)}, f32[16,1280]{1,0:T(8,128)}, /*index=5*/f32[16,640]{1,0:T(8,128)}) custom-call(s32[4]{0:T(128)} %pad_add_fusion.1.place, f32[512,1280]{1,0:T(8,128)} %get-tuple-element.140.res_ref, ...), custom_call_target="tpu_custom_call" | custom-call | flops 30000001024 | bytes 40000000 | tf_op jit(solution)/shard_map/attend_back/pallas_call | solution.py:733
  173.5 2.4 copy-done.9
  178.5 4.7 %others.1 = (f32[1,512,640]{2,1,0:T(8,128)S(1)}, bf16[1,512,640]{2,1,0:T(8,128)(2,1)}) custom-call(s32[4]{0:T(128)S(1)} %copy-done.8, bf16[4,2,128,640]{3,2,1,0:T(8,128)(2,1)S(1)} %bitcast.124, bf16[4,2,128,640]{3,2,1,0:T(8,128)(2,1)S(1)} %bitcast.126, bf16[3,1280,640]{2,1,0:T(8,128)(2,1)S(1)} %copy-done.9, bf16[48,1280]{1,0:T(8,128)(2,1)S(1)} %bitcast.118, ...), custom_call_target="tpu_custom_call" | custom-call | flops 7000000000 | bytes 10000000 | tf_op jit(solution)/shard_map/others/pallas_call | solution.py:812
  189.5 4.0 %grads.1 = bf16[2,4,2,16,640]{4,3,2,1,0:T(8,128)(2,1)S(1)} custom-call(s32[4]{0:T(128)S(1)} %copy-done.8, bf16[512,640]{1,0:T(8,128)(2,1)S(1)} %copy-done.16, bf16[1024,640]{1,0:T(8,128)(2,1)S(1)} %copy-done.11, bf16[1024,640]{1,0:T(8,128)(2,1)S(1)} %copy-done.13, bf16[3,16,640]{2,1,0:T(8,128)(2,1)S(1)} %copy-done.7, bf16[1024,48]{1,0:T(8,128)(2,1)S(1)} %copy-done.18, ...), custom_call_target="tpu_custom_call" | custom-call | flops 10000000000 | bytes 10000000 | tf_op jit(solution)/shard_map/grads/pallas_call | solution.py:971
  195.7 10.7 %collective-permute-done.27 = bf16[2,128,640]{2,1,0:T(8,128)(2,1)S(1)} collective-permute-done((bf16[2,128,640]{2,1,0:T(8,128)(2,1)S(1)}, bf16[2,128,640]{2,1,0:T(8,128)(2,1)S(1)}, u32[]{:S(2)}, u32[]{:S(2)}) %collective-permute-start.27) | collective-permute-done | bytes 327712 | tf_op jit(solution)/shard_map/ppermute | solution.py:1136
  207.1 6.7 %own.1 = (f32[512,640]{1,0:T(8,128)S(1)}, bf16[512,640]{1,0:T(8,128)(2,1)}) custom-call(s32[4]{0:T(128)S(1)} %copy-done.8, bf16[512,640]{1,0:T(8,128)(2,1)S(1)} %copy-done.16, bf16[4,2,128,640]{3,2,1,0:T(8,128)(2,1)S(1)} %bitcast.125, bf16[4,2,128,640]{3,2,1,0:T(8,128)(2,1)S(1)} %bitcast.127, bf16[3,1280,640]{2,1,0:T(8,128)(2,1)S(1)} %bitcast.123, ...), custom_call_target="tpu_custom_call" | custom-call | flops 7000000000 | bytes 10000000 | tf_op jit(solution)/shard_map/own/pallas_call | solution.py:870
  222.7 2.0 collective-permute-start.32
  227.3 1.7 join.2
  229.0 3.5 %unpack_early.1 = (f32[8,2,16,40]{3,2,1,0:T(8,128)S(1)}, f32[8,16,80]{2,1,0:T(8,128)S(1)}, f32[8,16,8,20]{3,2,1,0:T(8,128)}, f32[8,2,16,8,20]{4,3,2,1,0:T(8,128)}) custom-call(s32[4]{0:T(128)S(1)} %copy-done.8, s32[2,4]{1,0:T(2,128)S(1)} %bitcast.120, bf16[4,24,640]{2,1,0:T(8,128)(2,1)S(1)} %get-tuple-element.225.refs_0_, ...), custom_call_target="tpu_custom_call" | custom-call | flops 1000000 | bytes 8000000 | tf_op jit(solution)/shard_map/unpack_early/pallas_call | solution.py:1085
  232.5 7.6 %collective-permute-done.33.refs_2_ = bf16[160,640]{1,0:T(8,128)(2,1)S(1)} collective-permute-done((bf16[160,640]{1,0:T(8,128)(2,1)S(1)}, bf16[160,640]{1,0:T(8,128)(2,1)S(1)}, u32[]{:S(2)}, u32[]{:S(2)}) %collective-permute-start.33) | collective-permute-done | bytes 204832 | tf_op jit(solution)/shard_map/ppermute | solution.py:1132
  242.5 2.2 join.3
  247.0 2.0 unpack_late.1
  (264 shorter events, 59.3 us)
Async XLA Ops:
  2.9 20.9 %collective-permute-start = (bf16[136,640]{1,0:T(8,128)(2,1)S(1)}, bf16[136,640]{1,0:T(8,128)(2,1)S(1)}, u32[]{:S(2)}, u32[]{:S(2)}) collective-permute-start(bf16[136,640]{1,0:T(8,128)(2,1)S(1)} %pad_maximum_fusion.8), channel_id=1, source_target_pairs={{0,8},{2,10},{4,12},{6,14},{8,0},{10,2},{12,4},{14,6},{1,9},{3,11}... | collective-permute-start | bytes 522248 | tf_op jit(solution)/shard_map/ppermute | solution.py:1132
  7.0 18.1 %collective-permute-start.5 = (bf16[136,640]{1,0:T(8,128)(2,1)S(1)}, bf16[136,640]{1,0:T(8,128)(2,1)S(1)}, u32[]{:S(2)}, u32[]{:S(2)}) collective-permute-start(bf16[136,640]{1,0:T(8,128)(2,1)S(1)} %pad_maximum_fusion.10), channel_id=1, source_target_pairs={{0,4},{2,6},{4,8},{6,10},{8,12},{10,14},{12,0},{14,2},{1,5},{3,7},... | collective-permute-start | bytes 522248 | tf_op jit(solution)/shard_map/ppermute | solution.py:1132
  8.7 18.1 %collective-permute-start.8 = (bf16[136,640]{1,0:T(8,128)(2,1)S(1)}, bf16[136,640]{1,0:T(8,128)(2,1)S(1)}, u32[]{:S(2)}, u32[]{:S(2)}) collective-permute-start(bf16[136,640]{1,0:T(8,128)(2,1)S(1)} %pad_maximum_fusion.11), channel_id=1, source_target_pairs={{0,12},{2,14},{4,0},{6,2},{8,4},{10,6},{12,8},{14,10},{1,13},{3,15... | collective-permute-start | bytes 522248 | tf_op jit(solution)/shard_map/ppermute | solution.py:1132
  11.0 25.2 %collective-permute-start.10 = (bf16[136,640]{1,0:T(8,128)(2,1)S(1)}, bf16[136,640]{1,0:T(8,128)(2,1)S(1)}, u32[]{:S(2)}, u32[]{:S(2)}) collective-permute-start(bf16[136,640]{1,0:T(8,128)(2,1)S(1)} %pad_maximum_fusion.9.refs_1_), channel_id=1, source_target_pairs={{0,2},{2,0},{4,6},{6,4},{8,10},{10,8},{12,14},{14,12},{1,3},{3,1},... | collective-permute-start | bytes 522248 | tf_op jit(solution)/shard_map/ppermute | solution.py:1136
  12.6 14.1 %collective-permute-start.13 = (s32[4]{0:T(128)S(1)}, s32[4]{0:T(128)S(1)}, u32[]{:S(2)}, u32[]{:S(2)}) collective-permute-start(s32[4]{0:T(128)S(1)} %copy-done.31), channel_id=1, source_target_pairs={{0,16},{16,0},{1,17},{17,1},{2,18},{18,2},{3,19},{19,3},{4,20},{20... | collective-permute-start | bytes 56 | tf_op jit(solution)/shard_map/ppermute | solution.py:1139
  25.2 11.6 %collective-permute-start.11 = (bf16[136,640]{1,0:T(8,128)(2,1)S(1)}, bf16[136,640]{1,0:T(8,128)(2,1)S(1)}, u32[]{:S(2)}, u32[]{:S(2)}) collective-permute-start(bf16[136,640]{1,0:T(8,128)(2,1)S(1)} %collective-permute-done.5.refs_2_), channel_id=1, source_target_pairs={{0,2},{2,0},{4,6},{6,4},{8,10},{10,8},{12,14},{14,12},{1,3},{3,1},... | collective-permute-start | bytes 522248 | tf_op jit(solution)/shard_map/ppermute | solution.py:1136
  26.8 10.7 %collective-permute-start.6 = (bf16[136,640]{1,0:T(8,128)(2,1)S(1)}, bf16[136,640]{1,0:T(8,128)(2,1)S(1)}, u32[]{:S(2)}, u32[]{:S(2)}) collective-permute-start(bf16[136,640]{1,0:T(8,128)(2,1)S(1)} %collective-permute-done.5.refs_2_), channel_id=1, source_target_pairs={{0,1},{1,0},{2,3},{3,2},{4,5},{5,4},{6,7},{7,6},{8,9},{9,8},{10,11... | collective-permute-start | bytes 522248 | tf_op jit(solution)/shard_map/ppermute | solution.py:1142
  26.8 10.0 %collective-permute-start.12 = (bf16[136,640]{1,0:T(8,128)(2,1)S(1)}, bf16[136,640]{1,0:T(8,128)(2,1)S(1)}, u32[]{:S(2)}, u32[]{:S(2)}) collective-permute-start(bf16[136,640]{1,0:T(8,128)(2,1)S(1)} %collective-permute-done.8.refs_6_), channel_id=1, source_target_pairs={{0,2},{2,0},{4,6},{6,4},{8,10},{10,8},{12,14},{14,12},{1,3},{3,1},... | collective-permute-start | bytes 522248 | tf_op jit(solution)/shard_map/ppermute | solution.py:1136
  39.1 31.7 %collective-permute-start.2 = (bf16[128,640]{1,0:T(8,128)(2,1)S(1)}, bf16[128,640]{1,0:T(8,128)(2,1)S(1)}, u32[]{:S(2)}, u32[]{:S(2)}) collective-permute-start(bf16[128,640]{1,0:T(8,128)(2,1)S(1)} %get-tuple-element.105), channel_id=1, source_target_pairs={{0,4},{2,6},{4,8},{6,10},{8,12},{10,14},{12,0},{14,2},{1,5},{3,7},... | collective-permute-start | bytes 491528 | tf_op jit(solution)/shard_map/ppermute | solution.py:1132
  39.1 31.7 %collective-permute-start.3 = (bf16[128,640]{1,0:T(8,128)(2,1)S(1)}, bf16[128,640]{1,0:T(8,128)(2,1)S(1)}, u32[]{:S(2)}, u32[]{:S(2)}) collective-permute-start(bf16[128,640]{1,0:T(8,128)(2,1)S(1)} %get-tuple-element.106), channel_id=1, source_target_pairs={{0,8},{2,10},{4,12},{6,14},{8,0},{10,2},{12,4},{14,6},{1,9},{3,11}... | collective-permute-start | bytes 491528 | tf_op jit(solution)/shard_map/ppermute | solution.py:1132
  40.0 30.8 %collective-permute-start.4 = (bf16[128,640]{1,0:T(8,128)(2,1)S(1)}, bf16[128,640]{1,0:T(8,128)(2,1)S(1)}, u32[]{:S(2)}, u32[]{:S(2)}) collective-permute-start(bf16[128,640]{1,0:T(8,128)(2,1)S(1)} %get-tuple-element.107), channel_id=1, source_target_pairs={{0,12},{2,14},{4,0},{6,2},{8,4},{10,6},{12,8},{14,10},{1,13},{3,15... | collective-permute-start | bytes 491528 | tf_op jit(solution)/shard_map/ppermute | solution.py:1132
  74.4 23.3 %collective-permute-start.19 = (bf16[3,128,640]{2,1,0:T(8,128)(2,1)S(1)}, bf16[3,128,640]{2,1,0:T(8,128)(2,1)S(1)}, u32[]{:S(2)}, u32[]{:S(2)}) collective-permute-start(bf16[3,128,640]{2,1,0:T(8,128)(2,1)S(1)} %pad_maximum_fusion.g_mine_ref), channel_id=1, source_target_pairs={{0,1},{1,0},{2,3},{3,2},{4,5},{5,4},{6,7},{7,6},{8,9},{9,8},{10,11... | collective-permute-start | bytes 1474568 | tf_op jit(solution)/shard_map/ppermute | solution.py:1142
  133.4 40.0 %collective-permute-start.21 = (bf16[224,640]{1,0:T(8,128)(2,1)S(1)}, bf16[224,640]{1,0:T(8,128)(2,1)S(1)}, u32[]{:S(2)}, u32[]{:S(2)}) collective-permute-start(bf16[224,640]{1,0:T(8,128)(2,1)S(1)} %get-tuple-element.217), channel_id=1, source_target_pairs={{0,4},{2,6},{4,8},{6,10},{8,12},{10,14},{12,0},{14,2},{1,5},{3,7},... | collective-permute-start | bytes 860168 | tf_op jit(solution)/shard_map/ppermute | solution.py:1132
  133.9 39.6 %collective-permute-start.22 = (bf16[224,640]{1,0:T(8,128)(2,1)S(1)}, bf16[224,640]{1,0:T(8,128)(2,1)S(1)}, u32[]{:S(2)}, u32[]{:S(2)}) collective-permute-start(bf16[224,640]{1,0:T(8,128)(2,1)S(1)} %get-tuple-element.218), channel_id=1, source_target_pairs={{0,8},{2,10},{4,12},{6,14},{8,0},{10,2},{12,4},{14,6},{1,9},{3,11}... | collective-permute-start | bytes 860168 | tf_op jit(solution)/shard_map/ppermute | solution.py:1132
  135.3 38.1 %collective-permute-start.23 = (bf16[224,640]{1,0:T(8,128)(2,1)S(1)}, bf16[224,640]{1,0:T(8,128)(2,1)S(1)}, u32[]{:S(2)}, u32[]{:S(2)}) collective-permute-start(bf16[224,640]{1,0:T(8,128)(2,1)S(1)} %get-tuple-element.215), channel_id=1, source_target_pairs={{0,12},{2,14},{4,0},{6,2},{8,4},{10,6},{12,8},{14,10},{1,13},{3,15... | collective-permute-start | bytes 860168 | tf_op jit(solution)/shard_map/ppermute | solution.py:1132
  183.5 9.9 %collective-permute-start.25 = (bf16[2,4,24,640]{3,2,1,0:T(8,128)(2,1)S(1)}, bf16[2,4,24,640]{3,2,1,0:T(8,128)(2,1)S(1)}, u32[]{:S(2)}, u32[]{:S(2)}) collective-permute-start(bf16[2,4,24,640]{3,2,1,0:T(8,128)(2,1)S(1)} %dynamic-slice_bitcast_fusion), channel_id=1, source_target_pairs={{0,2},{2,0},{4,6},{6,4},{8,10},{10,8},{12,14},{14,12},{1,3},{3,1},... | collective-permute-start | bytes 737288 | tf_op jit(solution)/shard_map/ppermute | solution.py:1136
  187.2 26.6 %collective-permute-start.30 = (bf16[2,128,640]{2,1,0:T(8,128)(2,1)S(1)}, bf16[2,128,640]{2,1,0:T(8,128)(2,1)}, u32[]{:S(2)}, u32[]{:S(2)}) collective-permute-start(bf16[2,128,640]{2,1,0:T(8,128)(2,1)S(1)} %pad_maximum_fusion.3), channel_id=1, source_target_pairs={{0,2},{2,0},{4,6},{6,4},{8,10},{10,8},{12,14},{14,12},{1,3},{3,1},... | collective-permute-start | bytes 983048 | tf_op jit(solution)/shard_map/ppermute | solution.py:1136
  188.1 18.3 %collective-permute-start.27 = (bf16[2,128,640]{2,1,0:T(8,128)(2,1)S(1)}, bf16[2,128,640]{2,1,0:T(8,128)(2,1)S(1)}, u32[]{:S(2)}, u32[]{:S(2)}) collective-permute-start(bf16[2,128,640]{2,1,0:T(8,128)(2,1)S(1)} %pad_maximum_fusion.2), channel_id=1, source_target_pairs={{0,2},{2,0},{4,6},{6,4},{8,10},{10,8},{12,14},{14,12},{1,3},{3,1},... | collective-permute-start | bytes 983048 | tf_op jit(solution)/shard_map/ppermute | solution.py:1136
  193.6 20.2 %collective-permute-start.29 = (bf16[4,24,640]{2,1,0:T(8,128)(2,1)S(1)}, bf16[4,24,640]{2,1,0:T(8,128)(2,1)}, u32[]{:S(2)}, u32[]{:S(2)}) collective-permute-start(bf16[4,24,640]{2,1,0:T(8,128)(2,1)S(1)} %get-tuple-element.226), channel_id=1, source_target_pairs={{0,16},{16,0},{1,17},{17,1},{2,18},{18,2},{3,19},{19,3},{4,20},{20... | collective-permute-start | bytes 368648 | tf_op jit(solution)/shard_map/ppermute | solution.py:1139
  194.9 18.9 %collective-permute-start.28 = (bf16[4,2,16,640]{3,2,1,0:T(8,128)(2,1)S(1)}, bf16[4,2,16,640]{3,2,1,0:T(8,128)(2,1)S(1)}, u32[]{:S(2)}, u32[]{:S(2)}) collective-permute-start(bf16[4,2,16,640]{3,2,1,0:T(8,128)(2,1)S(1)} %get-tuple-element.224), channel_id=1, source_target_pairs={{0,2},{2,0},{4,6},{6,4},{8,10},{10,8},{12,14},{14,12},{1,3},{3,1},... | collective-permute-start | bytes 491528 | tf_op jit(solution)/shard_map/ppermute | solution.py:1136
  217.0 11.9 %collective-permute-start.39 = (bf16[4,24,640]{2,1,0:T(8,128)(2,1)S(1)}, bf16[4,24,640]{2,1,0:T(8,128)(2,1)}, u32[]{:S(2)}, u32[]{:S(2)}) collective-permute-start(bf16[4,24,640]{2,1,0:T(8,128)(2,1)S(1)} %get-tuple-element.225.refs_0_), channel_id=1, source_target_pairs={{0,1},{1,0},{2,3},{3,2},{4,5},{5,4},{6,7},{7,6},{8,9},{9,8},{10,11... | collective-permute-start | bytes 368648 | tf_op jit(solution)/shard_map/ppermute | solution.py:1142
  220.1 12.4 %collective-permute-start.34 = (bf16[160,640]{1,0:T(8,128)(2,1)S(1)}, bf16[160,640]{1,0:T(8,128)(2,1)S(1)}, u32[]{:S(2)}, u32[]{:S(2)}) collective-permute-start(bf16[160,640]{1,0:T(8,128)(2,1)S(1)} %pad_maximum_fusion.7), channel_id=1, source_target_pairs={{0,12},{2,14},{4,0},{6,2},{8,4},{10,6},{12,8},{14,10},{1,13},{3,15... | collective-permute-start | bytes 614408 | tf_op jit(solution)/shard_map/ppermute | solution.py:1132
  220.9 19.2 %collective-permute-start.33 = (bf16[160,640]{1,0:T(8,128)(2,1)S(1)}, bf16[160,640]{1,0:T(8,128)(2,1)S(1)}, u32[]{:S(2)}, u32[]{:S(2)}) collective-permute-start(bf16[160,640]{1,0:T(8,128)(2,1)S(1)} %pad_maximum_fusion.6), channel_id=1, source_target_pairs={{0,8},{2,10},{4,12},{6,14},{8,0},{10,2},{12,4},{14,6},{1,9},{3,11}... | collective-permute-start | bytes 614408 | tf_op jit(solution)/shard_map/ppermute | solution.py:1132
  222.7 17.5 %collective-permute-start.32 = (bf16[160,640]{1,0:T(8,128)(2,1)S(1)}, bf16[160,640]{1,0:T(8,128)(2,1)S(1)}, u32[]{:S(2)}, u32[]{:S(2)}) collective-permute-start(bf16[160,640]{1,0:T(8,128)(2,1)S(1)} %pad_maximum_fusion.5), channel_id=1, source_target_pairs={{0,4},{2,6},{4,8},{6,10},{8,12},{10,14},{12,0},{14,2},{1,5},{3,7},... | collective-permute-start | bytes 614408 | tf_op jit(solution)/shard_map/ppermute | solution.py:1132
  (75 other events, 544.0 us)

commit v6 on v5

v6 whole, which is shorter than its diff:
```python
import functools

import jax
import jax.numpy as jnp
from jax import lax
from jax.experimental import pallas as pl
from jax.experimental.pallas import tpu as pltpu
from jax.sharding import PartitionSpec as P

epsilon = 1e-06
f32 = jnp.float32
bf16 = jnp.bfloat16
i32 = jnp.int32
VMEM_LIMIT = 58 * 1024 * 1024
SMALL_LIMIT = 24 * 1024 * 1024
log2e = 1.4426950408889634
LANES = 128


def dot(left, right, contract):
    return lax.dot_general(left, right, (contract, ((), ())), preferred_element_type=f32)


def nn(left, right):
    return dot(left, right, ((1,), (0,)))


def nt(left, right):
    return dot(left, right, ((1,), (1,)))


def tn(left, right):
    return dot(left, right, ((0,), (0,)))


def lane_iota(shape):
    return lax.broadcasted_iota(i32, shape, len(shape) - 1)


def row_iota(shape):
    return lax.broadcasted_iota(i32, shape, 0)


def row_mean(values):
    return jnp.mean(values, axis=-1, keepdims=True)


def inverse_rms(values):
    return lax.rsqrt(row_mean(values * values) + epsilon)


def at_rows(index, size):
    return pl.ds(pl.multiple_of(index * size, size), size)


def by_rows(total, size, step):
    lax.fori_loop(0, total // size, lambda i, c: (step(at_rows(i, size)), c)[1], 0)


def swap_halves(tile, half):
    lower = lane_iota(tile.shape) % (2 * half) < half
    return jnp.where(lower, pltpu.roll(tile, LANES - half, 1), pltpu.roll(tile, half, 1))


def head_sums(tile, head_dim):
    same = row_iota((LANES, LANES)) // head_dim == lane_iota((LANES, LANES)) // head_dim
    ones = jnp.where(same, 1.0, 0.0).astype(bf16)
    return nn(tile.astype(bf16), ones)


def prep_tile(raw, cosine, sine, scale, head_dim):
    mean = head_sums(raw * raw, head_dim) * (1.0 / head_dim)
    inverse = lax.rsqrt(mean + epsilon)
    turned = raw * cosine + swap_halves(raw, head_dim // 2) * sine
    return (turned * inverse * scale).astype(bf16), inverse.astype(bf16)


def prep_tile_back(grad, low, inverse, cosine, sine, scale, head_dim):
    unit = low.astype(f32) / scale
    grad_unit = grad * scale
    mean = head_sums(grad_unit * unit, head_dim) * (1.0 / head_dim)
    grad_turned = inverse.astype(f32) * (grad_unit - unit * mean)
    return (grad_turned * cosine - swap_halves(grad_turned, head_dim // 2) * sine).astype(bf16)


def spread_pair(tile, head_dim):
    lower = lane_iota(tile.shape) < head_dim
    zero = jnp.zeros_like(tile)
    return jnp.concatenate([jnp.where(lower, tile, zero), jnp.where(lower, zero, tile)], axis=0)


def allowed_mask(first, last, key_start, rows, diagonal):
    keys = key_start + row_iota((rows, first.shape[1]))
    mask = keys >= first
    if diagonal:
        mask = mask & (keys <= last)
    return mask


def query_bounds(start_ref, m, place, group, chunk):
    first = start_ref[m : m + 1, :]
    last = (m * group + place) * chunk + lane_iota((1, chunk))
    return jnp.concatenate([first, first], axis=1), jnp.concatenate([last, last], axis=1)


def whole_spec(shape, buffers=1):
    return pl.BlockSpec(
        shape, lambda *a: (0,) * len(shape), pipeline_mode=pl.Buffered(buffers)
    )


def col_spec(size, width=LANES, skip=0):
    return pl.BlockSpec((size, width), lambda p, s: (0, lax.max(p - skip, 0)))


def row_spec(size, width, last):
    return pl.BlockSpec((size, width), lambda p, s: (lax.min(p, last), 0))


def adapter_spec(shape):
    return pl.BlockSpec(
        (1,) + shape, lambda p, s: (s[4],) + (0,) * len(shape), pipeline_mode=pl.Buffered(1)
    )


def params(small=False, limit=None):
    limit = limit or (SMALL_LIMIT if small else VMEM_LIMIT)
    return pltpu.CompilerParams(vmem_limit_bytes=limit)


def cost(flops, moved, transcendentals=0):
    return pl.CostEstimate(
        flops=int(flops), bytes_accessed=int(moved), transcendentals=int(transcendentals)
    )


def attend_kernel(dims, place, *refs):
    slabs, chunk, group, head_dim, rank, half = dims
    count = 4 + (group - 1) * 4
    pieces = refs[:count]
    (
        wq_ref, w_ref, a_ref, b_table, a_table, cos_ref, sin_ref, scale_ref, wout_ref,
        hout_ref, ownout_ref, u_ref, q_ref, k_ref, v_ref, qi_ref, ki_ref, o_ref, inv_ref,
        msg_ref, start_ref, b_ref, ah_ref, vt_ref, all_ref, seg_ref, h_ref, own_ref, raw_ref,
    ) = refs[count:]
    inner, slab, core = place[0], place[1], place[2]
    block = group * chunk
    length = slabs * block
    rows = slabs * chunk
    model = 2 * half
    step = pl.program_id(0)

    @pl.when(step == 0)
    def _():
        mine = pl.ds(pl.multiple_of(core * half, half), half)
        other = pl.ds(pl.multiple_of((1 - core) * half, half), half)
        h_ref[at_rows(slab * group + inner, chunk), :] = pieces[0][0]
        seg_ref[...] = jnp.zeros_like(seg_ref)

        def keep_segments(where, piece):
            tail = piece[chunk:, :chunk].astype(f32)
            seg_ref[pl.ds(where, 1), :] = tail[0:1]

        keep_segments(slab * group + inner, pieces[1])

        def place_piece(shift, peer, ours, theirs):
            source = lax.rem(slab - shift + slabs, slabs)
            rows_at = at_rows(source * group + peer, chunk)
            h_ref[rows_at, mine] = ours[:chunk, :]
            h_ref[rows_at, other] = theirs[:chunk, :]
            keep_segments(source * group + peer, ours)

        for shift in range(1, slabs):
            place_piece(shift, inner, pieces[2].at[shift - 1], pieces[3].at[shift - 1])
        for turn in range(1, group):
            peer = lax.rem(inner - turn + group, group)
            near, near_other, rest, rest_other = pieces[4 * turn : 4 * turn + 4]
            place_piece(0, peer, near, near_other)
            for shift in range(1, slabs):
                place_piece(shift, peer, rest.at[shift - 1], rest_other.at[shift - 1])
        for m in range(slabs):
            own_ref[m * chunk : (m + 1) * chunk, :] = h_ref[
                at_rows(m * group + inner, chunk), :
            ]
        columns = seg_ref[...].T
        for m in range(slabs):
            line = seg_ref[pl.ds(m * group + inner, 1), :]
            below = jnp.zeros((chunk, chunk), f32)
            for c in range(slabs * group):
                below = below + jnp.where(columns[:, c : c + 1] < line, 1.0, 0.0)
            start_ref[m : m + 1, :] = jnp.sum(below, axis=0, keepdims=True).astype(i32)

        for n in range(b_ref.shape[2] // head_dim):
            cols = slice(n * head_dim, (n + 1) * head_dim)
            b_ref[:, :, cols] = b_table[0, :, n]
            ah_ref[:, cols] = a_table[0, n]
        down = a_ref[0, :3].reshape(3 * rank, model)

        def low_rows(sl):
            u_ref[sl, :] = nt(h_ref[sl, :], down).astype(bf16)

        by_rows(length, 512, low_rows)
        for m in range(slabs):
            low = u_ref[at_rows(m * group + inner, chunk), :rank]
            own = slice(m * chunk, (m + 1) * chunk)
            raw_ref[own, :] = nn(low, b_ref[0])
        raw_ref[...] += nn(own_ref[...], wq_ref[0])

    last_block = lax.min(step, slabs - 1)
    hout_ref[...] = h_ref[at_rows(last_block, block), :]
    ownout_ref[...] = own_ref[at_rows(last_block, chunk), :]
    here = pl.ds(pl.multiple_of(step * LANES, LANES), LANES)
    scale = scale_ref[...]
    w_kv = jnp.concatenate([w_ref[0], w_ref[1]], axis=1)
    none = jnp.zeros((rank, LANES), bf16)
    b_kv = jnp.concatenate(
        [
            jnp.zeros((rank, 2 * LANES), bf16),
            jnp.concatenate([b_ref[1, :, here], none], axis=1),
            jnp.concatenate([none, b_ref[2, :, here]], axis=1),
        ],
        axis=0,
    )

    def keys_rows(sl):
        both = nn(h_ref[sl, :], w_kv) + nn(u_ref[sl, :], b_kv)
        k_ref[sl, :], ki_ref[sl, :] = prep_tile(
            both[:, :LANES], cos_ref[sl, :], sin_ref[sl, :], scale, head_dim
        )
        v_ref[sl, :] = both[:, LANES:].astype(bf16)

    by_rows(length, 512, keys_rows)
    for m in range(slabs):
        own = slice(m * chunk, (m + 1) * chunk)
        there = at_rows(m * group + inner, chunk)
        q_ref[own, :], qi_ref[own, :] = prep_tile(
            raw_ref[own, here], cos_ref[there, :], sin_ref[there, :], scale, head_dim
        )
    vt_ref[...] = v_ref[...].T
    for m in range(slabs):
        own = slice(m * chunk, (m + 1) * chunk)
        pair = spread_pair(q_ref[own, :], head_dim)
        first, last = query_bounds(start_ref, m, inner, group, chunk)
        total = jnp.zeros((1, 2 * chunk), f32)
        gathered = jnp.zeros((LANES, 2 * chunk), f32)
        for b in range(m + 1):
            at = slice(b * block, (b + 1) * block)
            scores = nt(k_ref[at, :], pair)
            mask = allowed_mask(first, last, b * block, block, b == m)
            weights = jnp.where(mask, jnp.exp2(scores * (0.125 * log2e)), 0.0)
            total = total + jnp.sum(weights, axis=0, keepdims=True)
            gathered = gathered + nn(vt_ref[:, at], weights.astype(bf16))
        inverse = 1.0 / total
        gathered = gathered * inverse
        upper = row_iota((LANES, chunk)) < head_dim
        final = jnp.where(upper, gathered[:, :chunk], gathered[:, chunk:])
        final = final.T.astype(bf16)
        o_ref[own, :] = final
        all_ref[own, here] = final
        inv_ref[0, m : m + 1, :] = inverse

    @pl.when(step == pl.num_programs(0) - 1)
    def _():
        low_o = all_ref[...]
        msg_ref[:, :model] = nn(low_o, wout_ref[...]).astype(bf16)
        msg_ref[:, model:] = pad_to(nt(low_o, ah_ref[...]), LANES).astype(bf16)


def run_attend(place, tokens, pieces, w, a, b, ah, cos, sin, scale, wout, group, head_dim):
    slabs, chunk, model = tokens.shape
    width = w.shape[2]
    rank = a.shape[2]
    half = model // 2
    rows = slabs * chunk
    length = rows * group
    pairs = width // LANES
    in_specs = [pl.BlockSpec((1, chunk, model), lambda p, s: (s[1], 0, 0))]
    in_specs += [whole_spec(piece.shape) for piece in pieces]
    in_specs += [
        whole_spec((1, model, width)),
        pl.BlockSpec(
            (pl.Element(2), pl.Element(model), pl.Element(LANES)),
            lambda p, s: (1, 0, p * LANES),
        ),
        adapter_spec((5, rank, model)),
        adapter_spec(b.shape[1:]),
        adapter_spec(ah.shape[1:]),
        whole_spec((length, LANES)),
        whole_spec((length, LANES)),
        col_spec(1),
        whole_spec((width, model)),
    ]
    def step_rows(size):
        return pl.BlockSpec((size, model), lambda p, s: (lax.min(p, slabs - 1), 0))

    out = [
        ((length, model), bf16, step_rows(group * chunk)),
        ((rows, model), bf16, step_rows(chunk)),
        ((length, 3 * rank), bf16, whole_spec((length, 3 * rank))),
        ((rows, width), bf16, col_spec(rows)),
        ((length, width), bf16, col_spec(length)),
        ((length, width), bf16, col_spec(length)),
        ((rows, width), bf16, col_spec(rows)),
        ((length, width), bf16, col_spec(length)),
        ((rows, width), bf16, col_spec(rows)),
        (
            (pairs, slabs, 2 * chunk),
            f32,
            pl.BlockSpec((1, slabs, 2 * chunk), lambda p, s: (p, 0, 0)),
        ),
        ((rows, model + LANES), bf16, whole_spec((rows, model + LANES))),
        ((slabs, chunk), i32, whole_spec((slabs, chunk))),
        ((3, rank, width), bf16, whole_spec((3, rank, width))),
        ((rank, width), bf16, whole_spec((rank, width))),
    ]
    return pl.pallas_call(
        functools.partial(attend_kernel, (slabs, chunk, group, head_dim, rank, half)),
        grid_spec=pltpu.PrefetchScalarGridSpec(
            num_scalar_prefetch=1,
            grid=(pairs,),
            in_specs=in_specs,
            out_specs=[o[2] for o in out],
            scratch_shapes=[
                pltpu.VMEM((LANES, length), bf16),
                pltpu.VMEM((rows, width), bf16),
                pltpu.VMEM((chunk, chunk), f32),
                pltpu.VMEM((length, model), bf16),
                pltpu.VMEM((rows, model), bf16),
                pltpu.VMEM((rows, width), f32),
            ],
        ),
        out_shape=[jax.ShapeDtypeStruct(o[0], o[1]) for o in out],
        compiler_params=params(),
        cost_estimate=cost(1e8, 1e5),
        name="attend",
    )(place, tokens, *pieces, w, w, a, b, ah, cos, sin, scale, wout)


def join_tiles(ref, *at):
    block = ref[at]
    return jnp.concatenate([block[t] for t in range(block.shape[0])], axis=1)


def feed_kernel(
    dims, place, mine_ref, other_ref, h_ref, bo_ref, rate_ref, a_ref, wgu_ref, bgu_ref, wd_ref,
    ad_ref, scales_ref, mid_ref, u_ref, gate_ref, up_ref, msg_ref, low_ref, acc_ref,
):
    rank, model, slabs = dims
    chunk = h_ref.shape[0]
    step = pl.program_id(0)

    @pl.when(step < slabs)
    def _():
        both = mine_ref[...].astype(f32) + other_ref[...].astype(f32)
        low = both[:, model : model + rank].astype(bf16)
        raw = both[:, :model] + nn(low, bo_ref[0, 0])
        unit = raw * inverse_rms(raw)
        state = h_ref[...].astype(f32)
        mixed = state + rate_ref[0:1, :] * (unit - state)
        mixed = (mixed * inverse_rms(mixed)).astype(bf16)
        mid_ref[...] = mixed
        here = at_rows(step, chunk)
        low_ref[here, :] = mixed
        down = a_ref[0, 3:5].reshape(2 * rank, model)
        u_ref[here, :] = nt(mixed, down).astype(bf16)
        acc_ref[here, :] = jnp.zeros((chunk, model + LANES), f32)

    @pl.when(step >= slabs)
    def _():
        low = low_ref[...]
        u = u_ref[...]
        gate = nn(low, wgu_ref[0]) + nn(u[:, :rank], join_tiles(bgu_ref, 0, 0))
        up = nn(low, wgu_ref[1]) + nn(u[:, rank:], join_tiles(bgu_ref, 0, 1))
        gate_ref[...] = gate.astype(bf16)
        up_ref[...] = up.astype(bf16)
        turned = gate * scales_ref[1:2, :]
        hidden = (up * scales_ref[0:1, :] * (turned / (1.0 + jnp.exp(-turned)))).astype(bf16)
        acc_ref[:, :model] += nn(hidden, wd_ref[...])
        acc_ref[:, model : model + rank] += nt(hidden, join_tiles(ad_ref, 0))

    @pl.when(step == pl.num_programs(0) - 1)
    def _():
        msg_ref[...] = acc_ref[...].astype(bf16)


def hidden_specs(skip, model, rank, block, row_width):
    tiles = block // row_width
    at = lambda f: lax.max(f - skip, 0)
    return [
        pl.BlockSpec((2, model, block), lambda f, s: (0, 0, at(f))),
        pl.BlockSpec((1, 2, tiles, rank, row_width), lambda f, s: (s[4], 0, at(f), 0, 0)),
        pl.BlockSpec((block, model), lambda f, s: (at(f), 0)),
        pl.BlockSpec((1, tiles, rank, row_width), lambda f, s: (s[4], at(f), 0, 0)),
        pl.BlockSpec((2, block), lambda f, s: (0, at(f))),
    ]


def run_feed(place, mine, other, h_own, bm, rates, a, wgu, bgu, wd, ad, scales, block, slabs):
    rows, model = h_own.shape
    chunk = rows // slabs
    hidden = wd.shape[0]
    rank = a.shape[2]
    last = slabs - 1
    out = [
        ((rows, model), bf16, row_spec(chunk, model, last)),
        ((rows, 2 * rank), bf16, whole_spec((rows, 2 * rank))),
        ((rows, hidden), bf16, col_spec(rows, block, slabs)),
        ((rows, hidden), bf16, col_spec(rows, block, slabs)),
        ((rows, model + LANES), bf16, whole_spec((rows, model + LANES))),
    ]
    return pl.pallas_call(
        functools.partial(feed_kernel, (rank, model, slabs)),
        grid_spec=pltpu.PrefetchScalarGridSpec(
            num_scalar_prefetch=1,
            grid=(slabs + hidden // block,),
            in_specs=[
                row_spec(chunk, model + LANES, last),
                row_spec(chunk, model + LANES, last),
                row_spec(chunk, model, last),
                adapter_spec((2, rank, model)),
                whole_spec((2, model)),
                adapter_spec((5, rank, model)),
            ]
            + hidden_specs(slabs, model, rank, block, ad.shape[3]),
            out_specs=[o[2] for o in out],
            scratch_shapes=[
                pltpu.VMEM((rows, model), bf16),
                pltpu.VMEM((rows, model + LANES), f32),
            ],
        ),
        out_shape=[jax.ShapeDtypeStruct(o[0], o[1]) for o in out],
        compiler_params=params(),
        cost_estimate=cost(2.4e10, 3e7),
        name="feed",
    )(place, mine, other, h_own, bm, rates, a, wgu, bgu, wd, ad, scales)


def owner_index(place, group, slabs, n_seq):
    inner, slab, seq = place
    return seq * slabs * group + slab * group + inner


def pad_to(tile, lanes):
    return jnp.pad(tile, ((0, 0), (0, lanes - tile.shape[1])))


def late_rows(rank, units):
    return max(4 * rank, 2 * units)


def folded_rows(rows, groups):
    return (rows + groups * 8 - 1) // (groups * 8) * 8


def fold(tile, groups):
    size = folded_rows(tile.shape[0], groups)
    tile = jnp.pad(tile, ((0, size * groups - tile.shape[0]), (0, 0)))
    return jnp.concatenate([tile[g * size : (g + 1) * size] for g in range(groups)], axis=1)


def unfold(block):
    groups = block.shape[1] // LANES
    return jnp.concatenate(
        [block[:, g * LANES : (g + 1) * LANES] for g in range(groups)], axis=0
    ).astype(f32)


def feed_back_kernel(
    dims, place, mine_ref, other_ref, mid_ref, g_own_ref, g_mine_ref, g_other_ref, bd_ref,
    rate_ref, a_ref, u_ref, gate_ref, up_ref, wgu_ref, bgu_ref, wd_ref, ad_ref, scales_ref,
    out_ref, res_ref, msg_ref, table_ref,
    gd_ref, gdt_ref, ut_ref, udt_ref, gud_ref, gudt_ref, low_ref, acc_ref, gu_ref, hid_ref,
    g_ref, lo_ref,
):
    slabs, chunk, group, n_seq, rank, model, row_width, hidden_rows = dims
    half = model // 2
    step = pl.program_id(0)
    slab, core = place[1], place[2]
    block = gate_ref.shape[1]

    @pl.when(step < slabs)
    def _():
        mine = pl.ds(pl.multiple_of(core * half, half), half)
        other = pl.ds(pl.multiple_of((1 - core) * half, half), half)
        shift = lax.rem(slab - step + slabs, slabs)

        @pl.when(shift == 0)
        def _():
            g_ref[...] = g_own_ref[0]

        @pl.when(shift > 0)
        def _():
            g_ref[:, mine] = g_mine_ref[shift - 1]
            g_ref[:, other] = g_other_ref[shift - 1]

        here = at_rows(step, chunk)
        both = mine_ref[...].astype(f32) + other_ref[...].astype(f32)
        low = both[:, model : model + rank].astype(bf16)
        hid_ref[here, :] = low
        raw = both[:, :model] + nn(low, bd_ref[0, 1])
        raw_inv = inverse_rms(raw)
        unit = raw * raw_inv
        state = mid_ref[...]
        low_ref[here, :] = state
        state = state.astype(f32)
        rate = rate_ref[1:2, :]
        mixed = state + rate * (unit - state)
        mixed_inv = inverse_rms(mixed)
        out = mixed * mixed_inv
        lo_ref[...] = out.astype(bf16)
        grad = g_ref[...].astype(f32)
        grad_mixed = mixed_inv * (grad - out * row_mean(grad * out))
        res_ref[...] = (1.0 - rate) * grad_mixed
        grad_unit = rate * grad_mixed
        gd_ref[here, :] = (raw_inv * (grad_unit - unit * row_mean(grad_unit * unit))).astype(bf16)
        out_ref[0] = lo_ref[:, mine]
        acc_ref[here, :] = jnp.zeros((chunk, model), f32)
        gu_ref[here, :] = jnp.zeros((chunk, 2 * rank), f32)

    @pl.when(step == slabs)
    def _():
        ut_ref[...] = u_ref[...].T
        udt_ref[...] = hid_ref[...].T
        low_gud = nt(gd_ref[...], bd_ref[0, 1]).astype(bf16)
        gud_ref[...] = low_gud
        gudt_ref[...] = low_gud.T

    @pl.when(step >= slabs)
    def _():
        grad_hidden = nt(gd_ref[...], wd_ref[...]) + nn(gud_ref[...], join_tiles(ad_ref, 0))
        gate = gate_ref[...].astype(f32)
        up = up_ref[...].astype(f32)
        up_scale = scales_ref[0:1, :]
        gate_scale = scales_ref[1:2, :]
        turned = gate * gate_scale
        sigmoid = 1.0 / (1.0 + jnp.exp(-turned))
        silu = turned * sigmoid
        up_scaled = up * up_scale
        hidden = (up_scaled * silu).astype(bf16)
        grad_up = (grad_hidden * up_scale * silu).astype(bf16)
        slope = sigmoid * (1.0 + turned * (1.0 - sigmoid)) * gate_scale
        grad_gate = (grad_hidden * up_scaled * slope).astype(bf16)
        acc_ref[...] += nt(grad_gate, wgu_ref[0]) + nt(grad_up, wgu_ref[1])
        gu_ref[:, :rank] += nt(grad_gate, join_tiles(bgu_ref, 0, 0))
        gu_ref[:, rank:] += nt(grad_up, join_tiles(bgu_ref, 0, 1))
        ut = ut_ref[...]
        parts = jnp.concatenate(
            [nn(gudt_ref[...], hidden), nn(ut[:rank], grad_gate), nn(ut[rank:], grad_up)], axis=0
        ).astype(bf16)
        tiles = block // row_width
        for tile in range(tiles):
            gdt_ref[(step - slabs) * tiles + tile] = parts[
                :, tile * row_width : (tile + 1) * row_width
            ]

    @pl.when(step == pl.num_programs(0) - 1)
    def _():
        low_gu = gu_ref[...].astype(bf16)
        down = a_ref[0, 3:5].reshape(2 * rank, model)
        msg_ref[...] = (acc_ref[...] + nn(low_gu, down)).astype(bf16)
        low = low_ref[...]
        model_rows = jnp.concatenate(
            [nn(low_gu.T, low), nn(udt_ref[...], gd_ref[...])], axis=0
        ).astype(bf16).astype(f32)
        ranks = 3 * rank
        units = ranks * hidden_rows
        padded = (units + LANES - 1) // LANES * LANES
        flat = gdt_ref[...].reshape(units, row_width)
        lanes = lane_iota((1, padded))
        target = lanes % hidden_rows * ranks + lanes // hidden_rows
        target = jnp.where(lanes < units, target, -1)
        moved = jnp.where(row_iota((units, padded)) == target, 1.0, 0.0).astype(bf16)
        turned_rows = tn(flat, moved)
        owners = n_seq * slabs * group
        cols = model // owners
        units_each = row_width // owners
        for y in range(group):
            for z in range(slabs):
                for x in range(n_seq):
                    d = owner_index((y, z, x), group, slabs, n_seq)
                    head = pad_to(model_rows[:, d * cols : (d + 1) * cols], LANES)
                    mine = turned_rows[d * units_each : (d + 1) * units_each]
                    tail = [
                        mine[:, t * LANES : (t + 1) * LANES] for t in range(padded // LANES)
                    ]
                    packed = jnp.concatenate([head] + tail, axis=0)
                    table_ref[y, z, x] = fold(packed, half // LANES).astype(bf16)


def run_feed_back(
    place, mine, other, mid, cotangent, g_mine, g_other, bm, rates, a, u, gate, up, wgu, bgu,
    wd, ad, scales, block, group, n_seq,
):
    slabs, chunk, model = cotangent.shape
    rows = slabs * chunk
    half = model // 2
    hidden = wd.shape[0]
    rank = a.shape[2]
    row_width = ad.shape[3]
    last = slabs - 1
    hidden_rows = hidden // row_width
    owners = n_seq * slabs * group
    padded = (3 * rank * hidden_rows + LANES - 1) // LANES * LANES
    table_rows = 3 * rank + row_width // owners * (padded // LANES)
    table = (group, slabs, n_seq, folded_rows(table_rows, half // LANES), half)
    out = [
        (
            (slabs, chunk, half),
            bf16,
            pl.BlockSpec((1, chunk, half), lambda f, s: (lax.min(f, last), 0, 0)),
        ),
        ((rows, model), f32, row_spec(chunk, model, last)),
        ((rows, model), bf16, whole_spec((rows, model))),
        (table, bf16, whole_spec(table)),
    ]
    return pl.pallas_call(
        functools.partial(
            feed_back_kernel,
            (slabs, chunk, group, n_seq, rank, model, row_width, hidden_rows),
        ),
        grid_spec=pltpu.PrefetchScalarGridSpec(
            num_scalar_prefetch=1,
            grid=(slabs + hidden // block,),
            in_specs=[
                row_spec(chunk, model + LANES, last),
                row_spec(chunk, model + LANES, last),
                row_spec(chunk, model, last),
                pl.BlockSpec(
                    (1, chunk, model), lambda f, s: (s[1], 0, 0), pipeline_mode=pl.Buffered(1)
                ),
                whole_spec((slabs - 1, chunk, half)),
                whole_spec((slabs - 1, chunk, half)),
                adapter_spec((2, rank, model)),
                whole_spec((2, model)),
                adapter_spec((5, rank, model)),
                whole_spec((rows, 2 * rank)),
                col_spec(rows, block, slabs),
                col_spec(rows, block, slabs),
            ]
            + hidden_specs(slabs, model, rank, block, row_width),
            out_specs=[o[2] for o in out],
            scratch_shapes=[
                pltpu.VMEM((rows, model), bf16),
                pltpu.VMEM((hidden_rows, 3 * rank, row_width), bf16),
                pltpu.VMEM((2 * rank, rows), bf16),
                pltpu.VMEM((rank, rows), bf16),
                pltpu.VMEM((rows, rank), bf16),
                pltpu.VMEM((rank, rows), bf16),
                pltpu.VMEM((rows, model), bf16),
                pltpu.VMEM((rows, model), f32),
                pltpu.VMEM((rows, 2 * rank), f32),
                pltpu.VMEM((rows, rank), bf16),
                pltpu.VMEM((chunk, model), bf16),
                pltpu.VMEM((chunk, model), bf16),
            ],
        ),
        out_shape=[jax.ShapeDtypeStruct(o[0], o[1]) for o in out],
        compiler_params=params(),
        cost_estimate=cost(3e10, 4e7),
        name="feed_back",
    )(
        place, mine, other, mid, cotangent, g_mine, g_other, bm, rates, a, u, gate, up, wgu,
        bgu, wd, ad, scales,
    )


def attend_back_kernel(
    dims, place, res_ref, gm_ref, go_ref, h_ref, am_ref, ao_ref, rate_ref, bo_ref, wout_ref,
    ah_ref, start_ref, q_ref, k_ref, v_ref, o_ref, inv_ref, qi_ref, ki_ref, cos_ref, sin_ref,
    scale_ref,
    gq_ref, gk_ref, gv_ref, gres_ref, gbo_ref, gah_ref,
    kt_ref, gqt_ref, ga_ref, guo_ref, guot_ref, uo_ref,
):
    slabs, chunk, group, head_dim, rank, model = dims
    inner = place[0]
    step = pl.program_id(0)

    @pl.when(step < slabs)
    def _():
        here = at_rows(step, chunk)
        grad = res_ref[...] + gm_ref[...].astype(f32) + go_ref[...].astype(f32)
        both = am_ref[...].astype(f32) + ao_ref[...].astype(f32)
        low = both[:, model : model + rank].astype(bf16)
        uo_ref[here, :] = low
        raw = both[:, :model] + nn(low, bo_ref[0, 0])
        raw_inv = inverse_rms(raw)
        unit = raw * raw_inv
        state = h_ref[...].astype(f32)
        rate = rate_ref[0:1, :]
        mixed = state + rate * (unit - state)
        mixed_inv = inverse_rms(mixed)
        out = mixed * mixed_inv
        grad_mixed = mixed_inv * (grad - out * row_mean(grad * out))
        gres_ref[...] = (1.0 - rate) * grad_mixed
        grad_unit = rate * grad_mixed
        ga_ref[here, :] = (raw_inv * (grad_unit - unit * row_mean(grad_unit * unit))).astype(bf16)

    @pl.when(step == slabs)
    def _():
        gbo_ref[...] = nn(uo_ref[...].T, ga_ref[...])
        low_g = nt(ga_ref[...], bo_ref[0, 0]).astype(bf16)
        guo_ref[...] = low_g
        guot_ref[...] = low_g.T

    @pl.when(step >= slabs)
    def _():
        attend_back_pair(
            dims, inner, wout_ref, ah_ref, start_ref, q_ref, k_ref, v_ref, o_ref, inv_ref,
            qi_ref, ki_ref, cos_ref, sin_ref, scale_ref, gq_ref, gk_ref, gv_ref, gah_ref,
            kt_ref, gqt_ref, ga_ref, guo_ref, guot_ref,
        )


def attend_back_pair(
    dims, inner, wout_ref, ah_ref, start_ref, q_ref, k_ref, v_ref, o_ref, inv_ref, qi_ref,
    ki_ref, cos_ref, sin_ref, scale_ref, gq_ref, gk_ref, gv_ref, gah_ref, kt_ref, gqt_ref,
    ga_ref, guo_ref, guot_ref,
):
    slabs, chunk, group, head_dim, rank, model = dims
    block = group * chunk
    kt_ref[...] = k_ref[...].T
    scale = scale_ref[...]
    grad_o = (nt(ga_ref[...], wout_ref[...]) + nn(guo_ref[...], ah_ref[...])).astype(bf16)
    gah_ref[...] = nn(guot_ref[...], o_ref[...])
    pairs_q, pairs_g, deltas, bounds = [], [], [], []
    for m in range(slabs):
        own = slice(m * chunk, (m + 1) * chunk)
        pairs_q.append(spread_pair(q_ref[own, :], head_dim))
        grad = grad_o[own]
        pairs_g.append(spread_pair(grad, head_dim))
        products = (grad.astype(f32) * o_ref[own, :].astype(f32)).T
        deltas.append(
            jnp.concatenate(
                [
                    jnp.sum(products[:head_dim], axis=0, keepdims=True),
                    jnp.sum(products[head_dim:], axis=0, keepdims=True),
                ],
                axis=1,
            )
        )
        bounds.append(query_bounds(start_ref, m, inner, group, chunk))
    for b in range(slabs):
        at = slice(b * block, (b + 1) * block)
        grad_key = jnp.zeros((block, LANES), f32)
        grad_value = jnp.zeros((block, LANES), f32)
        for m in range(b, slabs):
            first, last = bounds[m]
            scores = nt(k_ref[at, :], pairs_q[m])
            mask = allowed_mask(first, last, b * block, block, b == m)
            weights = jnp.exp2(scores * (0.125 * log2e)) * inv_ref[0, m : m + 1, :]
            weights = jnp.where(mask, weights, 0.0)
            grad_value = grad_value + nn(weights.astype(bf16), pairs_g[m])
            grad_weights = nt(v_ref[at, :], pairs_g[m])
            grad_scores = (weights * (grad_weights - deltas[m])).astype(bf16)
            grad_key = grad_key + nn(grad_scores, pairs_q[m])
            part = nn(kt_ref[:, at], grad_scores)
            if b == 0:
                gqt_ref[m] = part
            else:
                gqt_ref[m] += part
        gv_ref[at, :] = grad_value.astype(bf16)
        gk_ref[at, :] = prep_tile_back(
            grad_key * 0.125, k_ref[at, :], ki_ref[at, :], cos_ref[at, :], sin_ref[at, :],
            scale, head_dim,
        )
    upper = row_iota((LANES, chunk)) < head_dim
    for m in range(slabs):
        own = slice(m * chunk, (m + 1) * chunk)
        both = gqt_ref[m]
        grad = jnp.where(upper, both[:, :chunk], both[:, chunk:]).T * 0.125
        there = at_rows(m * group + inner, chunk)
        gq_ref[own, :] = prep_tile_back(
            grad, q_ref[own, :], qi_ref[own, :], cos_ref[there, :], sin_ref[there, :],
            scale, head_dim,
        )


def run_attend_back(
    place, res, gm, go, h_own, am, ao, rates, bm, wout, ah, start, q, k, v, o, inv, qi, ki, cos, sin, scale, slabs, group, head_dim,
):
    rows, model = h_own.shape
    chunk = rows // slabs
    width = q.shape[1]
    length = k.shape[0]
    rank = bm.shape[2]
    pairs = width // LANES
    last = slabs - 1
    wide = row_spec(chunk, model + LANES, last)
    narrow = row_spec(chunk, model, last)
    cols = lambda size: col_spec(size, LANES, slabs)
    out = [
        ((rows, width), bf16, cols(rows)),
        ((length, width), bf16, cols(length)),
        ((length, width), bf16, cols(length)),
        ((rows, model), f32, narrow),
        ((rank, model), f32, whole_spec((rank, model))),
        ((rank, width), f32, cols(rank)),
    ]
    return pl.pallas_call(
        functools.partial(attend_back_kernel, (slabs, chunk, group, head_dim, rank, model)),
        grid_spec=pltpu.PrefetchScalarGridSpec(
            num_scalar_prefetch=1,
            grid=(slabs + pairs,),
            in_specs=[
                narrow,
                narrow,
                narrow,
                narrow,
                wide,
                wide,
                whole_spec((2, model)),
                adapter_spec((2, rank, model)),
                pl.BlockSpec((LANES, model), lambda p, s: (lax.max(p - slabs, 0), 0)),
                cols(rank),
                whole_spec((slabs, chunk)),
                cols(rows),
                cols(length),
                cols(length),
                cols(rows),
                pl.BlockSpec(
                    (1, slabs, 2 * chunk), lambda p, s: (lax.max(p - slabs, 0), 0, 0)
                ),
                cols(rows),
                cols(length),
                whole_spec((length, LANES)),
                whole_spec((length, LANES)),
                cols(1),
            ],
            out_specs=[o_[2] for o_ in out],
            scratch_shapes=[
                pltpu.VMEM((LANES, length), bf16),
                pltpu.VMEM((slabs, LANES, 2 * chunk), f32),
                pltpu.VMEM((rows, model), bf16),
                pltpu.VMEM((rows, rank), bf16),
                pltpu.VMEM((rank, rows), bf16),
                pltpu.VMEM((rows, rank), bf16),
            ],
        ),
        out_shape=[jax.ShapeDtypeStruct(o_[0], o_[1]) for o_ in out],
        compiler_params=params(),
        cost_estimate=cost(3e10, 4e7),
        name="attend_back",
    )(
        place, res, gm, go, h_own, am, ao, rates, bm, wout, ah, start, q, k, v, o, inv, qi, ki,
        cos, sin, scale,
    )


def apart(blocks):
    none = jnp.zeros_like(blocks[0])
    return jnp.concatenate(
        [
            jnp.concatenate([b if n == m else none for n in range(len(blocks))], axis=1)
            for m, b in enumerate(blocks)
        ],
        axis=0,
    )


def others_kernel(
    place, gk_ref, gv_ref, wk_ref, wv_ref, a_ref, b_ref, keep_ref, send_ref, low_ref
):
    rows, width = keep_ref.shape[1], gk_ref.shape[-1]
    half = keep_ref.shape[2]
    rank = b_ref.shape[1]
    both = jnp.concatenate(
        [gk_ref[...].reshape(rows, width), gv_ref[...].reshape(rows, width)], axis=1
    )
    turn = pl.program_id(1)

    @pl.when(turn == 0)
    def _():
        low_ref[...] = nt(both, apart([b_ref[1], b_ref[2]])).astype(bf16)

    weights = jnp.concatenate([wk_ref[0], wv_ref[0]], axis=1)
    part = nt(both, weights) + nn(low_ref[...], a_ref[0, 1:3].reshape(2 * rank, half))

    @pl.when(turn == 0)
    def _():
        send_ref[0] = part.astype(bf16)

    @pl.when(turn == 1)
    def _():
        keep_ref[0] = part


def half_weight(half, width, member):
    return pl.BlockSpec(
        (1, half, width), lambda *a: (member, lax.rem(a[-1][2] + 1 + a[-2], 2), 0)
    )


def half_factors(rank, half):
    return pl.BlockSpec(
        (1, 5, rank, half), lambda *a: (a[-1][4], 0, 0, lax.rem(a[-1][2] + 1 + a[-2], 2))
    )


def run_others(place, gk, gv, w, a, b, slabs, group):
    length, width = gk.shape
    chunk = length // (slabs * group)
    rows = slabs * chunk
    half = w.shape[1] // 2
    rank = b.shape[1]
    shaped = (slabs, group, chunk, width)
    peer = pl.BlockSpec(
        (slabs, 1, chunk, width), lambda g, t, s: (0, lax.rem(s[0] + 1 + g, group), 0, 0)
    )
    return pl.pallas_call(
        others_kernel,
        grid_spec=pltpu.PrefetchScalarGridSpec(
            num_scalar_prefetch=1,
            grid=(group - 1, 2),
            in_specs=[
                peer,
                peer,
                half_weight(half, width, 1),
                half_weight(half, width, 2),
                half_factors(rank, half),
                whole_spec((3, rank, width)),
            ],
            out_specs=[pl.BlockSpec((1, rows, half), lambda g, t, s: (g, 0, 0))] * 2,
            scratch_shapes=[pltpu.VMEM((rows, 2 * rank), bf16)],
        ),
        out_shape=[
            jax.ShapeDtypeStruct((group - 1, rows, half), f32),
            jax.ShapeDtypeStruct((group - 1, rows, half), bf16),
        ],
        compiler_params=params(True),
        cost_estimate=cost(7e9, 1e7),
        name="others",
    )(place, gk.reshape(shaped), gv.reshape(shaped), w, w, a, b)


def own_kernel(
    place, gq_ref, gk_ref, gv_ref, wq_ref, wk_ref, wv_ref, a_ref, b_ref, res_ref, keep_ref,
    send_ref, low_ref,
):
    rows, width = gq_ref.shape
    half = keep_ref.shape[1]
    rank = b_ref.shape[1]
    grads = jnp.concatenate(
        [gq_ref[...], gk_ref[...].reshape(rows, width), gv_ref[...].reshape(rows, width)], axis=1
    )
    turn = pl.program_id(0)

    @pl.when(turn == 0)
    def _():
        low_ref[...] = nt(grads, apart([b_ref[0], b_ref[1], b_ref[2]])).astype(bf16)

    weights = jnp.concatenate([wq_ref[0], wk_ref[0], wv_ref[0]], axis=1)
    part = nt(grads, weights) + nn(low_ref[...], a_ref[0, 0:3].reshape(3 * rank, half))

    @pl.when(turn == 0)
    def _():
        send_ref[...] = part.astype(bf16)

    @pl.when(turn == 1)
    def _():
        keep_ref[...] = part + res_ref[...]


def run_own(place, gq, gk, gv, w, a, b, res, slabs, group):
    length, width = gk.shape
    rows, model = res.shape
    chunk = rows // slabs
    half = model // 2
    rank = b.shape[1]
    shaped = (slabs, group, chunk, width)
    peer = pl.BlockSpec((slabs, 1, chunk, width), lambda t, s: (0, s[0], 0, 0))
    out = [((rows, half), f32), ((rows, half), bf16)]
    return pl.pallas_call(
        own_kernel,
        grid_spec=pltpu.PrefetchScalarGridSpec(
            num_scalar_prefetch=1,
            grid=(2,),
            in_specs=[
                whole_spec((rows, width)),
                peer,
                peer,
                half_weight(half, width, 0),
                half_weight(half, width, 1),
                half_weight(half, width, 2),
                half_factors(rank, half),
                whole_spec((3, rank, width)),
                pl.BlockSpec((rows, half), lambda t, s: (0, s[2])),
            ],
            out_specs=[whole_spec(o[0]) for o in out],
            scratch_shapes=[pltpu.VMEM((rows, 3 * rank), bf16)],
        ),
        out_shape=[jax.ShapeDtypeStruct(o[0], o[1]) for o in out],
        compiler_params=params(True),
        cost_estimate=cost(7e9, 1e7),
        name="own",
    )(place, gq, gk.reshape(shaped), gv.reshape(shaped), w, w, w, a, b, res)


def grads_kernel(
    dims, place, gq_ref, gk_ref, gv_ref, b_ref, u_ref, h_ref, gbo_ref, gah_ref, table_ref,
    uq_ref, low_ref,
):
    slabs, chunk, group, n_seq, rank, model, head_dim = dims
    inner = place[0]
    width = gq_ref.shape[1]
    heads = width // head_dim
    gq = gq_ref[...]
    both = jnp.concatenate([gk_ref[...], gv_ref[...]], axis=1)
    low_q = nt(gq, b_ref[0]).astype(bf16)
    low_ref[:, : 2 * rank] = nt(both, apart([b_ref[1], b_ref[2]])).astype(bf16)
    low_ref[:, 2 * rank :] = jnp.zeros((low_ref.shape[0], rank), bf16)
    for m in range(slabs):
        there = at_rows(m * group + inner, chunk)
        uq_ref[m * chunk : (m + 1) * chunk, :] = u_ref[there, :]
        low_ref[there, 2 * rank :] = low_q[m * chunk : (m + 1) * chunk]
    products = nn(low_ref[...].T, h_ref[...])
    model_rows = jnp.concatenate(
        [products[2 * rank :], products[: 2 * rank], gbo_ref[...]], axis=0
    ).astype(bf16).astype(f32)
    uqt = uq_ref[...].T
    pair = nn(u_ref[...].T[rank:], both)
    head_rows = jnp.concatenate(
        [gah_ref[...], nn(uqt[:rank], gq), pair[:rank, :width], pair[rank:, width:]], axis=0
    ).astype(bf16)
    owners = n_seq * slabs * group
    cols = model // owners
    each = head_dim // owners
    units = heads * each
    spots = lax.broadcasted_iota(i32, (width, 1), 0)
    owner = spots // units
    inside = spots % units
    source = inside // each * head_dim + owner * each + inside % each
    moved = jnp.where(lane_iota((width, width)) == source, 1.0, 0.0).astype(bf16)
    turned = nt(moved, head_rows)
    for y in range(group):
        for z in range(slabs):
            for x in range(n_seq):
                d = owner_index((y, z, x), group, slabs, n_seq)
                left = model_rows[:, d * cols : (d + 1) * cols]
                heads_part = turned[d * units : (d + 1) * units]
                right = jnp.concatenate(
                    [heads_part[:, rank:], pad_to(heads_part[:, :rank], 3 * rank)], axis=0
                )
                tall = late_rows(rank, units)
                packed = jnp.concatenate(
                    [
                        jnp.pad(left, ((0, tall - left.shape[0]), (0, 0))),
                        jnp.pad(right, ((0, tall - right.shape[0]), (0, 0))),
                    ],
                    axis=1,
                )
                packed = pad_to(packed, LANES)
                table_ref[y, z, x] = fold(packed, table_ref.shape[4] // LANES).astype(bf16)


def run_grads(place, gq, gk, gv, b, u, h, gbo, gah, slabs, group, n_seq, head_dim):
    length, width = gk.shape
    rows, model = gq.shape[0], h.shape[1]
    chunk = rows // slabs
    rank = b.shape[1]
    heads = width // head_dim
    owners = n_seq * slabs * group
    units = heads * (head_dim // owners)
    half = model // 2
    shape = (group, slabs, n_seq, folded_rows(late_rows(rank, units), half // LANES), half)
    operands = (gq, gk, gv, b, u, h, gbo, gah)
    return pl.pallas_call(
        functools.partial(grads_kernel, (slabs, chunk, group, n_seq, rank, model, head_dim)),
        grid_spec=pltpu.PrefetchScalarGridSpec(
            num_scalar_prefetch=1,
            grid=(1,),
            in_specs=[whole_spec(operand.shape) for operand in operands],
            out_specs=whole_spec(shape),
            scratch_shapes=[
                pltpu.VMEM((rows, 3 * rank), bf16),
                pltpu.VMEM((length, 3 * rank), bf16),
            ],
        ),
        out_shape=jax.ShapeDtypeStruct(shape, bf16),
        compiler_params=params(True),
        cost_estimate=cost(1e10, 1e7),
        name="grads",
    )(place, *operands)


def join_kernel(slabs, place, *refs):
    out_ref = refs[-1]
    chunk, half = out_ref.shape[1], refs[0].shape[-1]
    core, slab = place[2], place[1]
    for shift in range(slabs):
        source = lax.rem(slab - shift + slabs, slabs)
        for which, ref in ((core, refs[shift]), (1 - core, refs[slabs + shift])):
            out_ref[source, :, pl.ds(pl.multiple_of(which * half, half), half)] = ref[
                :chunk, :
            ].astype(out_ref.dtype)


def run_join(place, mine, other, chunk, dtype):
    slabs = len(mine)
    half = mine[0].shape[1]
    return pl.pallas_call(
        functools.partial(join_kernel, slabs),
        grid_spec=pltpu.PrefetchScalarGridSpec(
            num_scalar_prefetch=1,
            grid=(1,),
            in_specs=[whole_spec(piece.shape) for piece in (*mine, *other)],
            out_specs=whole_spec((slabs, chunk, 2 * half)),
        ),
        out_shape=jax.ShapeDtypeStruct((slabs, chunk, 2 * half), dtype),
        compiler_params=params(True),
        cost_estimate=cost(1e6, 8e6),
        name="join",
    )(place, *mine, *other)


def for_tables(where, place, index, refs, put):
    n_seq, slabs, chunk, size = where
    home, home_other = refs[:slabs], refs[slabs : 2 * slabs]
    far, far_other = refs[2 * slabs : 2 * slabs + n_seq - 1], refs[2 * slabs + n_seq - 1 :]
    for r in range(slabs):
        at = pl.ds(pl.multiple_of(chunk + place[3] * size, 8), size)
        put(index[0, r], unfold(home[r][at, :]), unfold(home_other[r][at, :]))
    for s in range(1, n_seq):

        def one(r, carry, s=s):
            put(index[s, r], unfold(far[s - 1][r]), unfold(far_other[s - 1][r]))
            return carry

        lax.fori_loop(0, slabs, one, 0)


def unpack_early_kernel(dims, where, place, index, *refs):
    rank, cols, each, hidden_rows, tiles = dims
    am_ref, bm_ref, ad_ref, bd_ref = refs[-4:]
    core = place[2]

    def put(adapter, block, other):
        both = block[: 2 * rank] + other[: 2 * rank]
        am = jnp.where(core == 0, both[:, : cols // 2], both[:, cols // 2 : cols])
        am_ref[adapter] = am.reshape(2, rank, cols // 2)
        bm_ref[adapter] = block[2 * rank : 3 * rank, :cols]
        base = 3 * rank
        wide = jnp.concatenate(
            [block[base + t * each : base + (t + 1) * each] for t in range(tiles)], axis=1
        )
        for k in range(rank):
            ad_ref[adapter, k] = wide[:, k * hidden_rows : (k + 1) * hidden_rows]
        for j in range(2):
            for k in range(rank):
                at = ((j + 1) * rank + k) * hidden_rows
                bd_ref[adapter, j, k] = wide[:, at : at + hidden_rows]

    for_tables(where, place, index, refs[:-4], put)


def unpack_late_kernel(dims, where, place, index, *refs):
    rank, cols, heads, each = dims
    am_gu_ref, bm_down_ref, am_ref, bm_ref, ah_ref, bh_ref = refs[-6:]
    core = place[2]

    def put(adapter, block, other):
        both = block[: 3 * rank] + other[: 3 * rank]
        am = jnp.where(core == 0, both[:, : cols // 2], both[:, cols // 2 : cols])
        am_ref[adapter, 0:3] = am.reshape(3, rank, cols // 2)
        am_ref[adapter, 3:5] = am_gu_ref[adapter]
        bm_ref[adapter, 0] = block[3 * rank : 4 * rank, :cols]
        bm_ref[adapter, 1] = bm_down_ref[adapter]
        units = heads * each
        for n in range(heads):
            at = n * each
            ah_ref[adapter, n] = block[units + at : units + at + each, cols : cols + rank]
            for j in range(3):
                lanes = slice(cols + j * rank, cols + (j + 1) * rank)
                bh_ref[adapter, j, n] = block[at : at + each, lanes]

    for_tables(where, place, index, refs[:-6], put)


def run_unpack(kernel, dims, where, place, index, tables, extra, shapes, name):
    operands = [*tables, *extra]
    return pl.pallas_call(
        functools.partial(kernel, dims, where),
        grid_spec=pltpu.PrefetchScalarGridSpec(
            num_scalar_prefetch=2,
            grid=(1,),
            in_specs=[whole_spec(operand.shape) for operand in operands],
            out_specs=[whole_spec(shape) for shape in shapes],
        ),
        out_shape=[jax.ShapeDtypeStruct(shape, f32) for shape in shapes],
        compiler_params=params(True),
        cost_estimate=cost(1e6, 8e6),
        name=name,
    )(place, index, *operands)


def pick(array, index):
    return lax.dynamic_index_in_dim(array, index, 0, keepdims=False)


def body(
    tokens, segments, adapter_index, w_attn_in, w_attn_out, w_gate_up, w_down, qk_scale,
    mix_rates, mlp_scales, a_model, b_model, a_heads, b_heads, a_hidden, b_hidden, cotangent,
):
    slabs, chunk, model = tokens.shape
    n_seq = lax.axis_size("seq")
    n_ctx = lax.axis_size("ctx")
    group = n_ctx // slabs
    local_width = w_attn_out.shape[0]
    head_dim = a_heads.shape[-1]
    row_width = a_hidden.shape[-1]
    local_hidden = w_down.shape[0]
    local_heads = local_width // head_dim
    rank = a_model.shape[2]
    adapters = a_model.shape[0]
    half = model // 2
    ctx_place = lax.axis_index("ctx")
    slab = ctx_place // group
    inner = ctx_place % group
    core = lax.axis_index("wt")
    seq_place = lax.axis_index("seq")
    owners = n_seq * n_ctx
    rows = slabs * chunk
    length = rows * group
    place = jnp.stack([inner, slab, core, seq_place, pick(adapter_index, slab)]).astype(i32)
    a_heads = jnp.transpose(a_heads, (0, 2, 1, 3))
    b_heads = jnp.transpose(b_heads, (0, 1, 3, 2, 4))
    a_hidden = jnp.transpose(a_hidden, (0, 2, 1, 3))
    b_hidden = jnp.transpose(b_hidden, (0, 1, 3, 2, 4))

    def to_slab(array, shift):
        pairs = [(c, (c + shift * group) % n_ctx) for c in range(n_ctx)]
        return lax.ppermute(array, "ctx", pairs)

    def within_slab(array, shift):
        pairs = [(c, c - c % group + (c % group + shift) % group) for c in range(n_ctx)]
        return lax.ppermute(array, "ctx", pairs)

    def to_seq(array, shift):
        return lax.ppermute(array, "seq", [(c, (c + shift) % n_seq) for c in range(n_seq)])

    def other_core(array):
        return lax.ppermute(array, "wt", [(0, 1), (1, 0)])

    def half_piece(array, index, which):
        return lax.dynamic_slice(array, (index, 0, which * half), (1, chunk, half))[0]

    def token_piece(index):
        seg = jnp.pad(pick(segments, index).astype(bf16), (0, half - chunk))
        return jnp.concatenate(
            [half_piece(tokens, index, core), jnp.broadcast_to(seg, (8, half))], axis=0
        )

    tie = lax.optimization_barrier

    spot = (jnp.arange(LANES, dtype=i32) % (head_dim // 2)).astype(f32)
    frequency = 10000.0 ** (-spot / (head_dim // 2))
    turn = jnp.arange(length, dtype=i32).astype(f32)[:, None] * frequency[None, :]
    cos = jnp.cos(turn)
    lower = jnp.arange(LANES) % head_dim < head_dim // 2
    sin = jnp.sin(turn) * jnp.where(lower, -1.0, 1.0)[None, :]
    scale = qk_scale[None, :]

    own_piece = token_piece(slab)
    got = [own_piece] + [
        to_slab(token_piece((slab + shift) % slabs), shift) for shift in range(1, slabs)
    ]
    index = [adapter_index]
    for shift in range(1, n_seq):
        index.append(to_seq(adapter_index, shift))
    got, cos, sin, place, index = tie((got, cos, sin, place, index))
    near = [within_slab(own_piece, turn) for turn in range(1, group)]
    g_send = [half_piece(cotangent, (slab + shift) % slabs, core) for shift in range(1, slabs)]
    rest, near, g_send = tie((jnp.stack(got[1:]), near, g_send))
    rest_other = other_core(rest)
    peers = [within_slab(rest, turn) for turn in range(1, group)]
    g_mine = [to_slab(g_send[shift - 1], shift) for shift in range(1, slabs)]
    pieces = [own_piece, rest, rest_other]
    for turn in range(1, group):
        pieces += [
            near[turn - 1], other_core(near[turn - 1]),
            peers[turn - 1], other_core(peers[turn - 1]),
        ]
    h_full, h_own, u, q, k, v, qi, ki, o, inv, attn_msg, start, bh, ah = run_attend(
        place, tokens, pieces, w_attn_in, a_model, b_heads, a_heads, cos, sin, scale,
        w_attn_out, group, head_dim,
    )
    g_mine, attn_msg = tie((g_mine, attn_msg))
    attn_other = other_core(attn_msg)
    g_mine, attn_msg = tie((jnp.stack(g_mine), attn_msg))
    g_mine, attn_other = tie((g_mine, attn_other))
    g_other = other_core(g_mine)
    mid, u_gu, gate, up, down_msg = run_feed(
        place, attn_msg, attn_other, h_own, b_model, mix_rates, a_model, w_gate_up, b_hidden,
        w_down, a_hidden, mlp_scales, 512, slabs,
    )
    g_other, down_msg = tie((g_other, down_msg))
    down_other = other_core(down_msg)
    out_half, mid_res, mid_msg, early = run_feed_back(
        place, down_msg, down_other, mid, cotangent, g_mine, g_other, b_model, mix_rates,
        a_model, u_gu, gate, up, w_gate_up, b_hidden, w_down, a_hidden, mlp_scales, 512, group,
        n_seq,
    )
    mid_other = other_core(mid_msg)

    order = (slab - jnp.arange(slabs, dtype=i32)) % slabs
    index = jnp.stack(index)[:, order]

    def sum_inner(table):
        return pick(table, inner), [
            within_slab(pick(table, (inner + turn) % group), turn) for turn in range(1, group)
        ]

    def add_inner(own, got):
        total = own.astype(f32)
        for piece in got:
            total = total + piece.astype(f32)
        return total.astype(bf16)

    def over_slabs(total):
        return [pick(total, slab)] + [
            to_slab(pick(total, (slab + shift) % slabs), shift) for shift in range(1, slabs)
        ]

    def pack(rows_part, table):
        return jnp.concatenate([rows_part, table.reshape(slabs, -1, half)], axis=1)

    early_size = early.shape[3]
    early_own, early_got = sum_inner(early)
    gq, gk, gv, h_res, gbo, gah = run_attend_back(
        place, mid_res, mid_msg, mid_other, h_own, attn_msg, attn_other, mix_rates, b_model,
        w_attn_out, ah, start, q, k, v, o, inv, qi, ki, cos, sin, scale, slabs, group,
        head_dim,
    )
    early_got, gk, gv = tie((early_got, gk, gv))
    keep, send = run_others(place, gk, gv, w_attn_in, a_model, bh, slabs, group)
    others = (keep + other_core(send).astype(f32)).astype(bf16)
    others, gq, gk, gv = tie((others, gq, gk, gv))
    waves = [[2, 1], [3, 0]] if slabs == 4 else [list(range(slabs))]
    others = others.reshape(group - 1, slabs, chunk, half)
    others_got = []
    for wave in waves:
        if others_got:
            others_got[-1], others = tie((others_got[-1], others))
        others_got.append(
            [
                within_slab(
                    jnp.stack(
                        [pick(others[turn - 1], (slab + shift) % slabs) for shift in wave]
                    ),
                    turn,
                )
                for turn in range(1, group)
            ]
        )
    home = over_slabs(pack(out_half, add_inner(early_own, early_got)))
    late = run_grads(
        place, gq, gk, gv, bh, u, h_full, gbo, gah, slabs, group, n_seq, head_dim
    )
    late_own, late_got = sum_inner(late)
    late_own, gq, home, others_got[0] = tie((late_own, gq, home, others_got[0]))
    home_other = [other_core(piece) for piece in home]
    early_far = []
    for shift in range(1, n_seq):
        at = chunk + (seq_place + shift) % n_seq * early_size
        sent = [lax.dynamic_slice_in_dim(piece, at, early_size, 0) for piece in home]
        early_far.append(to_seq(jnp.stack(sent), shift))
    own_keep, own_send = run_own(
        place, gq, gk, gv, w_attn_in, a_model, bh, h_res, slabs, group
    )
    late_got, early_far, own_send, others_got = tie(
        (late_got, early_far, own_send, others_got)
    )
    own_got = other_core(own_send)
    late_total = add_inner(late_own, late_got)
    own_sum = (own_keep + own_got.astype(f32)).reshape(slabs, chunk, half)
    size = late.shape[3]
    result = [None] * slabs
    for wave, got_wave in zip(waves, others_got):
        for n, shift in enumerate(wave):
            target = (slab + shift) % slabs
            total = pick(own_sum, target)
            for got_part in got_wave:
                total = total + got_part[n].astype(f32)
            result[shift] = jnp.concatenate(
                [total.astype(bf16), pick(late_total, target).reshape(n_seq * size, half)],
                axis=0,
            )
    result, home, home_other, early_far = tie((result, home, home_other, early_far))
    result = result[:1] + [to_slab(result[shift], shift) for shift in range(1, slabs)]
    early_tables = [*home, *home_other, *early_far, *(other_core(t) for t in early_far)]
    layer_out = run_join(place, home, home_other, chunk, bf16)
    cols = model // owners
    each = row_width // owners
    hidden_rows = local_hidden // row_width
    grad_am_gu, grad_bm_down, grad_ad, grad_bd = run_unpack(
        unpack_early_kernel,
        (rank, cols, each, hidden_rows, (3 * rank * hidden_rows + LANES - 1) // LANES),
        (n_seq, slabs, chunk, early_size),
        place, index, early_tables, [],
        [
            (adapters, 2, rank, cols // 2),
            (adapters, rank, cols),
            (adapters, rank, each, hidden_rows),
            (adapters, 2, rank, each, hidden_rows),
        ],
        "unpack_early",
    )
    result, layer_out, grad_am_gu, grad_bm_down = tie(
        (result, layer_out, grad_am_gu, grad_bm_down)
    )
    result_other = [other_core(piece) for piece in result]
    far = []
    for shift in range(1, n_seq):
        at = chunk + (seq_place + shift) % n_seq * size
        sent = [lax.dynamic_slice_in_dim(piece, at, size, 0) for piece in result]
        far.append(to_seq(jnp.stack(sent), shift))
    input_grad = run_join(place, result, result_other, chunk, f32)
    far, input_grad = tie((far, input_grad))
    each = head_dim // owners
    grad_am, grad_bm, grad_ah, grad_bh = run_unpack(
        unpack_late_kernel,
        (rank, cols, local_heads, each),
        (n_seq, slabs, chunk, size),
        place, index, [*result, *result_other, *far, *(other_core(piece) for piece in far)],
        [grad_am_gu, grad_bm_down],
        [
            (adapters, 5, rank, cols // 2),
            (adapters, 2, rank, cols),
            (adapters, local_heads, each, rank),
            (adapters, 3, local_heads, each, rank),
        ],
        "unpack_late",
    )
    return (
        layer_out,
        input_grad,
        grad_am,
        grad_bm,
        jnp.transpose(grad_ah, (0, 3, 1, 2)),
        jnp.transpose(grad_bh, (0, 1, 4, 2, 3)),
        jnp.transpose(grad_ad, (0, 1, 3, 2)),
        jnp.transpose(grad_bd, (0, 1, 2, 4, 3)),
    )


def solution(mesh):
    return jax.shard_map(
        body,
        mesh=mesh,
        in_specs=(
            P("seq", "ctx", None),
            P("seq", "ctx"),
            P("seq"),
            P(None, None, "wt"),
            P("wt", None),
            P(None, None, "wt"),
            P("wt", None),
            P("wt"),
            P(),
            P(None, "wt"),
            P(),
            P(),
            P(None, None, "wt", None),
            P(None, None, None, "wt", None),
            P(None, None, "wt", None),
            P(None, None, None, "wt", None),
            P("seq", "ctx", None),
        ),
        out_specs=(
            P("seq", "ctx", None),
            P("seq", "ctx", None),
            P(None, None, None, ("seq", "ctx", "wt")),
            P(None, None, None, ("seq", "ctx")),
            P(None, None, "wt", ("seq", "ctx")),
            P(None, None, None, "wt", ("seq", "ctx")),
            P(None, None, "wt", ("seq", "ctx")),
            P(None, None, None, "wt", ("seq", "ctx")),
        ),
        check_vma=False,
    )
```

time: 250 us -> 240 us (0.960)
  local copies, waits for them, and re-layouts: 29.3 us -> 15.6 us
  starting transfers between devices: 35.9 us -> 41.2 us
  waiting for transfers between devices: 32.3 us -> 36 us
    unnamed x105 -> x72, local copies, waits for them, and re-layouts: 13.5 us -> 8.66 us
    ppermute x12, starting transfers between devices: 20.1 us -> 24.7 us  [to_slab(): return lax.ppermute(array, 'ctx', pairs)]
    dynamic_slice x11 -> x4, local copies, waits for them, and re-layouts: 4.98 us -> 0.68 us  [pick(): return lax.dynamic_index_in_dim(array, index, 0, keepdims=False)]
    ppermute x24 -> x19, starting transfers between devices: 5.12 us -> 3.63 us  [other_core(): return lax.ppermute(array, 'wt', [(0, 1), (1, 0)])]
    ppermute x24 -> x19, waiting for transfers between devices: 9.37 us -> 10.8 us  [other_core(): return lax.ppermute(array, 'wt', [(0, 1), (1, 0)])]
    ppermute x8 -> x6, starting transfers between devices: 7.97 us -> 9.27 us  [within_slab(): return lax.ppermute(array, 'ctx', pairs)]
    ppermute x8 -> x6, waiting for transfers between devices: 14.2 us -> 14.5 us  [within_slab(): return lax.ppermute(array, 'ctx', pairs)]
  transfers between devices with their start and end apart: 47 -> 40, of which waited for: 11 -> 17; matrix products, arithmetic and copies ran while one was open for 10% -> 6% of each run, Pallas kernels for 40% -> 42%
where the time goes in v6:
time: 240 us; the launch traced here: 238 us
  Pallas kernels  135 us (56%)
  starting transfers between devices  41.2 us (17%)
  waiting for transfers between devices  36 us (15%)
  local copies, waits for them, and re-layouts  15.6 us (6%)
  other arithmetic  8.71 us (4%)
    pallas_call x1, Pallas kernels, run_attend_back(): pl.pallas_call(functools.partial(attend_back_kernel, (slabs, chunk, group...  32.4 us
    pallas_call x1, Pallas kernels, run_feed_back(): pl.pallas_call(functools.partial(feed_back_kernel, (slabs, chunk, group,...  28.6 us
    pallas_call x1, Pallas kernels, run_attend(): pl.pallas_call(functools.partial(attend_kernel, (slabs, chunk, group, hea...  26.3 us
    ppermute x12, starting transfers between devices, to_slab(): return lax.ppermute(array, 'ctx', pairs)  24.7 us
    pallas_call x1, Pallas kernels, run_feed(): pl.pallas_call(functools.partial(feed_kernel, (rank, model, slabs)), grid...  22.9 us
    ppermute x6, waiting for transfers between devices, within_slab(): return lax.ppermute(array, 'ctx', pairs)  14.5 us
    ppermute x19, waiting for transfers between devices, other_core(): return lax.ppermute(array, 'wt', [(0, 1), (1, 0)])  10.8 us
    ppermute x12, waiting for transfers between devices, to_slab(): return lax.ppermute(array, 'ctx', pairs)  9.7 us
  transfers between devices with their start and end apart: 40, of which 17 were waited for; matrix products, arithmetic and copies ran while one was open for 6% of the time, Pallas kernels for 42%

profile of v6, /device:TPU:0, one launch (start us, length us, event | category | flops | bytes accessed | tf_op | source)
XLA Modules:
  0.0 237.7 jit_solution(3587259372655956769)
XLA Ops:
  2.8 3.1 %collective-permute-start = (bf16[136,640]{1,0:T(8,128)(2,1)S(1)}, bf16[136,640]{1,0:T(8,128)(2,1)S(1)}, u32[]{:S(2)}, u32[]{:S(2)}) collective-permute-start(bf16[136,640]{1,0:T(8,128)(2,1)S(1)} %pad_maximum_fusion.9), channel_id=1, source_target_pairs={{0,4},{2,6},{4,8},{6,10},{8,12},{10,14},{12,0},{14,2},{1,5},{3,7},... | collective-permute-start | bytes 522248 | tf_op jit(solution)/shard_map/ppermute | solution.py:1231
  6.0 2.7 %collective-permute-start.1 = (bf16[136,640]{1,0:T(8,128)(2,1)S(1)}, bf16[136,640]{1,0:T(8,128)(2,1)S(1)}, u32[]{:S(2)}, u32[]{:S(2)}) collective-permute-start(bf16[136,640]{1,0:T(8,128)(2,1)S(1)} %pad_maximum_fusion.10), channel_id=1, source_target_pairs={{0,8},{2,10},{4,12},{6,14},{8,0},{10,2},{12,4},{14,6},{1,9},{3,11}... | collective-permute-start | bytes 522248 | tf_op jit(solution)/shard_map/ppermute | solution.py:1231
  13.2 3.1 %fusion = (f32[1024,128]{1,0:T(8,128)}, f32[1024,128]{1,0:T(8,128)}) fusion(f32[128]{0:T(128)S(1)} %get-tuple-element.255, f32[128]{0:T(128)S(1)} %get-tuple-element.256, f32[1024]{0:T(1024)S(1)} %iota_convert_fusion), kind=kLoop, calls=%fused_computation.13 | loop fusion | flops 262144 | bytes 1053696 | tf_op jit(solution)/shard_map/mul | solution.py:1259
  21.6 12.2 %collective-permute-done.10.refs_6_ = bf16[3,136,640]{2,1,0:T(8,128)(2,1)S(1)} collective-permute-done((bf16[3,136,640]{2,1,0:T(8,128)(2,1)S(1)}, bf16[3,136,640]{2,1,0:T(8,128)(2,1)S(1)}, u32[]{:S(2)}, u32[]{:S(2)}) %collective-permute-start.10) | collective-permute-done | bytes 522272 | tf_op jit(solution)/shard_map/ppermute | solution.py:1235
  34.3 4.3 %collective-permute-start.5 = (bf16[128,640]{1,0:T(8,128)(2,1)S(1)}, bf16[128,640]{1,0:T(8,128)(2,1)S(1)}, u32[]{:S(2)}, u32[]{:S(2)}) collective-permute-start(bf16[128,640]{1,0:T(8,128)(2,1)S(1)} %get-tuple-element.119), channel_id=1, source_target_pairs={{0,4},{2,6},{4,8},{6,10},{8,12},{10,14},{12,0},{14,2},{1,5},{3,7},... | collective-permute-start | bytes 491528 | tf_op jit(solution)/shard_map/ppermute | solution.py:1231
  39.2 1.8 collective-permute-start.7
  42.5 26.3 %attend.1 = (bf16[1024,1280]{1,0:T(8,128)(2,1)}, bf16[512,1280]{1,0:T(8,128)(2,1)}, bf16[1024,48]{1,0:T(8,128)(2,1)}, bf16[512,640]{1,0:T(8,128)(2,1)}, bf16[102...) custom-call(s32[5]{0:T(128)} %stack.93.place, ...), custom_call_target="tpu_custom_call" | custom-call | flops 100000000 | bytes 100000 | tf_op jit(solution)/shard_map/attend/pallas_call | solution.py:316
  69.0 3.3 %collective-permute-done.12.other_ref.ao_ref = bf16[512,1408]{1,0:T(8,128)(2,1)S(1)} collective-permute-done((bf16[512,1408]{1,0:T(8,128)(2,1)}, bf16[512,1408]{1,0:T(8,128)(2,1)S(1)}, u32[]{:S(2)}, u32[]{:S(2)}) %collective-permute-start.12) | collective-permute-done | bytes 1441824 | tf_op jit(solution)/shard_map/ppermute | solution.py:1241
  73.5 22.9 %feed.1 = (bf16[512,1280]{1,0:T(8,128)(2,1)}, bf16[512,32]{1,0:T(8,128)(2,1)}, bf16[512,2560]{1,0:T(8,128)(2,1)}, bf16[512,2560]{1,0:T(8,128)(2,1)}, bf16[512,1408]{1,0:T(8,128)(2,1)}) custom-call(s32[5]{0:T(128)} %stack.93.place, bf16[512,1408]{1,0:T(8,128)(2,1)} %get-tuple-element.133.mine_ref.am_ref, bf16[512,1408]{1,0:T(8,128)(2,1)} %copy-done.29, ...), custom_call_target="tpu_custom_call" | custom-call | flops 24000000000 | bytes 30000000 | tf_op jit(solution)/shard_map/feed/pallas_call | solution.py:411
  96.6 3.3 %collective-permute-done.14.other_ref = bf16[512,1408]{1,0:T(8,128)(2,1)S(1)} collective-permute-done((bf16[512,1408]{1,0:T(8,128)(2,1)}, bf16[512,1408]{1,0:T(8,128)(2,1)S(1)}, u32[]{:S(2)}, u32[]{:S(2)}) %collective-permute-start.14) | collective-permute-done | bytes 1441824 | tf_op jit(solution)/shard_map/ppermute | solution.py:1241
  101.1 28.6 %feed_back.1 = (bf16[4,128,640]{2,1,0:T(8,128)(2,1)}, f32[512,1280]{1,0:T(8,128)}, bf16[512,1280]{1,0:T(8,128)(2,1)}, bf16[2,4,2,24,640]{4,3,2,1,0:T(8,128)(2,1)}) custom-call(s32[5]{0:T(128)} %stack.93.place, bf16[512,1408]{1,0:T(8,128)(2,1)} %get-tuple-element.137.mine_ref, bf16[512,1408]{1,0:T(8,128)(2,1)} %copy-done.30, ...), custom_call_target="tpu_custom_call" | custom-call | flops 30000001024 | bytes 40000000 | tf_op jit(solution)/shard_map/feed_back/pallas_call | solution.py:616
  133.1 32.4 %attend_back.1 = (bf16[512,640]{1,0:T(8,128)(2,1)}, bf16[1024,640]{1,0:T(8,128)(2,1)}, bf16[1024,640]{1,0:T(8,128)(2,1)}, f32[512,1280]{1,0:T(8,128)}, f32[16,1280]{1,0:T(8,128)}, /*index=5*/f32[16,640]{1,0:T(8,128)}) custom-call(s32[5]{0:T(128)} %stack.93.place, f32[512,1280]{1,0:T(8,128)} %get-tuple-element.144.res_ref, ...), custom_call_target="tpu_custom_call" | custom-call | flops 30000001024 | bytes 40000000 | tf_op jit(solution)/shard_map/attend_back/pallas_call | solution.py:799
  171.2 5.3 %others.1 = (f32[1,512,640]{2,1,0:T(8,128)S(1)}, bf16[1,512,640]{2,1,0:T(8,128)(2,1)}) custom-call(s32[5]{0:T(128)S(1)} %copy-done.2, bf16[4,2,128,640]{3,2,1,0:T(8,128)(2,1)S(1)} %bitcast.108, bf16[4,2,128,640]{3,2,1,0:T(8,128)(2,1)S(1)} %bitcast.110, bf16[3,1280,640]{2,1,0:T(8,128)(2,1)S(1)} %bitcast.103, bf16[3,1280,640]{2,1,0:T(8,128)(2,1)S(1)} %bitcast.103, ...), custom_call_target="tpu_custom_call" | custom-call | flops 7000000000 | bytes 10000000 | tf_op jit(solution)/shard_map/others/pallas_call | solution.py:909
  179.5 2.3 collective-permute-start.19
  186.3 5.0 %grads.1 = bf16[2,4,2,16,640]{4,3,2,1,0:T(8,128)(2,1)S(1)} custom-call(s32[5]{0:T(128)S(1)} %copy-done.3, bf16[512,640]{1,0:T(8,128)(2,1)S(1)} %copy-done.13, bf16[1024,640]{1,0:T(8,128)(2,1)S(1)} %copy-done.9, bf16[1024,640]{1,0:T(8,128)(2,1)S(1)} %copy-done.11, bf16[3,16,640]{2,1,0:T(8,128)(2,1)S(1)} %copy-done.7, bf16[1024,48]{1,0:T(8,128)(2,1)S(1)} %copy-done.5, ...), custom_call_target="tpu_custom_call" | custom-call | flops 10000000000 | bytes 10000000 | tf_op jit(solution)/shard_map/grads/pallas_call | solution.py:1066
  192.3 2.3 collective-permute-done.21
  194.7 2.0 collective-permute-start.24
  196.7 1.8 collective-permute-done.19.refs_2_
  200.2 5.8 %own.1 = (f32[512,640]{1,0:T(8,128)S(1)}, bf16[512,640]{1,0:T(8,128)(2,1)S(1)}) custom-call(s32[5]{0:T(128)S(1)} %copy-done.3, bf16[512,640]{1,0:T(8,128)(2,1)S(1)} %copy-done.13, bf16[4,2,128,640]{3,2,1,0:T(8,128)(2,1)S(1)} %bitcast.109, bf16[4,2,128,640]{3,2,1,0:T(8,128)(2,1)S(1)} %bitcast.111, bf16[3,1280,640]{2,1,0:T(8,128)(2,1)S(1)} %bitcast.105, ...), custom_call_target="tpu_custom_call" | custom-call | flops 7000000000 | bytes 10000000 | tf_op jit(solution)/shard_map/own/pallas_call | solution.py:972
  209.6 4.7 %collective-permute-start.30 = (bf16[160,640]{1,0:T(8,128)(2,1)S(1)}, bf16[160,640]{1,0:T(8,128)(2,1)S(1)}, u32[]{:S(2)}, u32[]{:S(2)}) collective-permute-start(bf16[160,640]{1,0:T(8,128)(2,1)S(1)} %pad_maximum_fusion.5), channel_id=1, source_target_pairs={{0,4},{2,6},{4,8},{6,10},{8,12},{10,14},{12,0},{14,2},{1,5},{3,7},... | collective-permute-start | bytes 614408 | tf_op jit(solution)/shard_map/ppermute | solution.py:1231
  219.3 2.3 unpack_early.1
  221.6 7.3 %collective-permute-done.31.refs_2_ = bf16[160,640]{1,0:T(8,128)(2,1)S(1)} collective-permute-done((bf16[160,640]{1,0:T(8,128)(2,1)S(1)}, bf16[160,640]{1,0:T(8,128)(2,1)S(1)}, u32[]{:S(2)}, u32[]{:S(2)}) %collective-permute-start.31) | collective-permute-done | bytes 204832 | tf_op jit(solution)/shard_map/ppermute | solution.py:1231
  231.2 2.2 join.3
  235.7 2.0 unpack_late.1
  (198 shorter events, 49.3 us)
Async XLA Ops:
  2.8 16.5 %collective-permute-start = (bf16[136,640]{1,0:T(8,128)(2,1)S(1)}, bf16[136,640]{1,0:T(8,128)(2,1)S(1)}, u32[]{:S(2)}, u32[]{:S(2)}) collective-permute-start(bf16[136,640]{1,0:T(8,128)(2,1)S(1)} %pad_maximum_fusion.9), channel_id=1, source_target_pairs={{0,4},{2,6},{4,8},{6,10},{8,12},{10,14},{12,0},{14,2},{1,5},{3,7},... | collective-permute-start | bytes 522248 | tf_op jit(solution)/shard_map/ppermute | solution.py:1231
  6.0 14.0 %collective-permute-start.1 = (bf16[136,640]{1,0:T(8,128)(2,1)S(1)}, bf16[136,640]{1,0:T(8,128)(2,1)S(1)}, u32[]{:S(2)}, u32[]{:S(2)}) collective-permute-start(bf16[136,640]{1,0:T(8,128)(2,1)S(1)} %pad_maximum_fusion.10), channel_id=1, source_target_pairs={{0,8},{2,10},{4,12},{6,14},{8,0},{10,2},{12,4},{14,6},{1,9},{3,11}... | collective-permute-start | bytes 522248 | tf_op jit(solution)/shard_map/ppermute | solution.py:1231
  8.6 11.3 %collective-permute-start.2 = (bf16[136,640]{1,0:T(8,128)(2,1)S(1)}, bf16[136,640]{1,0:T(8,128)(2,1)S(1)}, u32[]{:S(2)}, u32[]{:S(2)}) collective-permute-start(bf16[136,640]{1,0:T(8,128)(2,1)S(1)} %pad_maximum_fusion.11), channel_id=1, source_target_pairs={{0,12},{2,14},{4,0},{6,2},{8,4},{10,6},{12,8},{14,10},{1,13},{3,15... | collective-permute-start | bytes 522248 | tf_op jit(solution)/shard_map/ppermute | solution.py:1231
  10.1 9.2 %collective-permute-start.3 = (s32[4]{0:T(128)S(1)}, s32[4]{0:T(128)S(1)}, u32[]{:S(2)}, u32[]{:S(2)}) collective-permute-start(s32[4]{0:T(128)S(1)} %copy-done.25), channel_id=1, source_target_pairs={{0,16},{16,0},{1,17},{17,1},{2,18},{18,2},{3,19},{19,3},{4,20},{20... | collective-permute-start | bytes 56 | tf_op jit(solution)/shard_map/ppermute | solution.py:1238
  11.6 8.4 %collective-permute-start.4 = (bf16[136,640]{1,0:T(8,128)(2,1)S(1)}, bf16[136,640]{1,0:T(8,128)(2,1)S(1)}, u32[]{:S(2)}, u32[]{:S(2)}) collective-permute-start(bf16[136,640]{1,0:T(8,128)(2,1)S(1)} %pad_maximum_fusion.8.refs_1_), channel_id=1, source_target_pairs={{0,2},{2,0},{4,6},{6,4},{8,10},{10,8},{12,14},{14,12},{1,3},{3,1},... | collective-permute-start | bytes 522248 | tf_op jit(solution)/shard_map/ppermute | solution.py:1235
  20.0 13.8 %collective-permute-start.10 = (bf16[3,136,640]{2,1,0:T(8,128)(2,1)S(1)}, bf16[3,136,640]{2,1,0:T(8,128)(2,1)S(1)}, u32[]{:S(2)}, u32[]{:S(2)}) collective-permute-start(bf16[3,136,640]{2,1,0:T(8,128)(2,1)S(1)} %pad_maximum_fusion.refs_2_), channel_id=1, source_target_pairs={{0,2},{2,0},{4,6},{6,4},{8,10},{10,8},{12,14},{14,12},{1,3},{3,1},... | collective-permute-start | bytes 1566728 | tf_op jit(solution)/shard_map/ppermute | solution.py:1235
  21.6 20.0 %collective-permute-start.8 = (bf16[3,136,640]{2,1,0:T(8,128)(2,1)S(1)}, bf16[3,136,640]{2,1,0:T(8,128)(2,1)S(1)}, u32[]{:S(2)}, u32[]{:S(2)}) collective-permute-start(bf16[3,136,640]{2,1,0:T(8,128)(2,1)S(1)} %pad_maximum_fusion.refs_2_), channel_id=1, source_target_pairs={{0,1},{1,0},{2,3},{3,2},{4,5},{5,4},{6,7},{7,6},{8,9},{9,8},{10,11... | collective-permute-start | bytes 1566728 | tf_op jit(solution)/shard_map/ppermute | solution.py:1241
  33.8 7.8 %collective-permute-start.11 = (bf16[3,136,640]{2,1,0:T(8,128)(2,1)S(1)}, bf16[3,136,640]{2,1,0:T(8,128)(2,1)S(1)}, u32[]{:S(2)}, u32[]{:S(2)}) collective-permute-start(bf16[3,136,640]{2,1,0:T(8,128)(2,1)S(1)} %collective-permute-done.10.refs_6_), channel_id=1, source_target_pairs={{0,1},{1,0},{2,3},{3,2},{4,5},{5,4},{6,7},{7,6},{8,9},{9,8},{10,11... | collective-permute-start | bytes 1566728 | tf_op jit(solution)/shard_map/ppermute | solution.py:1241
  34.3 34.5 %collective-permute-start.5 = (bf16[128,640]{1,0:T(8,128)(2,1)S(1)}, bf16[128,640]{1,0:T(8,128)(2,1)S(1)}, u32[]{:S(2)}, u32[]{:S(2)}) collective-permute-start(bf16[128,640]{1,0:T(8,128)(2,1)S(1)} %get-tuple-element.119), channel_id=1, source_target_pairs={{0,4},{2,6},{4,8},{6,10},{8,12},{10,14},{12,0},{14,2},{1,5},{3,7},... | collective-permute-start | bytes 491528 | tf_op jit(solution)/shard_map/ppermute | solution.py:1231
  38.6 30.2 %collective-permute-start.6 = (bf16[128,640]{1,0:T(8,128)(2,1)S(1)}, bf16[128,640]{1,0:T(8,128)(2,1)S(1)}, u32[]{:S(2)}, u32[]{:S(2)}) collective-permute-start(bf16[128,640]{1,0:T(8,128)(2,1)S(1)} %get-tuple-element.120), channel_id=1, source_target_pairs={{0,8},{2,10},{4,12},{6,14},{8,0},{10,2},{12,4},{14,6},{1,9},{3,11}... | collective-permute-start | bytes 491528 | tf_op jit(solution)/shard_map/ppermute | solution.py:1231
  39.2 29.7 %collective-permute-start.7 = (bf16[128,640]{1,0:T(8,128)(2,1)S(1)}, bf16[128,640]{1,0:T(8,128)(2,1)S(1)}, u32[]{:S(2)}, u32[]{:S(2)}) collective-permute-start(bf16[128,640]{1,0:T(8,128)(2,1)S(1)} %get-tuple-element.121), channel_id=1, source_target_pairs={{0,12},{2,14},{4,0},{6,2},{8,4},{10,6},{12,8},{14,10},{1,13},{3,15... | collective-permute-start | bytes 491528 | tf_op jit(solution)/shard_map/ppermute | solution.py:1231
  72.4 24.0 %collective-permute-start.13 = (bf16[3,128,640]{2,1,0:T(8,128)(2,1)S(1)}, bf16[3,128,640]{2,1,0:T(8,128)(2,1)S(1)}, u32[]{:S(2)}, u32[]{:S(2)}) collective-permute-start(bf16[3,128,640]{2,1,0:T(8,128)(2,1)S(1)} %pad_maximum_fusion.1.g_mine_ref), channel_id=1, source_target_pairs={{0,1},{1,0},{2,3},{3,2},{4,5},{5,4},{6,7},{7,6},{8,9},{9,8},{10,11... | collective-permute-start | bytes 1474568 | tf_op jit(solution)/shard_map/ppermute | solution.py:1241
  131.0 34.6 %collective-permute-start.15 = (bf16[4,2,24,640]{3,2,1,0:T(8,128)(2,1)S(1)}, bf16[4,2,24,640]{3,2,1,0:T(8,128)(2,1)}, u32[]{:S(2)}, u32[]{:S(2)}) collective-permute-start(bf16[4,2,24,640]{3,2,1,0:T(8,128)(2,1)S(1)} %dynamic-slice_bitcast_fusion), channel_id=1, source_target_pairs={{0,2},{2,0},{4,6},{6,4},{8,10},{10,8},{12,14},{14,12},{1,3},{3,1},... | collective-permute-start | bytes 737288 | tf_op jit(solution)/shard_map/ppermute | solution.py:1235
  179.2 17.5 %collective-permute-start.18 = (bf16[176,640]{1,0:T(8,128)(2,1)S(1)}, bf16[176,640]{1,0:T(8,128)(2,1)S(1)}, u32[]{:S(2)}, u32[]{:S(2)}) collective-permute-start(bf16[176,640]{1,0:T(8,128)(2,1)S(1)} %get-tuple-element.237), channel_id=1, source_target_pairs={{0,4},{2,6},{4,8},{6,10},{8,12},{10,14},{12,0},{14,2},{1,5},{3,7},... | collective-permute-start | bytes 675848 | tf_op jit(solution)/shard_map/ppermute | solution.py:1231
  179.5 19.0 %collective-permute-start.19 = (bf16[176,640]{1,0:T(8,128)(2,1)S(1)}, bf16[176,640]{1,0:T(8,128)(2,1)S(1)}, u32[]{:S(2)}, u32[]{:S(2)}) collective-permute-start(bf16[176,640]{1,0:T(8,128)(2,1)S(1)} %get-tuple-element.238), channel_id=1, source_target_pairs={{0,8},{2,10},{4,12},{6,14},{8,0},{10,2},{12,4},{14,6},{1,9},{3,11}... | collective-permute-start | bytes 675848 | tf_op jit(solution)/shard_map/ppermute | solution.py:1231
  181.9 16.6 %collective-permute-start.20 = (bf16[176,640]{1,0:T(8,128)(2,1)S(1)}, bf16[176,640]{1,0:T(8,128)(2,1)S(1)}, u32[]{:S(2)}, u32[]{:S(2)}) collective-permute-start(bf16[176,640]{1,0:T(8,128)(2,1)S(1)} %get-tuple-element.235), channel_id=1, source_target_pairs={{0,12},{2,14},{4,0},{6,2},{8,4},{10,6},{12,8},{14,10},{1,13},{3,15... | collective-permute-start | bytes 675848 | tf_op jit(solution)/shard_map/ppermute | solution.py:1231
  184.6 10.0 %collective-permute-start.21 = (bf16[2,128,640]{2,1,0:T(8,128)(2,1)S(1)}, bf16[2,128,640]{2,1,0:T(8,128)(2,1)S(1)}, u32[]{:S(2)}, u32[]{:S(2)}) collective-permute-start(bf16[2,128,640]{2,1,0:T(8,128)(2,1)S(1)} %pad_maximum_fusion.2), channel_id=1, source_target_pairs={{0,2},{2,0},{4,6},{6,4},{8,10},{10,8},{12,14},{14,12},{1,3},{3,1},... | collective-permute-start | bytes 983048 | tf_op jit(solution)/shard_map/ppermute | solution.py:1235
  191.4 14.6 %collective-permute-start.22 = (bf16[4,2,16,640]{3,2,1,0:T(8,128)(2,1)S(1)}, bf16[4,2,16,640]{3,2,1,0:T(8,128)(2,1)S(1)}, u32[]{:S(2)}, u32[]{:S(2)}) collective-permute-start(bf16[4,2,16,640]{3,2,1,0:T(8,128)(2,1)S(1)} %get-tuple-element.244), channel_id=1, source_target_pairs={{0,2},{2,0},{4,6},{6,4},{8,10},{10,8},{12,14},{14,12},{1,3},{3,1},... | collective-permute-start | bytes 491528 | tf_op jit(solution)/shard_map/ppermute | solution.py:1235
  194.7 11.3 %collective-permute-start.24 = (bf16[2,128,640]{2,1,0:T(8,128)(2,1)S(1)}, bf16[2,128,640]{2,1,0:T(8,128)(2,1)S(1)}, u32[]{:S(2)}, u32[]{:S(2)}) collective-permute-start(bf16[2,128,640]{2,1,0:T(8,128)(2,1)S(1)} %pad_maximum_fusion.3), channel_id=1, source_target_pairs={{0,2},{2,0},{4,6},{6,4},{8,10},{10,8},{12,14},{14,12},{1,3},{3,1},... | collective-permute-start | bytes 983048 | tf_op jit(solution)/shard_map/ppermute | solution.py:1235
  198.6 7.4 %collective-permute-start.23 = (bf16[4,24,640]{2,1,0:T(8,128)(2,1)S(1)}, bf16[4,24,640]{2,1,0:T(8,128)(2,1)S(1)}, u32[]{:S(2)}, u32[]{:S(2)}) collective-permute-start(bf16[4,24,640]{2,1,0:T(8,128)(2,1)S(1)} %pad_maximum_fusion.12), channel_id=1, source_target_pairs={{0,16},{16,0},{1,17},{17,1},{2,18},{18,2},{3,19},{19,3},{4,20},{20... | collective-permute-start | bytes 368648 | tf_op jit(solution)/shard_map/ppermute | solution.py:1238
  209.5 9.8 %collective-permute-start.33 = (bf16[4,24,640]{2,1,0:T(8,128)(2,1)S(1)}, bf16[4,24,640]{2,1,0:T(8,128)(2,1)S(1)}, u32[]{:S(2)}, u32[]{:S(2)}) collective-permute-start(bf16[4,24,640]{2,1,0:T(8,128)(2,1)S(1)} %collective-permute-done.23.refs_8_), channel_id=1, source_target_pairs={{0,1},{1,0},{2,3},{3,2},{4,5},{5,4},{6,7},{7,6},{8,9},{9,8},{10,11... | collective-permute-start | bytes 368648 | tf_op jit(solution)/shard_map/ppermute | solution.py:1241
  209.6 12.0 %collective-permute-start.30 = (bf16[160,640]{1,0:T(8,128)(2,1)S(1)}, bf16[160,640]{1,0:T(8,128)(2,1)S(1)}, u32[]{:S(2)}, u32[]{:S(2)}) collective-permute-start(bf16[160,640]{1,0:T(8,128)(2,1)S(1)} %pad_maximum_fusion.5), channel_id=1, source_target_pairs={{0,4},{2,6},{4,8},{6,10},{8,12},{10,14},{12,0},{14,2},{1,5},{3,7},... | collective-permute-start | bytes 614408 | tf_op jit(solution)/shard_map/ppermute | solution.py:1231
  214.3 14.6 %collective-permute-start.31 = (bf16[160,640]{1,0:T(8,128)(2,1)S(1)}, bf16[160,640]{1,0:T(8,128)(2,1)S(1)}, u32[]{:S(2)}, u32[]{:S(2)}) collective-permute-start(bf16[160,640]{1,0:T(8,128)(2,1)S(1)} %pad_maximum_fusion.6), channel_id=1, source_target_pairs={{0,8},{2,10},{4,12},{6,14},{8,0},{10,2},{12,4},{14,6},{1,9},{3,11}... | collective-permute-start | bytes 614408 | tf_op jit(solution)/shard_map/ppermute | solution.py:1231
  214.9 13.9 %collective-permute-start.32 = (bf16[160,640]{1,0:T(8,128)(2,1)S(1)}, bf16[160,640]{1,0:T(8,128)(2,1)S(1)}, u32[]{:S(2)}, u32[]{:S(2)}) collective-permute-start(bf16[160,640]{1,0:T(8,128)(2,1)S(1)} %pad_maximum_fusion.7), channel_id=1, source_target_pairs={{0,12},{2,14},{4,0},{6,2},{8,4},{10,6},{12,8},{14,10},{1,13},{3,15... | collective-permute-start | bytes 614408 | tf_op jit(solution)/shard_map/ppermute | solution.py:1231
  (52 other events, 440.9 us)

commit v7 on v6

--- a/solution.py
+++ b/solution.py
@@ -141,7 +141,7 @@
     (
         wq_ref, w_ref, a_ref, b_table, a_table, cos_ref, sin_ref, scale_ref, wout_ref,
         hout_ref, ownout_ref, u_ref, q_ref, k_ref, v_ref, qi_ref, ki_ref, o_ref, inv_ref,
-        msg_ref, start_ref, b_ref, ah_ref, vt_ref, all_ref, seg_ref, h_ref, own_ref, raw_ref,
+        msg_ref, start_ref, b_ref, ah_ref, first_ref, all_ref, seg_ref, h_ref, own_ref, raw_ref,
     ) = refs[count:]
     inner, slab, core = place[0], place[1], place[2]
     block = group * chunk
@@ -188,7 +188,11 @@
             below = jnp.zeros((chunk, chunk), f32)
             for c in range(slabs * group):
                 below = below + jnp.where(columns[:, c : c + 1] < line, 1.0, 0.0)
-            start_ref[m : m + 1, :] = jnp.sum(below, axis=0, keepdims=True).astype(i32)
+            count = jnp.sum(below, axis=0, keepdims=True)
+            start_ref[m : m + 1, :] = count.astype(i32)
+            first_ref[m * chunk : (m + 1) * chunk, :] = (
+                jnp.broadcast_to(count, (LANES, chunk)).T.astype(i32)
+            )
 
         for n in range(b_ref.shape[2] // head_dim):
             cols = slice(n * head_dim, (n + 1) * head_dim)
@@ -236,28 +240,31 @@
         q_ref[own, :], qi_ref[own, :] = prep_tile(
             raw_ref[own, here], cos_ref[there, :], sin_ref[there, :], scale, head_dim
         )
-    vt_ref[...] = v_ref[...].T
+    ones = jnp.ones((block, LANES), bf16)
+    left = lane_iota((chunk, LANES)) < head_dim
     for m in range(slabs):
         own = slice(m * chunk, (m + 1) * chunk)
         pair = spread_pair(q_ref[own, :], head_dim)
-        first, last = query_bounds(start_ref, m, inner, group, chunk)
-        total = jnp.zeros((1, 2 * chunk), f32)
-        gathered = jnp.zeros((LANES, 2 * chunk), f32)
+        first = first_ref[own, :]
+        first = jnp.concatenate([first] * (block // LANES), axis=1)
+        first = jnp.concatenate([first, first], axis=0)
+        gathered = jnp.zeros((2 * chunk, 2 * LANES), f32)
         for b in range(m + 1):
             at = slice(b * block, (b + 1) * block)
-            scores = nt(k_ref[at, :], pair)
-            mask = allowed_mask(first, last, b * block, block, b == m)
-            weights = jnp.where(mask, jnp.exp2(scores * (0.125 * log2e)), 0.0)
-            total = total + jnp.sum(weights, axis=0, keepdims=True)
-            gathered = gathered + nn(vt_ref[:, at], weights.astype(bf16))
-        inverse = 1.0 / total
-        gathered = gathered * inverse
-        upper = row_iota((LANES, chunk)) < head_dim
-        final = jnp.where(upper, gathered[:, :chunk], gathered[:, chunk:])
-        final = final.T.astype(bf16)
+            scores = nt(pair, k_ref[at, :])
+            keys = b * block + lane_iota(scores.shape)
+            mask = keys >= first
+            if b == m:
+                queries = lax.rem(row_iota(scores.shape), chunk)
+                mask = mask & (keys <= queries + (m * group + inner) * chunk)
+            weights = jnp.where(mask, jnp.exp2(scores * (0.125 * log2e)), 0.0).astype(bf16)
+            gathered = gathered + nn(weights, jnp.concatenate([v_ref[at, :], ones], axis=1))
+        inverse = 1.0 / gathered[:, LANES:]
+        final = gathered[:, :LANES] * inverse
+        final = jnp.where(left, final[:chunk], final[chunk:]).astype(bf16)
         o_ref[own, :] = final
         all_ref[own, here] = final
-        inv_ref[0, m : m + 1, :] = inverse
+        inv_ref[0, m : m + 1, :] = inverse.T[0:1, :]
 
     @pl.when(step == pl.num_programs(0) - 1)
     def _():
@@ -321,7 +328,7 @@
             in_specs=in_specs,
             out_specs=[o[2] for o in out],
             scratch_shapes=[
-                pltpu.VMEM((LANES, length), bf16),
+                pltpu.VMEM((rows, LANES), i32),
                 pltpu.VMEM((rows, width), bf16),
                 pltpu.VMEM((chunk, chunk), f32),
                 pltpu.VMEM((length, model), bf16),
@@ -669,7 +676,7 @@
     ah_ref, start_ref, q_ref, k_ref, v_ref, o_ref, inv_ref, qi_ref, ki_ref, cos_ref, sin_ref,
     scale_ref,
     gq_ref, gk_ref, gv_ref, gres_ref, gbo_ref, gah_ref,
-    kt_ref, gqt_ref, ga_ref, guo_ref, guot_ref, uo_ref,
+    kt_ref, gqt_ref, ga_ref, go_all_ref, guot_ref, uo_ref,
 ):
     slabs, chunk, group, head_dim, rank, model = dims
     inner = place[0]
@@ -699,28 +706,28 @@
     def _():
         gbo_ref[...] = nn(uo_ref[...].T, ga_ref[...])
         low_g = nt(ga_ref[...], bo_ref[0, 0]).astype(bf16)
-        guo_ref[...] = low_g
         guot_ref[...] = low_g.T
+        go_all_ref[...] = (nt(ga_ref[...], wout_ref[...]) + nn(low_g, ah_ref[...])).astype(bf16)
 
     @pl.when(step >= slabs)
     def _():
         attend_back_pair(
-            dims, inner, wout_ref, ah_ref, start_ref, q_ref, k_ref, v_ref, o_ref, inv_ref,
+            dims, inner, step - slabs, start_ref, q_ref, k_ref, v_ref, o_ref, inv_ref,
             qi_ref, ki_ref, cos_ref, sin_ref, scale_ref, gq_ref, gk_ref, gv_ref, gah_ref,
-            kt_ref, gqt_ref, ga_ref, guo_ref, guot_ref,
+            kt_ref, gqt_ref, go_all_ref, guot_ref,
         )
 
 
 def attend_back_pair(
-    dims, inner, wout_ref, ah_ref, start_ref, q_ref, k_ref, v_ref, o_ref, inv_ref, qi_ref,
-    ki_ref, cos_ref, sin_ref, scale_ref, gq_ref, gk_ref, gv_ref, gah_ref, kt_ref, gqt_ref,
-    ga_ref, guo_ref, guot_ref,
+    dims, inner, turn, start_ref, q_ref, k_ref, v_ref, o_ref, inv_ref, qi_ref, ki_ref,
+    cos_ref, sin_ref, scale_ref, gq_ref, gk_ref, gv_ref, gah_ref, kt_ref, gqt_ref,
+    go_all_ref, guot_ref,
 ):
     slabs, chunk, group, head_dim, rank, model = dims
     block = group * chunk
     kt_ref[...] = k_ref[...].T
     scale = scale_ref[...]
-    grad_o = (nt(ga_ref[...], wout_ref[...]) + nn(guo_ref[...], ah_ref[...])).astype(bf16)
+    grad_o = go_all_ref[:, pl.ds(pl.multiple_of(turn * LANES, LANES), LANES)]
     gah_ref[...] = nn(guot_ref[...], o_ref[...])
     pairs_q, pairs_g, deltas, bounds = [], [], [], []
     for m in range(slabs):
@@ -810,8 +817,8 @@
                 wide,
                 whole_spec((2, model)),
                 adapter_spec((2, rank, model)),
-                pl.BlockSpec((LANES, model), lambda p, s: (lax.max(p - slabs, 0), 0)),
-                cols(rank),
+                whole_spec((width, model)),
+                whole_spec((rank, width)),
                 whole_spec((slabs, chunk)),
                 cols(rows),
                 cols(length),
@@ -831,7 +838,7 @@
                 pltpu.VMEM((LANES, length), bf16),
                 pltpu.VMEM((slabs, LANES, 2 * chunk), f32),
                 pltpu.VMEM((rows, model), bf16),
-                pltpu.VMEM((rows, rank), bf16),
+                pltpu.VMEM((rows, width), bf16),
                 pltpu.VMEM((rank, rows), bf16),
                 pltpu.VMEM((rows, rank), bf16),
             ],
@@ -926,7 +933,7 @@
             jax.ShapeDtypeStruct((group - 1, rows, half), f32),
             jax.ShapeDtypeStruct((group - 1, rows, half), bf16),
         ],
-        compiler_params=params(True),
+        compiler_params=params(),
         cost_estimate=cost(7e9, 1e7),
         name="others",
     )(place, gk.reshape(shaped), gv.reshape(shaped), w, w, a, b)
@@ -1273,6 +1280,7 @@
     rest_other = other_core(rest)
     peers = [within_slab(rest, turn) for turn in range(1, group)]
     g_mine = [to_slab(g_send[shift - 1], shift) for shift in range(1, slabs)]
+    peers, g_mine = tie((peers, g_mine))
     pieces = [own_piece, rest, rest_other]
     for turn in range(1, group):
         pieces += [

time: 240 us -> 232 us (0.967)
  local copies, waits for them, and re-layouts: 15.6 us -> 11.4 us
  Pallas kernels: 135 us -> 132 us
    ppermute x6, waiting for transfers between devices: 14.5 us -> 3.09 us  [within_slab(): return lax.ppermute(array, 'ctx', pairs)]
    ppermute x12, waiting for transfers between devices: 9.7 us -> 19.7 us  [to_slab(): return lax.ppermute(array, 'ctx', pairs)]
    unnamed x72 -> x58, local copies, waits for them, and re-layouts: 8.66 us -> 4.66 us
    pallas_call x1, Pallas kernels: 32.4 us -> 28.6 us  [run_attend_back(): pl.pallas_call(functools.partial(attend_back_kernel, (slabs, chunk, group...]
    ppermute x6, starting transfers between devices: 9.27 us -> 5.75 us  [within_slab(): return lax.ppermute(array, 'ctx', pairs)]
    ppermute x12, starting transfers between devices: 24.7 us -> 27.8 us  [to_slab(): return lax.ppermute(array, 'ctx', pairs)]
    pallas_call x1, Pallas kernels: 5.29 us -> 7.71 us  [run_others(): pl.pallas_call(others_kernel, grid_spec=pltpu.PrefetchScalarGridSpec(num_...]
  transfers between devices with their start and end apart: 40 -> 40, of which waited for: 17 -> 18; matrix products, arithmetic and copies ran while one was open for 6% -> 5% of each run, Pallas kernels for 42% -> 30%
where the time goes in v7:
time: 232 us; the launch traced here: 229 us
  Pallas kernels  132 us (57%)
  starting transfers between devices  41.1 us (18%)
  waiting for transfers between devices  36.6 us (16%)
  local copies, waits for them, and re-layouts  11.4 us (5%)
  other arithmetic  6.57 us (3%)
    pallas_call x1, Pallas kernels, run_attend_back(): pl.pallas_call(functools.partial(attend_back_kernel, (slabs, chunk, group...  28.6 us
    pallas_call x1, Pallas kernels, run_feed_back(): pl.pallas_call(functools.partial(feed_back_kernel, (slabs, chunk, group,...  28.5 us
    ppermute x12, starting transfers between devices, to_slab(): return lax.ppermute(array, 'ctx', pairs)  27.8 us
    pallas_call x1, Pallas kernels, run_attend(): pl.pallas_call(functools.partial(attend_kernel, (slabs, chunk, group, hea...  25.5 us
    pallas_call x1, Pallas kernels, run_feed(): pl.pallas_call(functools.partial(feed_kernel, (rank, model, slabs)), grid...  22.9 us
    ppermute x12, waiting for transfers between devices, to_slab(): return lax.ppermute(array, 'ctx', pairs)  19.7 us
    ppermute x19, waiting for transfers between devices, other_core(): return lax.ppermute(array, 'wt', [(0, 1), (1, 0)])  12.8 us
    pallas_call x1, Pallas kernels, run_others(): pl.pallas_call(others_kernel, grid_spec=pltpu.PrefetchScalarGridSpec(num_...  7.71 us
  transfers between devices with their start and end apart: 40, of which 18 were waited for; matrix products, arithmetic and copies ran while one was open for 5% of the time, Pallas kernels for 30%

profile of v7, /device:TPU:0, one launch (start us, length us, event | category | flops | bytes accessed | tf_op | source)
XLA Modules:
  0.0 229.3 jit_solution(12116180905819983662)
XLA Ops:
  2.8 3.1 %collective-permute-start = (bf16[136,640]{1,0:T(8,128)(2,1)S(1)}, bf16[136,640]{1,0:T(8,128)(2,1)S(1)}, u32[]{:S(2)}, u32[]{:S(2)}) collective-permute-start(bf16[136,640]{1,0:T(8,128)(2,1)S(1)} %pad_maximum_fusion.9), channel_id=1, source_target_pairs={{0,4},{2,6},{4,8},{6,10},{8,12},{10,14},{12,0},{14,2},{1,5},{3,7},... | collective-permute-start | bytes 522248 | tf_op jit(solution)/shard_map/ppermute | solution.py:1238
  6.0 2.7 %collective-permute-start.1 = (bf16[136,640]{1,0:T(8,128)(2,1)S(1)}, bf16[136,640]{1,0:T(8,128)(2,1)S(1)}, u32[]{:S(2)}, u32[]{:S(2)}) collective-permute-start(bf16[136,640]{1,0:T(8,128)(2,1)S(1)} %pad_maximum_fusion.10), channel_id=1, source_target_pairs={{0,8},{2,10},{4,12},{6,14},{8,0},{10,2},{12,4},{14,6},{1,9},{3,11}... | collective-permute-start | bytes 522248 | tf_op jit(solution)/shard_map/ppermute | solution.py:1238
  13.2 3.1 %fusion = (f32[1024,128]{1,0:T(8,128)}, f32[1024,128]{1,0:T(8,128)}) fusion(f32[128]{0:T(128)S(1)} %get-tuple-element.263, f32[128]{0:T(128)S(1)} %get-tuple-element.264, f32[1024]{0:T(1024)S(1)} %iota_convert_fusion), kind=kLoop, calls=%fused_computation.13 | loop fusion | flops 262144 | bytes 1053696 | tf_op jit(solution)/shard_map/mul | solution.py:1266
  21.6 4.2 %collective-permute-start.6 = (bf16[128,640]{1,0:T(8,128)(2,1)S(1)}, bf16[128,640]{1,0:T(8,128)(2,1)S(1)}, u32[]{:S(2)}, u32[]{:S(2)}) collective-permute-start(bf16[128,640]{1,0:T(8,128)(2,1)S(1)} %get-tuple-element.124), channel_id=1, source_target_pairs={{0,4},{2,6},{4,8},{6,10},{8,12},{10,14},{12,0},{14,2},{1,5},{3,7},... | collective-permute-start | bytes 491528 | tf_op jit(solution)/shard_map/ppermute | solution.py:1238
  28.2 3.8 %collective-permute-done.6 = bf16[128,640]{1,0:T(8,128)(2,1)S(1)} collective-permute-done((bf16[128,640]{1,0:T(8,128)(2,1)S(1)}, bf16[128,640]{1,0:T(8,128)(2,1)S(1)}, u32[]{:S(2)}, u32[]{:S(2)}) %collective-permute-start.6) | collective-permute-done | bytes 163872 | tf_op jit(solution)/shard_map/ppermute | solution.py:1238
  32.0 5.3 %collective-permute-done.7 = bf16[128,640]{1,0:T(8,128)(2,1)S(1)} collective-permute-done((bf16[128,640]{1,0:T(8,128)(2,1)S(1)}, bf16[128,640]{1,0:T(8,128)(2,1)S(1)}, u32[]{:S(2)}, u32[]{:S(2)}) %collective-permute-start.7) | collective-permute-done | bytes 163872 | tf_op jit(solution)/shard_map/ppermute | solution.py:1238
  40.6 25.5 %attend.1 = (bf16[1024,1280]{1,0:T(8,128)(2,1)}, bf16[512,1280]{1,0:T(8,128)(2,1)}, bf16[1024,48]{1,0:T(8,128)(2,1)}, bf16[512,640]{1,0:T(8,128)(2,1)}, bf16[102...) custom-call(s32[5]{0:T(128)} %stack.93.place, ...), custom_call_target="tpu_custom_call" | custom-call | flops 100000000 | bytes 100000 | tf_op jit(solution)/shard_map/attend/pallas_call | solution.py:323
  66.4 3.2 %collective-permute-done.12.other_ref.ao_ref = bf16[512,1408]{1,0:T(8,128)(2,1)S(1)} collective-permute-done((bf16[512,1408]{1,0:T(8,128)(2,1)}, bf16[512,1408]{1,0:T(8,128)(2,1)S(1)}, u32[]{:S(2)}, u32[]{:S(2)}) %collective-permute-start.12) | collective-permute-done | bytes 1441824 | tf_op jit(solution)/shard_map/ppermute | solution.py:1248
  70.7 22.9 %feed.1 = (bf16[512,1280]{1,0:T(8,128)(2,1)}, bf16[512,32]{1,0:T(8,128)(2,1)}, bf16[512,2560]{1,0:T(8,128)(2,1)}, bf16[512,2560]{1,0:T(8,128)(2,1)}, bf16[512,1408]{1,0:T(8,128)(2,1)}) custom-call(s32[5]{0:T(128)} %stack.93.place, bf16[512,1408]{1,0:T(8,128)(2,1)} %get-tuple-element.141.mine_ref.am_ref, bf16[512,1408]{1,0:T(8,128)(2,1)} %copy-done.23, ...), custom_call_target="tpu_custom_call" | custom-call | flops 24000000000 | bytes 30000000 | tf_op jit(solution)/shard_map/feed/pallas_call | solution.py:418
  93.9 3.3 %collective-permute-done.14.other_ref = bf16[512,1408]{1,0:T(8,128)(2,1)S(1)} collective-permute-done((bf16[512,1408]{1,0:T(8,128)(2,1)}, bf16[512,1408]{1,0:T(8,128)(2,1)S(1)}, u32[]{:S(2)}, u32[]{:S(2)}) %collective-permute-start.14) | collective-permute-done | bytes 1441824 | tf_op jit(solution)/shard_map/ppermute | solution.py:1248
  98.3 28.5 %feed_back.1 = (bf16[4,128,640]{2,1,0:T(8,128)(2,1)}, f32[512,1280]{1,0:T(8,128)}, bf16[512,1280]{1,0:T(8,128)(2,1)}, bf16[2,4,2,24,640]{4,3,2,1,0:T(8,128)(2,1)}) custom-call(s32[5]{0:T(128)} %stack.93.place, bf16[512,1408]{1,0:T(8,128)(2,1)} %get-tuple-element.145.mine_ref, bf16[512,1408]{1,0:T(8,128)(2,1)} %copy-done.24, ...), custom_call_target="tpu_custom_call" | custom-call | flops 30000001024 | bytes 40000000 | tf_op jit(solution)/shard_map/feed_back/pallas_call | solution.py:623
  131.3 28.6 %attend_back.1 = (bf16[512,640]{1,0:T(8,128)(2,1)}, bf16[1024,640]{1,0:T(8,128)(2,1)}, bf16[1024,640]{1,0:T(8,128)(2,1)}, f32[512,1280]{1,0:T(8,128)}, f32[16,1280]{1,0:T(8,128)}, /*index=5*/f32[16,640]{1,0:T(8,128)}) custom-call(s32[5]{0:T(128)} %stack.93.place, f32[512,1280]{1,0:T(8,128)} %get-tuple-element.152.res_ref, ...), custom_call_target="tpu_custom_call" | custom-call | flops 30000001024 | bytes 40000000 | tf_op jit(solution)/shard_map/attend_back/pallas_call | solution.py:806
  159.9 7.7 %others.1 = (f32[1,512,640]{2,1,0:T(8,128)}, bf16[1,512,640]{2,1,0:T(8,128)(2,1)}) custom-call(s32[5]{0:T(128)} %stack.93.place, bf16[4,2,128,640]{3,2,1,0:T(8,128)(2,1)} %bitcast.106, bf16[4,2,128,640]{3,2,1,0:T(8,128)(2,1)} %bitcast.108, bf16[3,1280,640]{2,1,0:T(8,128)(2,1)} %wv_ref.3, bf16[3,1280,640]{2,1,0:T(8,128)(2,1)} %wv_ref.3, ...), custom_call_target="tpu_custom_call" | custom-call | flops 7000000000 | bytes 10000000 | tf_op jit(solution)/shard_map/others/pallas_call | solution.py:916
  168.0 4.0 %collective-permute-start.18 = (bf16[176,640]{1,0:T(8,128)(2,1)S(1)}, bf16[176,640]{1,0:T(8,128)(2,1)S(1)}, u32[]{:S(2)}, u32[]{:S(2)}) collective-permute-start(bf16[176,640]{1,0:T(8,128)(2,1)S(1)} %get-tuple-element.245), channel_id=1, source_target_pairs={{0,4},{2,6},{4,8},{6,10},{8,12},{10,14},{12,0},{14,2},{1,5},{3,7},... | collective-permute-start | bytes 675848 | tf_op jit(solution)/shard_map/ppermute | solution.py:1238
  172.0 2.1 collective-permute-start.19
  177.2 5.0 %grads.1 = bf16[2,4,2,16,640]{4,3,2,1,0:T(8,128)(2,1)S(1)} custom-call(s32[5]{0:T(128)S(1)} %copy-done.1, bf16[512,640]{1,0:T(8,128)(2,1)S(1)} %copy-done.8, bf16[1024,640]{1,0:T(8,128)(2,1)S(1)} %copy-done.5, bf16[1024,640]{1,0:T(8,128)(2,1)S(1)} %copy-done.6, bf16[3,16,640]{2,1,0:T(8,128)(2,1)S(1)} %copy-done.4, bf16[1024,48]{1,0:T(8,128)(2,1)S(1)} %copy-done.3, ...), custom_call_target="tpu_custom_call" | custom-call | flops 10000000000 | bytes 10000000 | tf_op jit(solution)/shard_map/grads/pallas_call | solution.py:1073
  183.5 3.1 %collective-permute-done.21 = bf16[2,128,640]{2,1,0:T(8,128)(2,1)S(1)} collective-permute-done((bf16[2,128,640]{2,1,0:T(8,128)(2,1)S(1)}, bf16[2,128,640]{2,1,0:T(8,128)(2,1)S(1)}, u32[]{:S(2)}, u32[]{:S(2)}) %collective-permute-start.21) | collective-permute-done | bytes 327712 | tf_op jit(solution)/shard_map/ppermute | solution.py:1242
  186.8 2.5 %collective-permute-done.19.refs_2_ = bf16[176,640]{1,0:T(8,128)(2,1)S(1)} collective-permute-done((bf16[176,640]{1,0:T(8,128)(2,1)S(1)}, bf16[176,640]{1,0:T(8,128)(2,1)S(1)}, u32[]{:S(2)}, u32[]{:S(2)}) %collective-permute-start.19) | collective-permute-done | bytes 225312 | tf_op jit(solution)/shard_map/ppermute | solution.py:1238
  191.0 5.8 %own.1 = (f32[512,640]{1,0:T(8,128)S(1)}, bf16[512,640]{1,0:T(8,128)(2,1)S(1)}) custom-call(s32[5]{0:T(128)S(1)} %copy-done.1, bf16[512,640]{1,0:T(8,128)(2,1)S(1)} %copy-done.8, bf16[4,2,128,640]{3,2,1,0:T(8,128)(2,1)S(1)} %bitcast.107, bf16[4,2,128,640]{3,2,1,0:T(8,128)(2,1)S(1)} %bitcast.109, bf16[3,1280,640]{2,1,0:T(8,128)(2,1)S(1)} %bitcast.103, ...), custom_call_target="tpu_custom_call" | custom-call | flops 7000000000 | bytes 10000000 | tf_op jit(solution)/shard_map/own/pallas_call | solution.py:979
  200.5 5.3 %collective-permute-start.30 = (bf16[160,640]{1,0:T(8,128)(2,1)S(1)}, bf16[160,640]{1,0:T(8,128)(2,1)S(1)}, u32[]{:S(2)}, u32[]{:S(2)}) collective-permute-start(bf16[160,640]{1,0:T(8,128)(2,1)S(1)} %pad_maximum_fusion.5), channel_id=1, source_target_pairs={{0,4},{2,6},{4,8},{6,10},{8,12},{10,14},{12,0},{14,2},{1,5},{3,7},... | collective-permute-start | bytes 614408 | tf_op jit(solution)/shard_map/ppermute | solution.py:1238
  210.8 2.3 %unpack_early.1 = (f32[8,2,16,40]{3,2,1,0:T(8,128)S(1)}, f32[8,16,80]{2,1,0:T(8,128)S(1)}, f32[8,16,8,20]{3,2,1,0:T(8,128)}, f32[8,2,16,8,20]{4,3,2,1,0:T(8,128)}) custom-call(s32[5]{0:T(128)S(1)} %copy-done.1, s32[2,4]{1,0:T(2,128)S(1)} %bitcast.104, bf16[176,640]{1,0:T(8,128)(2,1)S(1)} %get-tuple-element.202.refs_0_, ...), custom_call_target="tpu_custom_call" | custom-call | flops 1000000 | bytes 8000000 | tf_op jit(solution)/shard_map/unpack_early/pallas_call | solution.py:1187
  213.1 7.3 %collective-permute-done.31.refs_2_ = bf16[160,640]{1,0:T(8,128)(2,1)S(1)} collective-permute-done((bf16[160,640]{1,0:T(8,128)(2,1)S(1)}, bf16[160,640]{1,0:T(8,128)(2,1)S(1)}, u32[]{:S(2)}, u32[]{:S(2)}) %collective-permute-start.31) | collective-permute-done | bytes 204832 | tf_op jit(solution)/shard_map/ppermute | solution.py:1238
  222.8 2.2 join.3
  227.3 2.0 unpack_late.1
  (183 shorter events, 44.4 us)
Async XLA Ops:
  2.8 16.4 %collective-permute-start = (bf16[136,640]{1,0:T(8,128)(2,1)S(1)}, bf16[136,640]{1,0:T(8,128)(2,1)S(1)}, u32[]{:S(2)}, u32[]{:S(2)}) collective-permute-start(bf16[136,640]{1,0:T(8,128)(2,1)S(1)} %pad_maximum_fusion.9), channel_id=1, source_target_pairs={{0,4},{2,6},{4,8},{6,10},{8,12},{10,14},{12,0},{14,2},{1,5},{3,7},... | collective-permute-start | bytes 522248 | tf_op jit(solution)/shard_map/ppermute | solution.py:1238
  6.0 14.0 %collective-permute-start.1 = (bf16[136,640]{1,0:T(8,128)(2,1)S(1)}, bf16[136,640]{1,0:T(8,128)(2,1)S(1)}, u32[]{:S(2)}, u32[]{:S(2)}) collective-permute-start(bf16[136,640]{1,0:T(8,128)(2,1)S(1)} %pad_maximum_fusion.10), channel_id=1, source_target_pairs={{0,8},{2,10},{4,12},{6,14},{8,0},{10,2},{12,4},{14,6},{1,9},{3,11}... | collective-permute-start | bytes 522248 | tf_op jit(solution)/shard_map/ppermute | solution.py:1238
  8.6 11.3 %collective-permute-start.2 = (bf16[136,640]{1,0:T(8,128)(2,1)S(1)}, bf16[136,640]{1,0:T(8,128)(2,1)S(1)}, u32[]{:S(2)}, u32[]{:S(2)}) collective-permute-start(bf16[136,640]{1,0:T(8,128)(2,1)S(1)} %pad_maximum_fusion.11), channel_id=1, source_target_pairs={{0,12},{2,14},{4,0},{6,2},{8,4},{10,6},{12,8},{14,10},{1,13},{3,15... | collective-permute-start | bytes 522248 | tf_op jit(solution)/shard_map/ppermute | solution.py:1238
  10.0 9.1 %collective-permute-start.3 = (s32[4]{0:T(128)S(1)}, s32[4]{0:T(128)S(1)}, u32[]{:S(2)}, u32[]{:S(2)}) collective-permute-start(s32[4]{0:T(128)S(1)} %copy-done.22), channel_id=1, source_target_pairs={{0,16},{16,0},{1,17},{17,1},{2,18},{18,2},{3,19},{19,3},{4,20},{20... | collective-permute-start | bytes 56 | tf_op jit(solution)/shard_map/ppermute | solution.py:1245
  11.6 8.4 %collective-permute-start.4 = (bf16[136,640]{1,0:T(8,128)(2,1)S(1)}, bf16[136,640]{1,0:T(8,128)(2,1)S(1)}, u32[]{:S(2)}, u32[]{:S(2)}) collective-permute-start(bf16[136,640]{1,0:T(8,128)(2,1)S(1)} %pad_maximum_fusion.8.refs_1_), channel_id=1, source_target_pairs={{0,2},{2,0},{4,6},{6,4},{8,10},{10,8},{12,14},{14,12},{1,3},{3,1},... | collective-permute-start | bytes 522248 | tf_op jit(solution)/shard_map/ppermute | solution.py:1242
  20.0 17.3 %collective-permute-start.5 = (bf16[3,136,640]{2,1,0:T(8,128)(2,1)S(1)}, bf16[3,136,640]{2,1,0:T(8,128)(2,1)S(1)}, u32[]{:S(2)}, u32[]{:S(2)}) collective-permute-start(bf16[3,136,640]{2,1,0:T(8,128)(2,1)S(1)} %pad_maximum_fusion.refs_2_), channel_id=1, source_target_pairs={{0,2},{2,0},{4,6},{6,4},{8,10},{10,8},{12,14},{14,12},{1,3},{3,1},... | collective-permute-start | bytes 1566728 | tf_op jit(solution)/shard_map/ppermute | solution.py:1242
  21.6 10.3 %collective-permute-start.6 = (bf16[128,640]{1,0:T(8,128)(2,1)S(1)}, bf16[128,640]{1,0:T(8,128)(2,1)S(1)}, u32[]{:S(2)}, u32[]{:S(2)}) collective-permute-start(bf16[128,640]{1,0:T(8,128)(2,1)S(1)} %get-tuple-element.124), channel_id=1, source_target_pairs={{0,4},{2,6},{4,8},{6,10},{8,12},{10,14},{12,0},{14,2},{1,5},{3,7},... | collective-permute-start | bytes 491528 | tf_op jit(solution)/shard_map/ppermute | solution.py:1238
  25.8 11.5 %collective-permute-start.7 = (bf16[128,640]{1,0:T(8,128)(2,1)S(1)}, bf16[128,640]{1,0:T(8,128)(2,1)S(1)}, u32[]{:S(2)}, u32[]{:S(2)}) collective-permute-start(bf16[128,640]{1,0:T(8,128)(2,1)S(1)} %get-tuple-element.125), channel_id=1, source_target_pairs={{0,8},{2,10},{4,12},{6,14},{8,0},{10,2},{12,4},{14,6},{1,9},{3,11}... | collective-permute-start | bytes 491528 | tf_op jit(solution)/shard_map/ppermute | solution.py:1238
  27.5 9.8 %collective-permute-start.8 = (bf16[128,640]{1,0:T(8,128)(2,1)S(1)}, bf16[128,640]{1,0:T(8,128)(2,1)S(1)}, u32[]{:S(2)}, u32[]{:S(2)}) collective-permute-start(bf16[128,640]{1,0:T(8,128)(2,1)S(1)} %get-tuple-element.126), channel_id=1, source_target_pairs={{0,12},{2,14},{4,0},{6,2},{8,4},{10,6},{12,8},{14,10},{1,13},{3,15... | collective-permute-start | bytes 491528 | tf_op jit(solution)/shard_map/ppermute | solution.py:1238
  28.2 11.4 %collective-permute-start.9 = (bf16[3,136,640]{2,1,0:T(8,128)(2,1)S(1)}, bf16[3,136,640]{2,1,0:T(8,128)(2,1)S(1)}, u32[]{:S(2)}, u32[]{:S(2)}) collective-permute-start(bf16[3,136,640]{2,1,0:T(8,128)(2,1)S(1)} %pad_maximum_fusion.refs_2_), channel_id=1, source_target_pairs={{0,1},{1,0},{2,3},{3,2},{4,5},{5,4},{6,7},{7,6},{8,9},{9,8},{10,11... | collective-permute-start | bytes 1566728 | tf_op jit(solution)/shard_map/ppermute | solution.py:1248
  69.6 24.0 %collective-permute-start.13 = (bf16[3,128,640]{2,1,0:T(8,128)(2,1)S(1)}, bf16[3,128,640]{2,1,0:T(8,128)(2,1)S(1)}, u32[]{:S(2)}, u32[]{:S(2)}) collective-permute-start(bf16[3,128,640]{2,1,0:T(8,128)(2,1)S(1)} %pad_maximum_fusion.1.g_mine_ref), channel_id=1, source_target_pairs={{0,1},{1,0},{2,3},{3,2},{4,5},{5,4},{6,7},{7,6},{8,9},{9,8},{10,11... | collective-permute-start | bytes 1474568 | tf_op jit(solution)/shard_map/ppermute | solution.py:1248
  128.0 31.9 %collective-permute-start.15 = (bf16[4,2,24,640]{3,2,1,0:T(8,128)(2,1)S(1)}, bf16[4,2,24,640]{3,2,1,0:T(8,128)(2,1)S(1)}, u32[]{:S(2)}, u32[]{:S(2)}) collective-permute-start(bf16[4,2,24,640]{3,2,1,0:T(8,128)(2,1)S(1)} %dynamic-slice_bitcast_fusion), channel_id=1, source_target_pairs={{0,2},{2,0},{4,6},{6,4},{8,10},{10,8},{12,14},{14,12},{1,3},{3,1},... | collective-permute-start | bytes 737288 | tf_op jit(solution)/shard_map/ppermute | solution.py:1242
  167.6 6.8 %collective-permute-start.17 = (bf16[1,512,640]{2,1,0:T(8,128)(2,1)}, bf16[1,512,640]{2,1,0:T(8,128)(2,1)S(1)}, u32[]{:S(2)}, u32[]{:S(2)}) collective-permute-start(bf16[1,512,640]{2,1,0:T(8,128)(2,1)} %get-tuple-element.169), channel_id=1, source_target_pairs={{0,1},{1,0},{2,3},{3,2},{4,5},{5,4},{6,7},{7,6},{8,9},{9,8},{10,11... | collective-permute-start | bytes 1966088 | tf_op jit(solution)/shard_map/ppermute | solution.py:1248
  168.0 18.9 %collective-permute-start.18 = (bf16[176,640]{1,0:T(8,128)(2,1)S(1)}, bf16[176,640]{1,0:T(8,128)(2,1)S(1)}, u32[]{:S(2)}, u32[]{:S(2)}) collective-permute-start(bf16[176,640]{1,0:T(8,128)(2,1)S(1)} %get-tuple-element.245), channel_id=1, source_target_pairs={{0,4},{2,6},{4,8},{6,10},{8,12},{10,14},{12,0},{14,2},{1,5},{3,7},... | collective-permute-start | bytes 675848 | tf_op jit(solution)/shard_map/ppermute | solution.py:1238
  172.0 17.4 %collective-permute-start.19 = (bf16[176,640]{1,0:T(8,128)(2,1)S(1)}, bf16[176,640]{1,0:T(8,128)(2,1)S(1)}, u32[]{:S(2)}, u32[]{:S(2)}) collective-permute-start(bf16[176,640]{1,0:T(8,128)(2,1)S(1)} %get-tuple-element.246), channel_id=1, source_target_pairs={{0,8},{2,10},{4,12},{6,14},{8,0},{10,2},{12,4},{14,6},{1,9},{3,11}... | collective-permute-start | bytes 675848 | tf_op jit(solution)/shard_map/ppermute | solution.py:1238
  174.1 15.2 %collective-permute-start.20 = (bf16[176,640]{1,0:T(8,128)(2,1)S(1)}, bf16[176,640]{1,0:T(8,128)(2,1)S(1)}, u32[]{:S(2)}, u32[]{:S(2)}) collective-permute-start(bf16[176,640]{1,0:T(8,128)(2,1)S(1)} %get-tuple-element.243), channel_id=1, source_target_pairs={{0,12},{2,14},{4,0},{6,2},{8,4},{10,6},{12,8},{14,10},{1,13},{3,15... | collective-permute-start | bytes 675848 | tf_op jit(solution)/shard_map/ppermute | solution.py:1238
  176.2 10.4 %collective-permute-start.21 = (bf16[2,128,640]{2,1,0:T(8,128)(2,1)S(1)}, bf16[2,128,640]{2,1,0:T(8,128)(2,1)S(1)}, u32[]{:S(2)}, u32[]{:S(2)}) collective-permute-start(bf16[2,128,640]{2,1,0:T(8,128)(2,1)S(1)} %pad_maximum_fusion.2), channel_id=1, source_target_pairs={{0,2},{2,0},{4,6},{6,4},{8,10},{10,8},{12,14},{14,12},{1,3},{3,1},... | collective-permute-start | bytes 983048 | tf_op jit(solution)/shard_map/ppermute | solution.py:1242
  182.3 14.6 %collective-permute-start.22 = (bf16[4,2,16,640]{3,2,1,0:T(8,128)(2,1)S(1)}, bf16[4,2,16,640]{3,2,1,0:T(8,128)(2,1)S(1)}, u32[]{:S(2)}, u32[]{:S(2)}) collective-permute-start(bf16[4,2,16,640]{3,2,1,0:T(8,128)(2,1)S(1)} %get-tuple-element.252), channel_id=1, source_target_pairs={{0,2},{2,0},{4,6},{6,4},{8,10},{10,8},{12,14},{14,12},{1,3},{3,1},... | collective-permute-start | bytes 491528 | tf_op jit(solution)/shard_map/ppermute | solution.py:1242
  186.7 10.2 %collective-permute-start.24 = (bf16[2,128,640]{2,1,0:T(8,128)(2,1)S(1)}, bf16[2,128,640]{2,1,0:T(8,128)(2,1)S(1)}, u32[]{:S(2)}, u32[]{:S(2)}) collective-permute-start(bf16[2,128,640]{2,1,0:T(8,128)(2,1)S(1)} %pad_maximum_fusion.3), channel_id=1, source_target_pairs={{0,2},{2,0},{4,6},{6,4},{8,10},{10,8},{12,14},{14,12},{1,3},{3,1},... | collective-permute-start | bytes 983048 | tf_op jit(solution)/shard_map/ppermute | solution.py:1242
  189.5 7.4 %collective-permute-start.23 = (bf16[4,24,640]{2,1,0:T(8,128)(2,1)S(1)}, bf16[4,24,640]{2,1,0:T(8,128)(2,1)S(1)}, u32[]{:S(2)}, u32[]{:S(2)}) collective-permute-start(bf16[4,24,640]{2,1,0:T(8,128)(2,1)S(1)} %pad_maximum_fusion.12), channel_id=1, source_target_pairs={{0,16},{16,0},{1,17},{17,1},{2,18},{18,2},{3,19},{19,3},{4,20},{20... | collective-permute-start | bytes 368648 | tf_op jit(solution)/shard_map/ppermute | solution.py:1245
  200.3 10.4 %collective-permute-start.33 = (bf16[4,24,640]{2,1,0:T(8,128)(2,1)S(1)}, bf16[4,24,640]{2,1,0:T(8,128)(2,1)S(1)}, u32[]{:S(2)}, u32[]{:S(2)}) collective-permute-start(bf16[4,24,640]{2,1,0:T(8,128)(2,1)S(1)} %collective-permute-done.23.refs_8_), channel_id=1, source_target_pairs={{0,1},{1,0},{2,3},{3,2},{4,5},{5,4},{6,7},{7,6},{8,9},{9,8},{10,11... | collective-permute-start | bytes 368648 | tf_op jit(solution)/shard_map/ppermute | solution.py:1248
  200.5 12.6 %collective-permute-start.30 = (bf16[160,640]{1,0:T(8,128)(2,1)S(1)}, bf16[160,640]{1,0:T(8,128)(2,1)S(1)}, u32[]{:S(2)}, u32[]{:S(2)}) collective-permute-start(bf16[160,640]{1,0:T(8,128)(2,1)S(1)} %pad_maximum_fusion.5), channel_id=1, source_target_pairs={{0,4},{2,6},{4,8},{6,10},{8,12},{10,14},{12,0},{14,2},{1,5},{3,7},... | collective-permute-start | bytes 614408 | tf_op jit(solution)/shard_map/ppermute | solution.py:1238
  205.8 14.7 %collective-permute-start.31 = (bf16[160,640]{1,0:T(8,128)(2,1)S(1)}, bf16[160,640]{1,0:T(8,128)(2,1)S(1)}, u32[]{:S(2)}, u32[]{:S(2)}) collective-permute-start(bf16[160,640]{1,0:T(8,128)(2,1)S(1)} %pad_maximum_fusion.6), channel_id=1, source_target_pairs={{0,8},{2,10},{4,12},{6,14},{8,0},{10,2},{12,4},{14,6},{1,9},{3,11}... | collective-permute-start | bytes 614408 | tf_op jit(solution)/shard_map/ppermute | solution.py:1238
  206.5 13.9 %collective-permute-start.32 = (bf16[160,640]{1,0:T(8,128)(2,1)S(1)}, bf16[160,640]{1,0:T(8,128)(2,1)S(1)}, u32[]{:S(2)}, u32[]{:S(2)}) collective-permute-start(bf16[160,640]{1,0:T(8,128)(2,1)S(1)} %pad_maximum_fusion.7), channel_id=1, source_target_pairs={{0,12},{2,14},{4,0},{6,2},{8,4},{10,6},{12,8},{14,10},{1,13},{3,15... | collective-permute-start | bytes 614408 | tf_op jit(solution)/shard_map/ppermute | solution.py:1238
  (45 other events, 260.1 us)

commit v8 on v7

--- a/solution.py
+++ b/solution.py
@@ -888,7 +888,7 @@
 
     @pl.when(turn == 1)
     def _():
-        keep_ref[0] = part
+        keep_ref[0] = part.astype(bf16)
 
 
 def half_weight(half, width, member):
@@ -930,7 +930,7 @@
             scratch_shapes=[pltpu.VMEM((rows, 2 * rank), bf16)],
         ),
         out_shape=[
-            jax.ShapeDtypeStruct((group - 1, rows, half), f32),
+            jax.ShapeDtypeStruct((group - 1, rows, half), bf16),
             jax.ShapeDtypeStruct((group - 1, rows, half), bf16),
         ],
         compiler_params=params(),
@@ -964,7 +964,7 @@
 
     @pl.when(turn == 1)
     def _():
-        keep_ref[...] = part + res_ref[...]
+        keep_ref[...] = (part + res_ref[...]).astype(bf16)
 
 
 def run_own(place, gq, gk, gv, w, a, b, res, slabs, group):
@@ -975,7 +975,7 @@
     rank = b.shape[1]
     shaped = (slabs, group, chunk, width)
     peer = pl.BlockSpec((slabs, 1, chunk, width), lambda t, s: (0, s[0], 0, 0))
-    out = [((rows, half), f32), ((rows, half), bf16)]
+    out = [((rows, half), bf16), ((rows, half), bf16)]
     return pl.pallas_call(
         own_kernel,
         grid_spec=pltpu.PrefetchScalarGridSpec(
@@ -1280,7 +1280,7 @@
     rest_other = other_core(rest)
     peers = [within_slab(rest, turn) for turn in range(1, group)]
     g_mine = [to_slab(g_send[shift - 1], shift) for shift in range(1, slabs)]
-    peers, g_mine = tie((peers, g_mine))
+    peers, g_mine[0], g_mine[-1] = tie((peers, g_mine[0], g_mine[-1]))
     pieces = [own_piece, rest, rest_other]
     for turn in range(1, group):
         pieces += [
@@ -1340,7 +1340,7 @@
     )
     early_got, gk, gv = tie((early_got, gk, gv))
     keep, send = run_others(place, gk, gv, w_attn_in, a_model, bh, slabs, group)
-    others = (keep + other_core(send).astype(f32)).astype(bf16)
+    others = (keep.astype(f32) + other_core(send).astype(f32)).astype(bf16)
     others, gq, gk, gv = tie((others, gq, gk, gv))
     waves = [[2, 1], [3, 0]] if slabs == 4 else [list(range(slabs))]
     others = others.reshape(group - 1, slabs, chunk, half)
@@ -1379,7 +1379,7 @@
     )
     own_got = other_core(own_send)
     late_total = add_inner(late_own, late_got)
-    own_sum = (own_keep + own_got.astype(f32)).reshape(slabs, chunk, half)
+    own_sum = (own_keep.astype(f32) + own_got.astype(f32)).reshape(slabs, chunk, half)
     size = late.shape[3]
     result = [None] * slabs
     for wave, got_wave in zip(waves, others_got):

time: 232 us -> 229 us (0.987)
  waiting for transfers between devices: 36.6 us -> 30.6 us
  starting transfers between devices: 41.1 us -> 44.4 us
    ppermute x12, waiting for transfers between devices: 19.7 us -> 15.7 us  [to_slab(): return lax.ppermute(array, 'ctx', pairs)]
    ppermute x6, starting transfers between devices: 5.75 us -> 9.23 us  [within_slab(): return lax.ppermute(array, 'ctx', pairs)]
  transfers between devices with their start and end apart: 40 -> 40, of which waited for: 18 -> 19; matrix products, arithmetic and copies ran while one was open for 5% -> 5% of each run, Pallas kernels for 30% -> 42%
where the time goes in v8:
time: 229 us; the launch traced here: 226 us
  Pallas kernels  132 us (58%)
  starting transfers between devices  44.4 us (19%)
  waiting for transfers between devices  30.6 us (13%)
  local copies, waits for them, and re-layouts  11 us (5%)
  other arithmetic  6.38 us (3%)
    pallas_call x1, Pallas kernels, run_attend_back(): pl.pallas_call(functools.partial(attend_back_kernel, (slabs, chunk, group...  28.6 us
    pallas_call x1, Pallas kernels, run_feed_back(): pl.pallas_call(functools.partial(feed_back_kernel, (slabs, chunk, group,...  28.5 us
    ppermute x12, starting transfers between devices, to_slab(): return lax.ppermute(array, 'ctx', pairs)  27.9 us
    pallas_call x1, Pallas kernels, run_attend(): pl.pallas_call(functools.partial(attend_kernel, (slabs, chunk, group, hea...  25.5 us
    pallas_call x1, Pallas kernels, run_feed(): pl.pallas_call(functools.partial(feed_kernel, (rank, model, slabs)), grid...  22.9 us
    ppermute x12, waiting for transfers between devices, to_slab(): return lax.ppermute(array, 'ctx', pairs)  15.7 us
    ppermute x19, waiting for transfers between devices, other_core(): return lax.ppermute(array, 'wt', [(0, 1), (1, 0)])  10.8 us
    ppermute x6, starting transfers between devices, within_slab(): return lax.ppermute(array, 'ctx', pairs)  9.23 us
  transfers between devices with their start and end apart: 40, of which 19 were waited for; matrix products, arithmetic and copies ran while one was open for 5% of the time, Pallas kernels for 42%

profile of v8, /device:TPU:0, one launch (start us, length us, event | category | flops | bytes accessed | tf_op | source)
XLA Modules:
  0.0 225.9 jit_solution(158676046642644226)
XLA Ops:
  2.8 3.1 %collective-permute-start = (bf16[136,640]{1,0:T(8,128)(2,1)S(1)}, bf16[136,640]{1,0:T(8,128)(2,1)S(1)}, u32[]{:S(2)}, u32[]{:S(2)}) collective-permute-start(bf16[136,640]{1,0:T(8,128)(2,1)S(1)} %pad_maximum_fusion.9), channel_id=1, source_target_pairs={{0,4},{2,6},{4,8},{6,10},{8,12},{10,14},{12,0},{14,2},{1,5},{3,7},... | collective-permute-start | bytes 522248 | tf_op jit(solution)/shard_map/ppermute | solution.py:1238
  6.0 2.7 %collective-permute-start.1 = (bf16[136,640]{1,0:T(8,128)(2,1)S(1)}, bf16[136,640]{1,0:T(8,128)(2,1)S(1)}, u32[]{:S(2)}, u32[]{:S(2)}) collective-permute-start(bf16[136,640]{1,0:T(8,128)(2,1)S(1)} %pad_maximum_fusion.10), channel_id=1, source_target_pairs={{0,8},{2,10},{4,12},{6,14},{8,0},{10,2},{12,4},{14,6},{1,9},{3,11}... | collective-permute-start | bytes 522248 | tf_op jit(solution)/shard_map/ppermute | solution.py:1238
  13.2 3.1 %fusion = (f32[1024,128]{1,0:T(8,128)}, f32[1024,128]{1,0:T(8,128)}) fusion(f32[128]{0:T(128)S(1)} %get-tuple-element.261, f32[128]{0:T(128)S(1)} %get-tuple-element.262, f32[1024]{0:T(1024)S(1)} %iota_convert_fusion), kind=kLoop, calls=%fused_computation.13 | loop fusion | flops 262144 | bytes 1053696 | tf_op jit(solution)/shard_map/mul | solution.py:1266
  21.6 4.2 %collective-permute-start.6 = (bf16[128,640]{1,0:T(8,128)(2,1)S(1)}, bf16[128,640]{1,0:T(8,128)(2,1)S(1)}, u32[]{:S(2)}, u32[]{:S(2)}) collective-permute-start(bf16[128,640]{1,0:T(8,128)(2,1)S(1)} %get-tuple-element.123), channel_id=1, source_target_pairs={{0,4},{2,6},{4,8},{6,10},{8,12},{10,14},{12,0},{14,2},{1,5},{3,7},... | collective-permute-start | bytes 491528 | tf_op jit(solution)/shard_map/ppermute | solution.py:1238
  26.9 4.8 %collective-permute-done.6 = bf16[128,640]{1,0:T(8,128)(2,1)S(1)} collective-permute-done((bf16[128,640]{1,0:T(8,128)(2,1)S(1)}, bf16[128,640]{1,0:T(8,128)(2,1)S(1)}, u32[]{:S(2)}, u32[]{:S(2)}) %collective-permute-start.6) | collective-permute-done | bytes 163872 | tf_op jit(solution)/shard_map/ppermute | solution.py:1238
  34.3 3.3 %collective-permute-start.8 = (bf16[128,640]{1,0:T(8,128)(2,1)S(1)}, bf16[128,640]{1,0:T(8,128)(2,1)S(1)}, u32[]{:S(2)}, u32[]{:S(2)}) collective-permute-start(bf16[128,640]{1,0:T(8,128)(2,1)S(1)} %get-tuple-element.126), channel_id=1, source_target_pairs={{0,8},{2,10},{4,12},{6,14},{8,0},{10,2},{12,4},{14,6},{1,9},{3,11}... | collective-permute-start | bytes 491528 | tf_op jit(solution)/shard_map/ppermute | solution.py:1238
  39.2 25.5 %attend.1 = (bf16[1024,1280]{1,0:T(8,128)(2,1)}, bf16[512,1280]{1,0:T(8,128)(2,1)}, bf16[1024,48]{1,0:T(8,128)(2,1)}, bf16[512,640]{1,0:T(8,128)(2,1)}, bf16[102...) custom-call(s32[5]{0:T(128)} %stack.93.place, ...), custom_call_target="tpu_custom_call" | custom-call | flops 100000000 | bytes 100000 | tf_op jit(solution)/shard_map/attend/pallas_call | solution.py:323
  64.9 3.3 %collective-permute-done.12.other_ref.ao_ref = bf16[512,1408]{1,0:T(8,128)(2,1)S(1)} collective-permute-done((bf16[512,1408]{1,0:T(8,128)(2,1)}, bf16[512,1408]{1,0:T(8,128)(2,1)S(1)}, u32[]{:S(2)}, u32[]{:S(2)}) %collective-permute-start.12) | collective-permute-done | bytes 1441824 | tf_op jit(solution)/shard_map/ppermute | solution.py:1248
  69.4 22.9 %feed.1 = (bf16[512,1280]{1,0:T(8,128)(2,1)}, bf16[512,32]{1,0:T(8,128)(2,1)}, bf16[512,2560]{1,0:T(8,128)(2,1)}, bf16[512,2560]{1,0:T(8,128)(2,1)}, bf16[512,1408]{1,0:T(8,128)(2,1)}) custom-call(s32[5]{0:T(128)} %stack.93.place, bf16[512,1408]{1,0:T(8,128)(2,1)} %get-tuple-element.139.mine_ref.am_ref, bf16[512,1408]{1,0:T(8,128)(2,1)} %copy-done.23, ...), custom_call_target="tpu_custom_call" | custom-call | flops 24000000000 | bytes 30000000 | tf_op jit(solution)/shard_map/feed/pallas_call | solution.py:418
  92.5 3.3 %collective-permute-done.14.other_ref = bf16[512,1408]{1,0:T(8,128)(2,1)S(1)} collective-permute-done((bf16[512,1408]{1,0:T(8,128)(2,1)}, bf16[512,1408]{1,0:T(8,128)(2,1)S(1)}, u32[]{:S(2)}, u32[]{:S(2)}) %collective-permute-start.14) | collective-permute-done | bytes 1441824 | tf_op jit(solution)/shard_map/ppermute | solution.py:1248
  96.9 28.5 %feed_back.1 = (bf16[4,128,640]{2,1,0:T(8,128)(2,1)}, f32[512,1280]{1,0:T(8,128)}, bf16[512,1280]{1,0:T(8,128)(2,1)}, bf16[2,4,2,24,640]{4,3,2,1,0:T(8,128)(2,1)}) custom-call(s32[5]{0:T(128)} %stack.93.place, bf16[512,1408]{1,0:T(8,128)(2,1)} %get-tuple-element.143.mine_ref, bf16[512,1408]{1,0:T(8,128)(2,1)} %copy-done.24, ...), custom_call_target="tpu_custom_call" | custom-call | flops 30000001024 | bytes 40000000 | tf_op jit(solution)/shard_map/feed_back/pallas_call | solution.py:623
  129.9 28.6 %attend_back.1 = (bf16[512,640]{1,0:T(8,128)(2,1)}, bf16[1024,640]{1,0:T(8,128)(2,1)}, bf16[1024,640]{1,0:T(8,128)(2,1)}, f32[512,1280]{1,0:T(8,128)}, f32[16,1280]{1,0:T(8,128)}, /*index=5*/f32[16,640]{1,0:T(8,128)}) custom-call(s32[5]{0:T(128)} %stack.93.place, f32[512,1280]{1,0:T(8,128)} %get-tuple-element.150.res_ref, ...), custom_call_target="tpu_custom_call" | custom-call | flops 30000001024 | bytes 40000000 | tf_op jit(solution)/shard_map/attend_back/pallas_call | solution.py:806
  158.6 7.5 %others.1 = (bf16[1,512,640]{2,1,0:T(8,128)(2,1)}, bf16[1,512,640]{2,1,0:T(8,128)(2,1)}) custom-call(s32[5]{0:T(128)} %stack.93.place, bf16[4,2,128,640]{3,2,1,0:T(8,128)(2,1)} %bitcast.106, bf16[4,2,128,640]{3,2,1,0:T(8,128)(2,1)} %bitcast.108, bf16[3,1280,640]{2,1,0:T(8,128)(2,1)} %wv_ref.3, bf16[3,1280,640]{2,1,0:T(8,128)(2,1)} %wv_ref.3, ...), custom_call_target="tpu_custom_call" | custom-call | flops 7000000000 | bytes 10000000 | tf_op jit(solution)/shard_map/others/pallas_call | solution.py:916
  166.4 2.1 collective-permute-start.18
  168.5 1.9 collective-permute-start.19
  174.2 5.0 %grads.1 = bf16[2,4,2,16,640]{4,3,2,1,0:T(8,128)(2,1)S(1)} custom-call(s32[5]{0:T(128)S(1)} %copy-done.1, bf16[512,640]{1,0:T(8,128)(2,1)S(1)} %copy-done.8, bf16[1024,640]{1,0:T(8,128)(2,1)S(1)} %copy-done.5, bf16[1024,640]{1,0:T(8,128)(2,1)S(1)} %copy-done.6, bf16[3,16,640]{2,1,0:T(8,128)(2,1)S(1)} %copy-done.4, bf16[1024,48]{1,0:T(8,128)(2,1)S(1)} %copy-done.3, ...), custom_call_target="tpu_custom_call" | custom-call | flops 10000000000 | bytes 10000000 | tf_op jit(solution)/shard_map/grads/pallas_call | solution.py:1073
  179.9 2.6 %collective-permute-done.21 = bf16[2,128,640]{2,1,0:T(8,128)(2,1)S(1)} collective-permute-done((bf16[2,128,640]{2,1,0:T(8,128)(2,1)S(1)}, bf16[2,128,640]{2,1,0:T(8,128)(2,1)S(1)}, u32[]{:S(2)}, u32[]{:S(2)}) %collective-permute-start.21) | collective-permute-done | bytes 327712 | tf_op jit(solution)/shard_map/ppermute | solution.py:1242
  182.6 2.3 %collective-permute-start.24 = (bf16[2,128,640]{2,1,0:T(8,128)(2,1)S(1)}, bf16[2,128,640]{2,1,0:T(8,128)(2,1)S(1)}, u32[]{:S(2)}, u32[]{:S(2)}) collective-permute-start(bf16[2,128,640]{2,1,0:T(8,128)(2,1)S(1)} %pad_maximum_fusion.3), channel_id=1, source_target_pairs={{0,2},{2,0},{4,6},{6,4},{8,10},{10,8},{12,14},{14,12},{1,3},{3,1},... | collective-permute-start | bytes 983048 | tf_op jit(solution)/shard_map/ppermute | solution.py:1242
  187.5 5.8 %own.1 = (bf16[512,640]{1,0:T(8,128)(2,1)S(1)}, bf16[512,640]{1,0:T(8,128)(2,1)S(1)}) custom-call(s32[5]{0:T(128)S(1)} %copy-done.1, bf16[512,640]{1,0:T(8,128)(2,1)S(1)} %copy-done.8, bf16[4,2,128,640]{3,2,1,0:T(8,128)(2,1)S(1)} %bitcast.107, bf16[4,2,128,640]{3,2,1,0:T(8,128)(2,1)S(1)} %bitcast.109, bf16[3,1280,640]{2,1,0:T(8,128)(2,1)S(1)} %bitcast.103, ...), custom_call_target="tpu_custom_call" | custom-call | flops 7000000000 | bytes 10000000 | tf_op jit(solution)/shard_map/own/pallas_call | solution.py:979
  197.0 5.3 %collective-permute-start.30 = (bf16[160,640]{1,0:T(8,128)(2,1)S(1)}, bf16[160,640]{1,0:T(8,128)(2,1)S(1)}, u32[]{:S(2)}, u32[]{:S(2)}) collective-permute-start(bf16[160,640]{1,0:T(8,128)(2,1)S(1)} %pad_maximum_fusion.5), channel_id=1, source_target_pairs={{0,4},{2,6},{4,8},{6,10},{8,12},{10,14},{12,0},{14,2},{1,5},{3,7},... | collective-permute-start | bytes 614408 | tf_op jit(solution)/shard_map/ppermute | solution.py:1238
  207.3 2.3 %unpack_early.1 = (f32[8,2,16,40]{3,2,1,0:T(8,128)S(1)}, f32[8,16,80]{2,1,0:T(8,128)S(1)}, f32[8,16,8,20]{3,2,1,0:T(8,128)}, f32[8,2,16,8,20]{4,3,2,1,0:T(8,128)}) custom-call(s32[5]{0:T(128)S(1)} %copy-done.1, s32[2,4]{1,0:T(2,128)S(1)} %bitcast.104, bf16[176,640]{1,0:T(8,128)(2,1)S(1)} %get-tuple-element.200.refs_0_, ...), custom_call_target="tpu_custom_call" | custom-call | flops 1000000 | bytes 8000000 | tf_op jit(solution)/shard_map/unpack_early/pallas_call | solution.py:1187
  209.6 7.4 %collective-permute-done.31.refs_2_ = bf16[160,640]{1,0:T(8,128)(2,1)S(1)} collective-permute-done((bf16[160,640]{1,0:T(8,128)(2,1)S(1)}, bf16[160,640]{1,0:T(8,128)(2,1)S(1)}, u32[]{:S(2)}, u32[]{:S(2)}) %collective-permute-start.31) | collective-permute-done | bytes 204832 | tf_op jit(solution)/shard_map/ppermute | solution.py:1238
  219.4 2.2 join.3
  223.9 2.0 unpack_late.1
  (183 shorter events, 44.7 us)
Async XLA Ops:
  2.8 16.4 %collective-permute-start = (bf16[136,640]{1,0:T(8,128)(2,1)S(1)}, bf16[136,640]{1,0:T(8,128)(2,1)S(1)}, u32[]{:S(2)}, u32[]{:S(2)}) collective-permute-start(bf16[136,640]{1,0:T(8,128)(2,1)S(1)} %pad_maximum_fusion.9), channel_id=1, source_target_pairs={{0,4},{2,6},{4,8},{6,10},{8,12},{10,14},{12,0},{14,2},{1,5},{3,7},... | collective-permute-start | bytes 522248 | tf_op jit(solution)/shard_map/ppermute | solution.py:1238
  6.0 14.0 %collective-permute-start.1 = (bf16[136,640]{1,0:T(8,128)(2,1)S(1)}, bf16[136,640]{1,0:T(8,128)(2,1)S(1)}, u32[]{:S(2)}, u32[]{:S(2)}) collective-permute-start(bf16[136,640]{1,0:T(8,128)(2,1)S(1)} %pad_maximum_fusion.10), channel_id=1, source_target_pairs={{0,8},{2,10},{4,12},{6,14},{8,0},{10,2},{12,4},{14,6},{1,9},{3,11}... | collective-permute-start | bytes 522248 | tf_op jit(solution)/shard_map/ppermute | solution.py:1238
  8.6 11.3 %collective-permute-start.2 = (bf16[136,640]{1,0:T(8,128)(2,1)S(1)}, bf16[136,640]{1,0:T(8,128)(2,1)S(1)}, u32[]{:S(2)}, u32[]{:S(2)}) collective-permute-start(bf16[136,640]{1,0:T(8,128)(2,1)S(1)} %pad_maximum_fusion.11), channel_id=1, source_target_pairs={{0,12},{2,14},{4,0},{6,2},{8,4},{10,6},{12,8},{14,10},{1,13},{3,15... | collective-permute-start | bytes 522248 | tf_op jit(solution)/shard_map/ppermute | solution.py:1238
  10.0 9.1 %collective-permute-start.3 = (s32[4]{0:T(128)S(1)}, s32[4]{0:T(128)S(1)}, u32[]{:S(2)}, u32[]{:S(2)}) collective-permute-start(s32[4]{0:T(128)S(1)} %copy-done.22), channel_id=1, source_target_pairs={{0,16},{16,0},{1,17},{17,1},{2,18},{18,2},{3,19},{19,3},{4,20},{20... | collective-permute-start | bytes 56 | tf_op jit(solution)/shard_map/ppermute | solution.py:1245
  11.6 8.4 %collective-permute-start.4 = (bf16[136,640]{1,0:T(8,128)(2,1)S(1)}, bf16[136,640]{1,0:T(8,128)(2,1)S(1)}, u32[]{:S(2)}, u32[]{:S(2)}) collective-permute-start(bf16[136,640]{1,0:T(8,128)(2,1)S(1)} %pad_maximum_fusion.8.refs_1_), channel_id=1, source_target_pairs={{0,2},{2,0},{4,6},{6,4},{8,10},{10,8},{12,14},{14,12},{1,3},{3,1},... | collective-permute-start | bytes 522248 | tf_op jit(solution)/shard_map/ppermute | solution.py:1242
  20.0 13.8 %collective-permute-start.5 = (bf16[3,136,640]{2,1,0:T(8,128)(2,1)S(1)}, bf16[3,136,640]{2,1,0:T(8,128)(2,1)S(1)}, u32[]{:S(2)}, u32[]{:S(2)}) collective-permute-start(bf16[3,136,640]{2,1,0:T(8,128)(2,1)S(1)} %pad_maximum_fusion.refs_2_), channel_id=1, source_target_pairs={{0,2},{2,0},{4,6},{6,4},{8,10},{10,8},{12,14},{14,12},{1,3},{3,1},... | collective-permute-start | bytes 1566728 | tf_op jit(solution)/shard_map/ppermute | solution.py:1242
  21.6 10.1 %collective-permute-start.6 = (bf16[128,640]{1,0:T(8,128)(2,1)S(1)}, bf16[128,640]{1,0:T(8,128)(2,1)S(1)}, u32[]{:S(2)}, u32[]{:S(2)}) collective-permute-start(bf16[128,640]{1,0:T(8,128)(2,1)S(1)} %get-tuple-element.123), channel_id=1, source_target_pairs={{0,4},{2,6},{4,8},{6,10},{8,12},{10,14},{12,0},{14,2},{1,5},{3,7},... | collective-permute-start | bytes 491528 | tf_op jit(solution)/shard_map/ppermute | solution.py:1238
  25.8 7.6 %collective-permute-start.7 = (bf16[128,640]{1,0:T(8,128)(2,1)S(1)}, bf16[128,640]{1,0:T(8,128)(2,1)S(1)}, u32[]{:S(2)}, u32[]{:S(2)}) collective-permute-start(bf16[128,640]{1,0:T(8,128)(2,1)S(1)} %get-tuple-element.124), channel_id=1, source_target_pairs={{0,12},{2,14},{4,0},{6,2},{8,4},{10,6},{12,8},{14,10},{1,13},{3,15... | collective-permute-start | bytes 491528 | tf_op jit(solution)/shard_map/ppermute | solution.py:1238
  26.9 11.3 %collective-permute-start.9 = (bf16[3,136,640]{2,1,0:T(8,128)(2,1)S(1)}, bf16[3,136,640]{2,1,0:T(8,128)(2,1)S(1)}, u32[]{:S(2)}, u32[]{:S(2)}) collective-permute-start(bf16[3,136,640]{2,1,0:T(8,128)(2,1)S(1)} %pad_maximum_fusion.refs_2_), channel_id=1, source_target_pairs={{0,1},{1,0},{2,3},{3,2},{4,5},{5,4},{6,7},{7,6},{8,9},{9,8},{10,11... | collective-permute-start | bytes 1566728 | tf_op jit(solution)/shard_map/ppermute | solution.py:1248
  34.3 30.4 %collective-permute-start.8 = (bf16[128,640]{1,0:T(8,128)(2,1)S(1)}, bf16[128,640]{1,0:T(8,128)(2,1)S(1)}, u32[]{:S(2)}, u32[]{:S(2)}) collective-permute-start(bf16[128,640]{1,0:T(8,128)(2,1)S(1)} %get-tuple-element.126), channel_id=1, source_target_pairs={{0,8},{2,10},{4,12},{6,14},{8,0},{10,2},{12,4},{14,6},{1,9},{3,11}... | collective-permute-start | bytes 491528 | tf_op jit(solution)/shard_map/ppermute | solution.py:1238
  68.3 24.0 %collective-permute-start.13 = (bf16[3,128,640]{2,1,0:T(8,128)(2,1)S(1)}, bf16[3,128,640]{2,1,0:T(8,128)(2,1)S(1)}, u32[]{:S(2)}, u32[]{:S(2)}) collective-permute-start(bf16[3,128,640]{2,1,0:T(8,128)(2,1)S(1)} %pad_maximum_fusion.1.g_mine_ref), channel_id=1, source_target_pairs={{0,1},{1,0},{2,3},{3,2},{4,5},{5,4},{6,7},{7,6},{8,9},{9,8},{10,11... | collective-permute-start | bytes 1474568 | tf_op jit(solution)/shard_map/ppermute | solution.py:1248
  126.6 31.9 %collective-permute-start.15 = (bf16[4,2,24,640]{3,2,1,0:T(8,128)(2,1)S(1)}, bf16[4,2,24,640]{3,2,1,0:T(8,128)(2,1)S(1)}, u32[]{:S(2)}, u32[]{:S(2)}) collective-permute-start(bf16[4,2,24,640]{3,2,1,0:T(8,128)(2,1)S(1)} %dynamic-slice_bitcast_fusion), channel_id=1, source_target_pairs={{0,2},{2,0},{4,6},{6,4},{8,10},{10,8},{12,14},{14,12},{1,3},{3,1},... | collective-permute-start | bytes 737288 | tf_op jit(solution)/shard_map/ppermute | solution.py:1242
  166.1 4.9 %collective-permute-start.17 = (bf16[1,512,640]{2,1,0:T(8,128)(2,1)}, bf16[1,512,640]{2,1,0:T(8,128)(2,1)S(1)}, u32[]{:S(2)}, u32[]{:S(2)}) collective-permute-start(bf16[1,512,640]{2,1,0:T(8,128)(2,1)} %get-tuple-element.167), channel_id=1, source_target_pairs={{0,1},{1,0},{2,3},{3,2},{4,5},{5,4},{6,7},{7,6},{8,9},{9,8},{10,11... | collective-permute-start | bytes 1966088 | tf_op jit(solution)/shard_map/ppermute | solution.py:1248
  166.4 18.5 %collective-permute-start.18 = (bf16[176,640]{1,0:T(8,128)(2,1)S(1)}, bf16[176,640]{1,0:T(8,128)(2,1)S(1)}, u32[]{:S(2)}, u32[]{:S(2)}) collective-permute-start(bf16[176,640]{1,0:T(8,128)(2,1)S(1)} %get-tuple-element.243), channel_id=1, source_target_pairs={{0,4},{2,6},{4,8},{6,10},{8,12},{10,14},{12,0},{14,2},{1,5},{3,7},... | collective-permute-start | bytes 675848 | tf_op jit(solution)/shard_map/ppermute | solution.py:1238
  168.5 17.3 %collective-permute-start.19 = (bf16[176,640]{1,0:T(8,128)(2,1)S(1)}, bf16[176,640]{1,0:T(8,128)(2,1)S(1)}, u32[]{:S(2)}, u32[]{:S(2)}) collective-permute-start(bf16[176,640]{1,0:T(8,128)(2,1)S(1)} %get-tuple-element.244), channel_id=1, source_target_pairs={{0,8},{2,10},{4,12},{6,14},{8,0},{10,2},{12,4},{14,6},{1,9},{3,11}... | collective-permute-start | bytes 675848 | tf_op jit(solution)/shard_map/ppermute | solution.py:1238
  170.4 15.4 %collective-permute-start.20 = (bf16[176,640]{1,0:T(8,128)(2,1)S(1)}, bf16[176,640]{1,0:T(8,128)(2,1)S(1)}, u32[]{:S(2)}, u32[]{:S(2)}) collective-permute-start(bf16[176,640]{1,0:T(8,128)(2,1)S(1)} %get-tuple-element.241), channel_id=1, source_target_pairs={{0,12},{2,14},{4,0},{6,2},{8,4},{10,6},{12,8},{14,10},{1,13},{3,15... | collective-permute-start | bytes 675848 | tf_op jit(solution)/shard_map/ppermute | solution.py:1238
  172.6 10.0 %collective-permute-start.21 = (bf16[2,128,640]{2,1,0:T(8,128)(2,1)S(1)}, bf16[2,128,640]{2,1,0:T(8,128)(2,1)S(1)}, u32[]{:S(2)}, u32[]{:S(2)}) collective-permute-start(bf16[2,128,640]{2,1,0:T(8,128)(2,1)S(1)} %pad_maximum_fusion.2), channel_id=1, source_target_pairs={{0,2},{2,0},{4,6},{6,4},{8,10},{10,8},{12,14},{14,12},{1,3},{3,1},... | collective-permute-start | bytes 983048 | tf_op jit(solution)/shard_map/ppermute | solution.py:1242
  179.3 14.1 %collective-permute-start.22 = (bf16[4,2,16,640]{3,2,1,0:T(8,128)(2,1)S(1)}, bf16[4,2,16,640]{3,2,1,0:T(8,128)(2,1)S(1)}, u32[]{:S(2)}, u32[]{:S(2)}) collective-permute-start(bf16[4,2,16,640]{3,2,1,0:T(8,128)(2,1)S(1)} %get-tuple-element.250), channel_id=1, source_target_pairs={{0,2},{2,0},{4,6},{6,4},{8,10},{10,8},{12,14},{14,12},{1,3},{3,1},... | collective-permute-start | bytes 491528 | tf_op jit(solution)/shard_map/ppermute | solution.py:1242
  182.6 10.8 %collective-permute-start.24 = (bf16[2,128,640]{2,1,0:T(8,128)(2,1)S(1)}, bf16[2,128,640]{2,1,0:T(8,128)(2,1)S(1)}, u32[]{:S(2)}, u32[]{:S(2)}) collective-permute-start(bf16[2,128,640]{2,1,0:T(8,128)(2,1)S(1)} %pad_maximum_fusion.3), channel_id=1, source_target_pairs={{0,2},{2,0},{4,6},{6,4},{8,10},{10,8},{12,14},{14,12},{1,3},{3,1},... | collective-permute-start | bytes 983048 | tf_op jit(solution)/shard_map/ppermute | solution.py:1242
  185.9 7.4 %collective-permute-start.23 = (bf16[4,24,640]{2,1,0:T(8,128)(2,1)S(1)}, bf16[4,24,640]{2,1,0:T(8,128)(2,1)S(1)}, u32[]{:S(2)}, u32[]{:S(2)}) collective-permute-start(bf16[4,24,640]{2,1,0:T(8,128)(2,1)S(1)} %pad_maximum_fusion.12), channel_id=1, source_target_pairs={{0,16},{16,0},{1,17},{17,1},{2,18},{18,2},{3,19},{19,3},{4,20},{20... | collective-permute-start | bytes 368648 | tf_op jit(solution)/shard_map/ppermute | solution.py:1245
  196.8 10.4 %collective-permute-start.33 = (bf16[4,24,640]{2,1,0:T(8,128)(2,1)S(1)}, bf16[4,24,640]{2,1,0:T(8,128)(2,1)S(1)}, u32[]{:S(2)}, u32[]{:S(2)}) collective-permute-start(bf16[4,24,640]{2,1,0:T(8,128)(2,1)S(1)} %collective-permute-done.23.refs_8_), channel_id=1, source_target_pairs={{0,1},{1,0},{2,3},{3,2},{4,5},{5,4},{6,7},{7,6},{8,9},{9,8},{10,11... | collective-permute-start | bytes 368648 | tf_op jit(solution)/shard_map/ppermute | solution.py:1248
  197.0 12.6 %collective-permute-start.30 = (bf16[160,640]{1,0:T(8,128)(2,1)S(1)}, bf16[160,640]{1,0:T(8,128)(2,1)S(1)}, u32[]{:S(2)}, u32[]{:S(2)}) collective-permute-start(bf16[160,640]{1,0:T(8,128)(2,1)S(1)} %pad_maximum_fusion.5), channel_id=1, source_target_pairs={{0,4},{2,6},{4,8},{6,10},{8,12},{10,14},{12,0},{14,2},{1,5},{3,7},... | collective-permute-start | bytes 614408 | tf_op jit(solution)/shard_map/ppermute | solution.py:1238
  202.3 14.8 %collective-permute-start.31 = (bf16[160,640]{1,0:T(8,128)(2,1)S(1)}, bf16[160,640]{1,0:T(8,128)(2,1)S(1)}, u32[]{:S(2)}, u32[]{:S(2)}) collective-permute-start(bf16[160,640]{1,0:T(8,128)(2,1)S(1)} %pad_maximum_fusion.6), channel_id=1, source_target_pairs={{0,8},{2,10},{4,12},{6,14},{8,0},{10,2},{12,4},{14,6},{1,9},{3,11}... | collective-permute-start | bytes 614408 | tf_op jit(solution)/shard_map/ppermute | solution.py:1238
  203.1 13.9 %collective-permute-start.32 = (bf16[160,640]{1,0:T(8,128)(2,1)S(1)}, bf16[160,640]{1,0:T(8,128)(2,1)S(1)}, u32[]{:S(2)}, u32[]{:S(2)}) collective-permute-start(bf16[160,640]{1,0:T(8,128)(2,1)S(1)} %pad_maximum_fusion.7), channel_id=1, source_target_pairs={{0,12},{2,14},{4,0},{6,2},{8,4},{10,6},{12,8},{14,10},{1,13},{3,15... | collective-permute-start | bytes 614408 | tf_op jit(solution)/shard_map/ppermute | solution.py:1238
  (45 other events, 277.0 us)

commit v9 on v8

--- a/solution.py
+++ b/solution.py
@@ -126,6 +126,13 @@
 def params(small=False, limit=None):
     limit = limit or (SMALL_LIMIT if small else VMEM_LIMIT)
     return pltpu.CompilerParams(vmem_limit_bytes=limit)
+
+
+def near_last(out, place):
+    return [
+        pltpu.VMEM(o[0], o[1]) if n == place else jax.ShapeDtypeStruct(o[0], o[1])
+        for n, o in enumerate(out)
+    ]
 
 
 def cost(flops, moved, transcendentals=0):
@@ -435,7 +442,7 @@
                 pltpu.VMEM((rows, model + LANES), f32),
             ],
         ),
-        out_shape=[jax.ShapeDtypeStruct(o[0], o[1]) for o in out],
+        out_shape=near_last(out, 4),
         compiler_params=params(),
         cost_estimate=cost(2.4e10, 3e7),
         name="feed",
@@ -661,7 +668,7 @@
                 pltpu.VMEM((chunk, model), bf16),
             ],
         ),
-        out_shape=[jax.ShapeDtypeStruct(o[0], o[1]) for o in out],
+        out_shape=near_last(out, 2),
         compiler_params=params(),
         cost_estimate=cost(3e10, 4e7),
         name="feed_back",
@@ -1297,17 +1304,18 @@
     g_mine, attn_other = tie((g_mine, attn_other))
     g_other = other_core(g_mine)
     mid, u_gu, gate, up, down_msg = run_feed(
-        place, attn_msg, attn_other, h_own, b_model, mix_rates, a_model, w_gate_up, b_hidden,
+        place, attn_msg, pltpu.with_memory_space_constraint(attn_other, pltpu.VMEM), h_own,
+        b_model, mix_rates, a_model, w_gate_up, b_hidden,
         w_down, a_hidden, mlp_scales, 512, slabs,
     )
     g_other, down_msg = tie((g_other, down_msg))
-    down_other = other_core(down_msg)
+    down_other = pltpu.with_memory_space_constraint(other_core(down_msg), pltpu.VMEM)
     out_half, mid_res, mid_msg, early = run_feed_back(
         place, down_msg, down_other, mid, cotangent, g_mine, g_other, b_model, mix_rates,
         a_model, u_gu, gate, up, w_gate_up, b_hidden, w_down, a_hidden, mlp_scales, 512, group,
         n_seq,
     )
-    mid_other = other_core(mid_msg)
+    mid_other = pltpu.with_memory_space_constraint(other_core(mid_msg), pltpu.VMEM)
 
     order = (slab - jnp.arange(slabs, dtype=i32)) % slabs
     index = jnp.stack(index)[:, order]

time: 229 us -> 224 us (0.978)
  local copies, waits for them, and re-layouts: 11 us -> 7.88 us
    unnamed x58 -> x56, local copies, waits for them, and re-layouts: 4.29 us -> 1.1 us
where the time goes in v9:
time: 224 us; the launch traced here: 221 us
  Pallas kernels  131 us (58%)
  starting transfers between devices  45.3 us (20%)
  waiting for transfers between devices  29.4 us (13%)
  local copies, waits for them, and re-layouts  7.88 us (4%)
  other arithmetic  6.36 us (3%)
    pallas_call x1, Pallas kernels, run_attend_back(): pl.pallas_call(functools.partial(attend_back_kernel, (slabs, chunk, group...  28.4 us
    pallas_call x1, Pallas kernels, run_feed_back(): pl.pallas_call(functools.partial(feed_back_kernel, (slabs, chunk, group,...  28.3 us
    ppermute x12, starting transfers between devices, to_slab(): return lax.ppermute(array, 'ctx', pairs)  27.9 us
    pallas_call x1, Pallas kernels, run_attend(): pl.pallas_call(functools.partial(attend_kernel, (slabs, chunk, group, hea...  25.5 us
    pallas_call x1, Pallas kernels, run_feed(): pl.pallas_call(functools.partial(feed_kernel, (rank, model, slabs)), grid...  22.2 us
    ppermute x12, waiting for transfers between devices, to_slab(): return lax.ppermute(array, 'ctx', pairs)  15.5 us
    ppermute x19, waiting for transfers between devices, other_core(): return lax.ppermute(array, 'wt', [(0, 1), (1, 0)])  10.2 us
    ppermute x6, starting transfers between devices, within_slab(): return lax.ppermute(array, 'ctx', pairs)  9.45 us
  transfers between devices with their start and end apart: 40, of which 19 were waited for; matrix products, arithmetic and copies ran while one was open for 5% of the time, Pallas kernels for 42%

profile of v9, /device:TPU:0, one launch (start us, length us, event | category | flops | bytes accessed | tf_op | source)
XLA Modules:
  0.0 221.4 jit_solution(17364058854303311777)
XLA Ops:
  2.8 3.1 %collective-permute-start = (bf16[136,640]{1,0:T(8,128)(2,1)S(1)}, bf16[136,640]{1,0:T(8,128)(2,1)S(1)}, u32[]{:S(2)}, u32[]{:S(2)}) collective-permute-start(bf16[136,640]{1,0:T(8,128)(2,1)S(1)} %pad_maximum_fusion.9), channel_id=1, source_target_pairs={{0,4},{2,6},{4,8},{6,10},{8,12},{10,14},{12,0},{14,2},{1,5},{3,7},... | collective-permute-start | bytes 522248 | tf_op jit(solution)/shard_map/ppermute | solution.py:1245
  6.0 2.7 %collective-permute-start.1 = (bf16[136,640]{1,0:T(8,128)(2,1)S(1)}, bf16[136,640]{1,0:T(8,128)(2,1)S(1)}, u32[]{:S(2)}, u32[]{:S(2)}) collective-permute-start(bf16[136,640]{1,0:T(8,128)(2,1)S(1)} %pad_maximum_fusion.10), channel_id=1, source_target_pairs={{0,8},{2,10},{4,12},{6,14},{8,0},{10,2},{12,4},{14,6},{1,9},{3,11}... | collective-permute-start | bytes 522248 | tf_op jit(solution)/shard_map/ppermute | solution.py:1245
  13.2 3.1 %fusion = (f32[1024,128]{1,0:T(8,128)}, f32[1024,128]{1,0:T(8,128)}) fusion(f32[128]{0:T(128)S(1)} %get-tuple-element.261, f32[128]{0:T(128)S(1)} %get-tuple-element.262, f32[1024]{0:T(1024)S(1)} %iota_convert_fusion), kind=kLoop, calls=%fused_computation.13 | loop fusion | flops 262144 | bytes 1053696 | tf_op jit(solution)/shard_map/mul | solution.py:1273
  21.6 4.2 %collective-permute-start.6 = (bf16[128,640]{1,0:T(8,128)(2,1)S(1)}, bf16[128,640]{1,0:T(8,128)(2,1)S(1)}, u32[]{:S(2)}, u32[]{:S(2)}) collective-permute-start(bf16[128,640]{1,0:T(8,128)(2,1)S(1)} %get-tuple-element.123), channel_id=1, source_target_pairs={{0,4},{2,6},{4,8},{6,10},{8,12},{10,14},{12,0},{14,2},{1,5},{3,7},... | collective-permute-start | bytes 491528 | tf_op jit(solution)/shard_map/ppermute | solution.py:1245
  26.9 4.8 %collective-permute-done.6 = bf16[128,640]{1,0:T(8,128)(2,1)S(1)} collective-permute-done((bf16[128,640]{1,0:T(8,128)(2,1)S(1)}, bf16[128,640]{1,0:T(8,128)(2,1)S(1)}, u32[]{:S(2)}, u32[]{:S(2)}) %collective-permute-start.6) | collective-permute-done | bytes 163872 | tf_op jit(solution)/shard_map/ppermute | solution.py:1245
  34.3 3.3 %collective-permute-start.8 = (bf16[128,640]{1,0:T(8,128)(2,1)S(1)}, bf16[128,640]{1,0:T(8,128)(2,1)S(1)}, u32[]{:S(2)}, u32[]{:S(2)}) collective-permute-start(bf16[128,640]{1,0:T(8,128)(2,1)S(1)} %get-tuple-element.126), channel_id=1, source_target_pairs={{0,8},{2,10},{4,12},{6,14},{8,0},{10,2},{12,4},{14,6},{1,9},{3,11}... | collective-permute-start | bytes 491528 | tf_op jit(solution)/shard_map/ppermute | solution.py:1245
  39.2 25.5 %attend.1 = (bf16[1024,1280]{1,0:T(8,128)(2,1)}, bf16[512,1280]{1,0:T(8,128)(2,1)}, bf16[1024,48]{1,0:T(8,128)(2,1)}, bf16[512,640]{1,0:T(8,128)(2,1)}, bf16[102...) custom-call(s32[5]{0:T(128)} %stack.93.place, ...), custom_call_target="tpu_custom_call" | custom-call | flops 100000000 | bytes 100000 | tf_op jit(solution)/shard_map/attend/pallas_call | solution.py:330
  64.9 3.3 %collective-permute-done.12.other_ref.ao_ref = bf16[512,1408]{1,0:T(8,128)(2,1)S(1)} collective-permute-done((bf16[512,1408]{1,0:T(8,128)(2,1)}, bf16[512,1408]{1,0:T(8,128)(2,1)S(1)}, u32[]{:S(2)}, u32[]{:S(2)}) %collective-permute-start.12) | collective-permute-done | bytes 1441824 | tf_op jit(solution)/shard_map/ppermute | solution.py:1255
  68.4 22.2 %feed.1 = (bf16[512,1280]{1,0:T(8,128)(2,1)}, bf16[512,32]{1,0:T(8,128)(2,1)}, bf16[512,2560]{1,0:T(8,128)(2,1)}, bf16[512,2560]{1,0:T(8,128)(2,1)}, bf16[512,1408]{1,0:T(8,128)(2,1)S(1)}) custom-call(s32[5]{0:T(128)} %stack.93.place, bf16[512,1408]{1,0:T(8,128)(2,1)} %get-tuple-element.139.mine_ref.am_ref, ...), custom_call_target="tpu_custom_call" | custom-call | flops 24000000000 | bytes 30000000 | tf_op jit(solution)/shard_map/feed/pallas_call | solution.py:425
  91.1 2.8 %collective-permute-done.14.other_ref = bf16[512,1408]{1,0:T(8,128)(2,1)S(1)} collective-permute-done((bf16[512,1408]{1,0:T(8,128)(2,1)S(1)}, bf16[512,1408]{1,0:T(8,128)(2,1)S(1)}, u32[]{:S(2)}, u32[]{:S(2)}) %collective-permute-start.14) | collective-permute-done | bytes 1441824 | tf_op jit(solution)/shard_map/ppermute | solution.py:1255
  94.0 28.3 %feed_back.1 = (bf16[4,128,640]{2,1,0:T(8,128)(2,1)}, f32[512,1280]{1,0:T(8,128)}, bf16[512,1280]{1,0:T(8,128)(2,1)}, bf16[2,4,2,24,640]{4,3,2,1,0:T(8,128)(2,1)}) custom-call(s32[5]{0:T(128)} %stack.93.place, bf16[512,1408]{1,0:T(8,128)(2,1)} %copy-done.4, bf16[512,1408]{1,0:T(8,128)(2,1)S(1)} %collective-permute-done.14.other_ref, ...), custom_call_target="tpu_custom_call" | custom-call | flops 30000001024 | bytes 40000000 | tf_op jit(solution)/shard_map/feed_back/pallas_call | solution.py:630
  125.6 28.4 %attend_back.1 = (bf16[512,640]{1,0:T(8,128)(2,1)}, bf16[1024,640]{1,0:T(8,128)(2,1)}, bf16[1024,640]{1,0:T(8,128)(2,1)}, f32[512,1280]{1,0:T(8,128)}, f32[16,1280]{1,0:T(8,128)}, /*index=5*/f32[16,640]{1,0:T(8,128)}) custom-call(s32[5]{0:T(128)} %stack.93.place, f32[512,1280]{1,0:T(8,128)} %get-tuple-element.150.res_ref, ...), custom_call_target="tpu_custom_call" | custom-call | flops 30000001024 | bytes 40000000 | tf_op jit(solution)/shard_map/attend_back/pallas_call | solution.py:813
  154.1 7.5 %others.1 = (bf16[1,512,640]{2,1,0:T(8,128)(2,1)}, bf16[1,512,640]{2,1,0:T(8,128)(2,1)}) custom-call(s32[5]{0:T(128)} %stack.93.place, bf16[4,2,128,640]{3,2,1,0:T(8,128)(2,1)} %bitcast.106, bf16[4,2,128,640]{3,2,1,0:T(8,128)(2,1)} %bitcast.108, bf16[3,1280,640]{2,1,0:T(8,128)(2,1)} %wv_ref.3, bf16[3,1280,640]{2,1,0:T(8,128)(2,1)} %wv_ref.3, ...), custom_call_target="tpu_custom_call" | custom-call | flops 7000000000 | bytes 10000000 | tf_op jit(solution)/shard_map/others/pallas_call | solution.py:923
  162.1 2.1 collective-permute-start.18
  164.2 1.9 collective-permute-start.19
  169.9 5.0 %grads.1 = bf16[2,4,2,16,640]{4,3,2,1,0:T(8,128)(2,1)S(1)} custom-call(s32[5]{0:T(128)S(1)} %copy-done.1, bf16[512,640]{1,0:T(8,128)(2,1)S(1)} %copy-done.10, bf16[1024,640]{1,0:T(8,128)(2,1)S(1)} %copy-done.7, bf16[1024,640]{1,0:T(8,128)(2,1)S(1)} %copy-done.8, bf16[3,16,640]{2,1,0:T(8,128)(2,1)S(1)} %copy-done.6, bf16[1024,48]{1,0:T(8,128)(2,1)S(1)} %copy-done.5, ...), custom_call_target="tpu_custom_call" | custom-call | flops 10000000000 | bytes 10000000 | tf_op jit(solution)/shard_map/grads/pallas_call | solution.py:1080
  175.6 2.4 %collective-permute-done.21 = bf16[2,128,640]{2,1,0:T(8,128)(2,1)S(1)} collective-permute-done((bf16[2,128,640]{2,1,0:T(8,128)(2,1)S(1)}, bf16[2,128,640]{2,1,0:T(8,128)(2,1)S(1)}, u32[]{:S(2)}, u32[]{:S(2)}) %collective-permute-start.21) | collective-permute-done | bytes 327712 | tf_op jit(solution)/shard_map/ppermute | solution.py:1249
  178.1 2.5 %collective-permute-start.24 = (bf16[2,128,640]{2,1,0:T(8,128)(2,1)S(1)}, bf16[2,128,640]{2,1,0:T(8,128)(2,1)S(1)}, u32[]{:S(2)}, u32[]{:S(2)}) collective-permute-start(bf16[2,128,640]{2,1,0:T(8,128)(2,1)S(1)} %pad_maximum_fusion.3), channel_id=1, source_target_pairs={{0,2},{2,0},{4,6},{6,4},{8,10},{10,8},{12,14},{14,12},{1,3},{3,1},... | collective-permute-start | bytes 983048 | tf_op jit(solution)/shard_map/ppermute | solution.py:1249
  183.0 5.8 %own.1 = (bf16[512,640]{1,0:T(8,128)(2,1)S(1)}, bf16[512,640]{1,0:T(8,128)(2,1)S(1)}) custom-call(s32[5]{0:T(128)S(1)} %copy-done.1, bf16[512,640]{1,0:T(8,128)(2,1)S(1)} %copy-done.10, bf16[4,2,128,640]{3,2,1,0:T(8,128)(2,1)S(1)} %bitcast.107, bf16[4,2,128,640]{3,2,1,0:T(8,128)(2,1)S(1)} %bitcast.109, bf16[3,1280,640]{2,1,0:T(8,128)(2,1)S(1)} %bitcast.103, ...), custom_call_target="tpu_custom_call" | custom-call | flops 7000000000 | bytes 10000000 | tf_op jit(solution)/shard_map/own/pallas_call | solution.py:986
  192.5 5.3 %collective-permute-start.30 = (bf16[160,640]{1,0:T(8,128)(2,1)S(1)}, bf16[160,640]{1,0:T(8,128)(2,1)S(1)}, u32[]{:S(2)}, u32[]{:S(2)}) collective-permute-start(bf16[160,640]{1,0:T(8,128)(2,1)S(1)} %pad_maximum_fusion.5), channel_id=1, source_target_pairs={{0,4},{2,6},{4,8},{6,10},{8,12},{10,14},{12,0},{14,2},{1,5},{3,7},... | collective-permute-start | bytes 614408 | tf_op jit(solution)/shard_map/ppermute | solution.py:1245
  202.8 2.3 %unpack_early.1 = (f32[8,2,16,40]{3,2,1,0:T(8,128)S(1)}, f32[8,16,80]{2,1,0:T(8,128)S(1)}, f32[8,16,8,20]{3,2,1,0:T(8,128)}, f32[8,2,16,8,20]{4,3,2,1,0:T(8,128)}) custom-call(s32[5]{0:T(128)S(1)} %copy-done.1, s32[2,4]{1,0:T(2,128)S(1)} %bitcast.104, bf16[176,640]{1,0:T(8,128)(2,1)S(1)} %get-tuple-element.200.refs_0_, ...), custom_call_target="tpu_custom_call" | custom-call | flops 1000000 | bytes 8000000 | tf_op jit(solution)/shard_map/unpack_early/pallas_call | solution.py:1194
  205.1 7.5 %collective-permute-done.31.refs_2_ = bf16[160,640]{1,0:T(8,128)(2,1)S(1)} collective-permute-done((bf16[160,640]{1,0:T(8,128)(2,1)S(1)}, bf16[160,640]{1,0:T(8,128)(2,1)S(1)}, u32[]{:S(2)}, u32[]{:S(2)}) %collective-permute-start.31) | collective-permute-done | bytes 204832 | tf_op jit(solution)/shard_map/ppermute | solution.py:1245
  214.9 2.2 join.3
  219.4 2.0 unpack_late.1
  (181 shorter events, 41.7 us)
Async XLA Ops:
  2.8 16.4 %collective-permute-start = (bf16[136,640]{1,0:T(8,128)(2,1)S(1)}, bf16[136,640]{1,0:T(8,128)(2,1)S(1)}, u32[]{:S(2)}, u32[]{:S(2)}) collective-permute-start(bf16[136,640]{1,0:T(8,128)(2,1)S(1)} %pad_maximum_fusion.9), channel_id=1, source_target_pairs={{0,4},{2,6},{4,8},{6,10},{8,12},{10,14},{12,0},{14,2},{1,5},{3,7},... | collective-permute-start | bytes 522248 | tf_op jit(solution)/shard_map/ppermute | solution.py:1245
  6.0 14.0 %collective-permute-start.1 = (bf16[136,640]{1,0:T(8,128)(2,1)S(1)}, bf16[136,640]{1,0:T(8,128)(2,1)S(1)}, u32[]{:S(2)}, u32[]{:S(2)}) collective-permute-start(bf16[136,640]{1,0:T(8,128)(2,1)S(1)} %pad_maximum_fusion.10), channel_id=1, source_target_pairs={{0,8},{2,10},{4,12},{6,14},{8,0},{10,2},{12,4},{14,6},{1,9},{3,11}... | collective-permute-start | bytes 522248 | tf_op jit(solution)/shard_map/ppermute | solution.py:1245
  8.6 11.3 %collective-permute-start.2 = (bf16[136,640]{1,0:T(8,128)(2,1)S(1)}, bf16[136,640]{1,0:T(8,128)(2,1)S(1)}, u32[]{:S(2)}, u32[]{:S(2)}) collective-permute-start(bf16[136,640]{1,0:T(8,128)(2,1)S(1)} %pad_maximum_fusion.11), channel_id=1, source_target_pairs={{0,12},{2,14},{4,0},{6,2},{8,4},{10,6},{12,8},{14,10},{1,13},{3,15... | collective-permute-start | bytes 522248 | tf_op jit(solution)/shard_map/ppermute | solution.py:1245
  10.0 9.2 %collective-permute-start.3 = (s32[4]{0:T(128)S(1)}, s32[4]{0:T(128)S(1)}, u32[]{:S(2)}, u32[]{:S(2)}) collective-permute-start(s32[4]{0:T(128)S(1)} %copy-done.24), channel_id=1, source_target_pairs={{0,16},{16,0},{1,17},{17,1},{2,18},{18,2},{3,19},{19,3},{4,20},{20... | collective-permute-start | bytes 56 | tf_op jit(solution)/shard_map/ppermute | solution.py:1252
  11.6 8.4 %collective-permute-start.4 = (bf16[136,640]{1,0:T(8,128)(2,1)S(1)}, bf16[136,640]{1,0:T(8,128)(2,1)S(1)}, u32[]{:S(2)}, u32[]{:S(2)}) collective-permute-start(bf16[136,640]{1,0:T(8,128)(2,1)S(1)} %pad_maximum_fusion.8.refs_1_), channel_id=1, source_target_pairs={{0,2},{2,0},{4,6},{6,4},{8,10},{10,8},{12,14},{14,12},{1,3},{3,1},... | collective-permute-start | bytes 522248 | tf_op jit(solution)/shard_map/ppermute | solution.py:1249
  20.0 13.8 %collective-permute-start.5 = (bf16[3,136,640]{2,1,0:T(8,128)(2,1)S(1)}, bf16[3,136,640]{2,1,0:T(8,128)(2,1)S(1)}, u32[]{:S(2)}, u32[]{:S(2)}) collective-permute-start(bf16[3,136,640]{2,1,0:T(8,128)(2,1)S(1)} %pad_maximum_fusion.refs_2_), channel_id=1, source_target_pairs={{0,2},{2,0},{4,6},{6,4},{8,10},{10,8},{12,14},{14,12},{1,3},{3,1},... | collective-permute-start | bytes 1566728 | tf_op jit(solution)/shard_map/ppermute | solution.py:1249
  21.6 10.1 %collective-permute-start.6 = (bf16[128,640]{1,0:T(8,128)(2,1)S(1)}, bf16[128,640]{1,0:T(8,128)(2,1)S(1)}, u32[]{:S(2)}, u32[]{:S(2)}) collective-permute-start(bf16[128,640]{1,0:T(8,128)(2,1)S(1)} %get-tuple-element.123), channel_id=1, source_target_pairs={{0,4},{2,6},{4,8},{6,10},{8,12},{10,14},{12,0},{14,2},{1,5},{3,7},... | collective-permute-start | bytes 491528 | tf_op jit(solution)/shard_map/ppermute | solution.py:1245
  25.8 7.6 %collective-permute-start.7 = (bf16[128,640]{1,0:T(8,128)(2,1)S(1)}, bf16[128,640]{1,0:T(8,128)(2,1)S(1)}, u32[]{:S(2)}, u32[]{:S(2)}) collective-permute-start(bf16[128,640]{1,0:T(8,128)(2,1)S(1)} %get-tuple-element.124), channel_id=1, source_target_pairs={{0,12},{2,14},{4,0},{6,2},{8,4},{10,6},{12,8},{14,10},{1,13},{3,15... | collective-permute-start | bytes 491528 | tf_op jit(solution)/shard_map/ppermute | solution.py:1245
  26.9 11.3 %collective-permute-start.9 = (bf16[3,136,640]{2,1,0:T(8,128)(2,1)S(1)}, bf16[3,136,640]{2,1,0:T(8,128)(2,1)S(1)}, u32[]{:S(2)}, u32[]{:S(2)}) collective-permute-start(bf16[3,136,640]{2,1,0:T(8,128)(2,1)S(1)} %pad_maximum_fusion.refs_2_), channel_id=1, source_target_pairs={{0,1},{1,0},{2,3},{3,2},{4,5},{5,4},{6,7},{7,6},{8,9},{9,8},{10,11... | collective-permute-start | bytes 1566728 | tf_op jit(solution)/shard_map/ppermute | solution.py:1255
  34.3 30.4 %collective-permute-start.8 = (bf16[128,640]{1,0:T(8,128)(2,1)S(1)}, bf16[128,640]{1,0:T(8,128)(2,1)S(1)}, u32[]{:S(2)}, u32[]{:S(2)}) collective-permute-start(bf16[128,640]{1,0:T(8,128)(2,1)S(1)} %get-tuple-element.126), channel_id=1, source_target_pairs={{0,8},{2,10},{4,12},{6,14},{8,0},{10,2},{12,4},{14,6},{1,9},{3,11}... | collective-permute-start | bytes 491528 | tf_op jit(solution)/shard_map/ppermute | solution.py:1245
  68.3 22.4 %collective-permute-start.13 = (bf16[3,128,640]{2,1,0:T(8,128)(2,1)S(1)}, bf16[3,128,640]{2,1,0:T(8,128)(2,1)S(1)}, u32[]{:S(2)}, u32[]{:S(2)}) collective-permute-start(bf16[3,128,640]{2,1,0:T(8,128)(2,1)S(1)} %pad_maximum_fusion.1.g_mine_ref), channel_id=1, source_target_pairs={{0,1},{1,0},{2,3},{3,2},{4,5},{5,4},{6,7},{7,6},{8,9},{9,8},{10,11... | collective-permute-start | bytes 1474568 | tf_op jit(solution)/shard_map/ppermute | solution.py:1255
  123.7 30.4 %collective-permute-start.15 = (bf16[4,2,24,640]{3,2,1,0:T(8,128)(2,1)S(1)}, bf16[4,2,24,640]{3,2,1,0:T(8,128)(2,1)S(1)}, u32[]{:S(2)}, u32[]{:S(2)}) collective-permute-start(bf16[4,2,24,640]{3,2,1,0:T(8,128)(2,1)S(1)} %dynamic-slice_bitcast_fusion), channel_id=1, source_target_pairs={{0,2},{2,0},{4,6},{6,4},{8,10},{10,8},{12,14},{14,12},{1,3},{3,1},... | collective-permute-start | bytes 737288 | tf_op jit(solution)/shard_map/ppermute | solution.py:1249
  161.5 5.1 %collective-permute-start.17 = (bf16[1,512,640]{2,1,0:T(8,128)(2,1)}, bf16[1,512,640]{2,1,0:T(8,128)(2,1)S(1)}, u32[]{:S(2)}, u32[]{:S(2)}) collective-permute-start(bf16[1,512,640]{2,1,0:T(8,128)(2,1)} %get-tuple-element.167), channel_id=1, source_target_pairs={{0,1},{1,0},{2,3},{3,2},{4,5},{5,4},{6,7},{7,6},{8,9},{9,8},{10,11... | collective-permute-start | bytes 1966088 | tf_op jit(solution)/shard_map/ppermute | solution.py:1255
  162.1 18.5 %collective-permute-start.18 = (bf16[176,640]{1,0:T(8,128)(2,1)S(1)}, bf16[176,640]{1,0:T(8,128)(2,1)S(1)}, u32[]{:S(2)}, u32[]{:S(2)}) collective-permute-start(bf16[176,640]{1,0:T(8,128)(2,1)S(1)} %get-tuple-element.243), channel_id=1, source_target_pairs={{0,4},{2,6},{4,8},{6,10},{8,12},{10,14},{12,0},{14,2},{1,5},{3,7},... | collective-permute-start | bytes 675848 | tf_op jit(solution)/shard_map/ppermute | solution.py:1245
  164.2 17.1 %collective-permute-start.19 = (bf16[176,640]{1,0:T(8,128)(2,1)S(1)}, bf16[176,640]{1,0:T(8,128)(2,1)S(1)}, u32[]{:S(2)}, u32[]{:S(2)}) collective-permute-start(bf16[176,640]{1,0:T(8,128)(2,1)S(1)} %get-tuple-element.244), channel_id=1, source_target_pairs={{0,8},{2,10},{4,12},{6,14},{8,0},{10,2},{12,4},{14,6},{1,9},{3,11}... | collective-permute-start | bytes 675848 | tf_op jit(solution)/shard_map/ppermute | solution.py:1245
  166.1 15.2 %collective-permute-start.20 = (bf16[176,640]{1,0:T(8,128)(2,1)S(1)}, bf16[176,640]{1,0:T(8,128)(2,1)S(1)}, u32[]{:S(2)}, u32[]{:S(2)}) collective-permute-start(bf16[176,640]{1,0:T(8,128)(2,1)S(1)} %get-tuple-element.241), channel_id=1, source_target_pairs={{0,12},{2,14},{4,0},{6,2},{8,4},{10,6},{12,8},{14,10},{1,13},{3,15... | collective-permute-start | bytes 675848 | tf_op jit(solution)/shard_map/ppermute | solution.py:1245
  168.2 9.7 %collective-permute-start.21 = (bf16[2,128,640]{2,1,0:T(8,128)(2,1)S(1)}, bf16[2,128,640]{2,1,0:T(8,128)(2,1)S(1)}, u32[]{:S(2)}, u32[]{:S(2)}) collective-permute-start(bf16[2,128,640]{2,1,0:T(8,128)(2,1)S(1)} %pad_maximum_fusion.2), channel_id=1, source_target_pairs={{0,2},{2,0},{4,6},{6,4},{8,10},{10,8},{12,14},{14,12},{1,3},{3,1},... | collective-permute-start | bytes 983048 | tf_op jit(solution)/shard_map/ppermute | solution.py:1249
  175.0 13.8 %collective-permute-start.22 = (bf16[4,2,16,640]{3,2,1,0:T(8,128)(2,1)S(1)}, bf16[4,2,16,640]{3,2,1,0:T(8,128)(2,1)S(1)}, u32[]{:S(2)}, u32[]{:S(2)}) collective-permute-start(bf16[4,2,16,640]{3,2,1,0:T(8,128)(2,1)S(1)} %get-tuple-element.250), channel_id=1, source_target_pairs={{0,2},{2,0},{4,6},{6,4},{8,10},{10,8},{12,14},{14,12},{1,3},{3,1},... | collective-permute-start | bytes 491528 | tf_op jit(solution)/shard_map/ppermute | solution.py:1249
  178.1 10.8 %collective-permute-start.24 = (bf16[2,128,640]{2,1,0:T(8,128)(2,1)S(1)}, bf16[2,128,640]{2,1,0:T(8,128)(2,1)S(1)}, u32[]{:S(2)}, u32[]{:S(2)}) collective-permute-start(bf16[2,128,640]{2,1,0:T(8,128)(2,1)S(1)} %pad_maximum_fusion.3), channel_id=1, source_target_pairs={{0,2},{2,0},{4,6},{6,4},{8,10},{10,8},{12,14},{14,12},{1,3},{3,1},... | collective-permute-start | bytes 983048 | tf_op jit(solution)/shard_map/ppermute | solution.py:1249
  181.4 7.4 %collective-permute-start.23 = (bf16[4,24,640]{2,1,0:T(8,128)(2,1)S(1)}, bf16[4,24,640]{2,1,0:T(8,128)(2,1)S(1)}, u32[]{:S(2)}, u32[]{:S(2)}) collective-permute-start(bf16[4,24,640]{2,1,0:T(8,128)(2,1)S(1)} %pad_maximum_fusion.12), channel_id=1, source_target_pairs={{0,16},{16,0},{1,17},{17,1},{2,18},{18,2},{3,19},{19,3},{4,20},{20... | collective-permute-start | bytes 368648 | tf_op jit(solution)/shard_map/ppermute | solution.py:1252
  192.3 10.4 %collective-permute-start.33 = (bf16[4,24,640]{2,1,0:T(8,128)(2,1)S(1)}, bf16[4,24,640]{2,1,0:T(8,128)(2,1)S(1)}, u32[]{:S(2)}, u32[]{:S(2)}) collective-permute-start(bf16[4,24,640]{2,1,0:T(8,128)(2,1)S(1)} %collective-permute-done.23.refs_8_), channel_id=1, source_target_pairs={{0,1},{1,0},{2,3},{3,2},{4,5},{5,4},{6,7},{7,6},{8,9},{9,8},{10,11... | collective-permute-start | bytes 368648 | tf_op jit(solution)/shard_map/ppermute | solution.py:1255
  192.5 12.6 %collective-permute-start.30 = (bf16[160,640]{1,0:T(8,128)(2,1)S(1)}, bf16[160,640]{1,0:T(8,128)(2,1)S(1)}, u32[]{:S(2)}, u32[]{:S(2)}) collective-permute-start(bf16[160,640]{1,0:T(8,128)(2,1)S(1)} %pad_maximum_fusion.5), channel_id=1, source_target_pairs={{0,4},{2,6},{4,8},{6,10},{8,12},{10,14},{12,0},{14,2},{1,5},{3,7},... | collective-permute-start | bytes 614408 | tf_op jit(solution)/shard_map/ppermute | solution.py:1245
  197.8 14.8 %collective-permute-start.31 = (bf16[160,640]{1,0:T(8,128)(2,1)S(1)}, bf16[160,640]{1,0:T(8,128)(2,1)S(1)}, u32[]{:S(2)}, u32[]{:S(2)}) collective-permute-start(bf16[160,640]{1,0:T(8,128)(2,1)S(1)} %pad_maximum_fusion.6), channel_id=1, source_target_pairs={{0,8},{2,10},{4,12},{6,14},{8,0},{10,2},{12,4},{14,6},{1,9},{3,11}... | collective-permute-start | bytes 614408 | tf_op jit(solution)/shard_map/ppermute | solution.py:1245
  198.6 13.9 %collective-permute-start.32 = (bf16[160,640]{1,0:T(8,128)(2,1)S(1)}, bf16[160,640]{1,0:T(8,128)(2,1)S(1)}, u32[]{:S(2)}, u32[]{:S(2)}) collective-permute-start(bf16[160,640]{1,0:T(8,128)(2,1)S(1)} %pad_maximum_fusion.7), channel_id=1, source_target_pairs={{0,12},{2,14},{4,0},{6,2},{8,4},{10,6},{12,8},{14,10},{1,13},{3,15... | collective-permute-start | bytes 614408 | tf_op jit(solution)/shard_map/ppermute | solution.py:1245
  (44 other events, 296.9 us)

commit v10 on v9

--- a/solution.py
+++ b/solution.py
@@ -1294,6 +1294,9 @@
             near[turn - 1], other_core(near[turn - 1]),
             peers[turn - 1], other_core(peers[turn - 1]),
         ]
+    if length * model < (1 << 21):
+        pieces[2:] = [pltpu.with_memory_space_constraint(p, pltpu.VMEM) for p in pieces[2:]]
+
     h_full, h_own, u, q, k, v, qi, ki, o, inv, attn_msg, start, bh, ah = run_attend(
         place, tokens, pieces, w_attn_in, a_model, b_heads, a_heads, cos, sin, scale,
         w_attn_out, group, head_dim,

time: 224 us -> 222 us (level)
  no operation moved by 1% of the time
where the time goes in v10:
time: 222 us; the launch traced here: 220 us
  Pallas kernels  130 us (59%)
  starting transfers between devices  45.4 us (20%)
  waiting for transfers between devices  29.4 us (13%)
  local copies, waits for them, and re-layouts  6.92 us (3%)
  other arithmetic  6.36 us (3%)
    pallas_call x1, Pallas kernels, run_attend_back(): pl.pallas_call(functools.partial(attend_back_kernel, (slabs, chunk, group...  28.4 us
    pallas_call x1, Pallas kernels, run_feed_back(): pl.pallas_call(functools.partial(feed_back_kernel, (slabs, chunk, group,...  28.4 us
    ppermute x12, starting transfers between devices, to_slab(): return lax.ppermute(array, 'ctx', pairs)  27.9 us
    pallas_call x1, Pallas kernels, run_attend(): pl.pallas_call(functools.partial(attend_kernel, (slabs, chunk, group, hea...  24.9 us
    pallas_call x1, Pallas kernels, run_feed(): pl.pallas_call(functools.partial(feed_kernel, (rank, model, slabs)), grid...  22.2 us
    ppermute x12, waiting for transfers between devices, to_slab(): return lax.ppermute(array, 'ctx', pairs)  15.4 us
    ppermute x19, waiting for transfers between devices, other_core(): return lax.ppermute(array, 'wt', [(0, 1), (1, 0)])  10.2 us
    ppermute x6, starting transfers between devices, within_slab(): return lax.ppermute(array, 'ctx', pairs)  9.47 us
  transfers between devices with their start and end apart: 40, of which 19 were waited for; matrix products, arithmetic and copies ran while one was open for 5% of the time, Pallas kernels for 42%

profile of v10, /device:TPU:0, one launch (start us, length us, event | category | flops | bytes accessed | tf_op | source)
XLA Modules:
  0.0 219.8 jit_solution(8658539034433912478)
XLA Ops:
  2.8 3.1 %collective-permute-start = (bf16[136,640]{1,0:T(8,128)(2,1)S(1)}, bf16[136,640]{1,0:T(8,128)(2,1)S(1)}, u32[]{:S(2)}, u32[]{:S(2)}) collective-permute-start(bf16[136,640]{1,0:T(8,128)(2,1)S(1)} %pad_maximum_fusion.9), channel_id=1, source_target_pairs={{0,4},{2,6},{4,8},{6,10},{8,12},{10,14},{12,0},{14,2},{1,5},{3,7},... | collective-permute-start | bytes 522248 | tf_op jit(solution)/shard_map/ppermute | solution.py:1245
  6.0 2.7 %collective-permute-start.1 = (bf16[136,640]{1,0:T(8,128)(2,1)S(1)}, bf16[136,640]{1,0:T(8,128)(2,1)S(1)}, u32[]{:S(2)}, u32[]{:S(2)}) collective-permute-start(bf16[136,640]{1,0:T(8,128)(2,1)S(1)} %pad_maximum_fusion.10), channel_id=1, source_target_pairs={{0,8},{2,10},{4,12},{6,14},{8,0},{10,2},{12,4},{14,6},{1,9},{3,11}... | collective-permute-start | bytes 522248 | tf_op jit(solution)/shard_map/ppermute | solution.py:1245
  13.2 3.1 %fusion = (f32[1024,128]{1,0:T(8,128)}, f32[1024,128]{1,0:T(8,128)}) fusion(f32[128]{0:T(128)S(1)} %get-tuple-element.261, f32[128]{0:T(128)S(1)} %get-tuple-element.262, f32[1024]{0:T(1024)S(1)} %iota_convert_fusion), kind=kLoop, calls=%fused_computation.13 | loop fusion | flops 262144 | bytes 1053696 | tf_op jit(solution)/shard_map/mul | solution.py:1273
  21.6 4.2 %collective-permute-start.6 = (bf16[128,640]{1,0:T(8,128)(2,1)S(1)}, bf16[128,640]{1,0:T(8,128)(2,1)S(1)}, u32[]{:S(2)}, u32[]{:S(2)}) collective-permute-start(bf16[128,640]{1,0:T(8,128)(2,1)S(1)} %get-tuple-element.123), channel_id=1, source_target_pairs={{0,4},{2,6},{4,8},{6,10},{8,12},{10,14},{12,0},{14,2},{1,5},{3,7},... | collective-permute-start | bytes 491528 | tf_op jit(solution)/shard_map/ppermute | solution.py:1245
  26.9 4.8 %collective-permute-done.6 = bf16[128,640]{1,0:T(8,128)(2,1)S(1)} collective-permute-done((bf16[128,640]{1,0:T(8,128)(2,1)S(1)}, bf16[128,640]{1,0:T(8,128)(2,1)S(1)}, u32[]{:S(2)}, u32[]{:S(2)}) %collective-permute-start.6) | collective-permute-done | bytes 163872 | tf_op jit(solution)/shard_map/ppermute | solution.py:1245
  34.3 3.3 %collective-permute-start.8 = (bf16[128,640]{1,0:T(8,128)(2,1)S(1)}, bf16[128,640]{1,0:T(8,128)(2,1)S(1)}, u32[]{:S(2)}, u32[]{:S(2)}) collective-permute-start(bf16[128,640]{1,0:T(8,128)(2,1)S(1)} %get-tuple-element.126), channel_id=1, source_target_pairs={{0,8},{2,10},{4,12},{6,14},{8,0},{10,2},{12,4},{14,6},{1,9},{3,11}... | collective-permute-start | bytes 491528 | tf_op jit(solution)/shard_map/ppermute | solution.py:1245
  38.2 24.9 %attend.1 = (bf16[1024,1280]{1,0:T(8,128)(2,1)}, bf16[512,1280]{1,0:T(8,128)(2,1)}, bf16[1024,48]{1,0:T(8,128)(2,1)}, bf16[512,640]{1,0:T(8,128)(2,1)}, bf16[102...) custom-call(s32[5]{0:T(128)} %stack.93.place, ...), custom_call_target="tpu_custom_call" | custom-call | flops 100000000 | bytes 100000 | tf_op jit(solution)/shard_map/attend/pallas_call | solution.py:330
  63.3 3.3 %collective-permute-done.12.other_ref.ao_ref = bf16[512,1408]{1,0:T(8,128)(2,1)S(1)} collective-permute-done((bf16[512,1408]{1,0:T(8,128)(2,1)}, bf16[512,1408]{1,0:T(8,128)(2,1)S(1)}, u32[]{:S(2)}, u32[]{:S(2)}) %collective-permute-start.12) | collective-permute-done | bytes 1441824 | tf_op jit(solution)/shard_map/ppermute | solution.py:1255
  66.7 22.2 %feed.1 = (bf16[512,1280]{1,0:T(8,128)(2,1)}, bf16[512,32]{1,0:T(8,128)(2,1)}, bf16[512,2560]{1,0:T(8,128)(2,1)}, bf16[512,2560]{1,0:T(8,128)(2,1)}, bf16[512,1408]{1,0:T(8,128)(2,1)S(1)}) custom-call(s32[5]{0:T(128)} %stack.93.place, bf16[512,1408]{1,0:T(8,128)(2,1)} %get-tuple-element.139.mine_ref.am_ref, ...), custom_call_target="tpu_custom_call" | custom-call | flops 24000000000 | bytes 30000000 | tf_op jit(solution)/shard_map/feed/pallas_call | solution.py:425
  89.4 2.8 %collective-permute-done.14.other_ref = bf16[512,1408]{1,0:T(8,128)(2,1)S(1)} collective-permute-done((bf16[512,1408]{1,0:T(8,128)(2,1)S(1)}, bf16[512,1408]{1,0:T(8,128)(2,1)S(1)}, u32[]{:S(2)}, u32[]{:S(2)}) %collective-permute-start.14) | collective-permute-done | bytes 1441824 | tf_op jit(solution)/shard_map/ppermute | solution.py:1255
  92.3 28.4 %feed_back.1 = (bf16[4,128,640]{2,1,0:T(8,128)(2,1)}, f32[512,1280]{1,0:T(8,128)}, bf16[512,1280]{1,0:T(8,128)(2,1)}, bf16[2,4,2,24,640]{4,3,2,1,0:T(8,128)(2,1)}) custom-call(s32[5]{0:T(128)} %stack.93.place, bf16[512,1408]{1,0:T(8,128)(2,1)} %copy-done.4, bf16[512,1408]{1,0:T(8,128)(2,1)S(1)} %collective-permute-done.14.other_ref, ...), custom_call_target="tpu_custom_call" | custom-call | flops 30000001024 | bytes 40000000 | tf_op jit(solution)/shard_map/feed_back/pallas_call | solution.py:630
  124.0 28.4 %attend_back.1 = (bf16[512,640]{1,0:T(8,128)(2,1)}, bf16[1024,640]{1,0:T(8,128)(2,1)}, bf16[1024,640]{1,0:T(8,128)(2,1)}, f32[512,1280]{1,0:T(8,128)}, f32[16,1280]{1,0:T(8,128)}, /*index=5*/f32[16,640]{1,0:T(8,128)}) custom-call(s32[5]{0:T(128)} %stack.93.place, f32[512,1280]{1,0:T(8,128)} %get-tuple-element.150.res_ref, ...), custom_call_target="tpu_custom_call" | custom-call | flops 30000001024 | bytes 40000000 | tf_op jit(solution)/shard_map/attend_back/pallas_call | solution.py:813
  152.4 7.5 %others.1 = (bf16[1,512,640]{2,1,0:T(8,128)(2,1)}, bf16[1,512,640]{2,1,0:T(8,128)(2,1)}) custom-call(s32[5]{0:T(128)} %stack.93.place, bf16[4,2,128,640]{3,2,1,0:T(8,128)(2,1)} %bitcast.106, bf16[4,2,128,640]{3,2,1,0:T(8,128)(2,1)} %bitcast.108, bf16[3,1280,640]{2,1,0:T(8,128)(2,1)} %wv_ref.3, bf16[3,1280,640]{2,1,0:T(8,128)(2,1)} %wv_ref.3, ...), custom_call_target="tpu_custom_call" | custom-call | flops 7000000000 | bytes 10000000 | tf_op jit(solution)/shard_map/others/pallas_call | solution.py:923
  160.5 2.1 collective-permute-start.18
  162.6 1.9 collective-permute-start.19
  168.3 5.0 %grads.1 = bf16[2,4,2,16,640]{4,3,2,1,0:T(8,128)(2,1)S(1)} custom-call(s32[5]{0:T(128)S(1)} %copy-done.1, bf16[512,640]{1,0:T(8,128)(2,1)S(1)} %copy-done.10, bf16[1024,640]{1,0:T(8,128)(2,1)S(1)} %copy-done.7, bf16[1024,640]{1,0:T(8,128)(2,1)S(1)} %copy-done.8, bf16[3,16,640]{2,1,0:T(8,128)(2,1)S(1)} %copy-done.6, bf16[1024,48]{1,0:T(8,128)(2,1)S(1)} %copy-done.5, ...), custom_call_target="tpu_custom_call" | custom-call | flops 10000000000 | bytes 10000000 | tf_op jit(solution)/shard_map/grads/pallas_call | solution.py:1080
  174.0 2.4 %collective-permute-done.21 = bf16[2,128,640]{2,1,0:T(8,128)(2,1)S(1)} collective-permute-done((bf16[2,128,640]{2,1,0:T(8,128)(2,1)S(1)}, bf16[2,128,640]{2,1,0:T(8,128)(2,1)S(1)}, u32[]{:S(2)}, u32[]{:S(2)}) %collective-permute-start.21) | collective-permute-done | bytes 327712 | tf_op jit(solution)/shard_map/ppermute | solution.py:1249
  176.5 2.5 %collective-permute-start.24 = (bf16[2,128,640]{2,1,0:T(8,128)(2,1)S(1)}, bf16[2,128,640]{2,1,0:T(8,128)(2,1)S(1)}, u32[]{:S(2)}, u32[]{:S(2)}) collective-permute-start(bf16[2,128,640]{2,1,0:T(8,128)(2,1)S(1)} %pad_maximum_fusion.3), channel_id=1, source_target_pairs={{0,2},{2,0},{4,6},{6,4},{8,10},{10,8},{12,14},{14,12},{1,3},{3,1},... | collective-permute-start | bytes 983048 | tf_op jit(solution)/shard_map/ppermute | solution.py:1249
  181.4 5.8 %own.1 = (bf16[512,640]{1,0:T(8,128)(2,1)S(1)}, bf16[512,640]{1,0:T(8,128)(2,1)S(1)}) custom-call(s32[5]{0:T(128)S(1)} %copy-done.1, bf16[512,640]{1,0:T(8,128)(2,1)S(1)} %copy-done.10, bf16[4,2,128,640]{3,2,1,0:T(8,128)(2,1)S(1)} %bitcast.107, bf16[4,2,128,640]{3,2,1,0:T(8,128)(2,1)S(1)} %bitcast.109, bf16[3,1280,640]{2,1,0:T(8,128)(2,1)S(1)} %bitcast.103, ...), custom_call_target="tpu_custom_call" | custom-call | flops 7000000000 | bytes 10000000 | tf_op jit(solution)/shard_map/own/pallas_call | solution.py:986
  190.8 5.3 %collective-permute-start.30 = (bf16[160,640]{1,0:T(8,128)(2,1)S(1)}, bf16[160,640]{1,0:T(8,128)(2,1)S(1)}, u32[]{:S(2)}, u32[]{:S(2)}) collective-permute-start(bf16[160,640]{1,0:T(8,128)(2,1)S(1)} %pad_maximum_fusion.5), channel_id=1, source_target_pairs={{0,4},{2,6},{4,8},{6,10},{8,12},{10,14},{12,0},{14,2},{1,5},{3,7},... | collective-permute-start | bytes 614408 | tf_op jit(solution)/shard_map/ppermute | solution.py:1245
  201.1 2.3 %unpack_early.1 = (f32[8,2,16,40]{3,2,1,0:T(8,128)S(1)}, f32[8,16,80]{2,1,0:T(8,128)S(1)}, f32[8,16,8,20]{3,2,1,0:T(8,128)}, f32[8,2,16,8,20]{4,3,2,1,0:T(8,128)}) custom-call(s32[5]{0:T(128)S(1)} %copy-done.1, s32[2,4]{1,0:T(2,128)S(1)} %bitcast.104, bf16[176,640]{1,0:T(8,128)(2,1)S(1)} %get-tuple-element.200.refs_0_, ...), custom_call_target="tpu_custom_call" | custom-call | flops 1000000 | bytes 8000000 | tf_op jit(solution)/shard_map/unpack_early/pallas_call | solution.py:1194
  203.5 7.5 %collective-permute-done.31.refs_2_ = bf16[160,640]{1,0:T(8,128)(2,1)S(1)} collective-permute-done((bf16[160,640]{1,0:T(8,128)(2,1)S(1)}, bf16[160,640]{1,0:T(8,128)(2,1)S(1)}, u32[]{:S(2)}, u32[]{:S(2)}) %collective-permute-start.31) | collective-permute-done | bytes 204832 | tf_op jit(solution)/shard_map/ppermute | solution.py:1245
  213.3 2.2 %join.3 = f32[4,128,1280]{2,1,0:T(8,128)} custom-call(s32[5]{0:T(128)S(1)} %copy-done.1, bf16[160,640]{1,0:T(8,128)(2,1)S(1)} %pad_maximum_fusion.4.refs_0_, bf16[160,640]{1,0:T(8,128)(2,1)S(1)} %collective-permute-done.30.refs_1_, bf16[160,640]{1,0:T(8,128)(2,1)S(1)} %collective-permute-done.31.refs_2_, ...), custom_call_target="tpu_custom_call" | custom-call | flops 1000000 | bytes 8000000 | tf_op jit(solution)/shard_map/join/pallas_call | solution.py:1114
  217.8 2.0 unpack_late.1
  (171 shorter events, 40.7 us)
Async XLA Ops:
  2.8 16.4 %collective-permute-start = (bf16[136,640]{1,0:T(8,128)(2,1)S(1)}, bf16[136,640]{1,0:T(8,128)(2,1)S(1)}, u32[]{:S(2)}, u32[]{:S(2)}) collective-permute-start(bf16[136,640]{1,0:T(8,128)(2,1)S(1)} %pad_maximum_fusion.9), channel_id=1, source_target_pairs={{0,4},{2,6},{4,8},{6,10},{8,12},{10,14},{12,0},{14,2},{1,5},{3,7},... | collective-permute-start | bytes 522248 | tf_op jit(solution)/shard_map/ppermute | solution.py:1245
  6.0 14.0 %collective-permute-start.1 = (bf16[136,640]{1,0:T(8,128)(2,1)S(1)}, bf16[136,640]{1,0:T(8,128)(2,1)S(1)}, u32[]{:S(2)}, u32[]{:S(2)}) collective-permute-start(bf16[136,640]{1,0:T(8,128)(2,1)S(1)} %pad_maximum_fusion.10), channel_id=1, source_target_pairs={{0,8},{2,10},{4,12},{6,14},{8,0},{10,2},{12,4},{14,6},{1,9},{3,11}... | collective-permute-start | bytes 522248 | tf_op jit(solution)/shard_map/ppermute | solution.py:1245
  8.6 11.3 %collective-permute-start.2 = (bf16[136,640]{1,0:T(8,128)(2,1)S(1)}, bf16[136,640]{1,0:T(8,128)(2,1)S(1)}, u32[]{:S(2)}, u32[]{:S(2)}) collective-permute-start(bf16[136,640]{1,0:T(8,128)(2,1)S(1)} %pad_maximum_fusion.11), channel_id=1, source_target_pairs={{0,12},{2,14},{4,0},{6,2},{8,4},{10,6},{12,8},{14,10},{1,13},{3,15... | collective-permute-start | bytes 522248 | tf_op jit(solution)/shard_map/ppermute | solution.py:1245
  10.0 9.2 %collective-permute-start.3 = (s32[4]{0:T(128)S(1)}, s32[4]{0:T(128)S(1)}, u32[]{:S(2)}, u32[]{:S(2)}) collective-permute-start(s32[4]{0:T(128)S(1)} %copy-done.19), channel_id=1, source_target_pairs={{0,16},{16,0},{1,17},{17,1},{2,18},{18,2},{3,19},{19,3},{4,20},{20... | collective-permute-start | bytes 56 | tf_op jit(solution)/shard_map/ppermute | solution.py:1252
  11.6 8.4 %collective-permute-start.4 = (bf16[136,640]{1,0:T(8,128)(2,1)S(1)}, bf16[136,640]{1,0:T(8,128)(2,1)S(1)}, u32[]{:S(2)}, u32[]{:S(2)}) collective-permute-start(bf16[136,640]{1,0:T(8,128)(2,1)S(1)} %pad_maximum_fusion.8.refs_1_), channel_id=1, source_target_pairs={{0,2},{2,0},{4,6},{6,4},{8,10},{10,8},{12,14},{14,12},{1,3},{3,1},... | collective-permute-start | bytes 522248 | tf_op jit(solution)/shard_map/ppermute | solution.py:1249
  20.0 13.8 %collective-permute-start.5 = (bf16[3,136,640]{2,1,0:T(8,128)(2,1)S(1)}, bf16[3,136,640]{2,1,0:T(8,128)(2,1)S(1)}, u32[]{:S(2)}, u32[]{:S(2)}) collective-permute-start(bf16[3,136,640]{2,1,0:T(8,128)(2,1)S(1)} %pad_maximum_fusion.refs_2_), channel_id=1, source_target_pairs={{0,2},{2,0},{4,6},{6,4},{8,10},{10,8},{12,14},{14,12},{1,3},{3,1},... | collective-permute-start | bytes 1566728 | tf_op jit(solution)/shard_map/ppermute | solution.py:1249
  21.6 10.1 %collective-permute-start.6 = (bf16[128,640]{1,0:T(8,128)(2,1)S(1)}, bf16[128,640]{1,0:T(8,128)(2,1)S(1)}, u32[]{:S(2)}, u32[]{:S(2)}) collective-permute-start(bf16[128,640]{1,0:T(8,128)(2,1)S(1)} %get-tuple-element.123), channel_id=1, source_target_pairs={{0,4},{2,6},{4,8},{6,10},{8,12},{10,14},{12,0},{14,2},{1,5},{3,7},... | collective-permute-start | bytes 491528 | tf_op jit(solution)/shard_map/ppermute | solution.py:1245
  25.8 7.6 %collective-permute-start.7 = (bf16[128,640]{1,0:T(8,128)(2,1)S(1)}, bf16[128,640]{1,0:T(8,128)(2,1)S(1)}, u32[]{:S(2)}, u32[]{:S(2)}) collective-permute-start(bf16[128,640]{1,0:T(8,128)(2,1)S(1)} %get-tuple-element.124), channel_id=1, source_target_pairs={{0,12},{2,14},{4,0},{6,2},{8,4},{10,6},{12,8},{14,10},{1,13},{3,15... | collective-permute-start | bytes 491528 | tf_op jit(solution)/shard_map/ppermute | solution.py:1245
  26.9 11.3 %collective-permute-start.9 = (bf16[3,136,640]{2,1,0:T(8,128)(2,1)S(1)}, bf16[3,136,640]{2,1,0:T(8,128)(2,1)S(1)}, u32[]{:S(2)}, u32[]{:S(2)}) collective-permute-start(bf16[3,136,640]{2,1,0:T(8,128)(2,1)S(1)} %pad_maximum_fusion.refs_2_), channel_id=1, source_target_pairs={{0,1},{1,0},{2,3},{3,2},{4,5},{5,4},{6,7},{7,6},{8,9},{9,8},{10,11... | collective-permute-start | bytes 1566728 | tf_op jit(solution)/shard_map/ppermute | solution.py:1255
  34.3 28.8 %collective-permute-start.8 = (bf16[128,640]{1,0:T(8,128)(2,1)S(1)}, bf16[128,640]{1,0:T(8,128)(2,1)S(1)}, u32[]{:S(2)}, u32[]{:S(2)}) collective-permute-start(bf16[128,640]{1,0:T(8,128)(2,1)S(1)} %get-tuple-element.126), channel_id=1, source_target_pairs={{0,8},{2,10},{4,12},{6,14},{8,0},{10,2},{12,4},{14,6},{1,9},{3,11}... | collective-permute-start | bytes 491528 | tf_op jit(solution)/shard_map/ppermute | solution.py:1245
  66.6 22.4 %collective-permute-start.13 = (bf16[3,128,640]{2,1,0:T(8,128)(2,1)S(1)}, bf16[3,128,640]{2,1,0:T(8,128)(2,1)S(1)}, u32[]{:S(2)}, u32[]{:S(2)}) collective-permute-start(bf16[3,128,640]{2,1,0:T(8,128)(2,1)S(1)} %pad_maximum_fusion.1.g_mine_ref), channel_id=1, source_target_pairs={{0,1},{1,0},{2,3},{3,2},{4,5},{5,4},{6,7},{7,6},{8,9},{9,8},{10,11... | collective-permute-start | bytes 1474568 | tf_op jit(solution)/shard_map/ppermute | solution.py:1255
  122.1 30.3 %collective-permute-start.15 = (bf16[4,2,24,640]{3,2,1,0:T(8,128)(2,1)S(1)}, bf16[4,2,24,640]{3,2,1,0:T(8,128)(2,1)S(1)}, u32[]{:S(2)}, u32[]{:S(2)}) collective-permute-start(bf16[4,2,24,640]{3,2,1,0:T(8,128)(2,1)S(1)} %dynamic-slice_bitcast_fusion), channel_id=1, source_target_pairs={{0,2},{2,0},{4,6},{6,4},{8,10},{10,8},{12,14},{14,12},{1,3},{3,1},... | collective-permute-start | bytes 737288 | tf_op jit(solution)/shard_map/ppermute | solution.py:1249
  159.9 5.2 %collective-permute-start.17 = (bf16[1,512,640]{2,1,0:T(8,128)(2,1)}, bf16[1,512,640]{2,1,0:T(8,128)(2,1)S(1)}, u32[]{:S(2)}, u32[]{:S(2)}) collective-permute-start(bf16[1,512,640]{2,1,0:T(8,128)(2,1)} %get-tuple-element.167), channel_id=1, source_target_pairs={{0,1},{1,0},{2,3},{3,2},{4,5},{5,4},{6,7},{7,6},{8,9},{9,8},{10,11... | collective-permute-start | bytes 1966088 | tf_op jit(solution)/shard_map/ppermute | solution.py:1255
  160.5 18.5 %collective-permute-start.18 = (bf16[176,640]{1,0:T(8,128)(2,1)S(1)}, bf16[176,640]{1,0:T(8,128)(2,1)S(1)}, u32[]{:S(2)}, u32[]{:S(2)}) collective-permute-start(bf16[176,640]{1,0:T(8,128)(2,1)S(1)} %get-tuple-element.243), channel_id=1, source_target_pairs={{0,4},{2,6},{4,8},{6,10},{8,12},{10,14},{12,0},{14,2},{1,5},{3,7},... | collective-permute-start | bytes 675848 | tf_op jit(solution)/shard_map/ppermute | solution.py:1245
  162.6 17.1 %collective-permute-start.19 = (bf16[176,640]{1,0:T(8,128)(2,1)S(1)}, bf16[176,640]{1,0:T(8,128)(2,1)S(1)}, u32[]{:S(2)}, u32[]{:S(2)}) collective-permute-start(bf16[176,640]{1,0:T(8,128)(2,1)S(1)} %get-tuple-element.244), channel_id=1, source_target_pairs={{0,8},{2,10},{4,12},{6,14},{8,0},{10,2},{12,4},{14,6},{1,9},{3,11}... | collective-permute-start | bytes 675848 | tf_op jit(solution)/shard_map/ppermute | solution.py:1245
  164.5 15.2 %collective-permute-start.20 = (bf16[176,640]{1,0:T(8,128)(2,1)S(1)}, bf16[176,640]{1,0:T(8,128)(2,1)S(1)}, u32[]{:S(2)}, u32[]{:S(2)}) collective-permute-start(bf16[176,640]{1,0:T(8,128)(2,1)S(1)} %get-tuple-element.241), channel_id=1, source_target_pairs={{0,12},{2,14},{4,0},{6,2},{8,4},{10,6},{12,8},{14,10},{1,13},{3,15... | collective-permute-start | bytes 675848 | tf_op jit(solution)/shard_map/ppermute | solution.py:1245
  166.6 9.7 %collective-permute-start.21 = (bf16[2,128,640]{2,1,0:T(8,128)(2,1)S(1)}, bf16[2,128,640]{2,1,0:T(8,128)(2,1)S(1)}, u32[]{:S(2)}, u32[]{:S(2)}) collective-permute-start(bf16[2,128,640]{2,1,0:T(8,128)(2,1)S(1)} %pad_maximum_fusion.2), channel_id=1, source_target_pairs={{0,2},{2,0},{4,6},{6,4},{8,10},{10,8},{12,14},{14,12},{1,3},{3,1},... | collective-permute-start | bytes 983048 | tf_op jit(solution)/shard_map/ppermute | solution.py:1249
  173.4 13.8 %collective-permute-start.22 = (bf16[4,2,16,640]{3,2,1,0:T(8,128)(2,1)S(1)}, bf16[4,2,16,640]{3,2,1,0:T(8,128)(2,1)S(1)}, u32[]{:S(2)}, u32[]{:S(2)}) collective-permute-start(bf16[4,2,16,640]{3,2,1,0:T(8,128)(2,1)S(1)} %get-tuple-element.250), channel_id=1, source_target_pairs={{0,2},{2,0},{4,6},{6,4},{8,10},{10,8},{12,14},{14,12},{1,3},{3,1},... | collective-permute-start | bytes 491528 | tf_op jit(solution)/shard_map/ppermute | solution.py:1249
  176.5 10.8 %collective-permute-start.24 = (bf16[2,128,640]{2,1,0:T(8,128)(2,1)S(1)}, bf16[2,128,640]{2,1,0:T(8,128)(2,1)S(1)}, u32[]{:S(2)}, u32[]{:S(2)}) collective-permute-start(bf16[2,128,640]{2,1,0:T(8,128)(2,1)S(1)} %pad_maximum_fusion.3), channel_id=1, source_target_pairs={{0,2},{2,0},{4,6},{6,4},{8,10},{10,8},{12,14},{14,12},{1,3},{3,1},... | collective-permute-start | bytes 983048 | tf_op jit(solution)/shard_map/ppermute | solution.py:1249
  179.8 7.4 %collective-permute-start.23 = (bf16[4,24,640]{2,1,0:T(8,128)(2,1)S(1)}, bf16[4,24,640]{2,1,0:T(8,128)(2,1)S(1)}, u32[]{:S(2)}, u32[]{:S(2)}) collective-permute-start(bf16[4,24,640]{2,1,0:T(8,128)(2,1)S(1)} %pad_maximum_fusion.12), channel_id=1, source_target_pairs={{0,16},{16,0},{1,17},{17,1},{2,18},{18,2},{3,19},{19,3},{4,20},{20... | collective-permute-start | bytes 368648 | tf_op jit(solution)/shard_map/ppermute | solution.py:1252
  190.7 10.4 %collective-permute-start.33 = (bf16[4,24,640]{2,1,0:T(8,128)(2,1)S(1)}, bf16[4,24,640]{2,1,0:T(8,128)(2,1)S(1)}, u32[]{:S(2)}, u32[]{:S(2)}) collective-permute-start(bf16[4,24,640]{2,1,0:T(8,128)(2,1)S(1)} %collective-permute-done.23.refs_8_), channel_id=1, source_target_pairs={{0,1},{1,0},{2,3},{3,2},{4,5},{5,4},{6,7},{7,6},{8,9},{9,8},{10,11... | collective-permute-start | bytes 368648 | tf_op jit(solution)/shard_map/ppermute | solution.py:1255
  190.8 12.6 %collective-permute-start.30 = (bf16[160,640]{1,0:T(8,128)(2,1)S(1)}, bf16[160,640]{1,0:T(8,128)(2,1)S(1)}, u32[]{:S(2)}, u32[]{:S(2)}) collective-permute-start(bf16[160,640]{1,0:T(8,128)(2,1)S(1)} %pad_maximum_fusion.5), channel_id=1, source_target_pairs={{0,4},{2,6},{4,8},{6,10},{8,12},{10,14},{12,0},{14,2},{1,5},{3,7},... | collective-permute-start | bytes 614408 | tf_op jit(solution)/shard_map/ppermute | solution.py:1245
  196.1 14.8 %collective-permute-start.31 = (bf16[160,640]{1,0:T(8,128)(2,1)S(1)}, bf16[160,640]{1,0:T(8,128)(2,1)S(1)}, u32[]{:S(2)}, u32[]{:S(2)}) collective-permute-start(bf16[160,640]{1,0:T(8,128)(2,1)S(1)} %pad_maximum_fusion.6), channel_id=1, source_target_pairs={{0,8},{2,10},{4,12},{6,14},{8,0},{10,2},{12,4},{14,6},{1,9},{3,11}... | collective-permute-start | bytes 614408 | tf_op jit(solution)/shard_map/ppermute | solution.py:1245
  197.0 13.9 %collective-permute-start.32 = (bf16[160,640]{1,0:T(8,128)(2,1)S(1)}, bf16[160,640]{1,0:T(8,128)(2,1)S(1)}, u32[]{:S(2)}, u32[]{:S(2)}) collective-permute-start(bf16[160,640]{1,0:T(8,128)(2,1)S(1)} %pad_maximum_fusion.7), channel_id=1, source_target_pairs={{0,12},{2,14},{4,0},{6,2},{8,4},{10,6},{12,8},{14,10},{1,13},{3,15... | collective-permute-start | bytes 614408 | tf_op jit(solution)/shard_map/ppermute | solution.py:1245
  (39 other events, 271.6 us)
